TPU v7x, 256 devices: a whole 4x4x8 slice. The times are simulated.
256 devices in a mesh: row: 32 (over z_lo, x, core), col: 8 (over z_hi, y).
Axes of the slice: x: 4, y: 4, z: 8 (z_hi: 2, z_lo: 4; z = z_hi * 4 + z_lo), core: 2. Of those that a mesh axis runs over, the one named last changes fastest.
Arguments:
- sequence_embedding: float32 [128, 512, 256], P('row', 'col'), may hold values from -6 to 6
- standardize_scale: float32 [256], replicated, may hold values from 0.25 to 1.75
- standardize_offset: float32 [256], replicated, may hold values from -0.5 to 0.5
- first_operand_matrix: float32 [256, 32], replicated, may hold values from -0.375 to 0.375
- first_operand_intercept: float32 [32], replicated, may hold values from -0.5 to 0.5
- second_operand_matrix: float32 [256, 32], replicated, may hold values from -0.375 to 0.375
- second_operand_intercept: float32 [32], replicated, may hold values from -0.5 to 0.5
- result_matrix: float32 [1024, 128], replicated, may hold values from -2 to 2
- result_intercept: float32 [128], replicated, may hold values from -0.5 to 0.5
- edge_incoming_sensitivity: float32 [512, 512, 128], P('row', 'col'), may hold values from -6 to 6
Outputs:
- pair_output_update: float32 [512, 512, 128], P('row', 'col')
- alignment_gradient: float32 [128, 512, 256], P('row', 'col')
- projection_gradient: float32 [1024, 128], P(('row', 'col'))
All inputs are finite; a program needn't handle non-finite values.
Results may differ from a plain program's by a relative error of at most 0.0001.
Values sent between devices are 32-bit elements; how exact they have to be, the bound alone decides.
No kernel may reach another device: no remote copies, remote signals or barrier semaphores. Data moves between devices by JAX's collectives and lax.ppermute only.
A program may use at most 64 MiB of HBM per device.

v0:
```python
import math

import jax
import jax.numpy as jnp
from jax import lax
from jax.sharding import PartitionSpec as P

precise = lax.Precision.HIGHEST


def laid_out(pieces, dim):
    pieces = jnp.moveaxis(pieces, 0, dim)
    dims = pieces.shape
    return pieces.reshape(*dims[:dim], dims[dim] * dims[dim + 1], *dims[dim + 2 :])


def copy_for_each(array, axis):
    peers = lax.axis_size(axis)
    return lax.all_to_all(
        jnp.broadcast_to(array[None], (peers, *array.shape)), axis, 0, 0, tiled=True
    )


def gathered_copies(array, axis, dim):
    return laid_out(copy_for_each(array, axis), dim)


def in_blocks(array, dim, peers):
    before, after = (array.shape[:dim], array.shape[dim + 1 :])
    return jnp.moveaxis(array.reshape(*before, peers, -1, *after), dim, 0)


def sum_at_owner(array, axis, dim):
    pieces = in_blocks(array, dim, lax.axis_size(axis))
    arrived = lax.all_to_all(pieces, axis, split_axis=0, concat_axis=0, tiled=True)
    return arrived.sum(axis=0)


def linear_transform(
    sequence_embedding,
    standardize_scale,
    standardize_offset,
    first_operand_matrix,
    first_operand_intercept,
    second_operand_matrix,
    second_operand_intercept,
):
    average_feature = jnp.mean(sequence_embedding, axis=-1, keepdims=True)
    demeaned_features = sequence_embedding - average_feature
    variance = jnp.mean(demeaned_features * demeaned_features, axis=-1, keepdims=True)
    normed = (
        demeaned_features * lax.rsqrt(variance + 1e-05) * standardize_scale + standardize_offset
    )
    first_operand_entries = (
        jnp.einsum("src,cd->srd", normed, first_operand_matrix, precision=precise)
        + first_operand_intercept
    )
    second_operand_entries = (
        jnp.einsum("src,cd->srd", normed, second_operand_matrix, precision=precise)
        + second_operand_intercept
    )
    return (first_operand_entries, second_operand_entries)


def tile_work(left_all, right_all, result_matrix, result_intercept, edge_incoming_sensitivity):
    rows_all, tile_i, chans = left_all.shape
    tile_j = right_all.shape[1]
    pair_ch = result_matrix.shape[1]
    block_rows = math.gcd(tile_i, 8)
    num_blocks = tile_i // block_rows
    left_blocks = left_all.reshape(rows_all, num_blocks, block_rows, chans).transpose(1, 0, 2, 3)
    cot_blocks = edge_incoming_sensitivity.reshape(num_blocks, block_rows, tile_j, pair_ch)

    def tile_step(carry, inputs):
        summed_weight, right_sum = carry
        left_blk, cot_blk = inputs
        products = jnp.einsum("sic,sje->ijce", left_blk, right_all, precision=precise)
        products = products.reshape(block_rows, tile_j, chans * chans)
        pair_blk = (
            jnp.einsum("ijk,kh->ijh", products, result_matrix, precision=precise) / rows_all
            + result_intercept
        )
        grad_outer = jnp.einsum("ijh,kh->ijk", cot_blk, result_matrix, precision=precise) / rows_all
        grad_outer = grad_outer.reshape(block_rows, tile_j, chans, chans)
        summed_weight = summed_weight + jnp.einsum(
            "ijk,ijh->kh", products, cot_blk, precision=precise
        )
        left_factor_gradient = jnp.einsum("ijce,sje->sic", grad_outer, right_all, precision=precise)
        right_sum = right_sum + jnp.einsum("sic,ijce->sje", left_blk, grad_outer, precision=precise)
        return ((summed_weight, right_sum), (pair_blk, left_factor_gradient))

    initial = (
        jnp.zeros((chans * chans, pair_ch), jnp.float32),
        jnp.zeros(right_all.shape, jnp.float32),
    )
    (summed_weight, right_sum), (pair_blocks, left_grads) = lax.scan(
        tile_step, initial, (left_blocks, cot_blocks)
    )
    pair_tile = pair_blocks.reshape(tile_i, tile_j, pair_ch)
    left_factor_gradient = left_grads.transpose(1, 0, 2, 3).reshape(rows_all, tile_i, chans)
    return (pair_tile, left_factor_gradient, summed_weight, right_sum)


def local(
    sequence_embedding,
    standardize_scale,
    standardize_offset,
    first_operand_matrix,
    first_operand_intercept,
    second_operand_matrix,
    second_operand_intercept,
    result_matrix,
    result_intercept,
    edge_incoming_sensitivity,
):

    def device_portion(values):
        return linear_transform(
            values,
            standardize_scale,
            standardize_offset,
            first_operand_matrix,
            first_operand_intercept,
            second_operand_matrix,
            second_operand_intercept,
        )

    (first_operand_portion, second_operand_portion), reverse_derivative = jax.vjp(
        device_portion, sequence_embedding
    )
    col_count = lax.axis_size("col")
    right_all = gathered_copies(second_operand_portion, "row", 0)
    widened = gathered_copies(first_operand_portion, "col", 1)
    left_all = lax.all_to_all(widened, "row", split_axis=1, concat_axis=0, tiled=True)
    pair_output_update, left_factor_gradient, summed_weight, right_sum = tile_work(
        left_all, right_all, result_matrix, result_intercept, edge_incoming_sensitivity
    )
    swapped = lax.all_to_all(left_factor_gradient, "row", split_axis=0, concat_axis=1, tiled=True)
    left_backprop = sum_at_owner(swapped, "col", 1)
    right_backprop = lax.psum_scatter(right_sum, "row", scatter_dimension=0, tiled=True)
    alignment_gradient = reverse_derivative((left_backprop, right_backprop))[0]
    res_total = right_all.shape[1] * col_count
    projection_gradient = (
        lax.psum_scatter(summed_weight, ("row", "col"), scatter_dimension=0, tiled=True) / res_total
    )
    return (pair_output_update, alignment_gradient, projection_gradient)


def solution(mesh):
    return jax.shard_map(
        local,
        mesh=mesh,
        in_specs=(
            P("row", "col", None),
            P(),
            P(),
            P(),
            P(),
            P(),
            P(),
            P(),
            P(),
            P("row", "col", None),
        ),
        out_specs=(P("row", "col", None), P("row", "col", None), P(("row", "col"), None)),
        check_vma=False,
    )
```

profile of v0, /device:TPU:32, one launch (start us, length us, event | category | flops | bytes accessed | tf_op | source)
XLA Modules:
  0.0 459.7 jit_solution(7254760447920322402)
XLA Ops:
  10.4 1.5 convolution_add_fusion.2
  12.3 23.9 %all_to_all.45 = f32[8,1,8192]{2,1,0:T(1,128)S(1)} all-to-all(f32[8,1,8192]{2,1,0:T(1,128)S(1)} %reshape.83), channel_id=1, replica_groups=mesh['row'=32,'col'=8] {'col'}, dimensions={0} | all-to-all | bytes 524288 | tf_op jit(solution)/shard_map/all_to_all | solution.py:19
  38.7 1.4 reshape.85
  40.1 6.4 %all-to-all-start.1 = ((f32[32,1,2048]{2,1,0:T(1,128)}), f32[32,1,2048]{2,1,0:T(1,128)S(1)}, u32[]{:S(2)}, u32[]{:S(2)}) async-start(f32[32,1,2048]{2,1,0:T(1,128)} %reshape.85), calls=%async_computation.1 | async-start | bytes 524288 | tf_op jit(solution)/shard_map/all_to_all | solution.py:134
  47.3 2.3 reshape.87
  49.6 6.9 %all-to-all-done.1 = f32[32,1,2048]{2,1,0:T(1,128)S(1)} async-done(((f32[32,1,2048]{2,1,0:T(1,128)}), f32[32,1,2048]{2,1,0:T(1,128)S(1)}, u32[]{:S(2)}, u32[]{:S(2)}) %all-to-all-start.1) | async-done | bytes 262176 | tf_op jit(solution)/shard_map/all_to_all | solution.py:134
  56.5 4.9 %all-to-all-start.2 = ((f32[32,1,8192]{2,1,0:T(1,128)}), f32[32,1,8192]{2,1,0:T(1,128)S(1)}, u32[]{:S(2)}, u32[]{:S(2)}) async-start(f32[32,1,8192]{2,1,0:T(1,128)} %reshape.87), calls=%async_computation.2 | async-start | bytes 2097152 | tf_op jit(solution)/shard_map/all_to_all | solution.py:19
  65.0 22.0 %all-to-all-done.2 = f32[32,1,8192]{2,1,0:T(1,128)S(1)} async-done(((f32[32,1,8192]{2,1,0:T(1,128)}), f32[32,1,8192]{2,1,0:T(1,128)S(1)}, u32[]{:S(2)}, u32[]{:S(2)}) %all-to-all-start.2) | async-done | bytes 1048608 | tf_op jit(solution)/shard_map/all_to_all | solution.py:19
  87.0 3.2 reduce.2
  91.1 1.3 copy.42
  92.3 107.2 %while.17 = (s32[]{:T(128)}, f32[1024,128]{1,0:T(8,128)}, f32[128,64,32]{0,1,2:T(8,128)}, f32[2,8,64,128]{3,2,1,0:T(8,128)}, f32[2,128,8,32]{1,3,2,0:T(8,128)}, ...) while((s32[]{:T(128)}, f32[1024,128]{1,0:T(8,128)}, ...), condition=%wide.region_3.4_spmd.clone, body=%wide.region_2.3_spmd.clone.sunk | while | flops 4833280000 | bytes 65143736 | solution.py:96
  112.9 2.9 convolution_multiply_fusion.3
  115.8 2.7 copy.77
  118.5 8.6 %fusion.89 = f32[2,128,8,32]{1,3,2,0:T(8,128)} fusion(f32[2,128,8,32]{1,3,2,0:T(8,128)} %get-tuple-element.214, s32[]{:T(128)S(6)} %copy.85, f32[8,64,32,32]{1,3,2,0:T(8,128)} %bitcast.133, f32[128,64,32]{0,1,2:T(8,128)S(1)} %get-tuple-element.228), kind=kOutput, calls=%fused_computation.15.clone.1 | convolution fusion | flops 805306368 | bytes 5373956 | tf_op jit(solution)/shard_map/while/body/eval_jaxpr/ijce,sje->sic/dot_general | solution.py:88
  127.1 9.5 %fusion.87 = f32[128,64,32]{0,1,2:T(8,128)S(1)} fusion(f32[8,64,32,32]{1,3,2,0:T(8,128)S(1)} %bitcast.134, f32[128,64,32]{0,1,2:T(8,128)S(1)} %copy-done.3, pred[]{:T(512)S(6)} %compare.3, f32[2,128,8,32]{1,3,2,0:T(8,128)} %get-tuple-element.227, s32[]{:T(128)S(6)} %copy.85), kind=kOutput, calls=%fused_computation.7.clone.1 | convolution fusion | flops 805830656 | bytes 4325381 | tf_op jit(solution)/shard_map/while/body/eval_jaxpr/sic,ijce->sje/dot_general | solution.py:89
  136.7 3.4 convolution_bitcast_fusion.3
  140.2 2.4 copy.76
  142.6 3.6 fusion.86
  146.3 6.7 %fusion.88 = f32[2,8,64,128]{3,2,1,0:T(8,128)S(1)} fusion(f32[2,8,64,128]{3,2,1,0:T(8,128)S(1)} %copy-done.16, s32[]{:T(128)S(6)} %copy.85, f32[8,64,1024]{1,2,0:T(8,128)S(1)} %bitcast.132, f32[1024,128]{1,0:T(8,128)S(1)} %copy-done.2, f32[128]{0:T(128)S(1)} %get-tuple-element.231), kind=kOutput, calls=%fused_computation.13.clone.1 | convolution fusion | flops 805437440 | bytes 4981252 | tf_op jit(solution)/shard_map/while/body/eval_jaxpr/ijk,kh->ijh/dot_general | solution.py:80
  153.8 2.9 convolution_multiply_fusion.3
  156.7 2.7 copy.77
  159.4 8.6 %fusion.89 = f32[2,128,8,32]{1,3,2,0:T(8,128)} fusion(f32[2,128,8,32]{1,3,2,0:T(8,128)} %get-tuple-element.214, s32[]{:T(128)S(6)} %copy.85, f32[8,64,32,32]{1,3,2,0:T(8,128)} %bitcast.133, f32[128,64,32]{0,1,2:T(8,128)S(1)} %get-tuple-element.228), kind=kOutput, calls=%fused_computation.15.clone.1 | convolution fusion | flops 805306368 | bytes 5373956 | tf_op jit(solution)/shard_map/while/body/eval_jaxpr/ijce,sje->sic/dot_general | solution.py:88
  168.0 9.5 %fusion.87 = f32[128,64,32]{0,1,2:T(8,128)S(1)} fusion(f32[8,64,32,32]{1,3,2,0:T(8,128)S(1)} %bitcast.134, f32[128,64,32]{0,1,2:T(8,128)S(1)} %copy-done.3, pred[]{:T(512)S(6)} %compare.3, f32[2,128,8,32]{1,3,2,0:T(8,128)} %get-tuple-element.227, s32[]{:T(128)S(6)} %copy.85), kind=kOutput, calls=%fused_computation.7.clone.1 | convolution fusion | flops 805830656 | bytes 4325381 | tf_op jit(solution)/shard_map/while/body/eval_jaxpr/sic,ijce->sje/dot_general | solution.py:89
  177.6 3.4 convolution_bitcast_fusion.3
  181.1 2.4 copy.76
  183.5 3.6 fusion.86
  187.2 6.7 %fusion.88 = f32[2,8,64,128]{3,2,1,0:T(8,128)S(1)} fusion(f32[2,8,64,128]{3,2,1,0:T(8,128)S(1)} %copy-done.16, s32[]{:T(128)S(6)} %copy.85, f32[8,64,1024]{1,2,0:T(8,128)S(1)} %bitcast.132, f32[1024,128]{1,0:T(8,128)S(1)} %copy-done.2, f32[128]{0:T(128)S(1)} %get-tuple-element.231), kind=kOutput, calls=%fused_computation.13.clone.1 | convolution fusion | flops 805437440 | bytes 4981252 | tf_op jit(solution)/shard_map/while/body/eval_jaxpr/ijk,kh->ijh/dot_general | solution.py:80
  199.7 4.1 copy.43
  204.7 16.8 %all_to_all.46 = f32[32,1,2048]{2,1,0:T(1,128)S(1)} all-to-all(f32[32,1,2048]{2,1,0:T(1,128)S(1)} %reshape.89), channel_id=1, replica_groups=mesh['row'=32,'col'=8] {'row'}, dimensions={0} | all-to-all | bytes 524288 | tf_op jit(solution)/shard_map/all_to_all | solution.py:138
  224.6 3.4 all-to-all-start.4
  228.0 218.2 %all-reduce.3.cloned.1.call-done = f32[1024,128]{1,0:T(8,128)} async-done(((f32[1024,128]{1,0:T(8,128)}), f32[1024,128]{1,0:T(8,128)}) %all-reduce.3.cloned.1.call-update) | async-done | bytes 524304
  446.2 1.3 dynamic-slice_multiply_fusion
  (101 shorter events, 20.5 us)
Async XLA Ops:
  8.0 2.4 copy-start
  9.1 37.4 %copy-start.8 = (f32[4,64,256]{2,1,0:T(8,128)S(1)}, f32[4,64,256]{2,1,0:T(8,128)}, u32[]{:S(2)}) copy-start(f32[4,64,256]{2,1,0:T(8,128)} %param.12) | copy-start | bytes 786436
  9.1 37.4 %copy-start.11 = (f32[256,32]{0,1:T(8,128)S(1)}, f32[256,32]{0,1:T(8,128)}, u32[]{:S(2)}) copy-start(f32[256,32]{0,1:T(8,128)} %param.17) | copy-start | bytes 98308
  9.1 37.4 %copy-start.13 = (f32[256]{0:T(256)S(1)}, f32[256]{0:T(256)}, u32[]{:S(2)}) copy-start(f32[256]{0:T(256)} %param.13) | copy-start | bytes 3076
  9.1 37.4 %copy-start.14 = (f32[256]{0:T(256)S(1)}, f32[256]{0:T(256)}, u32[]{:S(2)}) copy-start(f32[256]{0:T(256)} %param.14) | copy-start | bytes 3076
  9.1 37.4 %copy-start.15 = (f32[32]{0:T(128)S(1)}, f32[32]{0:T(128)}, u32[]{:S(2)}) copy-start(f32[32]{0:T(128)} %param.18) | copy-start | bytes 388
  40.1 16.4 %all-to-all-start.1 = ((f32[32,1,2048]{2,1,0:T(1,128)}), f32[32,1,2048]{2,1,0:T(1,128)S(1)}, u32[]{:S(2)}, u32[]{:S(2)}) async-start(f32[32,1,2048]{2,1,0:T(1,128)} %reshape.85), calls=%async_computation.1 | async-start | bytes 524288 | tf_op jit(solution)/shard_map/all_to_all | solution.py:134
  56.5 30.5 %all-to-all-start.2 = ((f32[32,1,8192]{2,1,0:T(1,128)}), f32[32,1,8192]{2,1,0:T(1,128)S(1)}, u32[]{:S(2)}, u32[]{:S(2)}) async-start(f32[32,1,8192]{2,1,0:T(1,128)} %reshape.87), calls=%async_computation.2 | async-start | bytes 2097152 | tf_op jit(solution)/shard_map/all_to_all | solution.py:19
  61.4 384.8 %all-reduce.3.cloned.1.call-start = ((), (), s32[]{:S(2)}) async-start(), calls=%async_computation.7 | async-start | bytes 1048576
  65.0 27.3 %copy-start.12 = (f32[128]{0:T(128)S(1)}, f32[128]{0:T(128)}, u32[]{:S(2)}) copy-start(f32[128]{0:T(128)} %param.20) | copy-start | bytes 1540
  118.5 8.7 %copy-start.1 = (f32[8,64,1024]{1,2,0:T(8,128)S(1)}, f32[8,64,1024]{1,2,0:T(8,128)}, u32[]{:S(2)}) copy-start(f32[8,64,1024]{1,2,0:T(8,128)} %copy.77) | copy-start | bytes 6291460 | tf_op jit(solution)/shard_map/while
  118.5 8.7 %copy-start.3 = (f32[128,64,32]{0,1,2:T(8,128)S(1)}, f32[128,64,32]{0,1,2:T(8,128)}, u32[]{:S(2)}) copy-start(f32[128,64,32]{0,1,2:T(8,128)} %get-tuple-element.212) | copy-start | bytes 3145732 | tf_op jit(solution)/shard_map/while
  127.1 9.5 %copy-start.9 = (f32[2,128,8,32]{1,3,2,0:T(8,128)S(1)}, f32[2,128,8,32]{1,3,2,0:T(8,128)}, u32[]{:S(2)}) copy-start(f32[2,128,8,32]{1,3,2,0:T(8,128)} %get-tuple-element.227) | copy-start | bytes 786436 | tf_op jit(solution)/shard_map/while
  136.7 5.9 %copy-start.4 = (f32[128,64,32]{0,1,2:T(8,128)}, f32[128,64,32]{0,1,2:T(8,128)S(1)}, u32[]{:S(2)}) copy-start(f32[128,64,32]{0,1,2:T(8,128)S(1)} %fusion.87) | copy-start | bytes 3145732 | tf_op jit(solution)/shard_map/while
  140.2 2.4 copy-start.5
  140.2 2.4 copy-start.7
  142.6 3.7 copy-start.2
  142.6 3.7 copy-start.16
  146.3 6.7 %copy-start.6 = (f32[1024,128]{1,0:T(8,128)}, f32[1024,128]{1,0:T(8,128)S(1)}, u32[]{:S(2)}) copy-start(f32[1024,128]{1,0:T(8,128)S(1)} %fusion.86) | copy-start | bytes 1572868 | tf_op jit(solution)/shard_map/while
  153.0 0.8 copy-start.17
  159.4 8.7 %copy-start.1 = (f32[8,64,1024]{1,2,0:T(8,128)S(1)}, f32[8,64,1024]{1,2,0:T(8,128)}, u32[]{:S(2)}) copy-start(f32[8,64,1024]{1,2,0:T(8,128)} %copy.77) | copy-start | bytes 6291460 | tf_op jit(solution)/shard_map/while
  159.4 8.7 %copy-start.3 = (f32[128,64,32]{0,1,2:T(8,128)S(1)}, f32[128,64,32]{0,1,2:T(8,128)}, u32[]{:S(2)}) copy-start(f32[128,64,32]{0,1,2:T(8,128)} %get-tuple-element.212) | copy-start | bytes 3145732 | tf_op jit(solution)/shard_map/while
  168.0 9.6 %copy-start.9 = (f32[2,128,8,32]{1,3,2,0:T(8,128)S(1)}, f32[2,128,8,32]{1,3,2,0:T(8,128)}, u32[]{:S(2)}) copy-start(f32[2,128,8,32]{1,3,2,0:T(8,128)} %get-tuple-element.227) | copy-start | bytes 786436 | tf_op jit(solution)/shard_map/while
  177.6 5.9 %copy-start.4 = (f32[128,64,32]{0,1,2:T(8,128)}, f32[128,64,32]{0,1,2:T(8,128)S(1)}, u32[]{:S(2)}) copy-start(f32[128,64,32]{0,1,2:T(8,128)S(1)} %fusion.87) | copy-start | bytes 3145732 | tf_op jit(solution)/shard_map/while
  181.1 2.4 copy-start.5
  181.1 2.4 copy-start.7
  183.5 3.7 copy-start.2
  183.5 3.7 copy-start.16
  187.2 6.7 %copy-start.6 = (f32[1024,128]{1,0:T(8,128)}, f32[1024,128]{1,0:T(8,128)S(1)}, u32[]{:S(2)}) copy-start(f32[1024,128]{1,0:T(8,128)S(1)} %fusion.86) | copy-start | bytes 1572868 | tf_op jit(solution)/shard_map/while
  199.6 4.2 copy-start.10
  199.6 249.4 %reduce-scatter.2.cloned.1.call-start = ((), (), s32[]{:S(2)}) async-start(), calls=%async_computation.6 | async-start | bytes 2162688 | tf_op jit(solution)/shard_map/reduce_scatter | solution.py:140
  224.6 222.9 %all-to-all-start.4 = ((f32[8,1,8192]{2,1,0:T(1,128)}), f32[8,1,8192]{2,1,0:T(1,128)S(1)}, u32[]{:S(2)}, u32[]{:S(2)}) async-start(f32[8,1,8192]{2,1,0:T(1,128)} %reshape.91), calls=%async_computation.5 | async-start | bytes 524288 | tf_op jit(solution)/shard_map/all_to_all | solution.py:35
  (1 other events, 0.8 us)
Sparse Core Ops, SparseCore 0:
  199.7 246.4 all-reduce.2
Sparse Core Ops, SparseCore 1:
  203.8 122.4 reduce-scatter.1
where the time goes:
time: 467 us; the launch traced here: 460 us
  waiting for transfers between devices  247 us (53%)
  matrix products  73.6 us (16%)
  blocking collectives  40.7 us (9%)
  local copies, waits for them, and re-layouts  28.3 us (6%)
  loops' own time  25.7 us (6%)
  between operations  16.1 us (3%)
  starting transfers between devices  15.2 us (3%)
  other arithmetic  12.9 us (3%)
    unnamed x3, waiting for transfers between devices  218 us
    another operation x1, loops' own time, tile_work(): lax.scan(tile_step, initial, (left_blocks, cot_blocks))  25.7 us
    all_to_all x1, blocking collectives, copy_for_each(): lax.all_to_all(jnp.broadcast_to(array[None], (peers, *array.shape)), axis...  23.9 us
    all_to_all x1, waiting for transfers between devices, copy_for_each(): lax.all_to_all(jnp.broadcast_to(array[None], (peers, *array.shape)), axis...  22 us
    dot_general x2, matrix products, tile_step(): jnp.einsum('sic,ijce->sje', left_blk, grad_outer, precision=precise)  19.1 us
    dot_general x2, matrix products, tile_step(): jnp.einsum('ijce,sje->sic', grad_outer, right_all, precision=precise)  17.3 us
    all_to_all x1, blocking collectives, local(): lax.all_to_all(left_factor_gradient, 'row', split_axis=0, concat_axis=1,...  16.8 us
    dot_general x2, matrix products, tile_step(): jnp.einsum('ijk,kh->ijh', products, result_matrix, precision=precise)  13.4 us
  transfers between devices with their start and end apart: 5, of which 3 were waited for; matrix products, arithmetic and copies ran while one was open for 4% of the time, Pallas kernels for 0%

commit v1 on v0

v1 whole, which is shorter than its diff:
```python
import functools

import jax
import jax.numpy as jnp
from jax import lax
from jax.experimental import pallas as pl
from jax.experimental.pallas import tpu as pltpu
from jax.sharding import Mesh, PartitionSpec as P

exact = lax.Precision.HIGHEST
f32 = jnp.float32
bf16 = jnp.bfloat16

SIZES = (4, 4, 2, 2, 4)
NAMES = ("zl", "x", "core", "zh", "y")
CHIP = ("zl", "x")
ROW = ("zl", "x", "core")
COL = ("zh", "y")
VMEM = pl.BlockSpec(memory_space=pltpu.VMEM)

FWD = 96
BWD = 112


def contract(a, b, dims):
    return lax.dot_general(a, b, (dims, ((), ())), precision=exact, preferred_element_type=f32)


def matmul(a, b):
    return lax.dot_general(a, b, (((1,), (0,)), ((), ())), preferred_element_type=f32)


def halves(v):
    high = v.astype(bf16)
    return high, (v - high.astype(f32)).astype(bf16)


def standardized(x):
    demeaned = x - jnp.mean(x, axis=-1, keepdims=True)
    variance = jnp.mean(demeaned * demeaned, axis=-1, keepdims=True)
    inverse = lax.rsqrt(variance + 1e-05)
    return demeaned * inverse, inverse


def project_kernel(x_ref, scale_ref, offset_ref, w1_ref, b1_ref, w2_ref, b2_ref, left_ref, right_ref, tmp):
    core = lax.axis_index("core")
    normed = standardized(x_ref[...])[0] * scale_ref[...] + offset_ref[...]
    tmp[:, 0:32] = contract(normed, w1_ref[...], ((1,), (1,))) + b1_ref[...]
    wide = jnp.concatenate([tmp[pl.ds(u, 64, stride=4), :][:, 0:32] for u in range(4)], axis=1)
    for s in range(4):
        for q in range(4):
            left_ref[q // 2, lax.rem(q % 2 + core, 2), s * 4 : s * 4 + 4, :] = wide[
                s * 16 + q * 4 : s * 16 + q * 4 + 4
            ]
    right = contract(w2_ref[...], normed, ((1,), (1,))) + b2_ref[...]
    for s in range(4):
        cols = right[:, s * 64 : s * 64 + 64]
        right_ref[s * 16 : s * 16 + 16, :] = jnp.concatenate([cols[0:16], cols[16:32]], axis=1)


def pick(parts, chunk):
    low = jnp.where(chunk == 0, parts[0], parts[1])
    return jnp.where(chunk < 2, low, jnp.where(chunk == 2, parts[2], parts[3]))


def tile_kernel(
    own_ref, other_ref, w_ref, bias_ref, cot_ref,
    pair_ref, own_out, other_out,
    l_ref, lcat, lt, r_hl, rt, wide_t, a_hi, a_lo, w_hl, w_cat, cot_cat, cot_t, g_hi, g_lo, dw,
):
    core = lax.axis_index("core")
    chunk = lax.broadcasted_iota(jnp.int32, (64, 128), 1) // 32
    sides = ((own_ref, FWD, 32), (other_ref, FWD - 16, 16))

    def rows(row, right):
        got = []
        for ref, pitch, base in sides:
            for s in range(4):
                at = base + s * 16 + row if right else s * 4 + row
                got.append(ref[pl.ds(at, 16, stride=pitch), :])
        return jnp.concatenate(got, axis=0)

    for e in range(32):
        hi, lo = halves(w_ref[pl.ds(e, 32, stride=32), :])
        for d in range(4):
            at = (e // 4) * 128 + ((e % 4 + d) % 4) * 32
            w_hl[d, at : at + 32, 0:128] = hi
            w_hl[d, at : at + 32, 128:256] = lo
    for d in range(4):
        for quad in range(4):
            v = cot_ref[quad * 4 + d]
            hi, lo = halves(v)
            cot_cat[d, quad * 64 : quad * 64 + 64, 0:128] = hi
            cot_cat[d, quad * 64 : quad * 64 + 64, 128:256] = hi
            cot_cat[d, quad * 64 : quad * 64 + 64, 256:384] = lo
    for d in range(4):
        v = jnp.concatenate([cot_ref[quad * 4 + d] for quad in range(4)], axis=0).T
        hi, lo = halves(v)
        cot_t[d, 0:128, :] = hi
        cot_t[d, 128:256, :] = lo
    for d in range(4):
        w_cat[:, 0:256] = w_hl[d]
        w_cat[:, 256:384] = w_hl[d, :, 0:128]
        wide_t[d] = lax.dot_general(
            cot_cat[d], w_cat[...], (((1,), (1,)), ((), ())), preferred_element_type=f32
        )
    for block in range(8):
        h, g = block // 4, block % 4
        for quad in range(4):
            parts = [
                wide_t[d, quad * 64 : quad * 64 + 64, block * 128 : block * 128 + 128]
                for d in range(4)
            ]
            for m in range(4):
                hi, lo = halves(pick([parts[(p - m) % 4] for p in range(4)], chunk))
                at = g * 128 + h * 64
                g_hi[m, at : at + 64, quad * 128 : quad * 128 + 128] = hi
                g_lo[m, at : at + 64, quad * 128 : quad * 128 + 128] = lo
    for quad in range(4):
        v = rows(quad, False)
        for m in range(4):
            hi, lo = halves(pltpu.roll(v, 32 * m, axis=1) if m else v)
            lcat[m, 0:128, quad * 128 : quad * 128 + 128] = hi
            lcat[m, 128:256, quad * 128 : quad * 128 + 128] = lo
            lcat[m, 256:384, quad * 128 : quad * 128 + 128] = hi
        hi, lo = halves(v.T)
        for p in range(4):
            for m in range(4):
                at = quad * 128 + ((p + m) % 4) * 32
                lt[m, at : at + 32, 0:128] = hi[p * 32 : p * 32 + 32]
                lt[m, at : at + 32, 128:256] = lo[p * 32 : p * 32 + 32]
    for e in range(16):
        g, m = e // 4, e % 4
        v = rows(e, True)
        hi, lo = halves(v)
        r_hl[m, 0:128, g * 128 : g * 128 + 128] = hi
        r_hl[m, 128:256, g * 128 : g * 128 + 128] = lo
        hi, lo = halves(v.T)
        rt[m, g * 128 : g * 128 + 128, 0:128] = hi
        rt[m, g * 128 : g * 128 + 128, 128:256] = hi
        rt[m, g * 128 : g * 128 + 128, 256:384] = lo
    for m in range(4):
        at = m * 512
        l_ref[at : at + 512, :] = matmul(rt[m], lcat[m])
    for block in range(8):
        h, g = block // 4, block % 4
        for quad in range(4):
            at = g * 128 + h * 64
            parts = [
                l_ref[m * 512 + at : m * 512 + at + 64, quad * 128 : quad * 128 + 128]
                for m in range(4)
            ]
            for d in range(4):
                hi, lo = halves(pick([parts[(p - d) % 4] for p in range(4)], chunk))
                a_hi[d, quad * 64 : quad * 64 + 64, block * 128 : block * 128 + 128] = hi
                a_lo[d, quad * 64 : quad * 64 + 64, block * 128 : block * 128 + 128] = lo
    for d in range(4):
        both = matmul(a_hi[d], w_hl[d])
        pair = both[:, 0:128] + both[:, 128:256] + matmul(a_lo[d], w_hl[d, :, 0:128])
        pair = pair * (1.0 / 128) + bias_ref[...]
        for quad in range(4):
            pair_ref[quad * 4 + d] = pair[quad * 64 : quad * 64 + 64]
    for d in range(4):
        both = matmul(cot_t[d], a_hi[d])
        part = both[0:128] + both[128:256] + matmul(cot_t[d, 0:128, :], a_lo[d])
        for block in range(8):
            v = part[:, block * 128 : block * 128 + 128]
            if d == 0:
                dw[block] = v
            else:
                dw[block] += pltpu.roll(v, 128 - 32 * d, axis=1)
    for block in range(8):
        dw[block] = dw[block].T
    for block in range(8):
        for p in range(4):
            for out, side in ((own_out, core), (other_out, 1 - core)):
                out[pl.ds(64 + p * 8 + block, 16, stride=BWD), :] = dw[
                    block, pl.ds(p * 32 + side, 16, stride=2), :
                ]
    for m in range(4):
        both = matmul(g_hi[m], lt[m])
        v = both[:, 0:128] + both[:, 128:256] + matmul(g_lo[m], lt[m, :, 0:128])
        for g in range(4):
            t = v[g * 128 : g * 128 + 128].T * (1.0 / 128)
            e = g * 4 + m
            for half, out in ((0, own_out), (1, other_out)):
                for s in range(4):
                    at = (half * 4 + s) * 16
                    out[pl.ds(s * 16 + e, 16, stride=BWD), :] = t[at : at + 16]
    total = [None] * 4
    for m in range(4):
        both = matmul(r_hl[m], g_hi[m])
        v = both[0:128] + both[128:256] + matmul(r_hl[m, 0:128, :], g_lo[m])
        for quad in range(4):
            part = v[:, quad * 128 : quad * 128 + 128]
            if m:
                part = pltpu.roll(part, 128 - 32 * m, axis=1)
            total[quad] = part if total[quad] is None else total[quad] + part
    for quad in range(4):
        t = total[quad] * (1.0 / 128)
        for half, out in ((0, own_out), (1, other_out)):
            for s in range(4):
                at = (half * 4 + s) * 16
                out[pl.ds(96 + s * 4 + quad, 16, stride=BWD), :] = t[at : at + 16]


def finish_kernel(x_ref, scale_ref, w1_ref, w2_ref, right_ref, col_ref, out_ref, weight_ref, tmp):
    core = lax.axis_index("core")
    left = col_ref[0]
    for c in range(1, 8):
        left = left + col_ref[c]
    weight_ref[...] = left[64:68] * (1.0 / 512)
    for u in range(4):
        part = contract(left[0:64, u * 32 : u * 32 + 32], w1_ref[...], ((1,), (0,)))
        for q in range(4):
            side = lax.rem(q % 2 + core, 2)
            for s in range(4):
                at = s * 64 + 32 * (q // 2) + 16 * side + u
                block = (q * 4 + s) * 4
                for k in range(2):
                    tmp[k, pl.ds(at, 4, stride=4), :] = part[block : block + 4, k * 128 : k * 128 + 128]
    grads = []
    for s in range(4):
        rows = right_ref[s * 16 : s * 16 + 16, :]
        entries = jnp.concatenate([rows[:, 0:64], rows[:, 64:128]], axis=0)
        grads.append(contract(entries, w2_ref[...], ((0,), (0,))))
    grad = jnp.concatenate(grads, axis=0) + jnp.concatenate([tmp[0], tmp[1]], axis=1)
    unit, inverse = standardized(x_ref[...])
    grad = grad * scale_ref[...]
    mean = jnp.mean(grad, axis=-1, keepdims=True)
    along = jnp.mean(grad * unit, axis=-1, keepdims=True)
    out_ref[...] = inverse * (grad - mean - unit * along)


def cost(flops, moved):
    return pl.CostEstimate(flops=flops, bytes_accessed=moved, transcendentals=0)


def swap_cores(array):
    return lax.ppermute(array, "core", [(0, 1), (1, 0)])


def exchange(array, axes):
    return lax.all_to_all(array, axes, 0, 0, tiled=True)


def local(
    sequence_embedding,
    standardize_scale,
    standardize_offset,
    first_operand_matrix,
    first_operand_intercept,
    second_operand_matrix,
    second_operand_intercept,
    result_matrix,
    result_intercept,
    edge_incoming_sensitivity,
):
    x = sequence_embedding.reshape(256, 256)
    scale = standardize_scale.reshape(1, 256)
    w1 = first_operand_matrix.T
    w2 = second_operand_matrix.T
    left, right = pl.pallas_call(
        project_kernel,
        out_shape=(
            jax.ShapeDtypeStruct((2, 2, 16, 128), f32),
            jax.ShapeDtypeStruct((64, 128), f32),
        ),
        in_specs=[VMEM] * 7,
        out_specs=(VMEM, VMEM),
        scratch_shapes=[pltpu.VMEM((256, 128), f32)],
        cost_estimate=cost(2 * 256 * 256 * 64 * 6, 400000),
        name="project",
    )(
        x,
        scale,
        standardize_offset.reshape(1, 256),
        w1,
        first_operand_intercept.reshape(1, 32),
        w2,
        second_operand_intercept.reshape(32, 1),
    )
    left = exchange(jnp.broadcast_to(left.reshape(1, 64, 128), (8, 64, 128)), COL)
    sent = jnp.concatenate(
        [left.reshape(16, 32, 128), jnp.broadcast_to(right[None], (16, 64, 128))], axis=1
    )
    own = exchange(sent, CHIP)
    other = swap_cores(own[:, 16:])
    pair, own_grads, other_grads = pl.pallas_call(
        tile_kernel,
        out_shape=(
            jax.ShapeDtypeStruct((16, 64, 128), f32),
            jax.ShapeDtypeStruct((16 * BWD, 128), f32),
            jax.ShapeDtypeStruct((16 * BWD, 128), f32),
        ),
        in_specs=[VMEM] * 5,
        out_specs=(VMEM, VMEM, VMEM),
        scratch_shapes=[
            pltpu.VMEM((2048, 512), f32),
            pltpu.VMEM((4, 384, 512), bf16),
            pltpu.VMEM((4, 512, 256), bf16),
            pltpu.VMEM((4, 256, 512), bf16),
            pltpu.VMEM((4, 512, 384), bf16),
            pltpu.VMEM((4, 256, 1024), f32),
            pltpu.VMEM((4, 256, 1024), bf16),
            pltpu.VMEM((4, 256, 1024), bf16),
            pltpu.VMEM((4, 1024, 256), bf16),
            pltpu.VMEM((1024, 384), bf16),
            pltpu.VMEM((4, 256, 384), bf16),
            pltpu.VMEM((4, 256, 256), bf16),
            pltpu.VMEM((4, 512, 512), bf16),
            pltpu.VMEM((4, 512, 512), bf16),
            pltpu.VMEM((8, 128, 128), f32),
        ],
        compiler_params=pltpu.CompilerParams(vmem_limit_bytes=48 * 1024 * 1024),
        cost_estimate=cost(1610612736 * 3, 5000000),
        name="tile",
    )(
        own.reshape(16 * FWD, 128),
        other.reshape(16 * (FWD - 16), 128),
        result_matrix,
        result_intercept.reshape(1, 128),
        edge_incoming_sensitivity,
    )
    own_grads = own_grads.reshape(16, BWD, 128)
    got = swap_cores(other_grads.reshape(16, BWD, 128))
    sent = jnp.concatenate(
        [own_grads[:, :96] + got[:, :96], own_grads[:, 96:], got[:, 96:]], axis=1
    )
    back = exchange(sent, CHIP)
    right_grad = back[:, :64].sum(axis=0)
    weight = back[:, 64:96].sum(axis=0).reshape(4, 8, 128).transpose(1, 0, 2)
    sent = jnp.concatenate(
        [back[:, 96:].reshape(8, 64, 128), jnp.pad(weight, ((0, 0), (0, 4), (0, 0)))], axis=1
    )
    cols = exchange(sent, COL)
    grad, weight = pl.pallas_call(
        finish_kernel,
        out_shape=(
            jax.ShapeDtypeStruct((256, 256), f32),
            jax.ShapeDtypeStruct((4, 128), f32),
        ),
        in_specs=[VMEM] * 6,
        out_specs=(VMEM, VMEM),
        scratch_shapes=[pltpu.VMEM((2, 256, 128), f32)],
        cost_estimate=cost(2 * 256 * 256 * 64 * 6, 900000),
        name="finish",
    )(x, scale, w1, w2, right_grad, cols)
    return pair, grad.reshape(4, 64, 256), weight


def solution(mesh):
    fine = Mesh(mesh.devices.reshape(SIZES), NAMES)
    tile = P(ROW, COL, None)
    return jax.shard_map(
        local,
        mesh=fine,
        in_specs=(tile, P(), P(), P(), P(), P(), P(), P(), P(), tile),
        out_specs=(tile, tile, P(ROW + COL, None)),
        check_vma=False,
    )
```

time: 467 us -> 123 us (0.26); the launches traced: 460 us -> 122 us
  waiting for transfers between devices: 247 us -> 17.1 us
  matrix products: 73.6 us -> 0 us
  blocking collectives: 40.7 us -> 80.1 us
  loops' own time: 25.7 us -> 0 us
  local copies, waits for them, and re-layouts: 28.3 us -> 3.6 us
  Pallas kernels: 0 us -> 15.6 us
  between operations: 16.1 us -> 0.73 us
  starting transfers between devices: 15.2 us -> 3.65 us
  other arithmetic: 12.9 us -> 1.65 us
    unnamed x3 -> x0, waiting for transfers between devices: 218 us -> none
    dot_general x16 -> x0, matrix products: 73.6 us -> none  [the longest x2 19.1 us: tile_step(): jnp.einsum('sic,ijce->sje', left_blk, grad_outer, precision=precise)]
    all_to_all x2 -> x3, blocking collectives: 40.7 us -> 80.1 us  [exchange(): return lax.all_to_all(array, axes, 0, 0, tiled=True)]
    another operation x1 -> x0, loops' own time: 25.7 us -> none  [tile_work(): lax.scan(tile_step, initial, (left_blocks, cot_blocks))]
    all_to_all x3 -> x1, waiting for transfers between devices: 28.9 us -> 12.7 us  [exchange(): return lax.all_to_all(array, axes, 0, 0, tiled=True)]
    pallas_call x0 -> x3, Pallas kernels: none -> 15.6 us  [the longest x1 10.7 us: local(): pl.pallas_call(tile_kernel, out_shape=(jax.ShapeDtypeStruct((16, 64, 128)...]
    all_to_all x3 -> x1, starting transfers between devices: 14.7 us -> 3.42 us  [exchange(): return lax.all_to_all(array, axes, 0, 0, tiled=True)]
    unnamed x30 -> x12, local copies, waits for them, and re-layouts: 10.4 us -> 2.03 us
  transfers between devices with their start and end apart: 5 -> 3, of which waited for: 3 -> 3; matrix products, arithmetic and copies ran while one was open for 4% -> 1% of each run, Pallas kernels for 0% -> 0%
where the time goes in v1:
time: 123 us; the launch traced here: 122 us
  blocking collectives  80.1 us (65%)
  waiting for transfers between devices  17.1 us (14%)
  Pallas kernels  15.6 us (13%)
  starting transfers between devices  3.65 us (3%)
  local copies, waits for them, and re-layouts  3.6 us (3%)
  other arithmetic  1.65 us (1%)
    all_to_all x3, blocking collectives, exchange(): return lax.all_to_all(array, axes, 0, 0, tiled=True)  80.1 us
    all_to_all x1, waiting for transfers between devices, exchange(): return lax.all_to_all(array, axes, 0, 0, tiled=True)  12.7 us
    pallas_call x1, Pallas kernels, local(): pl.pallas_call(tile_kernel, out_shape=(jax.ShapeDtypeStruct((16, 64, 128)...  10.7 us
    ppermute x2, waiting for transfers between devices, swap_cores(): return lax.ppermute(array, 'core', [(0, 1), (1, 0)])  4.41 us
    all_to_all x1, starting transfers between devices, exchange(): return lax.all_to_all(array, axes, 0, 0, tiled=True)  3.42 us
    pallas_call x1, Pallas kernels, local(): pl.pallas_call(finish_kernel, out_shape=(jax.ShapeDtypeStruct((256, 256),...  2.51 us
  transfers between devices with their start and end apart: 3, of which 3 were waited for; matrix products, arithmetic and copies ran while one was open for 1% of the time, Pallas kernels for 0%

profile of v1, /device:TPU:32, one launch (start us, length us, event | category | flops | bytes accessed | tf_op | source)
XLA Modules:
  0.0 122.5 jit_solution(6977894287794347363)
XLA Ops:
  0.6 0.0 copy-start.5
  0.6 0.6 copy-done.5
  1.3 0.7 copy.14.b2_ref
  2.0 2.4 %project.1 = (f32[2,2,16,128]{3,2,1,0:T(8,128)}, f32[64,128]{1,0:T(8,128)}) custom-call(f32[256,256]{1,0:T(8,128)} %bitcast.26, f32[1,256]{1,0:T(1,128)} %bitcast.37, f32[1,256]{1,0:T(1,128)} %bitcast.39, f32[32,256]{1,0:T(8,128)} %bitcast.30, f32[1,32]{1,0:T(1,128)} %bitcast.40, f32[32,256]{1,0:T(8,128)} %bitcast.32, f32[32,1]{1,0:T(8,128)} %copy.14.b2_ref), custom_call_target="tpu_custom_call" | custom-call | flops 50331648 | bytes 400000 | tf_op jit(solution)/shard_map/project/pallas_call | solution.py:263
  4.4 0.8 broadcast_in_dim.14
  5.2 0.0 copy-start.4
  5.2 23.9 %all_to_all.20 = f32[8,64,128]{2,1,0:T(8,128)S(1)} all-to-all(f32[8,64,128]{2,1,0:T(8,128)S(1)} %broadcast_in_dim.14), channel_id=1, replica_groups=mesh['zl'=4,'x'=4,'core'=2,'zh'=2,'y'=4] {'zh','y'}, dimensions={0} | all-to-all | bytes 524288 | tf_op jit(solution)/shard_map/all_to_all | solution.py:244
  29.1 0.0 copy-done.4
  29.2 0.1 pad_maximum_fusion.1
  29.2 24.9 %all_to_all.21 = f32[16,96,128]{2,1,0:T(8,128)S(1)} all-to-all(f32[16,96,128]{2,1,0:T(8,128)S(1)} %pad_maximum_fusion.1), channel_id=1, replica_groups=mesh['zl'=4,'x'=4,'core'=2,'zh'=2,'y'=4] {'zl','x'}, dimensions={0} | all-to-all | bytes 1572864 | tf_op jit(solution)/shard_map/all_to_all | solution.py:244
  54.2 0.0 copy-start
  54.2 0.0 copy-start.1
  54.2 0.1 collective-permute-start
  54.3 2.1 %collective-permute-done = f32[16,80,128]{2,1,0:T(8,128)S(1)} collective-permute-done((f32[16,80,128]{2,1,0:T(8,128)S(1)}, f32[16,80,128]{2,1,0:T(8,128)S(1)}, u32[]{:S(2)}, u32[]{:S(2)}) %collective-permute-start) | collective-permute-done | bytes 655392 | tf_op jit(solution)/shard_map/ppermute | solution.py:240
  56.4 0.0 copy-start.2
  56.4 0.0 copy-done
  56.4 0.0 copy-done.1
  56.4 0.6 copy-done.2
  57.1 10.7 %tile.1 = (f32[16,64,128]{2,1,0:T(8,128)}, f32[1792,128]{1,0:T(8,128)S(1)}, f32[1792,128]{1,0:T(8,128)S(1)}) custom-call(f32[1536,128]{1,0:T(8,128)S(1)} %bitcast.20, f32[1280,128]{1,0:T(8,128)S(1)} %bitcast.24, f32[1024,128]{1,0:T(8,128)S(1)} %copy-done, f32[1,128]{1,0:T(1,128)S(1)} %bitcast.25, f32[16,64,128]{2,1,0:T(8,128)S(1)} %copy-done.1), custom_call_target="tpu_custom_call" | custom-call | flops 4831838208 | bytes 5000000 | tf_op jit(solution)/shard_map/tile/pallas_call | solution.py:289
  67.7 0.1 collective-permute-start.1
  67.9 2.3 %collective-permute-done.1 = f32[16,112,128]{2,1,0:T(8,128)S(1)} collective-permute-done((f32[16,112,128]{2,1,0:T(8,128)S(1)}, f32[16,112,128]{2,1,0:T(8,128)S(1)}, u32[]{:S(2)}, u32[]{:S(2)}) %collective-permute-start.1) | collective-permute-done | bytes 917536 | tf_op jit(solution)/shard_map/ppermute | solution.py:240
  70.2 0.1 slice_add_fusion
  70.3 0.1 pad_maximum_fusion
  70.4 31.2 %all_to_all.22 = f32[16,128,128]{2,1,0:T(8,128)S(1)} all-to-all(f32[16,128,128]{2,1,0:T(8,128)S(1)} %pad_maximum_fusion), channel_id=1, replica_groups=mesh['zl'=4,'x'=4,'core'=2,'zh'=2,'y'=4] {'zl','x'}, dimensions={0} | all-to-all | bytes 2097152 | tf_op jit(solution)/shard_map/all_to_all | solution.py:244
  101.7 0.7 select_maximum_fusion
  102.4 3.4 %all-to-all-start.3 = ((f32[8,72,128]{2,1,0:T(8,128)}), f32[8,72,128]{2,1,0:T(8,128)S(1)}, u32[]{:S(2)}, u32[]{:S(2)}) async-start(f32[8,72,128]{2,1,0:T(8,128)} %select_maximum_fusion), calls=%async_computation.3 | async-start | bytes 589824 | tf_op jit(solution)/shard_map/all_to_all | solution.py:244
  105.9 0.6 slice_reduce_fusion.right_ref
  106.5 12.7 %all-to-all-done.3.col_ref = f32[8,72,128]{2,1,0:T(8,128)S(1)} async-done(((f32[8,72,128]{2,1,0:T(8,128)}), f32[8,72,128]{2,1,0:T(8,128)S(1)}, u32[]{:S(2)}, u32[]{:S(2)}) %all-to-all-start.3) | async-done | bytes 294944 | tf_op jit(solution)/shard_map/all_to_all | solution.py:244
  119.3 0.0 copy-start.3
  119.3 0.7 copy-done.3
  120.0 2.5 %finish.1 = (f32[256,256]{1,0:T(8,128)}, f32[4,128]{1,0:T(4,128)}) custom-call(f32[256,256]{1,0:T(8,128)} %bitcast.27, f32[1,256]{1,0:T(1,128)} %bitcast.38, f32[32,256]{1,0:T(8,128)} %bitcast.31, f32[32,256]{1,0:T(8,128)} %bitcast.33, f32[64,128]{1,0:T(8,128)} %slice_reduce_fusion.right_ref, f32[8,72,128]{2,1,0:T(8,128)} %copy-done.3), custom_call_target="tpu_custom_call" | custom-call | flops 50331648 | bytes 900000 | tf_op jit(solution)/shard_map/finish/pallas_call | solution.py:337
  (6 shorter events, 0.2 us)
Async XLA Ops:
  0.6 0.7 copy-start.5
  5.2 23.9 %copy-start.4 = (f32[64,128]{1,0:T(8,128)S(1)}, f32[64,128]{1,0:T(8,128)}, u32[]{:S(2)}) copy-start(f32[64,128]{1,0:T(8,128)} %get-tuple-element.11) | copy-start | bytes 98308
  54.2 2.2 %copy-start = (f32[1024,128]{1,0:T(8,128)S(1)}, f32[1024,128]{1,0:T(8,128)}, u32[]{:S(2)}) copy-start(f32[1024,128]{1,0:T(8,128)} %w_ref.1) | copy-start | bytes 1572868
  54.2 2.2 %copy-start.1 = (f32[16,64,128]{2,1,0:T(8,128)S(1)}, f32[16,64,128]{2,1,0:T(8,128)}, u32[]{:S(2)}) copy-start(f32[16,64,128]{2,1,0:T(8,128)} %cot_ref.1) | copy-start | bytes 1572868
  54.2 2.2 %collective-permute-start = (f32[16,80,128]{2,1,0:T(8,128)S(1)}, f32[16,80,128]{2,1,0:T(8,128)S(1)}, u32[]{:S(2)}, u32[]{:S(2)}) collective-permute-start(f32[16,80,128]{2,1,0:T(8,128)S(1)} %slice.32), channel_id=1, source_target_pairs={{0,8},{8,0},{1,9},{9,1},{2,10},{10,2},{3,11},{11,3},{4,12},{12,4},... | collective-permute-start | bytes 1966088 | tf_op jit(solution)/shard_map/ppermute | solution.py:240
  56.4 0.7 copy-start.2
  67.7 2.5 %collective-permute-start.1 = (f32[16,112,128]{2,1,0:T(8,128)S(1)}, f32[16,112,128]{2,1,0:T(8,128)S(1)}, u32[]{:S(2)}, u32[]{:S(2)}) collective-permute-start(f32[16,112,128]{2,1,0:T(8,128)S(1)} %bitcast.23), channel_id=1, source_target_pairs={{0,8},{8,0},{1,9},{9,1},{2,10},{10,2},{3,11},{11,3},{4,12},{12,4},... | collective-permute-start | bytes 2752520 | tf_op jit(solution)/shard_map/ppermute | solution.py:240
  102.4 16.8 %all-to-all-start.3 = ((f32[8,72,128]{2,1,0:T(8,128)}), f32[8,72,128]{2,1,0:T(8,128)S(1)}, u32[]{:S(2)}, u32[]{:S(2)}) async-start(f32[8,72,128]{2,1,0:T(8,128)} %select_maximum_fusion), calls=%async_computation.3 | async-start | bytes 589824 | tf_op jit(solution)/shard_map/all_to_all | solution.py:244
  119.3 0.7 copy-start.3

commit v2 on v1

v2 whole, which is shorter than its diff:
```python
import jax
import jax.numpy as jnp
from jax import lax
from jax.experimental import pallas as pl
from jax.experimental.pallas import tpu as pltpu
from jax.sharding import Mesh, PartitionSpec as P

exact = lax.Precision.HIGHEST
f32 = jnp.float32
bf16 = jnp.bfloat16

SIZES = (4, 4, 2, 2, 4)
NAMES = ("zl", "x", "core", "zh", "y")
CHIP = ("zl", "x")
ROW = ("zl", "x", "core")
COL = ("zh", "y")
VMEM = pl.BlockSpec(memory_space=pltpu.VMEM)

FWD = 96
BWD = 112


def contract(a, b, dims):
    return lax.dot_general(a, b, (dims, ((), ())), precision=exact, preferred_element_type=f32)


def matmul(a, b):
    return lax.dot_general(a, b, (((1,), (0,)), ((), ())), preferred_element_type=f32)


def halves(v):
    high = v.astype(bf16)
    return high, (v - high.astype(f32)).astype(bf16)


def standardized(x):
    demeaned = x - jnp.mean(x, axis=-1, keepdims=True)
    variance = jnp.mean(demeaned * demeaned, axis=-1, keepdims=True)
    inverse = lax.rsqrt(variance + 1e-05)
    return demeaned * inverse, inverse


def project_kernel(x_ref, scale_ref, offset_ref, w1_ref, b1_ref, w2_ref, b2_ref, left_ref, right_ref, tmp):
    core = lax.axis_index("core")
    normed = standardized(x_ref[...])[0] * scale_ref[...] + offset_ref[...]
    tmp[:, 0:32] = contract(normed, w1_ref[...], ((1,), (1,))) + b1_ref[...]
    wide = jnp.concatenate([tmp[pl.ds(u, 64, stride=4), :][:, 0:32] for u in range(4)], axis=1)
    for q in range(4):
        part = jnp.concatenate([wide[s * 16 + q * 4 : s * 16 + q * 4 + 4] for s in range(4)], axis=0)
        at = pl.multiple_of((q // 2 * 2 + lax.rem(q % 2 + core, 2)) * 16, 16)
        for copy in range(8):
            left_ref[copy, pl.ds(at, 16), :] = part
    on = lax.broadcasted_iota(jnp.int32, (32, 32), 0) == lax.broadcasted_iota(jnp.int32, (32, 32), 1)
    b2 = jnp.sum(jnp.where(on, b2_ref[...], 0.0), axis=1, keepdims=True)
    right = contract(w2_ref[...], normed, ((1,), (1,))) + b2
    for s in range(4):
        cols = right[:, s * 64 : s * 64 + 64]
        right_ref[s * 16 : s * 16 + 16, :] = jnp.concatenate([cols[0:16], cols[16:32]], axis=1)


def pick(parts):
    chunk = lax.broadcasted_iota(jnp.int32, (64, 128), 1) // 32
    low = jnp.where(chunk == 0, parts[0], parts[1])
    return jnp.where(chunk < 2, low, jnp.where(chunk == 2, parts[2], parts[3]))


def rows(own_ref, other_ref, row, right):
    got = []
    for ref, pitch, base in ((own_ref, FWD, 32), (other_ref, FWD - 16, 16)):
        for s in range(4):
            at = base + s * 16 + row if right else s * 4 + row
            got.append(ref[pl.ds(at, 16, stride=pitch), :])
    return jnp.concatenate(got, axis=0)


def weights_by_class(w_ref, w_hl):
    for e in range(32):
        hi, lo = halves(w_ref[pl.ds(e, 32, stride=32), :])
        for d in range(4):
            at = (e // 4) * 128 + ((e % 4 + d) % 4) * 32
            w_hl[d, at : at + 32, 0:128] = hi
            w_hl[d, at : at + 32, 128:256] = lo


def cotangent_kernel(w_ref, cot_ref, g_hi, g_lo, cot_t, wide_t, w_hl, w_cat, cot_cat):
    weights_by_class(w_ref, w_hl)
    for d in range(4):
        for quad in range(4):
            hi, lo = halves(cot_ref[quad * 4 + d])
            cot_cat[d, quad * 64 : quad * 64 + 64, 0:128] = hi
            cot_cat[d, quad * 64 : quad * 64 + 64, 128:256] = hi
            cot_cat[d, quad * 64 : quad * 64 + 64, 256:384] = lo
    for d in range(4):
        hi, lo = halves(jnp.concatenate([cot_ref[quad * 4 + d] for quad in range(4)], axis=0).T)
        cot_t[d, 0:128, :] = hi
        cot_t[d, 128:256, :] = lo
    for d in range(4):
        w_cat[:, 0:256] = w_hl[d]
        w_cat[:, 256:384] = w_hl[d, :, 0:128]
        wide_t[d] = lax.dot_general(
            cot_cat[d], w_cat[...], (((1,), (1,)), ((), ())), preferred_element_type=f32
        )
    for block in range(8):
        h, g = block // 4, block % 4
        at = g * 128 + h * 64
        for quad in range(4):
            parts = [
                wide_t[d, quad * 64 : quad * 64 + 64, block * 128 : block * 128 + 128]
                for d in range(4)
            ]
            for m in range(4):
                hi, lo = halves(pick([parts[(p - m) % 4] for p in range(4)]))
                g_hi[m, at : at + 64, quad * 128 : quad * 128 + 128] = hi
                g_lo[m, at : at + 64, quad * 128 : quad * 128 + 128] = lo


def outer_product(own_ref, other_ref, outer, lcat, rt, a_hi, a_lo, lt=None, r_hl=None):
    for quad in range(4):
        v = rows(own_ref, other_ref, quad, False)
        for m in range(4):
            hi, lo = halves(pltpu.roll(v, 32 * m, axis=1) if m else v)
            lcat[m, 0:128, quad * 128 : quad * 128 + 128] = hi
            lcat[m, 128:256, quad * 128 : quad * 128 + 128] = lo
            lcat[m, 256:384, quad * 128 : quad * 128 + 128] = hi
        if lt is None:
            continue
        hi, lo = halves(v.T)
        for p in range(4):
            for m in range(4):
                at = quad * 128 + ((p + m) % 4) * 32
                lt[m, at : at + 32, 0:128] = hi[p * 32 : p * 32 + 32]
                lt[m, at : at + 32, 128:256] = lo[p * 32 : p * 32 + 32]
    for e in range(16):
        g, m = e // 4, e % 4
        v = rows(own_ref, other_ref, e, True)
        if r_hl is not None:
            hi, lo = halves(v)
            r_hl[m, 0:128, g * 128 : g * 128 + 128] = hi
            r_hl[m, 128:256, g * 128 : g * 128 + 128] = lo
        hi, lo = halves(v.T)
        rt[m, g * 128 : g * 128 + 128, 0:128] = hi
        rt[m, g * 128 : g * 128 + 128, 128:256] = hi
        rt[m, g * 128 : g * 128 + 128, 256:384] = lo
    for m in range(4):
        outer[m] = matmul(rt[m], lcat[m])
    for block in range(8):
        h, g = block // 4, block % 4
        at = g * 128 + h * 64
        for quad in range(4):
            parts = [outer[m, at : at + 64, quad * 128 : quad * 128 + 128] for m in range(4)]
            for d in range(4):
                hi, lo = halves(pick([parts[(p - d) % 4] for p in range(4)]))
                a_hi[d, quad * 64 : quad * 64 + 64, block * 128 : block * 128 + 128] = hi
                a_lo[d, quad * 64 : quad * 64 + 64, block * 128 : block * 128 + 128] = lo


def pair_kernel(own_ref, other_ref, w_ref, bias_ref, pair_ref, outer, lcat, rt, a_hi, a_lo, w_hl):
    weights_by_class(w_ref, w_hl)
    outer_product(own_ref, other_ref, outer, lcat, rt, a_hi, a_lo)
    for d in range(4):
        both = matmul(a_hi[d], w_hl[d])
        pair = both[:, 0:128] + both[:, 128:256] + matmul(a_lo[d], w_hl[d, :, 0:128])
        pair = pair * (1.0 / 128) + bias_ref[...]
        for quad in range(4):
            pair_ref[quad * 4 + d] = pair[quad * 64 : quad * 64 + 64]


def tile_kernel(
    own_ref, other_ref, g_hi, g_lo, cot_t, own_out, other_out,
    outer, lcat, rt, a_hi, a_lo, lt, r_hl, dw,
):
    core = lax.axis_index("core")
    outer_product(own_ref, other_ref, outer, lcat, rt, a_hi, a_lo, lt, r_hl)
    for d in range(4):
        both = matmul(cot_t[d], a_hi[d])
        part = both[0:128] + both[128:256] + matmul(cot_t[d, 0:128, :], a_lo[d])
        for block in range(8):
            v = part[:, block * 128 : block * 128 + 128]
            if d == 0:
                dw[block] = v
            else:
                dw[block] += pltpu.roll(v, 128 - 32 * d, axis=1)
    for block in range(8):
        dw[block] = dw[block].T
    for block in range(8):
        for p in range(4):
            for out, side in ((own_out, core), (other_out, 1 - core)):
                out[pl.ds(64 + p * 8 + block, 16, stride=BWD), :] = dw[
                    block, pl.ds(p * 32 + side, 16, stride=2), :
                ]
    for m in range(4):
        both = matmul(g_hi[m], lt[m])
        v = both[:, 0:128] + both[:, 128:256] + matmul(g_lo[m], lt[m, :, 0:128])
        for g in range(4):
            t = v[g * 128 : g * 128 + 128].T * (1.0 / 128)
            e = g * 4 + m
            for half, out in ((0, own_out), (1, other_out)):
                for s in range(4):
                    at = (half * 4 + s) * 16
                    out[pl.ds(s * 16 + e, 16, stride=BWD), :] = t[at : at + 16]
    total = [None] * 4
    for m in range(4):
        both = matmul(r_hl[m], g_hi[m])
        v = both[0:128] + both[128:256] + matmul(r_hl[m, 0:128, :], g_lo[m])
        for quad in range(4):
            part = v[:, quad * 128 : quad * 128 + 128]
            if m:
                part = pltpu.roll(part, 128 - 32 * m, axis=1)
            total[quad] = part if total[quad] is None else total[quad] + part
    for quad in range(4):
        t = total[quad] * (1.0 / 128)
        for half, out in ((0, own_out), (1, other_out)):
            for s in range(4):
                at = (half * 4 + s) * 16
                out[pl.ds(96 + s * 4 + quad, 16, stride=BWD), :] = t[at : at + 16]


def right_kernel(w2_ref, right_ref, out_ref):
    total = right_ref[0, 0:64]
    for chip in range(1, 16):
        total = total + right_ref[chip, 0:64]
    for s in range(4):
        part = total[s * 16 : s * 16 + 16, :]
        entries = jnp.concatenate([part[:, 0:64], part[:, 64:128]], axis=0)
        out_ref[s * 64 : s * 64 + 64, :] = contract(entries, w2_ref[...], ((0,), (0,)))


def finish_kernel(x_ref, scale_ref, w1_ref, part_ref, col_ref, out_ref, weight_ref, tmp):
    core = lax.axis_index("core")
    left = col_ref[0]
    for c in range(1, 8):
        left = left + col_ref[c]
    weight_ref[...] = left[64:68] * (1.0 / 512)
    for u in range(4):
        part = contract(left[0:64, u * 32 : u * 32 + 32], w1_ref[...], ((1,), (0,)))
        for q in range(4):
            side = lax.rem(q % 2 + core, 2)
            for s in range(4):
                at = s * 64 + 32 * (q // 2) + 16 * side + u
                block = (q * 4 + s) * 4
                for k in range(2):
                    tmp[k, pl.ds(at, 4, stride=4), :] = part[block : block + 4, k * 128 : k * 128 + 128]
    unit, inverse = standardized(x_ref[...])
    grad = (part_ref[...] + jnp.concatenate([tmp[0], tmp[1]], axis=1)) * scale_ref[...]
    mean = jnp.mean(grad, axis=-1, keepdims=True)
    along = jnp.mean(grad * unit, axis=-1, keepdims=True)
    out_ref[...] = inverse * (grad - mean - unit * along)


def call(kernel, name, outs, scratch, mib, flops, *args):
    shapes = tuple(jax.ShapeDtypeStruct(*out) for out in outs)
    moved = sum(a.size * a.dtype.itemsize for a in args + shapes)
    return pl.pallas_call(
        kernel,
        out_shape=shapes,
        in_specs=[VMEM] * len(args),
        out_specs=(VMEM,) * len(outs),
        scratch_shapes=[pltpu.VMEM(*s) for s in scratch],
        compiler_params=pltpu.CompilerParams(vmem_limit_bytes=mib * 1024 * 1024),
        cost_estimate=pl.CostEstimate(flops=flops, bytes_accessed=moved, transcendentals=0),
        name=name,
    )(*args)


def swap_cores(array):
    return lax.ppermute(array, "core", [(0, 1), (1, 0)])


def exchange(array, axes):
    return lax.all_to_all(array, axes, 0, 0, tiled=True)


def local(
    sequence_embedding,
    standardize_scale,
    standardize_offset,
    first_operand_matrix,
    first_operand_intercept,
    second_operand_matrix,
    second_operand_intercept,
    result_matrix,
    result_intercept,
    edge_incoming_sensitivity,
):
    x = sequence_embedding.reshape(256, 256)
    scale = standardize_scale.reshape(1, 256)
    w1 = first_operand_matrix.T
    w2 = second_operand_matrix.T
    small = 2 * 256 * 256 * 32 * 6
    step = 2 * 1024 * 1024 * 128 * 3
    left, right = call(
        project_kernel,
        "project",
        [((8, 64, 128), f32), ((64, 128), f32)],
        [((256, 128), f32)],
        8,
        2 * small,
        x,
        scale,
        standardize_offset.reshape(1, 256),
        w1,
        first_operand_intercept.reshape(1, 32),
        w2,
        second_operand_intercept.reshape(1, 32),
    )
    g_hi, g_lo, cot_t = call(
        cotangent_kernel,
        "cotangent",
        [((4, 512, 512), bf16), ((4, 512, 512), bf16), ((4, 256, 256), bf16)],
        [
            ((4, 256, 1024), f32),
            ((4, 1024, 256), bf16),
            ((1024, 384), bf16),
            ((4, 256, 384), bf16),
        ],
        24,
        step,
        result_matrix,
        edge_incoming_sensitivity,
    )
    left = exchange(left, COL)
    sent = jnp.concatenate(
        [left.reshape(16, 32, 128), jnp.broadcast_to(right[None], (16, 64, 128))], axis=1
    )
    sent, g_hi, g_lo, cot_t = lax.optimization_barrier((sent, g_hi, g_lo, cot_t))
    own = exchange(sent, CHIP)
    other = swap_cores(own[:, 16:]).reshape(16 * (FWD - 16), 128)
    own = own.reshape(16 * FWD, 128)
    working = [
        ((4, 512, 512), f32),
        ((4, 384, 512), bf16),
        ((4, 512, 384), bf16),
        ((4, 256, 1024), bf16),
        ((4, 256, 1024), bf16),
    ]
    own_grads, other_grads = call(
        tile_kernel,
        "tile",
        [((16 * BWD, 128), f32), ((16 * BWD, 128), f32)],
        working + [((4, 512, 256), bf16), ((4, 256, 512), bf16), ((8, 128, 128), f32)],
        32,
        4 * step,
        own,
        other,
        g_hi,
        g_lo,
        cot_t,
    )
    (pair,) = call(
        pair_kernel,
        "pair",
        [((16, 64, 128), f32)],
        working + [((4, 1024, 256), bf16)],
        28,
        2 * step,
        own,
        other,
        result_matrix,
        result_intercept.reshape(1, 128),
    )
    own_grads = own_grads.reshape(16, BWD, 128)
    got = swap_cores(other_grads.reshape(16, BWD, 128))
    sent = jnp.concatenate(
        [own_grads[:, :96] + got[:, :96], own_grads[:, 96:], got[:, 96:]], axis=1
    )
    back = exchange(sent, CHIP)
    weight = back[:, 64:96].sum(axis=0).reshape(4, 8, 128).transpose(1, 0, 2)
    sent = jnp.concatenate(
        [back[:, 96:].reshape(8, 64, 128), jnp.pad(weight, ((0, 0), (0, 4), (0, 0)))], axis=1
    )
    cols = exchange(sent, COL)
    (part,) = call(right_kernel, "right", [((256, 256), f32)], [], 8, small, w2, back)
    grad, weight = call(
        finish_kernel,
        "finish",
        [((256, 256), f32), ((4, 128), f32)],
        [((2, 256, 128), f32)],
        8,
        small,
        x,
        scale,
        w1,
        part,
        cols,
    )
    return pair, grad.reshape(4, 64, 256), weight


def solution(mesh):
    fine = Mesh(mesh.devices.reshape(SIZES), NAMES)
    tile = P(ROW, COL, None)
    return jax.shard_map(
        local,
        mesh=fine,
        in_specs=(tile, P(), P(), P(), P(), P(), P(), P(), P(), tile),
        out_specs=(tile, tile, P(ROW + COL, None)),
        check_vma=False,
    )
```

time: 123 us -> 120 us (0.976)
  blocking collectives: 80.1 us -> 56.4 us
  starting transfers between devices: 3.65 us -> 15.3 us
  local copies, waits for them, and re-layouts: 3.6 us -> 11 us
  Pallas kernels: 15.6 us -> 17.8 us
    all_to_all x3 -> x2, blocking collectives: 80.1 us -> 56.4 us  [exchange(): return lax.all_to_all(array, axes, 0, 0, tiled=True)]
    all_to_all x1 -> x2, starting transfers between devices: 3.42 us -> 14.9 us  [exchange(): return lax.all_to_all(array, axes, 0, 0, tiled=True)]
    unnamed x12 -> x38, local copies, waits for them, and re-layouts: 2.03 us -> 10.9 us
    pallas_call x3 -> x6, Pallas kernels: 15.6 us -> 17.8 us  [call(): pl.pallas_call(kernel, out_shape=shapes, in_specs=[VMEM] * len(args), out...]
    all_to_all x1 -> x2, waiting for transfers between devices: 12.7 us -> 12.9 us  [exchange(): return lax.all_to_all(array, axes, 0, 0, tiled=True)]
  transfers between devices with their start and end apart: 3 -> 4, of which waited for: 3 -> 4; matrix products, arithmetic and copies ran while one was open for 1% -> 0% of each run, Pallas kernels for 0% -> 7%
where the time goes in v2:
time: 120 us
  blocking collectives  56.4 us (47%)
  Pallas kernels  17.8 us (15%)
  waiting for transfers between devices  17.3 us (14%)
  starting transfers between devices  15.3 us (13%)
  local copies, waits for them, and re-layouts  11 us (9%)
    all_to_all x2, blocking collectives, exchange(): return lax.all_to_all(array, axes, 0, 0, tiled=True)  56.4 us
    pallas_call x6, Pallas kernels, call(): pl.pallas_call(kernel, out_shape=shapes, in_specs=[VMEM] * len(args), out...  17.8 us
    all_to_all x2, starting transfers between devices, exchange(): return lax.all_to_all(array, axes, 0, 0, tiled=True)  14.9 us
    all_to_all x2, waiting for transfers between devices, exchange(): return lax.all_to_all(array, axes, 0, 0, tiled=True)  12.9 us
    unnamed x38, local copies, waits for them, and re-layouts  10.9 us
    ppermute x2, waiting for transfers between devices, swap_cores(): return lax.ppermute(array, 'core', [(0, 1), (1, 0)])  4.41 us
  transfers between devices with their start and end apart: 4, of which 4 were waited for; matrix products, arithmetic and copies ran while one was open for 0% of the time, Pallas kernels for 7%

profile of v2, /device:TPU:32, one launch (start us, length us, event | category | flops | bytes accessed | tf_op | source)
XLA Modules:
  0.0 119.6 jit_solution(10571485503072585865)
XLA Ops:
  0.6 0.9 copy-done
  1.6 0.8 copy-done.2
  2.3 0.8 copy-done.4
  3.1 0.7 copy-done.6
  3.8 0.7 copy-done.8
  4.5 0.7 copy-done.9
  5.1 0.7 copy-done.10
  5.8 1.5 %project.1 = (f32[8,64,128]{2,1,0:T(8,128)}, f32[64,128]{1,0:T(8,128)S(1)}) custom-call(f32[256,256]{1,0:T(8,128)S(1)} %bitcast.21, f32[1,256]{1,0:T(1,128)S(1)} %bitcast.29, f32[1,256]{1,0:T(1,128)S(1)} %bitcast.31, f32[32,256]{1,0:T(8,128)S(1)} %bitcast.25, f32[1,32]{1,0:T(1,128)S(1)} %bitcast.32, f32[32,256]{1,0:T(8,128)S(1)} %bitcast.27, ...), custom_call_target="tpu_custom_call" | custom-call | flops 50331648 | bytes 624896 | tf_op jit(solution)/shard_map/project/pallas_call | solution.py:253
  7.3 10.2 %all-to-all-start = ((f32[8,64,128]{2,1,0:T(8,128)}), f32[8,64,128]{2,1,0:T(8,128)S(1)}, u32[]{:S(2)}, u32[]{:S(2)}) async-start(f32[8,64,128]{2,1,0:T(8,128)} %get-tuple-element.16), calls=%async_computation | async-start | bytes 524288 | tf_op jit(solution)/shard_map/all_to_all | solution.py:270
  17.5 1.0 copy-done.11
  18.5 1.0 copy-done.12
  19.6 2.7 %cotangent.1 = (bf16[4,512,512]{2,1,0:T(8,128)(2,1)S(1)}, bf16[4,512,512]{2,1,0:T(8,128)(2,1)S(1)}, bf16[4,256,256]{2,1,0:T(8,128)(2,1)S(1)}) custom-call(f32[1024,128]{1,0:T(8,128)S(1)} %copy-done.12, f32[16,64,128]{2,1,0:T(8,128)S(1)} %copy-done.11), custom_call_target="tpu_custom_call" | custom-call | flops 805306368 | bytes 5767168 | tf_op jit(solution)/shard_map/cotangent/pallas_call | solution.py:253
  22.3 1.3 %copy-done.15 = bf16[4,512,512]{2,1,0:T(8,128)(2,1)} copy-done((bf16[4,512,512]{2,1,0:T(8,128)(2,1)}, bf16[4,512,512]{2,1,0:T(8,128)(2,1)S(1)}, u32[]{:S(2)}) %copy-start.15) | copy-done | bytes 2097176
  23.7 1.3 %copy-done.17 = bf16[4,512,512]{2,1,0:T(8,128)(2,1)} copy-done((bf16[4,512,512]{2,1,0:T(8,128)(2,1)}, bf16[4,512,512]{2,1,0:T(8,128)(2,1)S(1)}, u32[]{:S(2)}) %copy-start.17) | copy-done | bytes 2097176
  24.9 6.5 %all-to-all-done = f32[8,64,128]{2,1,0:T(8,128)S(1)} async-done(((f32[8,64,128]{2,1,0:T(8,128)}), f32[8,64,128]{2,1,0:T(8,128)S(1)}, u32[]{:S(2)}, u32[]{:S(2)}) %all-to-all-start) | async-done | bytes 262176 | tf_op jit(solution)/shard_map/all_to_all | solution.py:270
  31.5 0.1 pad_maximum_fusion.1
  31.5 25.2 %all_to_all.20 = f32[16,96,128]{2,1,0:T(8,128)S(1)} all-to-all(f32[16,96,128]{2,1,0:T(8,128)S(1)} %pad_maximum_fusion.1), channel_id=1, replica_groups=mesh['zl'=4,'x'=4,'core'=2,'zh'=2,'y'=4] {'zl','x'}, dimensions={0} | all-to-all | bytes 1572864 | tf_op jit(solution)/shard_map/all_to_all | solution.py:270
  56.8 0.1 collective-permute-start
  56.9 2.1 %collective-permute-done = f32[16,80,128]{2,1,0:T(8,128)S(1)} collective-permute-done((f32[16,80,128]{2,1,0:T(8,128)S(1)}, f32[16,80,128]{2,1,0:T(8,128)S(1)}, u32[]{:S(2)}, u32[]{:S(2)}) %collective-permute-start) | collective-permute-done | bytes 655392 | tf_op jit(solution)/shard_map/ppermute | solution.py:266
  59.0 6.5 %tile.1 = (f32[1792,128]{1,0:T(8,128)S(1)}, f32[1792,128]{1,0:T(8,128)S(1)}) custom-call(f32[1536,128]{1,0:T(8,128)S(1)} %bitcast.19, f32[1280,128]{1,0:T(8,128)S(1)} %bitcast.35, bf16[4,512,512]{2,1,0:T(8,128)(2,1)S(1)} %copy-done.16, bf16[4,512,512]{2,1,0:T(8,128)(2,1)S(1)} %copy-done.18, bf16[4,256,256]{2,1,0:T(8,128)(2,1)S(1)} %get-tuple-element.24.cot_t), custom_call_target="tpu_custom_call" | custom-call | flops 3221225472 | bytes 7995392 | tf_op jit(solution)/shard_map/tile/pallas_call | solution.py:253
  65.5 0.2 collective-permute-start.1
  65.8 2.3 %collective-permute-done.1 = f32[16,112,128]{2,1,0:T(8,128)S(1)} collective-permute-done((f32[16,112,128]{2,1,0:T(8,128)S(1)}, f32[16,112,128]{2,1,0:T(8,128)S(1)}, u32[]{:S(2)}, u32[]{:S(2)}) %collective-permute-start.1) | collective-permute-done | bytes 917536 | tf_op jit(solution)/shard_map/ppermute | solution.py:266
  68.1 0.1 slice_add_fusion
  68.2 0.1 pad_maximum_fusion
  68.3 31.2 %all_to_all.21.right_ref = f32[16,128,128]{2,1,0:T(8,128)S(1)} all-to-all(f32[16,128,128]{2,1,0:T(8,128)S(1)} %pad_maximum_fusion), channel_id=1, replica_groups=mesh['zl'=4,'x'=4,'core'=2,'zh'=2,'y'=4] {'zl','x'}, dimensions={0} | all-to-all | bytes 2097152 | tf_op jit(solution)/shard_map/all_to_all | solution.py:270
  99.6 0.7 select_maximum_fusion
  100.3 4.7 %all-to-all-start.3 = ((f32[8,72,128]{2,1,0:T(8,128)}), f32[8,72,128]{2,1,0:T(8,128)S(1)}, u32[]{:S(2)}, u32[]{:S(2)}) async-start(f32[8,72,128]{2,1,0:T(8,128)} %select_maximum_fusion), calls=%async_computation.3 | async-start | bytes 589824 | tf_op jit(solution)/shard_map/all_to_all | solution.py:270
  105.1 1.0 copy-done.13
  106.1 5.2 %pair.1 = f32[16,64,128]{2,1,0:T(8,128)} custom-call(f32[1536,128]{1,0:T(8,128)S(1)} %bitcast.20, f32[1280,128]{1,0:T(8,128)S(1)} %bitcast.36, f32[1024,128]{1,0:T(8,128)S(1)} %copy-done.13, f32[1,128]{1,0:T(1,128)S(1)} %bitcast.37), custom_call_target="tpu_custom_call" | custom-call | flops 1610612736 | bytes 2490880 | tf_op jit(solution)/shard_map/pair/pallas_call | solution.py:253
  111.3 0.5 right.1.part_ref
  111.8 6.5 %all-to-all-done.3.col_ref = f32[8,72,128]{2,1,0:T(8,128)S(1)} async-done(((f32[8,72,128]{2,1,0:T(8,128)}), f32[8,72,128]{2,1,0:T(8,128)S(1)}, u32[]{:S(2)}, u32[]{:S(2)}) %all-to-all-start.3) | async-done | bytes 294944 | tf_op jit(solution)/shard_map/all_to_all | solution.py:270
  118.3 1.3 %finish.1 = (f32[256,256]{1,0:T(8,128)}, f32[4,128]{1,0:T(4,128)}) custom-call(f32[256,256]{1,0:T(8,128)S(1)} %bitcast.22, f32[1,256]{1,0:T(1,128)S(1)} %bitcast.30, f32[32,256]{1,0:T(8,128)S(1)} %bitcast.26, f32[256,256]{1,0:T(8,128)S(1)} %right.1.part_ref, f32[8,72,128]{2,1,0:T(8,128)S(1)} %all-to-all-done.3.col_ref), custom_call_target="tpu_custom_call" | custom-call | flops 25165824 | bytes 1117184 | tf_op jit(solution)/shard_map/finish/pallas_call | solution.py:253
  (32 shorter events, 0.2 us)
Async XLA Ops:
  0.6 1.0 copy-start
  1.6 0.8 copy-start.2
  2.3 0.8 copy-start.4
  3.1 0.7 copy-start.6
  3.8 0.7 copy-start.8
  4.5 0.7 copy-start.9
  5.1 0.7 copy-start.10
  7.3 24.1 %all-to-all-start = ((f32[8,64,128]{2,1,0:T(8,128)}), f32[8,64,128]{2,1,0:T(8,128)S(1)}, u32[]{:S(2)}, u32[]{:S(2)}) async-start(f32[8,64,128]{2,1,0:T(8,128)} %get-tuple-element.16), calls=%async_computation | async-start | bytes 524288 | tf_op jit(solution)/shard_map/all_to_all | solution.py:270
  17.5 1.0 copy-start.11
  18.5 1.0 copy-start.12
  22.3 1.3 %copy-start.15 = (bf16[4,512,512]{2,1,0:T(8,128)(2,1)}, bf16[4,512,512]{2,1,0:T(8,128)(2,1)S(1)}, u32[]{:S(2)}) copy-start(bf16[4,512,512]{2,1,0:T(8,128)(2,1)S(1)} %get-tuple-element.22.g_hi) | copy-start | bytes 6291460
  23.6 1.3 %copy-start.17 = (bf16[4,512,512]{2,1,0:T(8,128)(2,1)}, bf16[4,512,512]{2,1,0:T(8,128)(2,1)S(1)}, u32[]{:S(2)}) copy-start(bf16[4,512,512]{2,1,0:T(8,128)(2,1)S(1)} %get-tuple-element.23.g_lo) | copy-start | bytes 6291460
  31.5 27.5 %copy-start.16 = (bf16[4,512,512]{2,1,0:T(8,128)(2,1)S(1)}, bf16[4,512,512]{2,1,0:T(8,128)(2,1)}, u32[]{:S(2)}) copy-start(bf16[4,512,512]{2,1,0:T(8,128)(2,1)} %copy-done.15) | copy-start | bytes 6291460
  31.5 27.5 %copy-start.18 = (bf16[4,512,512]{2,1,0:T(8,128)(2,1)S(1)}, bf16[4,512,512]{2,1,0:T(8,128)(2,1)}, u32[]{:S(2)}) copy-start(bf16[4,512,512]{2,1,0:T(8,128)(2,1)} %copy-done.17) | copy-start | bytes 6291460
  56.8 2.2 %collective-permute-start = (f32[16,80,128]{2,1,0:T(8,128)S(1)}, f32[16,80,128]{2,1,0:T(8,128)S(1)}, u32[]{:S(2)}, u32[]{:S(2)}) collective-permute-start(f32[16,80,128]{2,1,0:T(8,128)S(1)} %slice.28), channel_id=1, source_target_pairs={{0,8},{8,0},{1,9},{9,1},{2,10},{10,2},{3,11},{11,3},{4,12},{12,4},... | collective-permute-start | bytes 1966088 | tf_op jit(solution)/shard_map/ppermute | solution.py:266
  65.5 2.6 %collective-permute-start.1 = (f32[16,112,128]{2,1,0:T(8,128)S(1)}, f32[16,112,128]{2,1,0:T(8,128)S(1)}, u32[]{:S(2)}, u32[]{:S(2)}) collective-permute-start(f32[16,112,128]{2,1,0:T(8,128)S(1)} %bitcast.34), channel_id=1, source_target_pairs={{0,8},{8,0},{1,9},{9,1},{2,10},{10,2},{3,11},{11,3},{4,12},{12,4},... | collective-permute-start | bytes 2752520 | tf_op jit(solution)/shard_map/ppermute | solution.py:266
  68.3 36.8 %copy-start.14 = (f32[128]{0:T(128)S(1)}, f32[128]{0:T(128)}, u32[]{:S(2)}) copy-start(f32[128]{0:T(128)} %param.18) | copy-start | bytes 1540
  100.3 17.9 %all-to-all-start.3 = ((f32[8,72,128]{2,1,0:T(8,128)}), f32[8,72,128]{2,1,0:T(8,128)S(1)}, u32[]{:S(2)}, u32[]{:S(2)}) async-start(f32[8,72,128]{2,1,0:T(8,128)} %select_maximum_fusion), calls=%async_computation.3 | async-start | bytes 589824 | tf_op jit(solution)/shard_map/all_to_all | solution.py:270
  105.1 1.0 copy-start.13
  106.1 5.2 %copy-start.5 = (f32[256,32]{0,1:T(8,128)S(1)}, f32[256,32]{0,1:T(8,128)}, u32[]{:S(2)}) copy-start(f32[256,32]{0,1:T(8,128)} %param.15) | copy-start | bytes 98308
  106.1 12.2 %copy-start.1 = (f32[4,64,256]{2,1,0:T(8,128)S(1)}, f32[4,64,256]{2,1,0:T(8,128)}, u32[]{:S(2)}) copy-start(f32[4,64,256]{2,1,0:T(8,128)} %param.10) | copy-start | bytes 786436
  106.1 12.2 %copy-start.3 = (f32[256,32]{0,1:T(8,128)S(1)}, f32[256,32]{0,1:T(8,128)}, u32[]{:S(2)}) copy-start(f32[256,32]{0,1:T(8,128)} %param.13) | copy-start | bytes 98308
  106.1 12.2 %copy-start.7 = (f32[256]{0:T(256)S(1)}, f32[256]{0:T(256)}, u32[]{:S(2)}) copy-start(f32[256]{0:T(256)} %param.11) | copy-start | bytes 3076

commit v3 on v2

--- a/solution.py
+++ b/solution.py
@@ -16,8 +16,7 @@
 COL = ("zh", "y")
 VMEM = pl.BlockSpec(memory_space=pltpu.VMEM)
 
-FWD = 96
-BWD = 112
+BWD = 48
 
 
 def contract(a, b, dims):
@@ -41,15 +40,13 @@
 
 
 def project_kernel(x_ref, scale_ref, offset_ref, w1_ref, b1_ref, w2_ref, b2_ref, left_ref, right_ref, tmp):
-    core = lax.axis_index("core")
     normed = standardized(x_ref[...])[0] * scale_ref[...] + offset_ref[...]
     tmp[:, 0:32] = contract(normed, w1_ref[...], ((1,), (1,))) + b1_ref[...]
     wide = jnp.concatenate([tmp[pl.ds(u, 64, stride=4), :][:, 0:32] for u in range(4)], axis=1)
     for q in range(4):
         part = jnp.concatenate([wide[s * 16 + q * 4 : s * 16 + q * 4 + 4] for s in range(4)], axis=0)
-        at = pl.multiple_of((q // 2 * 2 + lax.rem(q % 2 + core, 2)) * 16, 16)
         for copy in range(8):
-            left_ref[copy, pl.ds(at, 16), :] = part
+            left_ref[copy, q * 16 : q * 16 + 16, :] = part
     on = lax.broadcasted_iota(jnp.int32, (32, 32), 0) == lax.broadcasted_iota(jnp.int32, (32, 32), 1)
     b2 = jnp.sum(jnp.where(on, b2_ref[...], 0.0), axis=1, keepdims=True)
     right = contract(w2_ref[...], normed, ((1,), (1,))) + b2
@@ -64,13 +61,42 @@
     return jnp.where(chunk < 2, low, jnp.where(chunk == 2, parts[2], parts[3]))
 
 
-def rows(own_ref, other_ref, row, right):
+def chip_of(dz, dx):
+    return jnp.bitwise_xor(lax.axis_index("zl"), dz) * 4 + jnp.bitwise_xor(lax.axis_index("x"), dx)
+
+
+def left_rows(left_ref, quad):
+    core = lax.axis_index("core")
     got = []
-    for ref, pitch, base in ((own_ref, FWD, 32), (other_ref, FWD - 16, 16)):
+    for side in (core, 1 - core):
         for s in range(4):
-            at = base + s * 16 + row if right else s * 4 + row
-            got.append(ref[pl.ds(at, 16, stride=pitch), :])
+            got.append(left_ref[pl.ds(side * 16 + s * 4 + quad, 16, stride=32), :])
     return jnp.concatenate(got, axis=0)
+
+
+def gather_right(parts, right_all):
+    for at, ref in enumerate(parts):
+        for dz in range(4):
+            start = (at // 4) * 1024 + chip_of(dz, at % 4) * 64
+            right_all[pl.ds(pl.multiple_of(start, 64), 64), :] = ref[dz]
+
+
+def right_rows(right_all, e):
+    got = []
+    for half in range(2):
+        for s in range(4):
+            got.append(right_all[pl.ds(half * 1024 + s * 16 + e, 16, stride=64), :])
+    return jnp.concatenate(got, axis=0)
+
+
+def left_turned(left_ref, lt):
+    for quad in range(4):
+        hi, lo = halves(left_rows(left_ref, quad).T)
+        for p in range(4):
+            for m in range(4):
+                at = quad * 128 + ((p + m) % 4) * 32
+                lt[m, at : at + 32, 0:128] = hi[p * 32 : p * 32 + 32]
+                lt[m, at : at + 32, 128:256] = lo[p * 32 : p * 32 + 32]
 
 
 def weights_by_class(w_ref, w_hl):
@@ -114,25 +140,18 @@
                 g_lo[m, at : at + 64, quad * 128 : quad * 128 + 128] = lo
 
 
-def outer_product(own_ref, other_ref, outer, lcat, rt, a_hi, a_lo, lt=None, r_hl=None):
+def outer_product(left_ref, parts, right_all, outer, lcat, rt, a_hi, a_lo, r_hl=None):
+    gather_right(parts, right_all)
     for quad in range(4):
-        v = rows(own_ref, other_ref, quad, False)
+        v = left_rows(left_ref, quad)
         for m in range(4):
             hi, lo = halves(pltpu.roll(v, 32 * m, axis=1) if m else v)
             lcat[m, 0:128, quad * 128 : quad * 128 + 128] = hi
             lcat[m, 128:256, quad * 128 : quad * 128 + 128] = lo
             lcat[m, 256:384, quad * 128 : quad * 128 + 128] = hi
-        if lt is None:
-            continue
-        hi, lo = halves(v.T)
-        for p in range(4):
-            for m in range(4):
-                at = quad * 128 + ((p + m) % 4) * 32
-                lt[m, at : at + 32, 0:128] = hi[p * 32 : p * 32 + 32]
-                lt[m, at : at + 32, 128:256] = lo[p * 32 : p * 32 + 32]
     for e in range(16):
         g, m = e // 4, e % 4
-        v = rows(own_ref, other_ref, e, True)
+        v = right_rows(right_all, e)
         if r_hl is not None:
             hi, lo = halves(v)
             r_hl[m, 0:128, g * 128 : g * 128 + 128] = hi
@@ -154,9 +173,10 @@
                 a_lo[d, quad * 64 : quad * 64 + 64, block * 128 : block * 128 + 128] = lo
 
 
-def pair_kernel(own_ref, other_ref, w_ref, bias_ref, pair_ref, outer, lcat, rt, a_hi, a_lo, w_hl):
+def pair_kernel(left_ref, *refs):
+    parts, (w_ref, bias_ref, pair_ref, right_all, outer, lcat, rt, a_hi, a_lo, w_hl) = refs[:8], refs[8:]
     weights_by_class(w_ref, w_hl)
-    outer_product(own_ref, other_ref, outer, lcat, rt, a_hi, a_lo)
+    outer_product(left_ref, parts, right_all, outer, lcat, rt, a_hi, a_lo)
     for d in range(4):
         both = matmul(a_hi[d], w_hl[d])
         pair = both[:, 0:128] + both[:, 128:256] + matmul(a_lo[d], w_hl[d, :, 0:128])
@@ -165,12 +185,11 @@
             pair_ref[quad * 4 + d] = pair[quad * 64 : quad * 64 + 64]
 
 
-def tile_kernel(
-    own_ref, other_ref, g_hi, g_lo, cot_t, own_out, other_out,
-    outer, lcat, rt, a_hi, a_lo, lt, r_hl, dw,
-):
+def tile_kernel(left_ref, *refs):
+    parts, (g_hi, g_lo, cot_t, own_out, other_out) = refs[:8], refs[8:13]
+    right_all, outer, lcat, rt, a_hi, a_lo, r_hl, dw = refs[13:]
     core = lax.axis_index("core")
-    outer_product(own_ref, other_ref, outer, lcat, rt, a_hi, a_lo, lt, r_hl)
+    outer_product(left_ref, parts, right_all, outer, lcat, rt, a_hi, a_lo, r_hl)
     for d in range(4):
         both = matmul(cot_t[d], a_hi[d])
         part = both[0:128] + both[128:256] + matmul(cot_t[d, 0:128, :], a_lo[d])
@@ -185,19 +204,9 @@
     for block in range(8):
         for p in range(4):
             for out, side in ((own_out, core), (other_out, 1 - core)):
-                out[pl.ds(64 + p * 8 + block, 16, stride=BWD), :] = dw[
+                out[pl.ds(p * 8 + block, 16, stride=BWD), :] = dw[
                     block, pl.ds(p * 32 + side, 16, stride=2), :
                 ]
-    for m in range(4):
-        both = matmul(g_hi[m], lt[m])
-        v = both[:, 0:128] + both[:, 128:256] + matmul(g_lo[m], lt[m, :, 0:128])
-        for g in range(4):
-            t = v[g * 128 : g * 128 + 128].T * (1.0 / 128)
-            e = g * 4 + m
-            for half, out in ((0, own_out), (1, other_out)):
-                for s in range(4):
-                    at = (half * 4 + s) * 16
-                    out[pl.ds(s * 16 + e, 16, stride=BWD), :] = t[at : at + 16]
     total = [None] * 4
     for m in range(4):
         both = matmul(r_hl[m], g_hi[m])
@@ -212,13 +221,30 @@
         for half, out in ((0, own_out), (1, other_out)):
             for s in range(4):
                 at = (half * 4 + s) * 16
-                out[pl.ds(96 + s * 4 + quad, 16, stride=BWD), :] = t[at : at + 16]
-
-
-def right_kernel(w2_ref, right_ref, out_ref):
-    total = right_ref[0, 0:64]
-    for chip in range(1, 16):
-        total = total + right_ref[chip, 0:64]
+                out[pl.ds(32 + s * 4 + quad, 16, stride=BWD), :] = t[at : at + 16]
+
+
+def right_gradient_kernel(left_ref, g_hi, g_lo, *refs):
+    outs, (lt, total) = refs[:8], refs[8:]
+    left_turned(left_ref, lt)
+    for m in range(4):
+        both = matmul(g_hi[m], lt[m])
+        v = both[:, 0:128] + both[:, 128:256] + matmul(g_lo[m], lt[m, :, 0:128])
+        for g in range(4):
+            t = v[g * 128 : g * 128 + 128].T * (1.0 / 128)
+            for half in range(2):
+                for s in range(4):
+                    at = (half * 4 + s) * 16
+                    row = half * 1024 + s * 16 + g * 4 + m
+                    total[pl.ds(row, 16, stride=64), :] = t[at : at + 16]
+    for at, ref in enumerate(outs):
+        for dz in range(4):
+            start = (at // 4) * 1024 + chip_of(dz, at % 4) * 64
+            ref[dz] = total[pl.ds(pl.multiple_of(start, 64), 64), :]
+
+
+def right_kernel(w2_ref, a_ref, b_ref, c_ref, d_ref, out_ref):
+    total = (a_ref[...] + b_ref[...]) + (c_ref[...] + d_ref[...])
     for s in range(4):
         part = total[s * 16 : s * 16 + 16, :]
         entries = jnp.concatenate([part[:, 0:64], part[:, 64:128]], axis=0)
@@ -256,7 +282,9 @@
         in_specs=[VMEM] * len(args),
         out_specs=(VMEM,) * len(outs),
         scratch_shapes=[pltpu.VMEM(*s) for s in scratch],
-        compiler_params=pltpu.CompilerParams(vmem_limit_bytes=mib * 1024 * 1024),
+        compiler_params=pltpu.CompilerParams(
+            vmem_limit_bytes=mib * 1024 * 1024 if mib else None
+        ),
         cost_estimate=pl.CostEstimate(flops=flops, bytes_accessed=moved, transcendentals=0),
         name=name,
     )(*args)
@@ -264,6 +292,10 @@
 
 def swap_cores(array):
     return lax.ppermute(array, "core", [(0, 1), (1, 0)])
+
+
+def from_peer(array, axis, apart):
+    return lax.ppermute(array, axis, [(i, i ^ apart) for i in range(4)])
 
 
 def exchange(array, axes):
@@ -293,7 +325,7 @@
         "project",
         [((8, 64, 128), f32), ((64, 128), f32)],
         [((256, 128), f32)],
-        8,
+        None,
         2 * small,
         x,
         scale,
@@ -318,34 +350,50 @@
         result_matrix,
         edge_incoming_sensitivity,
     )
-    left = exchange(left, COL)
-    sent = jnp.concatenate(
-        [left.reshape(16, 32, 128), jnp.broadcast_to(right[None], (16, 64, 128))], axis=1
-    )
-    sent, g_hi, g_lo, cot_t = lax.optimization_barrier((sent, g_hi, g_lo, cot_t))
-    own = exchange(sent, CHIP)
-    other = swap_cores(own[:, 16:]).reshape(16 * (FWD - 16), 128)
-    own = own.reshape(16 * FWD, 128)
+    left = exchange(left, COL).reshape(32, 16, 128)
+    right = jnp.stack([right] + [from_peer(right, "zl", dz) for dz in (1, 2, 3)])
+    left, right, g_hi, g_lo, cot_t = lax.optimization_barrier((left, right, g_hi, g_lo, cot_t))
+    left = exchange(left, ROW).reshape(512, 128)
+    parts = [right] + [from_peer(right, "x", dx) for dx in (1, 2, 3)]
+    parts = parts + [swap_cores(part) for part in parts]
     working = [
+        ((2048, 128), f32),
         ((4, 512, 512), f32),
         ((4, 384, 512), bf16),
         ((4, 512, 384), bf16),
         ((4, 256, 1024), bf16),
         ((4, 256, 1024), bf16),
     ]
-    own_grads, other_grads = call(
+    own, other = call(
         tile_kernel,
         "tile",
         [((16 * BWD, 128), f32), ((16 * BWD, 128), f32)],
-        working + [((4, 512, 256), bf16), ((4, 256, 512), bf16), ((8, 128, 128), f32)],
-        32,
-        4 * step,
-        own,
-        other,
+        working + [((4, 256, 512), bf16), ((8, 128, 128), f32)],
+        28,
+        3 * step,
+        left,
+        *parts,
         g_hi,
         g_lo,
         cot_t,
     )
+    own = own.reshape(16, BWD, 128)
+    got = swap_cores(other.reshape(16, BWD, 128))
+    sent = jnp.concatenate([own[:, :32] + got[:, :32], own[:, 32:], got[:, 32:]], axis=1)
+    back = exchange(sent, CHIP)
+    sums = call(
+        right_gradient_kernel,
+        "right_gradient",
+        [((4, 64, 128), f32)] * 8,
+        [((4, 512, 256), bf16), ((2048, 128), f32)],
+        16,
+        step,
+        left,
+        g_hi,
+        g_lo,
+    )
+    sums = [a + swap_cores(b) for a, b in zip(sums[:4], sums[4:])]
+    right = sums[0] + sum(from_peer(sums[dx], "x", dx) for dx in (1, 2, 3))
     (pair,) = call(
         pair_kernel,
         "pair",
@@ -353,23 +401,19 @@
         working + [((4, 1024, 256), bf16)],
         28,
         2 * step,
-        own,
-        other,
+        left,
+        *parts,
         result_matrix,
         result_intercept.reshape(1, 128),
     )
-    own_grads = own_grads.reshape(16, BWD, 128)
-    got = swap_cores(other_grads.reshape(16, BWD, 128))
+    weight = back[:, :32].sum(axis=0).reshape(4, 8, 128).transpose(1, 0, 2)
     sent = jnp.concatenate(
-        [own_grads[:, :96] + got[:, :96], own_grads[:, 96:], got[:, 96:]], axis=1
-    )
-    back = exchange(sent, CHIP)
-    weight = back[:, 64:96].sum(axis=0).reshape(4, 8, 128).transpose(1, 0, 2)
-    sent = jnp.concatenate(
-        [back[:, 96:].reshape(8, 64, 128), jnp.pad(weight, ((0, 0), (0, 4), (0, 0)))], axis=1
-    )
+        [back[:, 32:].reshape(8, 64, 128), jnp.pad(weight, ((0, 0), (0, 4), (0, 0)))], axis=1
+    )
+    sent, right, pair = lax.optimization_barrier((sent, right, pair))
     cols = exchange(sent, COL)
-    (part,) = call(right_kernel, "right", [((256, 256), f32)], [], 8, small, w2, back)
+    right = [right[0]] + [from_peer(right[dz], "zl", dz) for dz in (1, 2, 3)]
+    (part,) = call(right_kernel, "right", [((256, 256), f32)], [], 8, small, w2, *right)
     grad, weight = call(
         finish_kernel,
         "finish",

time: 120 us -> 109 us (0.908)
  blocking collectives: 56.4 us -> 0 us
  starting transfers between devices: 15.3 us -> 47 us
  waiting for transfers between devices: 17.3 us -> 29.4 us
  local copies, waits for them, and re-layouts: 11 us -> 8.49 us
  Pallas kernels: 17.8 us -> 19.8 us
  other arithmetic: 0.98 us -> 2.79 us
    all_to_all x2 -> x0, blocking collectives: 56.4 us -> none  [exchange(): return lax.all_to_all(array, axes, 0, 0, tiled=True)]
    ppermute x0 -> x12, starting transfers between devices: none -> 17 us  [from_peer(): return lax.ppermute(array, axis, [(i, i ^ apart) for i in range(4)])]
    ppermute x0 -> x12, waiting for transfers between devices: none -> 16.6 us  [from_peer(): return lax.ppermute(array, axis, [(i, i ^ apart) for i in range(4)])]
    all_to_all x2 -> x4, starting transfers between devices: 14.9 us -> 28.6 us  [exchange(): return lax.all_to_all(array, axes, 0, 0, tiled=True)]
    all_to_all x2 -> x4, waiting for transfers between devices: 12.9 us -> 9.58 us  [exchange(): return lax.all_to_all(array, axes, 0, 0, tiled=True)]
    unnamed x38 -> x28, local copies, waits for them, and re-layouts: 10.9 us -> 8.46 us
    pallas_call x6 -> x7, Pallas kernels: 17.8 us -> 19.8 us  [call(): pl.pallas_call(kernel, out_shape=shapes, in_specs=[VMEM] * len(args), out...]
    ppermute x2 -> x9, waiting for transfers between devices: 4.41 us -> 3.23 us  [swap_cores(): return lax.ppermute(array, 'core', [(0, 1), (1, 0)])]
  transfers between devices with their start and end apart: 4 -> 25, of which waited for: 4 -> 10; matrix products, arithmetic and copies ran while one was open for 0% -> 0% of each run, Pallas kernels for 7% -> 10%
where the time goes in v3:
time: 109 us; the launch traced here: 108 us
  starting transfers between devices  47 us (43%)
  waiting for transfers between devices  29.4 us (27%)
  Pallas kernels  19.8 us (18%)
  local copies, waits for them, and re-layouts  8.49 us (8%)
  other arithmetic  2.79 us (3%)
    all_to_all x4, starting transfers between devices, exchange(): return lax.all_to_all(array, axes, 0, 0, tiled=True)  28.6 us
    pallas_call x7, Pallas kernels, call(): pl.pallas_call(kernel, out_shape=shapes, in_specs=[VMEM] * len(args), out...  19.8 us
    ppermute x12, starting transfers between devices, from_peer(): return lax.ppermute(array, axis, [(i, i ^ apart) for i in range(4)])  17 us
    ppermute x12, waiting for transfers between devices, from_peer(): return lax.ppermute(array, axis, [(i, i ^ apart) for i in range(4)])  16.6 us
    all_to_all x4, waiting for transfers between devices, exchange(): return lax.all_to_all(array, axes, 0, 0, tiled=True)  9.58 us
    unnamed x28, local copies, waits for them, and re-layouts  8.46 us
    ppermute x9, waiting for transfers between devices, swap_cores(): return lax.ppermute(array, 'core', [(0, 1), (1, 0)])  3.23 us
  transfers between devices with their start and end apart: 25, of which 10 were waited for; matrix products, arithmetic and copies ran while one was open for 0% of the time, Pallas kernels for 10%

profile of v3, /device:TPU:32, one launch (start us, length us, event | category | flops | bytes accessed | tf_op | source)
XLA Modules:
  0.0 108.4 jit_solution(17769961922222438511)
XLA Ops:
  0.6 2.5 %project.1 = (f32[8,64,128]{2,1,0:T(8,128)}, f32[64,128]{1,0:T(8,128)}) custom-call(f32[256,256]{1,0:T(8,128)} %bitcast.33, f32[1,256]{1,0:T(1,128)} %bitcast.41, f32[1,256]{1,0:T(1,128)} %bitcast.52, f32[32,256]{1,0:T(8,128)} %bitcast.39, f32[1,32]{1,0:T(1,128)} %bitcast.53, f32[32,256]{1,0:T(8,128)} %bitcast.37, f32[1,32]{1,0:T(1,128)} %bitcast.54), custom_call_target="tpu_custom_call" | custom-call | flops 50331648 | bytes 624896 | tf_op jit(solution)/shard_map/project/pallas_call | solution.py:279
  3.2 10.3 %all-to-all-start = ((f32[8,64,128]{2,1,0:T(8,128)}), f32[8,64,128]{2,1,0:T(8,128)}, u32[]{:S(2)}, u32[]{:S(2)}) async-start(f32[8,64,128]{2,1,0:T(8,128)} %get-tuple-element.28), calls=%async_computation | async-start | bytes 524288 | tf_op jit(solution)/shard_map/all_to_all | solution.py:302
  14.5 2.4 %collective-permute-start.1 = (f32[64,128]{1,0:T(8,128)}, f32[64,128]{1,0:T(8,128)S(1)}, u32[]{:S(2)}, u32[]{:S(2)}) collective-permute-start(f32[64,128]{1,0:T(8,128)} %get-tuple-element.29), channel_id=1, source_target_pairs={{0,128},{64,192},{128,0},{192,64},{1,129},{65,193},{129,1},{193,65... | collective-permute-start | bytes 98312 | tf_op jit(solution)/shard_map/ppermute | solution.py:298
  17.0 1.0 copy-done.7
  18.0 1.0 copy-done.8
  19.1 2.7 %cotangent.1 = (bf16[4,512,512]{2,1,0:T(8,128)(2,1)S(1)}, bf16[4,512,512]{2,1,0:T(8,128)(2,1)S(1)}, bf16[4,256,256]{2,1,0:T(8,128)(2,1)S(1)}) custom-call(f32[1024,128]{1,0:T(8,128)S(1)} %copy-done.8, f32[16,64,128]{2,1,0:T(8,128)S(1)} %copy-done.7), custom_call_target="tpu_custom_call" | custom-call | flops 805306368 | bytes 5767168 | tf_op jit(solution)/shard_map/cotangent/pallas_call | solution.py:279
  21.8 1.3 %copy-done = bf16[4,512,512]{2,1,0:T(8,128)(2,1)} copy-done((bf16[4,512,512]{2,1,0:T(8,128)(2,1)}, bf16[4,512,512]{2,1,0:T(8,128)(2,1)S(1)}, u32[]{:S(2)}) %copy-start) | copy-done | bytes 2097176
  24.0 3.9 %all-to-all-done = f32[8,64,128]{2,1,0:T(8,128)} async-done(((f32[8,64,128]{2,1,0:T(8,128)}), f32[8,64,128]{2,1,0:T(8,128)}, u32[]{:S(2)}, u32[]{:S(2)}) %all-to-all-start) | async-done | bytes 262176 | tf_op jit(solution)/shard_map/all_to_all | solution.py:302
  27.9 6.4 %all-to-all-start.1 = ((f32[32,16,128]{2,1,0:T(8,128)}), f32[32,16,128]{2,1,0:T(8,128)S(1)}, u32[]{:S(2)}, u32[]{:S(2)}) async-start(f32[32,16,128]{2,1,0:T(8,128)} %bitcast.7), calls=%async_computation.1 | async-start | bytes 524288 | tf_op jit(solution)/shard_map/all_to_all | solution.py:302
  34.2 1.6 %collective-permute-start.3 = (f32[4,64,128]{2,1,0:T(8,128)S(1)}, f32[4,64,128]{2,1,0:T(8,128)S(1)}, u32[]{:S(2)}, u32[]{:S(2)}) collective-permute-start(f32[4,64,128]{2,1,0:T(8,128)S(1)} %pad_maximum_fusion.1.refs_0_), channel_id=1, source_target_pairs={{0,16},{16,0},{32,48},{48,32},{1,17},{17,1},{33,49},{49,33},{2,18}... | collective-permute-start | bytes 393224 | tf_op jit(solution)/shard_map/ppermute | solution.py:298
  35.8 2.7 %collective-permute-start.4 = (f32[4,64,128]{2,1,0:T(8,128)S(1)}, f32[4,64,128]{2,1,0:T(8,128)S(1)}, u32[]{:S(2)}, u32[]{:S(2)}) collective-permute-start(f32[4,64,128]{2,1,0:T(8,128)S(1)} %pad_maximum_fusion.1.refs_0_), channel_id=1, source_target_pairs={{0,32},{16,48},{32,0},{48,16},{1,33},{17,49},{33,1},{49,17},{2,34}... | collective-permute-start | bytes 393224 | tf_op jit(solution)/shard_map/ppermute | solution.py:298
  39.0 3.4 %collective-permute-done.3.refs_1_ = f32[4,64,128]{2,1,0:T(8,128)S(1)} collective-permute-done((f32[4,64,128]{2,1,0:T(8,128)S(1)}, f32[4,64,128]{2,1,0:T(8,128)S(1)}, u32[]{:S(2)}, u32[]{:S(2)}) %collective-permute-start.3) | collective-permute-done | bytes 131104 | tf_op jit(solution)/shard_map/ppermute | solution.py:298
  42.5 4.4 %collective-permute-done.4.refs_2_ = f32[4,64,128]{2,1,0:T(8,128)S(1)} collective-permute-done((f32[4,64,128]{2,1,0:T(8,128)S(1)}, f32[4,64,128]{2,1,0:T(8,128)S(1)}, u32[]{:S(2)}, u32[]{:S(2)}) %collective-permute-start.4) | collective-permute-done | bytes 131104 | tf_op jit(solution)/shard_map/ppermute | solution.py:298
  46.9 1.4 %collective-permute-done.5.refs_3_ = f32[4,64,128]{2,1,0:T(8,128)S(1)} collective-permute-done((f32[4,64,128]{2,1,0:T(8,128)S(1)}, f32[4,64,128]{2,1,0:T(8,128)S(1)}, u32[]{:S(2)}, u32[]{:S(2)}) %collective-permute-start.5) | collective-permute-done | bytes 131104 | tf_op jit(solution)/shard_map/ppermute | solution.py:298
  48.3 1.3 %collective-permute-done.9.refs_7_ = f32[4,64,128]{2,1,0:T(8,128)S(1)} collective-permute-done((f32[4,64,128]{2,1,0:T(8,128)S(1)}, f32[4,64,128]{2,1,0:T(8,128)S(1)}, u32[]{:S(2)}, u32[]{:S(2)}) %collective-permute-start.9) | collective-permute-done | bytes 131104 | tf_op jit(solution)/shard_map/ppermute | solution.py:294
  49.7 1.6 %copy-done.1 = bf16[4,512,512]{2,1,0:T(8,128)(2,1)S(1)} copy-done((bf16[4,512,512]{2,1,0:T(8,128)(2,1)S(1)}, bf16[4,512,512]{2,1,0:T(8,128)(2,1)}, u32[]{:S(2)}) %copy-start.1) | copy-done | bytes 2097176
  51.3 1.0 copy-done.12
  52.3 5.5 %tile.1 = (f32[768,128]{1,0:T(8,128)S(1)}, f32[768,128]{1,0:T(8,128)S(1)}) custom-call(f32[512,128]{1,0:T(8,128)S(1)} %bitcast.30, f32[4,64,128]{2,1,0:T(8,128)S(1)} %pad_maximum_fusion.1.refs_0_, f32[4,64,128]{2,1,0:T(8,128)S(1)} %collective-permute-done.3.refs_1_, f32[4,64,128]{2,1,0:T(8,128)S(1)} %collective-permute-done.4.refs_2_, ...), custom_call_target="tpu_custom_call" | custom-call | flops 2415919104 | bytes 6815744 | tf_op jit(solution)/shard_map/tile/pallas_call | solution.py:279
  58.0 1.6 %collective-permute-done.10 = f32[16,48,128]{2,1,0:T(8,128)S(1)} collective-permute-done((f32[16,48,128]{2,1,0:T(8,128)S(1)}, f32[16,48,128]{2,1,0:T(8,128)S(1)}, u32[]{:S(2)}, u32[]{:S(2)}) %collective-permute-start.10) | collective-permute-done | bytes 393248 | tf_op jit(solution)/shard_map/ppermute | solution.py:294
  60.5 4.8 %all-to-all-start.2 = ((f32[16,64,128]{2,1,0:T(8,128)}), f32[16,64,128]{2,1,0:T(8,128)}, u32[]{:S(2)}, u32[]{:S(2)}) async-start(f32[16,64,128]{2,1,0:T(8,128)} %pad_maximum_fusion), calls=%async_computation.2 | async-start | bytes 1048576 | tf_op jit(solution)/shard_map/all_to_all | solution.py:302
  65.3 1.6 %copy-done.2 = bf16[4,512,512]{2,1,0:T(8,128)(2,1)S(1)} copy-done((bf16[4,512,512]{2,1,0:T(8,128)(2,1)S(1)}, bf16[4,512,512]{2,1,0:T(8,128)(2,1)}, u32[]{:S(2)}) %copy-start.2) | copy-done | bytes 2097176
  66.9 1.9 %right_gradient.1 = (f32[4,64,128]{2,1,0:T(8,128)S(1)}, f32[4,64,128]{2,1,0:T(8,128)S(1)}, f32[4,64,128]{2,1,0:T(8,128)S(1)}, f32[4,64,128]{2,1,0:T(8,128)S(1)},...) custom-call(f32[512,128]{1,0:T(8,128)S(1)} %bitcast.31, ...), custom_call_target="tpu_custom_call" | custom-call | flops 805306368 | bytes 5505024 | tf_op jit(solution)/shard_map/right_gradient/pallas_call | solution.py:279
  70.3 2.8 %collective-permute-start.17 = (f32[4,64,128]{2,1,0:T(8,128)S(1)}, f32[4,64,128]{2,1,0:T(8,128)S(1)}, u32[]{:S(2)}, u32[]{:S(2)}) collective-permute-start(f32[4,64,128]{2,1,0:T(8,128)S(1)} %add.31), channel_id=1, source_target_pairs={{0,48},{16,32},{32,16},{48,0},{1,49},{17,33},{33,17},{49,1},{2,50}... | collective-permute-start | bytes 393224 | tf_op jit(solution)/shard_map/ppermute | solution.py:298
  73.5 2.1 %collective-permute-start.15 = (f32[4,64,128]{2,1,0:T(8,128)S(1)}, f32[4,64,128]{2,1,0:T(8,128)S(1)}, u32[]{:S(2)}, u32[]{:S(2)}) collective-permute-start(f32[4,64,128]{2,1,0:T(8,128)S(1)} %add.29), channel_id=1, source_target_pairs={{0,32},{16,48},{32,0},{48,16},{1,33},{17,49},{33,1},{49,17},{2,34}... | collective-permute-start | bytes 393224 | tf_op jit(solution)/shard_map/ppermute | solution.py:298
  75.6 5.4 %pair.1 = f32[16,64,128]{2,1,0:T(8,128)} custom-call(f32[512,128]{1,0:T(8,128)S(1)} %bitcast.32, f32[4,64,128]{2,1,0:T(8,128)S(1)} %pad_maximum_fusion.1.refs_0_, f32[4,64,128]{2,1,0:T(8,128)S(1)} %collective-permute-done.3.refs_1_, f32[4,64,128]{2,1,0:T(8,128)S(1)} %collective-permute-done.4.refs_2_, f32[4,64,128]{2,1,0:T(8,128)S(1)} %collective-permute-done.5.refs_3_, ...), custom_call_target="tpu_custom_call" | custom-call | flops 1610612736 | bytes 2359808 | tf_op jit(solution)/shard_map/pair/pallas_call | solution.py:279
  81.0 2.7 %collective-permute-done.15 = f32[4,64,128]{2,1,0:T(8,128)S(1)} collective-permute-done((f32[4,64,128]{2,1,0:T(8,128)S(1)}, f32[4,64,128]{2,1,0:T(8,128)S(1)}, u32[]{:S(2)}, u32[]{:S(2)}) %collective-permute-start.15) | collective-permute-done | bytes 131104 | tf_op jit(solution)/shard_map/ppermute | solution.py:298
  83.8 1.1 fusion
  85.6 7.1 %all-to-all-start.3 = ((f32[8,72,128]{2,1,0:T(8,128)}), f32[8,72,128]{2,1,0:T(8,128)S(1)}, u32[]{:S(2)}, u32[]{:S(2)}) async-start(f32[8,72,128]{2,1,0:T(8,128)} %select_maximum_fusion), calls=%async_computation.3 | async-start | bytes 589824 | tf_op jit(solution)/shard_map/all_to_all | solution.py:302
  92.8 3.0 %collective-permute-start.19 = (f32[64,128]{1,0:T(8,128)S(1)}, f32[64,128]{1,0:T(8,128)S(1)}, u32[]{:S(2)}, u32[]{:S(2)}) collective-permute-start(f32[64,128]{1,0:T(8,128)S(1)} %get-tuple-element.56), channel_id=1, source_target_pairs={{0,128},{64,192},{128,0},{192,64},{1,129},{65,193},{129,1},{193,65... | collective-permute-start | bytes 98312 | tf_op jit(solution)/shard_map/ppermute | solution.py:298
  96.3 4.6 %collective-permute-done.18.b_ref = f32[64,128]{1,0:T(8,128)S(1)} collective-permute-done((f32[64,128]{1,0:T(8,128)S(1)}, f32[64,128]{1,0:T(8,128)S(1)}, u32[]{:S(2)}, u32[]{:S(2)}) %collective-permute-start.18) | collective-permute-done | bytes 32800 | tf_op jit(solution)/shard_map/ppermute | solution.py:298
  101.4 5.7 %all-to-all-done.3.col_ref = f32[8,72,128]{2,1,0:T(8,128)S(1)} async-done(((f32[8,72,128]{2,1,0:T(8,128)}), f32[8,72,128]{2,1,0:T(8,128)S(1)}, u32[]{:S(2)}, u32[]{:S(2)}) %all-to-all-start.3) | async-done | bytes 294944 | tf_op jit(solution)/shard_map/all_to_all | solution.py:302
  107.1 1.3 %finish.1 = (f32[256,256]{1,0:T(8,128)}, f32[4,128]{1,0:T(4,128)}) custom-call(f32[256,256]{1,0:T(8,128)S(1)} %bitcast.34, f32[1,256]{1,0:T(1,128)S(1)} %bitcast.42, f32[32,256]{1,0:T(8,128)S(1)} %bitcast.40, f32[256,256]{1,0:T(8,128)S(1)} %right.1.part_ref, f32[8,72,128]{2,1,0:T(8,128)S(1)} %all-to-all-done.3.col_ref), custom_call_target="tpu_custom_call" | custom-call | flops 25165824 | bytes 1117184 | tf_op jit(solution)/shard_map/finish/pallas_call | solution.py:279
  (66 shorter events, 7.4 us)
Async XLA Ops:
  3.2 20.8 %copy-start.13 = (f32[64,128]{1,0:T(8,128)S(1)}, f32[64,128]{1,0:T(8,128)}, u32[]{:S(2)}) copy-start(f32[64,128]{1,0:T(8,128)} %get-tuple-element.29) | copy-start | bytes 98308
  3.2 24.7 %all-to-all-start = ((f32[8,64,128]{2,1,0:T(8,128)}), f32[8,64,128]{2,1,0:T(8,128)}, u32[]{:S(2)}, u32[]{:S(2)}) async-start(f32[8,64,128]{2,1,0:T(8,128)} %get-tuple-element.28), calls=%async_computation | async-start | bytes 524288 | tf_op jit(solution)/shard_map/all_to_all | solution.py:302
  13.5 10.5 %collective-permute-start.2 = (f32[64,128]{1,0:T(8,128)}, f32[64,128]{1,0:T(8,128)S(1)}, u32[]{:S(2)}, u32[]{:S(2)}) collective-permute-start(f32[64,128]{1,0:T(8,128)} %get-tuple-element.29), channel_id=1, source_target_pairs={{0,192},{64,128},{128,64},{192,0},{1,193},{65,129},{129,65},{193,1... | collective-permute-start | bytes 98312 | tf_op jit(solution)/shard_map/ppermute | solution.py:298
  14.5 9.4 %collective-permute-start.1 = (f32[64,128]{1,0:T(8,128)}, f32[64,128]{1,0:T(8,128)S(1)}, u32[]{:S(2)}, u32[]{:S(2)}) collective-permute-start(f32[64,128]{1,0:T(8,128)} %get-tuple-element.29), channel_id=1, source_target_pairs={{0,128},{64,192},{128,0},{192,64},{1,129},{65,193},{129,1},{193,65... | collective-permute-start | bytes 98312 | tf_op jit(solution)/shard_map/ppermute | solution.py:298
  16.9 7.1 %collective-permute-start = (f32[64,128]{1,0:T(8,128)}, f32[64,128]{1,0:T(8,128)S(1)}, u32[]{:S(2)}, u32[]{:S(2)}) collective-permute-start(f32[64,128]{1,0:T(8,128)} %get-tuple-element.29), channel_id=1, source_target_pairs={{0,64},{64,0},{128,192},{192,128},{1,65},{65,1},{129,193},{193,129... | collective-permute-start | bytes 98312 | tf_op jit(solution)/shard_map/ppermute | solution.py:298
  27.9 21.8 %all-to-all-start.1 = ((f32[32,16,128]{2,1,0:T(8,128)}), f32[32,16,128]{2,1,0:T(8,128)S(1)}, u32[]{:S(2)}, u32[]{:S(2)}) async-start(f32[32,16,128]{2,1,0:T(8,128)} %bitcast.7), calls=%async_computation.1 | async-start | bytes 524288 | tf_op jit(solution)/shard_map/all_to_all | solution.py:302
  34.2 8.2 %collective-permute-start.3 = (f32[4,64,128]{2,1,0:T(8,128)S(1)}, f32[4,64,128]{2,1,0:T(8,128)S(1)}, u32[]{:S(2)}, u32[]{:S(2)}) collective-permute-start(f32[4,64,128]{2,1,0:T(8,128)S(1)} %pad_maximum_fusion.1.refs_0_), channel_id=1, source_target_pairs={{0,16},{16,0},{32,48},{48,32},{1,17},{17,1},{33,49},{49,33},{2,18}... | collective-permute-start | bytes 393224 | tf_op jit(solution)/shard_map/ppermute | solution.py:298
  35.8 11.1 %collective-permute-start.4 = (f32[4,64,128]{2,1,0:T(8,128)S(1)}, f32[4,64,128]{2,1,0:T(8,128)S(1)}, u32[]{:S(2)}, u32[]{:S(2)}) collective-permute-start(f32[4,64,128]{2,1,0:T(8,128)S(1)} %pad_maximum_fusion.1.refs_0_), channel_id=1, source_target_pairs={{0,32},{16,48},{32,0},{48,16},{1,33},{17,49},{33,1},{49,17},{2,34}... | collective-permute-start | bytes 393224 | tf_op jit(solution)/shard_map/ppermute | solution.py:298
  38.5 9.8 %collective-permute-start.5 = (f32[4,64,128]{2,1,0:T(8,128)S(1)}, f32[4,64,128]{2,1,0:T(8,128)S(1)}, u32[]{:S(2)}, u32[]{:S(2)}) collective-permute-start(f32[4,64,128]{2,1,0:T(8,128)S(1)} %pad_maximum_fusion.1.refs_0_), channel_id=1, source_target_pairs={{0,48},{16,32},{32,16},{48,0},{1,49},{17,33},{33,17},{49,1},{2,50}... | collective-permute-start | bytes 393224 | tf_op jit(solution)/shard_map/ppermute | solution.py:298
  39.0 9.3 %collective-permute-start.6 = (f32[4,64,128]{2,1,0:T(8,128)S(1)}, f32[4,64,128]{2,1,0:T(8,128)S(1)}, u32[]{:S(2)}, u32[]{:S(2)}) collective-permute-start(f32[4,64,128]{2,1,0:T(8,128)S(1)} %pad_maximum_fusion.1.refs_0_), channel_id=1, source_target_pairs={{0,8},{8,0},{1,9},{9,1},{2,10},{10,2},{3,11},{11,3},{4,12},{12,4},... | collective-permute-start | bytes 393224 | tf_op jit(solution)/shard_map/ppermute | solution.py:294
  42.5 5.8 %collective-permute-start.7 = (f32[4,64,128]{2,1,0:T(8,128)S(1)}, f32[4,64,128]{2,1,0:T(8,128)S(1)}, u32[]{:S(2)}, u32[]{:S(2)}) collective-permute-start(f32[4,64,128]{2,1,0:T(8,128)S(1)} %collective-permute-done.3.refs_1_), channel_id=1, source_target_pairs={{0,8},{8,0},{1,9},{9,1},{2,10},{10,2},{3,11},{11,3},{4,12},{12,4},... | collective-permute-start | bytes 393224 | tf_op jit(solution)/shard_map/ppermute | solution.py:294
  46.9 1.4 %collective-permute-start.8 = (f32[4,64,128]{2,1,0:T(8,128)S(1)}, f32[4,64,128]{2,1,0:T(8,128)S(1)}, u32[]{:S(2)}, u32[]{:S(2)}) collective-permute-start(f32[4,64,128]{2,1,0:T(8,128)S(1)} %collective-permute-done.4.refs_2_), channel_id=1, source_target_pairs={{0,8},{8,0},{1,9},{9,1},{2,10},{10,2},{3,11},{11,3},{4,12},{12,4},... | collective-permute-start | bytes 393224 | tf_op jit(solution)/shard_map/ppermute | solution.py:294
  48.3 1.3 %collective-permute-start.9 = (f32[4,64,128]{2,1,0:T(8,128)S(1)}, f32[4,64,128]{2,1,0:T(8,128)S(1)}, u32[]{:S(2)}, u32[]{:S(2)}) collective-permute-start(f32[4,64,128]{2,1,0:T(8,128)S(1)} %collective-permute-done.5.refs_3_), channel_id=1, source_target_pairs={{0,8},{8,0},{1,9},{9,1},{2,10},{10,2},{3,11},{11,3},{4,12},{12,4},... | collective-permute-start | bytes 393224 | tf_op jit(solution)/shard_map/ppermute | solution.py:294
  57.8 1.8 %collective-permute-start.10 = (f32[16,48,128]{2,1,0:T(8,128)S(1)}, f32[16,48,128]{2,1,0:T(8,128)S(1)}, u32[]{:S(2)}, u32[]{:S(2)}) collective-permute-start(f32[16,48,128]{2,1,0:T(8,128)S(1)} %bitcast.43), channel_id=1, source_target_pairs={{0,8},{8,0},{1,9},{9,1},{2,10},{10,2},{3,11},{11,3},{4,12},{12,4},... | collective-permute-start | bytes 1179656 | tf_op jit(solution)/shard_map/ppermute | solution.py:294
  60.5 23.3 %all-to-all-start.2 = ((f32[16,64,128]{2,1,0:T(8,128)}), f32[16,64,128]{2,1,0:T(8,128)}, u32[]{:S(2)}, u32[]{:S(2)}) async-start(f32[16,64,128]{2,1,0:T(8,128)} %pad_maximum_fusion), calls=%async_computation.2 | async-start | bytes 1048576 | tf_op jit(solution)/shard_map/all_to_all | solution.py:302
  66.9 8.6 %copy-start.9 = (f32[1024,128]{1,0:T(8,128)S(1)}, f32[1024,128]{1,0:T(8,128)}, u32[]{:S(2)}) copy-start(f32[1024,128]{1,0:T(8,128)} %refs_8_.1) | copy-start | bytes 1572868
  66.9 8.6 %copy-start.10 = (f32[128]{0:T(128)S(1)}, f32[128]{0:T(128)}, u32[]{:S(2)}) copy-start(f32[128]{0:T(128)} %param.18) | copy-start | bytes 1540
  68.9 1.4 %collective-permute-start.16 = (f32[4,64,128]{2,1,0:T(8,128)S(1)}, f32[4,64,128]{2,1,0:T(8,128)S(1)}, u32[]{:S(2)}, u32[]{:S(2)}) collective-permute-start(f32[4,64,128]{2,1,0:T(8,128)S(1)} %get-tuple-element.47), channel_id=1, source_target_pairs={{0,8},{8,0},{1,9},{9,1},{2,10},{10,2},{3,11},{11,3},{4,12},{12,4},... | collective-permute-start | bytes 393224 | tf_op jit(solution)/shard_map/ppermute | solution.py:294
  69.0 4.1 %collective-permute-start.12 = (f32[4,64,128]{2,1,0:T(8,128)S(1)}, f32[4,64,128]{2,1,0:T(8,128)S(1)}, u32[]{:S(2)}, u32[]{:S(2)}) collective-permute-start(f32[4,64,128]{2,1,0:T(8,128)S(1)} %get-tuple-element.43), channel_id=1, source_target_pairs={{0,8},{8,0},{1,9},{9,1},{2,10},{10,2},{3,11},{11,3},{4,12},{12,4},... | collective-permute-start | bytes 393224 | tf_op jit(solution)/shard_map/ppermute | solution.py:294
  69.5 4.0 %collective-permute-start.14 = (f32[4,64,128]{2,1,0:T(8,128)S(1)}, f32[4,64,128]{2,1,0:T(8,128)S(1)}, u32[]{:S(2)}, u32[]{:S(2)}) collective-permute-start(f32[4,64,128]{2,1,0:T(8,128)S(1)} %get-tuple-element.45), channel_id=1, source_target_pairs={{0,8},{8,0},{1,9},{9,1},{2,10},{10,2},{3,11},{11,3},{4,12},{12,4},... | collective-permute-start | bytes 393224 | tf_op jit(solution)/shard_map/ppermute | solution.py:294
  69.6 11.4 %collective-permute-start.11 = (f32[4,64,128]{2,1,0:T(8,128)S(1)}, f32[4,64,128]{2,1,0:T(8,128)S(1)}, u32[]{:S(2)}, u32[]{:S(2)}) collective-permute-start(f32[4,64,128]{2,1,0:T(8,128)S(1)} %get-tuple-element.41), channel_id=1, source_target_pairs={{0,8},{8,0},{1,9},{9,1},{2,10},{10,2},{3,11},{11,3},{4,12},{12,4},... | collective-permute-start | bytes 393224 | tf_op jit(solution)/shard_map/ppermute | solution.py:294
  70.3 10.6 %collective-permute-start.17 = (f32[4,64,128]{2,1,0:T(8,128)S(1)}, f32[4,64,128]{2,1,0:T(8,128)S(1)}, u32[]{:S(2)}, u32[]{:S(2)}) collective-permute-start(f32[4,64,128]{2,1,0:T(8,128)S(1)} %add.31), channel_id=1, source_target_pairs={{0,48},{16,32},{32,16},{48,0},{1,49},{17,33},{33,17},{49,1},{2,50}... | collective-permute-start | bytes 393224 | tf_op jit(solution)/shard_map/ppermute | solution.py:298
  73.1 7.8 %collective-permute-start.13 = (f32[4,64,128]{2,1,0:T(8,128)S(1)}, f32[4,64,128]{2,1,0:T(8,128)S(1)}, u32[]{:S(2)}, u32[]{:S(2)}) collective-permute-start(f32[4,64,128]{2,1,0:T(8,128)S(1)} %add.28), channel_id=1, source_target_pairs={{0,16},{16,0},{32,48},{48,32},{1,17},{17,1},{33,49},{49,33},{2,18}... | collective-permute-start | bytes 393224 | tf_op jit(solution)/shard_map/ppermute | solution.py:298
  73.5 10.2 %collective-permute-start.15 = (f32[4,64,128]{2,1,0:T(8,128)S(1)}, f32[4,64,128]{2,1,0:T(8,128)S(1)}, u32[]{:S(2)}, u32[]{:S(2)}) collective-permute-start(f32[4,64,128]{2,1,0:T(8,128)S(1)} %add.29), channel_id=1, source_target_pairs={{0,32},{16,48},{32,0},{48,16},{1,33},{17,49},{33,1},{49,17},{2,34}... | collective-permute-start | bytes 393224 | tf_op jit(solution)/shard_map/ppermute | solution.py:298
  80.9 20.0 %copy-start.4 = (f32[256,32]{0,1:T(8,128)S(1)}, f32[256,32]{0,1:T(8,128)}, u32[]{:S(2)}) copy-start(f32[256,32]{0,1:T(8,128)} %param.15) | copy-start | bytes 98308
  80.9 26.2 %copy-start.3 = (f32[4,64,256]{2,1,0:T(8,128)S(1)}, f32[4,64,256]{2,1,0:T(8,128)}, u32[]{:S(2)}) copy-start(f32[4,64,256]{2,1,0:T(8,128)} %param.10) | copy-start | bytes 786436
  80.9 26.2 %copy-start.5 = (f32[256,32]{0,1:T(8,128)S(1)}, f32[256,32]{0,1:T(8,128)}, u32[]{:S(2)}) copy-start(f32[256,32]{0,1:T(8,128)} %param.13) | copy-start | bytes 98308
  80.9 26.2 %copy-start.6 = (f32[256]{0:T(256)S(1)}, f32[256]{0:T(256)}, u32[]{:S(2)}) copy-start(f32[256]{0:T(256)} %param.11) | copy-start | bytes 3076
  85.6 21.5 %all-to-all-start.3 = ((f32[8,72,128]{2,1,0:T(8,128)}), f32[8,72,128]{2,1,0:T(8,128)S(1)}, u32[]{:S(2)}, u32[]{:S(2)}) async-start(f32[8,72,128]{2,1,0:T(8,128)} %select_maximum_fusion), calls=%async_computation.3 | async-start | bytes 589824 | tf_op jit(solution)/shard_map/all_to_all | solution.py:302
  92.7 8.2 %collective-permute-start.18 = (f32[64,128]{1,0:T(8,128)S(1)}, f32[64,128]{1,0:T(8,128)S(1)}, u32[]{:S(2)}, u32[]{:S(2)}) collective-permute-start(f32[64,128]{1,0:T(8,128)S(1)} %get-tuple-element.57), channel_id=1, source_target_pairs={{0,64},{64,0},{128,192},{192,128},{1,65},{65,1},{129,193},{193,129... | collective-permute-start | bytes 98312 | tf_op jit(solution)/shard_map/ppermute | solution.py:298
  92.8 8.1 %collective-permute-start.19 = (f32[64,128]{1,0:T(8,128)S(1)}, f32[64,128]{1,0:T(8,128)S(1)}, u32[]{:S(2)}, u32[]{:S(2)}) collective-permute-start(f32[64,128]{1,0:T(8,128)S(1)} %get-tuple-element.56), channel_id=1, source_target_pairs={{0,128},{64,192},{128,0},{192,64},{1,129},{65,193},{129,1},{193,65... | collective-permute-start | bytes 98312 | tf_op jit(solution)/shard_map/ppermute | solution.py:298
  95.8 5.1 %collective-permute-start.20 = (f32[64,128]{1,0:T(8,128)S(1)}, f32[64,128]{1,0:T(8,128)S(1)}, u32[]{:S(2)}, u32[]{:S(2)}) collective-permute-start(f32[64,128]{1,0:T(8,128)S(1)} %get-tuple-element.55), channel_id=1, source_target_pairs={{0,192},{64,128},{128,64},{192,0},{1,193},{65,129},{129,65},{193,1... | collective-permute-start | bytes 98312 | tf_op jit(solution)/shard_map/ppermute | solution.py:298
  (7 other events, 8.4 us)

commit v4 on v3

--- a/solution.py
+++ b/solution.py
@@ -15,8 +15,9 @@
 ROW = ("zl", "x", "core")
 COL = ("zh", "y")
 VMEM = pl.BlockSpec(memory_space=pltpu.VMEM)
-
-BWD = 48
+HBM = pl.BlockSpec(memory_space=pltpu.HBM)
+
+BWD = 32
 
 
 def contract(a, b, dims):
@@ -39,20 +40,29 @@
     return demeaned * inverse, inverse
 
 
-def project_kernel(x_ref, scale_ref, offset_ref, w1_ref, b1_ref, w2_ref, b2_ref, left_ref, right_ref, tmp):
+def project_kernel(
+    x_ref, scale_ref, offset_ref, w1_ref, b1_ref, w2_ref, b2_ref, left_ref, right_ref, tmp
+):
     normed = standardized(x_ref[...])[0] * scale_ref[...] + offset_ref[...]
+    on = lax.broadcasted_iota(jnp.int32, (32, 32), 0) == lax.broadcasted_iota(jnp.int32, (32, 32), 1)
+    b2 = jnp.sum(jnp.where(on, b2_ref[...], 0.0), axis=1, keepdims=True)
+    right = contract(w2_ref[...], normed, ((1,), (1,))) + b2
+    for s in range(4):
+        cols = right[:, s * 64 : s * 64 + 64]
+        right_ref[s * 16 : s * 16 + 16, :] = jnp.concatenate([cols[0:16], cols[16:32]], axis=1)
     tmp[:, 0:32] = contract(normed, w1_ref[...], ((1,), (1,))) + b1_ref[...]
     wide = jnp.concatenate([tmp[pl.ds(u, 64, stride=4), :][:, 0:32] for u in range(4)], axis=1)
     for q in range(4):
         part = jnp.concatenate([wide[s * 16 + q * 4 : s * 16 + q * 4 + 4] for s in range(4)], axis=0)
         for copy in range(8):
             left_ref[copy, q * 16 : q * 16 + 16, :] = part
-    on = lax.broadcasted_iota(jnp.int32, (32, 32), 0) == lax.broadcasted_iota(jnp.int32, (32, 32), 1)
-    b2 = jnp.sum(jnp.where(on, b2_ref[...], 0.0), axis=1, keepdims=True)
-    right = contract(w2_ref[...], normed, ((1,), (1,))) + b2
-    for s in range(4):
-        cols = right[:, s * 64 : s * 64 + 64]
-        right_ref[s * 16 : s * 16 + 16, :] = jnp.concatenate([cols[0:16], cols[16:32]], axis=1)
+
+
+def fetch(pairs, sems):
+    copies = [pltpu.make_async_copy(a, b, sems.at[i]) for i, (a, b) in enumerate(pairs)]
+    for copy in copies:
+        copy.start()
+    return copies
 
 
 def pick(parts):
@@ -140,7 +150,7 @@
                 g_lo[m, at : at + 64, quad * 128 : quad * 128 + 128] = lo
 
 
-def outer_product(left_ref, parts, right_all, outer, lcat, rt, a_hi, a_lo, r_hl=None):
+def outer_product(left_ref, parts, right_all, outer, lcat, rt, a_hi, a_lo):
     gather_right(parts, right_all)
     for quad in range(4):
         v = left_rows(left_ref, quad)
@@ -151,12 +161,7 @@
             lcat[m, 256:384, quad * 128 : quad * 128 + 128] = hi
     for e in range(16):
         g, m = e // 4, e % 4
-        v = right_rows(right_all, e)
-        if r_hl is not None:
-            hi, lo = halves(v)
-            r_hl[m, 0:128, g * 128 : g * 128 + 128] = hi
-            r_hl[m, 128:256, g * 128 : g * 128 + 128] = lo
-        hi, lo = halves(v.T)
+        hi, lo = halves(right_rows(right_all, e).T)
         rt[m, g * 128 : g * 128 + 128, 0:128] = hi
         rt[m, g * 128 : g * 128 + 128, 128:256] = hi
         rt[m, g * 128 : g * 128 + 128, 256:384] = lo
@@ -174,9 +179,12 @@
 
 
 def pair_kernel(left_ref, *refs):
-    parts, (w_ref, bias_ref, pair_ref, right_all, outer, lcat, rt, a_hi, a_lo, w_hl) = refs[:8], refs[8:]
+    parts, (bias_ref, w_far, pair_ref, right_all, outer, lcat, rt, a_hi, a_lo) = refs[:8], refs[8:17]
+    w_hl, w_ref, sems = refs[17:]
+    (fetched,) = fetch([(w_far, w_ref)], sems)
+    outer_product(left_ref, parts, right_all, outer, lcat, rt, a_hi, a_lo)
+    fetched.wait()
     weights_by_class(w_ref, w_hl)
-    outer_product(left_ref, parts, right_all, outer, lcat, rt, a_hi, a_lo)
     for d in range(4):
         both = matmul(a_hi[d], w_hl[d])
         pair = both[:, 0:128] + both[:, 128:256] + matmul(a_lo[d], w_hl[d, :, 0:128])
@@ -186,10 +194,12 @@
 
 
 def tile_kernel(left_ref, *refs):
-    parts, (g_hi, g_lo, cot_t, own_out, other_out) = refs[:8], refs[8:13]
-    right_all, outer, lcat, rt, a_hi, a_lo, r_hl, dw = refs[13:]
+    parts, (cot_far, own_out, other_out) = refs[:8], refs[8:11]
+    right_all, outer, lcat, rt, a_hi, a_lo, dw, cot_t, sems = refs[11:]
     core = lax.axis_index("core")
-    outer_product(left_ref, parts, right_all, outer, lcat, rt, a_hi, a_lo, r_hl)
+    (fetched,) = fetch([(cot_far, cot_t)], sems)
+    outer_product(left_ref, parts, right_all, outer, lcat, rt, a_hi, a_lo)
+    fetched.wait()
     for d in range(4):
         both = matmul(cot_t[d], a_hi[d])
         part = both[0:128] + both[128:256] + matmul(cot_t[d, 0:128, :], a_lo[d])
@@ -207,6 +217,19 @@
                 out[pl.ds(p * 8 + block, 16, stride=BWD), :] = dw[
                     block, pl.ds(p * 32 + side, 16, stride=2), :
                 ]
+
+
+def left_gradient_kernel(*refs):
+    parts, (hi_far, lo_far, own_out, other_out, right_all, r_hl, g_hi, g_lo, sems) = refs[:8], refs[8:]
+    copies = fetch([(hi_far, g_hi), (lo_far, g_lo)], sems)
+    gather_right(parts, right_all)
+    for e in range(16):
+        g, m = e // 4, e % 4
+        hi, lo = halves(right_rows(right_all, e))
+        r_hl[m, 0:128, g * 128 : g * 128 + 128] = hi
+        r_hl[m, 128:256, g * 128 : g * 128 + 128] = lo
+    for copy in copies:
+        copy.wait()
     total = [None] * 4
     for m in range(4):
         both = matmul(r_hl[m], g_hi[m])
@@ -221,12 +244,15 @@
         for half, out in ((0, own_out), (1, other_out)):
             for s in range(4):
                 at = (half * 4 + s) * 16
-                out[pl.ds(32 + s * 4 + quad, 16, stride=BWD), :] = t[at : at + 16]
-
-
-def right_gradient_kernel(left_ref, g_hi, g_lo, *refs):
-    outs, (lt, total) = refs[:8], refs[8:]
+                out[pl.ds(s * 4 + quad, 16, stride=16), :] = t[at : at + 16]
+
+
+def right_gradient_kernel(left_ref, hi_far, lo_far, *refs):
+    outs, (lt, total, g_hi, g_lo, sems) = refs[:8], refs[8:]
+    copies = fetch([(hi_far, g_hi), (lo_far, g_lo)], sems)
     left_turned(left_ref, lt)
+    for copy in copies:
+        copy.wait()
     for m in range(4):
         both = matmul(g_hi[m], lt[m])
         v = both[:, 0:128] + both[:, 128:256] + matmul(g_lo[m], lt[m, :, 0:128])
@@ -273,21 +299,22 @@
     out_ref[...] = inverse * (grad - mean - unit * along)
 
 
-def call(kernel, name, outs, scratch, mib, flops, *args):
+def call(kernel, name, outs, scratch, mib, flops, *args, far=(), copies=0):
     shapes = tuple(jax.ShapeDtypeStruct(*out) for out in outs)
-    moved = sum(a.size * a.dtype.itemsize for a in args + shapes)
+    moved = sum(a.size * a.dtype.itemsize for a in args + tuple(far) + shapes)
     return pl.pallas_call(
         kernel,
         out_shape=shapes,
-        in_specs=[VMEM] * len(args),
+        in_specs=[VMEM] * len(args) + [HBM] * len(far),
         out_specs=(VMEM,) * len(outs),
-        scratch_shapes=[pltpu.VMEM(*s) for s in scratch],
+        scratch_shapes=[pltpu.VMEM(*s) for s in scratch]
+        + ([pltpu.SemaphoreType.DMA((copies,))] if copies else []),
         compiler_params=pltpu.CompilerParams(
             vmem_limit_bytes=mib * 1024 * 1024 if mib else None
         ),
         cost_estimate=pl.CostEstimate(flops=flops, bytes_accessed=moved, transcendentals=0),
         name=name,
-    )(*args)
+    )(*args, *far)
 
 
 def swap_cores(array):
@@ -320,6 +347,7 @@
     w2 = second_operand_matrix.T
     small = 2 * 256 * 256 * 32 * 6
     step = 2 * 1024 * 1024 * 128 * 3
+    offset = standardize_offset.reshape(1, 256)
     left, right = call(
         project_kernel,
         "project",
@@ -329,7 +357,7 @@
         2 * small,
         x,
         scale,
-        standardize_offset.reshape(1, 256),
+        offset,
         w1,
         first_operand_intercept.reshape(1, 32),
         w2,
@@ -345,17 +373,30 @@
             ((1024, 384), bf16),
             ((4, 256, 384), bf16),
         ],
-        24,
+        None,
         step,
         result_matrix,
         edge_incoming_sensitivity,
     )
     left = exchange(left, COL).reshape(32, 16, 128)
     right = jnp.stack([right] + [from_peer(right, "zl", dz) for dz in (1, 2, 3)])
-    left, right, g_hi, g_lo, cot_t = lax.optimization_barrier((left, right, g_hi, g_lo, cot_t))
+    parts = [right] + [from_peer(right, "x", dx) for dx in (1, 2, 3)]
+    left, parts, g_hi, g_lo, cot_t = lax.optimization_barrier((left, parts, g_hi, g_lo, cot_t))
     left = exchange(left, ROW).reshape(512, 128)
-    parts = [right] + [from_peer(right, "x", dx) for dx in (1, 2, 3)]
     parts = parts + [swap_cores(part) for part in parts]
+    own_left, other_left = call(
+        left_gradient_kernel,
+        "left_gradient",
+        [((256, 128), f32), ((256, 128), f32)],
+        [((2048, 128), f32), ((4, 256, 512), bf16)] + [((4, 512, 512), bf16)] * 2,
+        14,
+        step,
+        *parts,
+        far=(g_hi, g_lo),
+        copies=2,
+    )
+    got_left = swap_cores(other_left)
+    left, own_left, got_left = lax.optimization_barrier((left, own_left, got_left))
     working = [
         ((2048, 128), f32),
         ((4, 512, 512), f32),
@@ -367,50 +408,50 @@
     own, other = call(
         tile_kernel,
         "tile",
-        [((16 * BWD, 128), f32), ((16 * BWD, 128), f32)],
-        working + [((4, 256, 512), bf16), ((8, 128, 128), f32)],
-        28,
-        3 * step,
+        [((16 * BWD, 128), f32)] * 2,
+        working + [((8, 128, 128), f32), ((4, 256, 256), bf16)],
+        22,
+        2 * step,
         left,
         *parts,
-        g_hi,
-        g_lo,
-        cot_t,
-    )
-    own = own.reshape(16, BWD, 128)
-    got = swap_cores(other.reshape(16, BWD, 128))
-    sent = jnp.concatenate([own[:, :32] + got[:, :32], own[:, 32:], got[:, 32:]], axis=1)
-    back = exchange(sent, CHIP)
+        far=(cot_t,),
+        copies=1,
+    )
+    got = swap_cores(other)
     sums = call(
         right_gradient_kernel,
         "right_gradient",
         [((4, 64, 128), f32)] * 8,
-        [((4, 512, 256), bf16), ((2048, 128), f32)],
-        16,
+        [((4, 512, 256), bf16), ((2048, 128), f32)] + [((4, 512, 512), bf16)] * 2,
+        None,
         step,
         left,
-        g_hi,
-        g_lo,
-    )
+        far=(g_hi, g_lo),
+        copies=2,
+    )
+    weight = (own + got).reshape(16, BWD, 128)
+    sent = [weight, own_left.reshape(16, 16, 128), got_left.reshape(16, 16, 128)]
+    back = exchange(jnp.concatenate(sent, axis=1), CHIP)
     sums = [a + swap_cores(b) for a, b in zip(sums[:4], sums[4:])]
     right = sums[0] + sum(from_peer(sums[dx], "x", dx) for dx in (1, 2, 3))
     (pair,) = call(
         pair_kernel,
         "pair",
         [((16, 64, 128), f32)],
-        working + [((4, 1024, 256), bf16)],
-        28,
+        working + [((4, 1024, 256), bf16), ((1024, 128), f32)],
+        24,
         2 * step,
         left,
         *parts,
-        result_matrix,
         result_intercept.reshape(1, 128),
+        far=(result_matrix,),
+        copies=1,
     )
     weight = back[:, :32].sum(axis=0).reshape(4, 8, 128).transpose(1, 0, 2)
     sent = jnp.concatenate(
         [back[:, 32:].reshape(8, 64, 128), jnp.pad(weight, ((0, 0), (0, 4), (0, 0)))], axis=1
     )
-    sent, right, pair = lax.optimization_barrier((sent, right, pair))
+    sent, right = lax.optimization_barrier((sent, right))
     cols = exchange(sent, COL)
     right = [right[0]] + [from_peer(right[dz], "zl", dz) for dz in (1, 2, 3)]
     (part,) = call(right_kernel, "right", [((256, 256), f32)], [], 8, small, w2, *right)

time: 109 us -> 115 us (1.055)
  Pallas kernels: 19.8 us -> 29.1 us
  waiting for transfers between devices: 29.4 us -> 21.8 us
  starting transfers between devices: 47 us -> 53.1 us
  local copies, waits for them, and re-layouts: 8.49 us -> 3.24 us
  other arithmetic: 2.79 us -> 6.22 us
    pallas_call x7 -> x8, Pallas kernels: 19.8 us -> 29.1 us  [call(): pl.pallas_call(kernel, out_shape=shapes, in_specs=[VMEM] * len(args) + [H...]
    unnamed x28 -> x22, local copies, waits for them, and re-layouts: 8.46 us -> 3.22 us
    ppermute x12, waiting for transfers between devices: 16.6 us -> 11.8 us  [from_peer(): return lax.ppermute(array, axis, [(i, i ^ apart) for i in range(4)])]
    all_to_all x4, starting transfers between devices: 28.6 us -> 33.1 us  [exchange(): return lax.all_to_all(array, axes, 0, 0, tiled=True)]
    all_to_all x4, waiting for transfers between devices: 9.58 us -> 6.14 us  [exchange(): return lax.all_to_all(array, axes, 0, 0, tiled=True)]
    add x3, other arithmetic: 0.05 us -> 2.85 us  [local(): sums = [a + swap_cores(b) for a, b in zip(sums[:4], sums[4:])]]
    ppermute x9 -> x10, starting transfers between devices: 1.34 us -> 3.15 us  [swap_cores(): return lax.ppermute(array, 'core', [(0, 1), (1, 0)])]
    ppermute x9 -> x10, waiting for transfers between devices: 3.23 us -> 3.86 us  [swap_cores(): return lax.ppermute(array, 'core', [(0, 1), (1, 0)])]
  transfers between devices with their start and end apart: 25 -> 26, of which waited for: 10 -> 14; matrix products, arithmetic and copies ran while one was open for 0% -> 4% of each run, Pallas kernels for 10% -> 18%
where the time goes in v4:
time: 115 us; the launch traced here: 114 us
  starting transfers between devices  53.1 us (46%)
  Pallas kernels  29.1 us (25%)
  waiting for transfers between devices  21.8 us (19%)
  other arithmetic  6.22 us (5%)
  local copies, waits for them, and re-layouts  3.24 us (3%)
    all_to_all x4, starting transfers between devices, exchange(): return lax.all_to_all(array, axes, 0, 0, tiled=True)  33.1 us
    pallas_call x8, Pallas kernels, call(): pl.pallas_call(kernel, out_shape=shapes, in_specs=[VMEM] * len(args) + [H...  29.1 us
    ppermute x12, starting transfers between devices, from_peer(): return lax.ppermute(array, axis, [(i, i ^ apart) for i in range(4)])  16.8 us
    ppermute x12, waiting for transfers between devices, from_peer(): return lax.ppermute(array, axis, [(i, i ^ apart) for i in range(4)])  11.8 us
    all_to_all x4, waiting for transfers between devices, exchange(): return lax.all_to_all(array, axes, 0, 0, tiled=True)  6.14 us
    ppermute x10, waiting for transfers between devices, swap_cores(): return lax.ppermute(array, 'core', [(0, 1), (1, 0)])  3.86 us
    unnamed x22, local copies, waits for them, and re-layouts  3.22 us
    ppermute x10, starting transfers between devices, swap_cores(): return lax.ppermute(array, 'core', [(0, 1), (1, 0)])  3.15 us
  transfers between devices with their start and end apart: 26, of which 14 were waited for; matrix products, arithmetic and copies ran while one was open for 4% of the time, Pallas kernels for 18%

profile of v4, /device:TPU:32, one launch (start us, length us, event | category | flops | bytes accessed | tf_op | source)
XLA Modules:
  0.0 114.2 jit_solution(1490028289227146237)
XLA Ops:
  0.6 2.5 %project.1 = (f32[8,64,128]{2,1,0:T(8,128)}, f32[64,128]{1,0:T(8,128)}) custom-call(f32[256,256]{1,0:T(8,128)} %bitcast.34, f32[1,256]{1,0:T(1,128)} %bitcast.41, f32[1,256]{1,0:T(1,128)} %bitcast.53, f32[32,256]{1,0:T(8,128)} %bitcast.39, f32[1,32]{1,0:T(1,128)} %bitcast.54, f32[32,256]{1,0:T(8,128)} %bitcast.36, f32[1,32]{1,0:T(1,128)} %bitcast.55), custom_call_target="tpu_custom_call" | custom-call | flops 50331648 | bytes 624896 | tf_op jit(solution)/shard_map/project/pallas_call | solution.py:305
  3.2 10.2 %all-to-all-start = ((f32[8,64,128]{2,1,0:T(8,128)}), f32[8,64,128]{2,1,0:T(8,128)}, u32[]{:S(2)}, u32[]{:S(2)}) async-start(f32[8,64,128]{2,1,0:T(8,128)} %get-tuple-element.35), calls=%async_computation | async-start | bytes 524288 | tf_op jit(solution)/shard_map/all_to_all | solution.py:329
  13.4 1.0 collective-permute-start.2
  14.4 2.4 %collective-permute-start.1 = (f32[64,128]{1,0:T(8,128)}, f32[64,128]{1,0:T(8,128)S(1)}, u32[]{:S(2)}, u32[]{:S(2)}) collective-permute-start(f32[64,128]{1,0:T(8,128)} %get-tuple-element.36), channel_id=1, source_target_pairs={{0,128},{64,192},{128,0},{192,64},{1,129},{65,193},{129,1},{193,65... | collective-permute-start | bytes 98312 | tf_op jit(solution)/shard_map/ppermute | solution.py:325
  16.8 4.6 %collective-permute-done.2 = f32[64,128]{1,0:T(8,128)S(1)} collective-permute-done((f32[64,128]{1,0:T(8,128)}, f32[64,128]{1,0:T(8,128)S(1)}, u32[]{:S(2)}, u32[]{:S(2)}) %collective-permute-start.2) | collective-permute-done | bytes 32800 | tf_op jit(solution)/shard_map/ppermute | solution.py:325
  22.2 1.6 %collective-permute-start.3 = (f32[4,64,128]{2,1,0:T(8,128)S(1)}, f32[4,64,128]{2,1,0:T(8,128)S(1)}, u32[]{:S(2)}, u32[]{:S(2)}) collective-permute-start(f32[4,64,128]{2,1,0:T(8,128)S(1)} %pad_maximum_fusion.1.refs_0_), channel_id=1, source_target_pairs={{0,16},{16,0},{32,48},{48,32},{1,17},{17,1},{33,49},{49,33},{2,18}... | collective-permute-start | bytes 393224 | tf_op jit(solution)/shard_map/ppermute | solution.py:325
  23.8 2.7 %collective-permute-start.4 = (f32[4,64,128]{2,1,0:T(8,128)S(1)}, f32[4,64,128]{2,1,0:T(8,128)S(1)}, u32[]{:S(2)}, u32[]{:S(2)}) collective-permute-start(f32[4,64,128]{2,1,0:T(8,128)S(1)} %pad_maximum_fusion.1.refs_0_), channel_id=1, source_target_pairs={{0,32},{16,48},{32,0},{48,16},{1,33},{17,49},{33,1},{49,17},{2,34}... | collective-permute-start | bytes 393224 | tf_op jit(solution)/shard_map/ppermute | solution.py:325
  27.0 6.1 %cotangent.1 = (bf16[4,512,512]{2,1,0:T(8,128)(2,1)}, bf16[4,512,512]{2,1,0:T(8,128)(2,1)}, bf16[4,256,256]{2,1,0:T(8,128)(2,1)}) custom-call(f32[1024,128]{1,0:T(8,128)} %refs_9_.1, f32[16,64,128]{2,1,0:T(8,128)} %cot_ref.1), custom_call_target="tpu_custom_call" | custom-call | flops 805306368 | bytes 5767168 | tf_op jit(solution)/shard_map/cotangent/pallas_call | solution.py:305
  33.2 1.7 %collective-permute-done.5.refs_3_ = f32[4,64,128]{2,1,0:T(8,128)S(1)} collective-permute-done((f32[4,64,128]{2,1,0:T(8,128)S(1)}, f32[4,64,128]{2,1,0:T(8,128)S(1)}, u32[]{:S(2)}, u32[]{:S(2)}) %collective-permute-start.5) | collective-permute-done | bytes 131104 | tf_op jit(solution)/shard_map/ppermute | solution.py:325
  34.9 6.2 %all-to-all-start.1 = ((f32[32,16,128]{2,1,0:T(8,128)}), f32[32,16,128]{2,1,0:T(8,128)S(1)}, u32[]{:S(2)}, u32[]{:S(2)}) async-start(f32[32,16,128]{2,1,0:T(8,128)} %bitcast.7), calls=%async_computation.1 | async-start | bytes 524288 | tf_op jit(solution)/shard_map/all_to_all | solution.py:329
  43.3 1.6 %copy-done = bf16[4,512,512]{2,1,0:T(8,128)(2,1)S(1)} copy-done((bf16[4,512,512]{2,1,0:T(8,128)(2,1)S(1)}, bf16[4,512,512]{2,1,0:T(8,128)(2,1)}, u32[]{:S(2)}) %copy-start) | copy-done | bytes 2097176
  44.9 1.6 %copy-done.1 = bf16[4,512,512]{2,1,0:T(8,128)(2,1)S(1)} copy-done((bf16[4,512,512]{2,1,0:T(8,128)(2,1)S(1)}, bf16[4,512,512]{2,1,0:T(8,128)(2,1)}, u32[]{:S(2)}) %copy-start.1) | copy-done | bytes 2097176
  46.5 2.2 %left_gradient.1 = (f32[256,128]{1,0:T(8,128)S(1)}, f32[256,128]{1,0:T(8,128)S(1)}) custom-call(f32[4,64,128]{2,1,0:T(8,128)S(1)} %pad_maximum_fusion.1.refs_0_, f32[4,64,128]{2,1,0:T(8,128)S(1)} %collective-permute-done.3.refs_1_, f32[4,64,128]{2,1,0:T(8,128)S(1)} %collective-permute-done.4.refs_2_, f32[4,64,128]{2,1,0:T(8,128)S(1)} %collective-permute-done.5.refs_3_, ...), custom_call_target="tpu_custom_call" | custom-call | flops 805306368 | bytes 5505024 | tf_op jit(solution)/shard_map/left_gradient/pallas_call | solution.py:305
  49.2 1.0 collective-permute-done.10
  50.2 0.9 all-to-all-done.1
  51.2 4.9 %tile.1 = (f32[512,128]{1,0:T(8,128)S(1)}, f32[512,128]{1,0:T(8,128)S(1)}) custom-call(f32[512,128]{1,0:T(8,128)S(1)} %bitcast.31, f32[4,64,128]{2,1,0:T(8,128)S(1)} %pad_maximum_fusion.1.refs_0_, f32[4,64,128]{2,1,0:T(8,128)S(1)} %collective-permute-done.3.refs_1_, f32[4,64,128]{2,1,0:T(8,128)S(1)} %collective-permute-done.4.refs_2_, ...), custom_call_target="tpu_custom_call" | custom-call | flops 1610612736 | bytes 2359296 | tf_op jit(solution)/shard_map/tile/pallas_call | solution.py:305
  56.4 1.3 %collective-permute-done.11 = f32[512,128]{1,0:T(8,128)S(1)} collective-permute-done((f32[512,128]{1,0:T(8,128)S(1)}, f32[512,128]{1,0:T(8,128)S(1)}, u32[]{:S(2)}, u32[]{:S(2)}) %collective-permute-start.11) | collective-permute-done | bytes 262176 | tf_op jit(solution)/shard_map/ppermute | solution.py:321
  58.6 6.7 %all-to-all-start.2 = ((f32[16,64,128]{2,1,0:T(8,128)}), f32[16,64,128]{2,1,0:T(8,128)S(1)}, u32[]{:S(2)}, u32[]{:S(2)}) async-start(f32[16,64,128]{2,1,0:T(8,128)} %pad_maximum_fusion), calls=%async_computation.2 | async-start | bytes 1048576 | tf_op jit(solution)/shard_map/all_to_all | solution.py:329
  65.2 6.0 %right_gradient.1 = (f32[4,64,128]{2,1,0:T(8,128)}, f32[4,64,128]{2,1,0:T(8,128)}, f32[4,64,128]{2,1,0:T(8,128)}, f32[4,64,128]{2,1,0:T(8,128)}, f32[4,64,128]{2...) custom-call(f32[512,128]{1,0:T(8,128)} %bitcast.32, ...), custom_call_target="tpu_custom_call" | custom-call | flops 805306368 | bytes 5505024 | tf_op jit(solution)/shard_map/right_gradient/pallas_call | solution.py:305
  72.9 1.0 add.31
  73.9 2.8 %collective-permute-start.18 = (f32[4,64,128]{2,1,0:T(8,128)S(1)}, f32[4,64,128]{2,1,0:T(8,128)S(1)}, u32[]{:S(2)}, u32[]{:S(2)}) collective-permute-start(f32[4,64,128]{2,1,0:T(8,128)S(1)} %add.31), channel_id=1, source_target_pairs={{0,48},{16,32},{32,16},{48,0},{1,49},{17,33},{33,17},{49,1},{2,50}... | collective-permute-start | bytes 393224 | tf_op jit(solution)/shard_map/ppermute | solution.py:325
  76.7 0.9 add.28
  77.9 0.9 add.29
  78.8 1.9 %collective-permute-start.16 = (f32[4,64,128]{2,1,0:T(8,128)S(1)}, f32[4,64,128]{2,1,0:T(8,128)S(1)}, u32[]{:S(2)}, u32[]{:S(2)}) collective-permute-start(f32[4,64,128]{2,1,0:T(8,128)S(1)} %add.29), channel_id=1, source_target_pairs={{0,32},{16,48},{32,0},{48,16},{1,33},{17,49},{33,1},{49,17},{2,34}... | collective-permute-start | bytes 393224 | tf_op jit(solution)/shard_map/ppermute | solution.py:325
  81.4 2.6 %collective-permute-done.14 = f32[4,64,128]{2,1,0:T(8,128)S(1)} collective-permute-done((f32[4,64,128]{2,1,0:T(8,128)S(1)}, f32[4,64,128]{2,1,0:T(8,128)S(1)}, u32[]{:S(2)}, u32[]{:S(2)}) %collective-permute-start.14) | collective-permute-done | bytes 131104 | tf_op jit(solution)/shard_map/ppermute | solution.py:325
  84.0 2.1 %collective-permute-done.16 = f32[4,64,128]{2,1,0:T(8,128)S(1)} collective-permute-done((f32[4,64,128]{2,1,0:T(8,128)S(1)}, f32[4,64,128]{2,1,0:T(8,128)S(1)}, u32[]{:S(2)}, u32[]{:S(2)}) %collective-permute-start.16) | collective-permute-done | bytes 131104 | tf_op jit(solution)/shard_map/ppermute | solution.py:325
  86.2 0.9 add_add_fusion
  87.9 10.0 %all-to-all-start.3 = ((f32[8,72,128]{2,1,0:T(8,128)}), f32[8,72,128]{2,1,0:T(8,128)S(1)}, u32[]{:S(2)}, u32[]{:S(2)}) async-start(f32[8,72,128]{2,1,0:T(8,128)} %select_maximum_fusion), calls=%async_computation.3 | async-start | bytes 589824 | tf_op jit(solution)/shard_map/all_to_all | solution.py:329
  98.6 2.0 %collective-permute-start.20 = (f32[64,128]{1,0:T(8,128)S(1)}, f32[64,128]{1,0:T(8,128)S(1)}, u32[]{:S(2)}, u32[]{:S(2)}) collective-permute-start(f32[64,128]{1,0:T(8,128)S(1)} %get-tuple-element.70), channel_id=1, source_target_pairs={{0,128},{64,192},{128,0},{192,64},{1,129},{65,193},{129,1},{193,65... | collective-permute-start | bytes 98312 | tf_op jit(solution)/shard_map/ppermute | solution.py:325
  101.6 5.6 %pair.1 = f32[16,64,128]{2,1,0:T(8,128)} custom-call(f32[512,128]{1,0:T(8,128)S(1)} %bitcast.33, f32[4,64,128]{2,1,0:T(8,128)S(1)} %pad_maximum_fusion.1.refs_0_, f32[4,64,128]{2,1,0:T(8,128)S(1)} %collective-permute-done.3.refs_1_, f32[4,64,128]{2,1,0:T(8,128)S(1)} %collective-permute-done.4.refs_2_, f32[4,64,128]{2,1,0:T(8,128)S(1)} %collective-permute-done.5.refs_3_, ...), custom_call_target="tpu_custom_call" | custom-call | flops 1610612736 | bytes 2359808 | tf_op jit(solution)/shard_map/pair/pallas_call | solution.py:305
  107.7 5.2 %all-to-all-done.3.col_ref = f32[8,72,128]{2,1,0:T(8,128)S(1)} async-done(((f32[8,72,128]{2,1,0:T(8,128)}), f32[8,72,128]{2,1,0:T(8,128)S(1)}, u32[]{:S(2)}, u32[]{:S(2)}) %all-to-all-start.3) | async-done | bytes 294944 | tf_op jit(solution)/shard_map/all_to_all | solution.py:329
  112.9 1.3 %finish.1 = (f32[256,256]{1,0:T(8,128)}, f32[4,128]{1,0:T(4,128)}) custom-call(f32[256,256]{1,0:T(8,128)S(1)} %bitcast.35, f32[1,256]{1,0:T(1,128)S(1)} %bitcast.42, f32[32,256]{1,0:T(8,128)S(1)} %bitcast.40, f32[256,256]{1,0:T(8,128)S(1)} %right.1.part_ref, f32[8,72,128]{2,1,0:T(8,128)S(1)} %all-to-all-done.3.col_ref), custom_call_target="tpu_custom_call" | custom-call | flops 25165824 | bytes 1117184 | tf_op jit(solution)/shard_map/finish/pallas_call | solution.py:305
  (61 shorter events, 10.9 us)
Async XLA Ops:
  3.2 31.7 %all-to-all-start = ((f32[8,64,128]{2,1,0:T(8,128)}), f32[8,64,128]{2,1,0:T(8,128)}, u32[]{:S(2)}, u32[]{:S(2)}) async-start(f32[8,64,128]{2,1,0:T(8,128)} %get-tuple-element.35), calls=%async_computation | async-start | bytes 524288 | tf_op jit(solution)/shard_map/all_to_all | solution.py:329
  13.4 8.1 %collective-permute-start.2 = (f32[64,128]{1,0:T(8,128)}, f32[64,128]{1,0:T(8,128)S(1)}, u32[]{:S(2)}, u32[]{:S(2)}) collective-permute-start(f32[64,128]{1,0:T(8,128)} %get-tuple-element.36), channel_id=1, source_target_pairs={{0,192},{64,128},{128,64},{192,0},{1,193},{65,129},{129,65},{193,1... | collective-permute-start | bytes 98312 | tf_op jit(solution)/shard_map/ppermute | solution.py:325
  14.4 7.1 %collective-permute-start.1 = (f32[64,128]{1,0:T(8,128)}, f32[64,128]{1,0:T(8,128)S(1)}, u32[]{:S(2)}, u32[]{:S(2)}) collective-permute-start(f32[64,128]{1,0:T(8,128)} %get-tuple-element.36), channel_id=1, source_target_pairs={{0,128},{64,192},{128,0},{192,64},{1,129},{65,193},{129,1},{193,65... | collective-permute-start | bytes 98312 | tf_op jit(solution)/shard_map/ppermute | solution.py:325
  16.7 4.7 %collective-permute-start = (f32[64,128]{1,0:T(8,128)}, f32[64,128]{1,0:T(8,128)S(1)}, u32[]{:S(2)}, u32[]{:S(2)}) collective-permute-start(f32[64,128]{1,0:T(8,128)} %get-tuple-element.36), channel_id=1, source_target_pairs={{0,64},{64,0},{128,192},{192,128},{1,65},{65,1},{129,193},{193,129... | collective-permute-start | bytes 98312 | tf_op jit(solution)/shard_map/ppermute | solution.py:325
  22.2 10.9 %collective-permute-start.3 = (f32[4,64,128]{2,1,0:T(8,128)S(1)}, f32[4,64,128]{2,1,0:T(8,128)S(1)}, u32[]{:S(2)}, u32[]{:S(2)}) collective-permute-start(f32[4,64,128]{2,1,0:T(8,128)S(1)} %pad_maximum_fusion.1.refs_0_), channel_id=1, source_target_pairs={{0,16},{16,0},{32,48},{48,32},{1,17},{17,1},{33,49},{49,33},{2,18}... | collective-permute-start | bytes 393224 | tf_op jit(solution)/shard_map/ppermute | solution.py:325
  23.8 9.3 %collective-permute-start.4 = (f32[4,64,128]{2,1,0:T(8,128)S(1)}, f32[4,64,128]{2,1,0:T(8,128)S(1)}, u32[]{:S(2)}, u32[]{:S(2)}) collective-permute-start(f32[4,64,128]{2,1,0:T(8,128)S(1)} %pad_maximum_fusion.1.refs_0_), channel_id=1, source_target_pairs={{0,32},{16,48},{32,0},{48,16},{1,33},{17,49},{33,1},{49,17},{2,34}... | collective-permute-start | bytes 393224 | tf_op jit(solution)/shard_map/ppermute | solution.py:325
  26.5 8.3 %collective-permute-start.5 = (f32[4,64,128]{2,1,0:T(8,128)S(1)}, f32[4,64,128]{2,1,0:T(8,128)S(1)}, u32[]{:S(2)}, u32[]{:S(2)}) collective-permute-start(f32[4,64,128]{2,1,0:T(8,128)S(1)} %pad_maximum_fusion.1.refs_0_), channel_id=1, source_target_pairs={{0,48},{16,32},{32,16},{48,0},{1,49},{17,33},{33,17},{49,1},{2,50}... | collective-permute-start | bytes 393224 | tf_op jit(solution)/shard_map/ppermute | solution.py:325
  34.9 16.3 %copy-start.10 = (bf16[4,256,256]{2,1,0:T(8,128)(2,1)S(1)}, bf16[4,256,256]{2,1,0:T(8,128)(2,1)}, u32[]{:S(2)}) copy-start(bf16[4,256,256]{2,1,0:T(8,128)(2,1)} %get-tuple-element.50.refs_8_) | copy-start | bytes 1572868
  34.9 16.3 %all-to-all-start.1 = ((f32[32,16,128]{2,1,0:T(8,128)}), f32[32,16,128]{2,1,0:T(8,128)S(1)}, u32[]{:S(2)}, u32[]{:S(2)}) async-start(f32[32,16,128]{2,1,0:T(8,128)} %bitcast.7), calls=%async_computation.1 | async-start | bytes 524288 | tf_op jit(solution)/shard_map/all_to_all | solution.py:329
  41.1 1.4 %collective-permute-start.6 = (f32[4,64,128]{2,1,0:T(8,128)S(1)}, f32[4,64,128]{2,1,0:T(8,128)S(1)}, u32[]{:S(2)}, u32[]{:S(2)}) collective-permute-start(f32[4,64,128]{2,1,0:T(8,128)S(1)} %pad_maximum_fusion.1.refs_0_), channel_id=1, source_target_pairs={{0,8},{8,0},{1,9},{9,1},{2,10},{10,2},{3,11},{11,3},{4,12},{12,4},... | collective-permute-start | bytes 393224 | tf_op jit(solution)/shard_map/ppermute | solution.py:321
  41.4 1.4 %collective-permute-start.7 = (f32[4,64,128]{2,1,0:T(8,128)S(1)}, f32[4,64,128]{2,1,0:T(8,128)S(1)}, u32[]{:S(2)}, u32[]{:S(2)}) collective-permute-start(f32[4,64,128]{2,1,0:T(8,128)S(1)} %collective-permute-done.3.refs_1_), channel_id=1, source_target_pairs={{0,8},{8,0},{1,9},{9,1},{2,10},{10,2},{3,11},{11,3},{4,12},{12,4},... | collective-permute-start | bytes 393224 | tf_op jit(solution)/shard_map/ppermute | solution.py:321
  41.7 1.3 %collective-permute-start.8 = (f32[4,64,128]{2,1,0:T(8,128)S(1)}, f32[4,64,128]{2,1,0:T(8,128)S(1)}, u32[]{:S(2)}, u32[]{:S(2)}) collective-permute-start(f32[4,64,128]{2,1,0:T(8,128)S(1)} %collective-permute-done.4.refs_2_), channel_id=1, source_target_pairs={{0,8},{8,0},{1,9},{9,1},{2,10},{10,2},{3,11},{11,3},{4,12},{12,4},... | collective-permute-start | bytes 393224 | tf_op jit(solution)/shard_map/ppermute | solution.py:321
  41.9 1.4 %collective-permute-start.9 = (f32[4,64,128]{2,1,0:T(8,128)S(1)}, f32[4,64,128]{2,1,0:T(8,128)S(1)}, u32[]{:S(2)}, u32[]{:S(2)}) collective-permute-start(f32[4,64,128]{2,1,0:T(8,128)S(1)} %collective-permute-done.5.refs_3_), channel_id=1, source_target_pairs={{0,8},{8,0},{1,9},{9,1},{2,10},{10,2},{3,11},{11,3},{4,12},{12,4},... | collective-permute-start | bytes 393224 | tf_op jit(solution)/shard_map/ppermute | solution.py:321
  48.6 1.6 %collective-permute-start.10 = (f32[256,128]{1,0:T(8,128)S(1)}, f32[256,128]{1,0:T(8,128)S(1)}, u32[]{:S(2)}, u32[]{:S(2)}) collective-permute-start(f32[256,128]{1,0:T(8,128)S(1)} %get-tuple-element.48), channel_id=1, source_target_pairs={{0,8},{8,0},{1,9},{9,1},{2,10},{10,2},{3,11},{11,3},{4,12},{12,4},... | collective-permute-start | bytes 393224 | tf_op jit(solution)/shard_map/ppermute | solution.py:321
  56.1 1.6 %collective-permute-start.11 = (f32[512,128]{1,0:T(8,128)S(1)}, f32[512,128]{1,0:T(8,128)S(1)}, u32[]{:S(2)}, u32[]{:S(2)}) collective-permute-start(f32[512,128]{1,0:T(8,128)S(1)} %get-tuple-element.52), channel_id=1, source_target_pairs={{0,8},{8,0},{1,9},{9,1},{2,10},{10,2},{3,11},{11,3},{4,12},{12,4},... | collective-permute-start | bytes 786440 | tf_op jit(solution)/shard_map/ppermute | solution.py:321
  58.6 28.5 %all-to-all-start.2 = ((f32[16,64,128]{2,1,0:T(8,128)}), f32[16,64,128]{2,1,0:T(8,128)S(1)}, u32[]{:S(2)}, u32[]{:S(2)}) async-start(f32[16,64,128]{2,1,0:T(8,128)} %pad_maximum_fusion), calls=%async_computation.2 | async-start | bytes 1048576 | tf_op jit(solution)/shard_map/all_to_all | solution.py:329
  71.2 1.6 %collective-permute-start.17 = (f32[4,64,128]{2,1,0:T(8,128)}, f32[4,64,128]{2,1,0:T(8,128)S(1)}, u32[]{:S(2)}, u32[]{:S(2)}) collective-permute-start(f32[4,64,128]{2,1,0:T(8,128)} %get-tuple-element.62), channel_id=1, source_target_pairs={{0,8},{8,0},{1,9},{9,1},{2,10},{10,2},{3,11},{11,3},{4,12},{12,4},... | collective-permute-start | bytes 393224 | tf_op jit(solution)/shard_map/ppermute | solution.py:321
  71.3 5.3 %collective-permute-start.13 = (f32[4,64,128]{2,1,0:T(8,128)}, f32[4,64,128]{2,1,0:T(8,128)S(1)}, u32[]{:S(2)}, u32[]{:S(2)}) collective-permute-start(f32[4,64,128]{2,1,0:T(8,128)} %get-tuple-element.58), channel_id=1, source_target_pairs={{0,8},{8,0},{1,9},{9,1},{2,10},{10,2},{3,11},{11,3},{4,12},{12,4},... | collective-permute-start | bytes 393224 | tf_op jit(solution)/shard_map/ppermute | solution.py:321
  71.8 6.1 %collective-permute-start.15 = (f32[4,64,128]{2,1,0:T(8,128)}, f32[4,64,128]{2,1,0:T(8,128)S(1)}, u32[]{:S(2)}, u32[]{:S(2)}) collective-permute-start(f32[4,64,128]{2,1,0:T(8,128)} %get-tuple-element.60), channel_id=1, source_target_pairs={{0,8},{8,0},{1,9},{9,1},{2,10},{10,2},{3,11},{11,3},{4,12},{12,4},... | collective-permute-start | bytes 393224 | tf_op jit(solution)/shard_map/ppermute | solution.py:321
  71.9 8.8 %collective-permute-start.12 = (f32[4,64,128]{2,1,0:T(8,128)}, f32[4,64,128]{2,1,0:T(8,128)S(1)}, u32[]{:S(2)}, u32[]{:S(2)}) collective-permute-start(f32[4,64,128]{2,1,0:T(8,128)} %get-tuple-element.56), channel_id=1, source_target_pairs={{0,8},{8,0},{1,9},{9,1},{2,10},{10,2},{3,11},{11,3},{4,12},{12,4},... | collective-permute-start | bytes 393224 | tf_op jit(solution)/shard_map/ppermute | solution.py:321
  72.9 28.7 %copy-start.3 = (f32[32,16,128]{2,1,0:T(8,128)S(1)}, f32[32,16,128]{2,1,0:T(8,128)}, u32[]{:S(2)}) copy-start(f32[32,16,128]{2,1,0:T(8,128)} %copy-done.2) | copy-start | bytes 786436
  72.9 28.7 %copy-start.8 = (f32[1024,128]{1,0:T(8,128)S(1)}, f32[1024,128]{1,0:T(8,128)}, u32[]{:S(2)}) copy-start(f32[1024,128]{1,0:T(8,128)} %refs_9_.1) | copy-start | bytes 1572868
  72.9 28.7 %copy-start.9 = (f32[128]{0:T(128)S(1)}, f32[128]{0:T(128)}, u32[]{:S(2)}) copy-start(f32[128]{0:T(128)} %param.18) | copy-start | bytes 1540
  73.9 7.5 %collective-permute-start.18 = (f32[4,64,128]{2,1,0:T(8,128)S(1)}, f32[4,64,128]{2,1,0:T(8,128)S(1)}, u32[]{:S(2)}, u32[]{:S(2)}) collective-permute-start(f32[4,64,128]{2,1,0:T(8,128)S(1)} %add.31), channel_id=1, source_target_pairs={{0,48},{16,32},{32,16},{48,0},{1,49},{17,33},{33,17},{49,1},{2,50}... | collective-permute-start | bytes 393224 | tf_op jit(solution)/shard_map/ppermute | solution.py:325
  77.6 6.5 %collective-permute-start.14 = (f32[4,64,128]{2,1,0:T(8,128)S(1)}, f32[4,64,128]{2,1,0:T(8,128)S(1)}, u32[]{:S(2)}, u32[]{:S(2)}) collective-permute-start(f32[4,64,128]{2,1,0:T(8,128)S(1)} %add.28), channel_id=1, source_target_pairs={{0,16},{16,0},{32,48},{48,32},{1,17},{17,1},{33,49},{49,33},{2,18}... | collective-permute-start | bytes 393224 | tf_op jit(solution)/shard_map/ppermute | solution.py:325
  78.8 7.3 %collective-permute-start.16 = (f32[4,64,128]{2,1,0:T(8,128)S(1)}, f32[4,64,128]{2,1,0:T(8,128)S(1)}, u32[]{:S(2)}, u32[]{:S(2)}) collective-permute-start(f32[4,64,128]{2,1,0:T(8,128)S(1)} %add.29), channel_id=1, source_target_pairs={{0,32},{16,48},{32,0},{48,16},{1,33},{17,49},{33,1},{49,17},{2,34}... | collective-permute-start | bytes 393224 | tf_op jit(solution)/shard_map/ppermute | solution.py:325
  87.9 25.0 %all-to-all-start.3 = ((f32[8,72,128]{2,1,0:T(8,128)}), f32[8,72,128]{2,1,0:T(8,128)S(1)}, u32[]{:S(2)}, u32[]{:S(2)}) async-start(f32[8,72,128]{2,1,0:T(8,128)} %select_maximum_fusion), calls=%async_computation.3 | async-start | bytes 589824 | tf_op jit(solution)/shard_map/all_to_all | solution.py:329
  98.0 9.3 %collective-permute-start.19 = (f32[64,128]{1,0:T(8,128)S(1)}, f32[64,128]{1,0:T(8,128)S(1)}, u32[]{:S(2)}, u32[]{:S(2)}) collective-permute-start(f32[64,128]{1,0:T(8,128)S(1)} %get-tuple-element.71), channel_id=1, source_target_pairs={{0,64},{64,0},{128,192},{192,128},{1,65},{65,1},{129,193},{193,129... | collective-permute-start | bytes 98312 | tf_op jit(solution)/shard_map/ppermute | solution.py:325
  98.6 8.6 %collective-permute-start.20 = (f32[64,128]{1,0:T(8,128)S(1)}, f32[64,128]{1,0:T(8,128)S(1)}, u32[]{:S(2)}, u32[]{:S(2)}) collective-permute-start(f32[64,128]{1,0:T(8,128)S(1)} %get-tuple-element.70), channel_id=1, source_target_pairs={{0,128},{64,192},{128,0},{192,64},{1,129},{65,193},{129,1},{193,65... | collective-permute-start | bytes 98312 | tf_op jit(solution)/shard_map/ppermute | solution.py:325
  100.7 6.5 %collective-permute-start.21 = (f32[64,128]{1,0:T(8,128)S(1)}, f32[64,128]{1,0:T(8,128)S(1)}, u32[]{:S(2)}, u32[]{:S(2)}) collective-permute-start(f32[64,128]{1,0:T(8,128)S(1)} %get-tuple-element.69), channel_id=1, source_target_pairs={{0,192},{64,128},{128,64},{192,0},{1,193},{65,129},{129,65},{193,1... | collective-permute-start | bytes 98312 | tf_op jit(solution)/shard_map/ppermute | solution.py:325
  101.5 11.4 %copy-start.4 = (f32[4,64,256]{2,1,0:T(8,128)S(1)}, f32[4,64,256]{2,1,0:T(8,128)}, u32[]{:S(2)}) copy-start(f32[4,64,256]{2,1,0:T(8,128)} %param.10) | copy-start | bytes 786436
  101.6 11.4 %copy-start.6 = (f32[256,32]{0,1:T(8,128)S(1)}, f32[256,32]{0,1:T(8,128)}, u32[]{:S(2)}) copy-start(f32[256,32]{0,1:T(8,128)} %param.13) | copy-start | bytes 98308
  (5 other events, 25.1 us)

commit v5 on v4

--- a/solution.py
+++ b/solution.py
@@ -40,9 +40,7 @@
     return demeaned * inverse, inverse
 
 
-def project_kernel(
-    x_ref, scale_ref, offset_ref, w1_ref, b1_ref, w2_ref, b2_ref, left_ref, right_ref, tmp
-):
+def project_right_kernel(x_ref, scale_ref, offset_ref, w2_ref, b2_ref, right_ref):
     normed = standardized(x_ref[...])[0] * scale_ref[...] + offset_ref[...]
     on = lax.broadcasted_iota(jnp.int32, (32, 32), 0) == lax.broadcasted_iota(jnp.int32, (32, 32), 1)
     b2 = jnp.sum(jnp.where(on, b2_ref[...], 0.0), axis=1, keepdims=True)
@@ -50,6 +48,10 @@
     for s in range(4):
         cols = right[:, s * 64 : s * 64 + 64]
         right_ref[s * 16 : s * 16 + 16, :] = jnp.concatenate([cols[0:16], cols[16:32]], axis=1)
+
+
+def project_left_kernel(x_ref, scale_ref, offset_ref, w1_ref, b1_ref, left_ref, tmp):
+    normed = standardized(x_ref[...])[0] * scale_ref[...] + offset_ref[...]
     tmp[:, 0:32] = contract(normed, w1_ref[...], ((1,), (1,))) + b1_ref[...]
     wide = jnp.concatenate([tmp[pl.ds(u, 64, stride=4), :][:, 0:32] for u in range(4)], axis=1)
     for q in range(4):
@@ -220,16 +222,13 @@
 
 
 def left_gradient_kernel(*refs):
-    parts, (hi_far, lo_far, own_out, other_out, right_all, r_hl, g_hi, g_lo, sems) = refs[:8], refs[8:]
-    copies = fetch([(hi_far, g_hi), (lo_far, g_lo)], sems)
+    parts, (g_hi, g_lo, own_out, other_out, right_all, r_hl) = refs[:8], refs[8:]
     gather_right(parts, right_all)
     for e in range(16):
         g, m = e // 4, e % 4
         hi, lo = halves(right_rows(right_all, e))
         r_hl[m, 0:128, g * 128 : g * 128 + 128] = hi
         r_hl[m, 128:256, g * 128 : g * 128 + 128] = lo
-    for copy in copies:
-        copy.wait()
     total = [None] * 4
     for m in range(4):
         both = matmul(r_hl[m], g_hi[m])
@@ -247,12 +246,9 @@
                 out[pl.ds(s * 4 + quad, 16, stride=16), :] = t[at : at + 16]
 
 
-def right_gradient_kernel(left_ref, hi_far, lo_far, *refs):
-    outs, (lt, total, g_hi, g_lo, sems) = refs[:8], refs[8:]
-    copies = fetch([(hi_far, g_hi), (lo_far, g_lo)], sems)
+def right_gradient_kernel(left_ref, g_hi, g_lo, *refs):
+    outs, (lt, total) = refs[:8], refs[8:]
     left_turned(left_ref, lt)
-    for copy in copies:
-        copy.wait()
     for m in range(4):
         both = matmul(g_hi[m], lt[m])
         v = both[:, 0:128] + both[:, 128:256] + matmul(g_lo[m], lt[m, :, 0:128])
@@ -348,21 +344,34 @@
     small = 2 * 256 * 256 * 32 * 6
     step = 2 * 1024 * 1024 * 128 * 3
     offset = standardize_offset.reshape(1, 256)
-    left, right = call(
-        project_kernel,
-        "project",
-        [((8, 64, 128), f32), ((64, 128), f32)],
+    (right,) = call(
+        project_right_kernel,
+        "project_right",
+        [((64, 128), f32)],
+        [],
+        None,
+        small,
+        x,
+        scale,
+        offset,
+        w2,
+        second_operand_intercept.reshape(1, 32),
+    )
+    (left,) = call(
+        project_left_kernel,
+        "project_left",
+        [((8, 64, 128), f32)],
         [((256, 128), f32)],
         None,
-        2 * small,
+        small,
         x,
         scale,
         offset,
         w1,
         first_operand_intercept.reshape(1, 32),
-        w2,
-        second_operand_intercept.reshape(1, 32),
-    )
+    )
+    right = [right] + [from_peer(right, "zl", dz) for dz in (1, 2, 3)]
+    left, right = lax.optimization_barrier((left, right))
     g_hi, g_lo, cot_t = call(
         cotangent_kernel,
         "cotangent",
@@ -373,13 +382,13 @@
             ((1024, 384), bf16),
             ((4, 256, 384), bf16),
         ],
-        None,
+        24,
         step,
         result_matrix,
         edge_incoming_sensitivity,
     )
     left = exchange(left, COL).reshape(32, 16, 128)
-    right = jnp.stack([right] + [from_peer(right, "zl", dz) for dz in (1, 2, 3)])
+    right = jnp.stack(right)
     parts = [right] + [from_peer(right, "x", dx) for dx in (1, 2, 3)]
     left, parts, g_hi, g_lo, cot_t = lax.optimization_barrier((left, parts, g_hi, g_lo, cot_t))
     left = exchange(left, ROW).reshape(512, 128)
@@ -388,12 +397,12 @@
         left_gradient_kernel,
         "left_gradient",
         [((256, 128), f32), ((256, 128), f32)],
-        [((2048, 128), f32), ((4, 256, 512), bf16)] + [((4, 512, 512), bf16)] * 2,
+        [((2048, 128), f32), ((4, 256, 512), bf16)],
         14,
         step,
         *parts,
-        far=(g_hi, g_lo),
-        copies=2,
+        g_hi,
+        g_lo,
     )
     got_left = swap_cores(other_left)
     left, own_left, got_left = lax.optimization_barrier((left, own_left, got_left))
@@ -422,12 +431,12 @@
         right_gradient_kernel,
         "right_gradient",
         [((4, 64, 128), f32)] * 8,
-        [((4, 512, 256), bf16), ((2048, 128), f32)] + [((4, 512, 512), bf16)] * 2,
-        None,
+        [((4, 512, 256), bf16), ((2048, 128), f32)],
+        16,
         step,
         left,
-        far=(g_hi, g_lo),
-        copies=2,
+        g_hi,
+        g_lo,
     )
     weight = (own + got).reshape(16, BWD, 128)
     sent = [weight, own_left.reshape(16, 16, 128), got_left.reshape(16, 16, 128)]

time: 115 us -> 112 us (0.974)
  Pallas kernels: 29.1 us -> 23 us
  local copies, waits for them, and re-layouts: 3.24 us -> 8.47 us
  other arithmetic: 6.22 us -> 4.48 us
    pallas_call x8 -> x9, Pallas kernels: 29.1 us -> 23 us  [call(): pl.pallas_call(kernel, out_shape=shapes, in_specs=[VMEM] * len(args) + [H...]
    unnamed x22 -> x26, local copies, waits for them, and re-layouts: 3.22 us -> 8.46 us
    add x3, other arithmetic: 2.85 us -> 0.07 us  [local(): sums = [a + swap_cores(b) for a, b in zip(sums[:4], sums[4:])]]
    ppermute x12, waiting for transfers between devices: 11.8 us -> 9.62 us  [from_peer(): return lax.ppermute(array, axis, [(i, i ^ apart) for i in range(4)])]
    all_to_all x4, waiting for transfers between devices: 6.14 us -> 8.19 us  [exchange(): return lax.all_to_all(array, axes, 0, 0, tiled=True)]
  transfers between devices with their start and end apart: 26 -> 26, of which waited for: 14 -> 14; matrix products, arithmetic and copies ran while one was open for 4% -> 1% of each run, Pallas kernels for 18% -> 13%
where the time goes in v5:
time: 112 us; the launch traced here: 111 us
  starting transfers between devices  52.9 us (47%)
  Pallas kernels  23 us (21%)
  waiting for transfers between devices  21.6 us (19%)
  local copies, waits for them, and re-layouts  8.47 us (8%)
  other arithmetic  4.48 us (4%)
    all_to_all x4, starting transfers between devices, exchange(): return lax.all_to_all(array, axes, 0, 0, tiled=True)  32.5 us
    pallas_call x9, Pallas kernels, call(): pl.pallas_call(kernel, out_shape=shapes, in_specs=[VMEM] * len(args) + [H...  23 us
    ppermute x12, starting transfers between devices, from_peer(): return lax.ppermute(array, axis, [(i, i ^ apart) for i in range(4)])  17.2 us
    ppermute x12, waiting for transfers between devices, from_peer(): return lax.ppermute(array, axis, [(i, i ^ apart) for i in range(4)])  9.62 us
    unnamed x26, local copies, waits for them, and re-layouts  8.46 us
    all_to_all x4, waiting for transfers between devices, exchange(): return lax.all_to_all(array, axes, 0, 0, tiled=True)  8.19 us
    ppermute x10, waiting for transfers between devices, swap_cores(): return lax.ppermute(array, 'core', [(0, 1), (1, 0)])  3.76 us
    ppermute x10, starting transfers between devices, swap_cores(): return lax.ppermute(array, 'core', [(0, 1), (1, 0)])  3.17 us
  transfers between devices with their start and end apart: 26, of which 14 were waited for; matrix products, arithmetic and copies ran while one was open for 1% of the time, Pallas kernels for 13%

profile of v5, /device:TPU:32, one launch (start us, length us, event | category | flops | bytes accessed | tf_op | source)
XLA Modules:
  0.0 111.3 jit_solution(10285069721419465750)
XLA Ops:
  0.6 2.2 %project_right.1 = f32[64,128]{1,0:T(8,128)} custom-call(f32[256,256]{1,0:T(8,128)} %bitcast.31, f32[1,256]{1,0:T(1,128)} %bitcast.42, f32[1,256]{1,0:T(1,128)} %bitcast.54, f32[32,256]{1,0:T(8,128)} %bitcast.37, f32[1,32]{1,0:T(1,128)} %bitcast.56), custom_call_target="tpu_custom_call" | custom-call | flops 25165824 | bytes 329856 | tf_op jit(solution)/shard_map/project_right/pallas_call | solution.py:301
  2.9 1.8 %collective-permute-start = (f32[64,128]{1,0:T(8,128)}, f32[64,128]{1,0:T(8,128)S(1)}, u32[]{:S(2)}, u32[]{:S(2)}) collective-permute-start(f32[64,128]{1,0:T(8,128)} %project_right.1), channel_id=1, source_target_pairs={{0,64},{64,0},{128,192},{192,128},{1,65},{65,1},{129,193},{193,129... | collective-permute-start | bytes 98312 | tf_op jit(solution)/shard_map/ppermute | solution.py:321
  4.7 1.5 %collective-permute-start.1 = (f32[64,128]{1,0:T(8,128)}, f32[64,128]{1,0:T(8,128)S(1)}, u32[]{:S(2)}, u32[]{:S(2)}) collective-permute-start(f32[64,128]{1,0:T(8,128)} %project_right.1), channel_id=1, source_target_pairs={{0,128},{64,192},{128,0},{192,64},{1,129},{65,193},{129,1},{193,65... | collective-permute-start | bytes 98312 | tf_op jit(solution)/shard_map/ppermute | solution.py:321
  6.7 2.3 %project_left.1 = f32[8,64,128]{2,1,0:T(8,128)} custom-call(f32[256,256]{1,0:T(8,128)} %bitcast.32, f32[1,256]{1,0:T(1,128)} %bitcast.43, f32[1,256]{1,0:T(1,128)} %bitcast.55, f32[32,256]{1,0:T(8,128)} %bitcast.40, f32[1,32]{1,0:T(1,128)} %bitcast.57), custom_call_target="tpu_custom_call" | custom-call | flops 25165824 | bytes 559232 | tf_op jit(solution)/shard_map/project_left/pallas_call | solution.py:301
  10.4 9.4 %all-to-all-start = ((f32[8,64,128]{2,1,0:T(8,128)}), f32[8,64,128]{2,1,0:T(8,128)}, u32[]{:S(2)}, u32[]{:S(2)}) async-start(f32[8,64,128]{2,1,0:T(8,128)} %project_left.1), calls=%async_computation | async-start | bytes 524288 | tf_op jit(solution)/shard_map/all_to_all | solution.py:325
  20.6 1.6 %collective-permute-start.3 = (f32[4,64,128]{2,1,0:T(8,128)S(1)}, f32[4,64,128]{2,1,0:T(8,128)S(1)}, u32[]{:S(2)}, u32[]{:S(2)}) collective-permute-start(f32[4,64,128]{2,1,0:T(8,128)S(1)} %pad_maximum_fusion.1.refs_0_), channel_id=1, source_target_pairs={{0,16},{16,0},{32,48},{48,32},{1,17},{17,1},{33,49},{49,33},{2,18}... | collective-permute-start | bytes 393224 | tf_op jit(solution)/shard_map/ppermute | solution.py:321
  22.1 2.7 %collective-permute-start.4 = (f32[4,64,128]{2,1,0:T(8,128)S(1)}, f32[4,64,128]{2,1,0:T(8,128)S(1)}, u32[]{:S(2)}, u32[]{:S(2)}) collective-permute-start(f32[4,64,128]{2,1,0:T(8,128)S(1)} %pad_maximum_fusion.1.refs_0_), channel_id=1, source_target_pairs={{0,32},{16,48},{32,0},{48,16},{1,33},{17,49},{33,1},{49,17},{2,34}... | collective-permute-start | bytes 393224 | tf_op jit(solution)/shard_map/ppermute | solution.py:321
  27.4 2.7 %cotangent.1 = (bf16[4,512,512]{2,1,0:T(8,128)(2,1)S(1)}, bf16[4,512,512]{2,1,0:T(8,128)(2,1)S(1)}, bf16[4,256,256]{2,1,0:T(8,128)(2,1)S(1)}) custom-call(f32[1024,128]{1,0:T(8,128)S(1)} %copy-done.8, f32[16,64,128]{2,1,0:T(8,128)S(1)} %copy-done.7), custom_call_target="tpu_custom_call" | custom-call | flops 805306368 | bytes 5767168 | tf_op jit(solution)/shard_map/cotangent/pallas_call | solution.py:301
  30.2 1.3 %copy-done = bf16[4,512,512]{2,1,0:T(8,128)(2,1)} copy-done((bf16[4,512,512]{2,1,0:T(8,128)(2,1)}, bf16[4,512,512]{2,1,0:T(8,128)(2,1)S(1)}, u32[]{:S(2)}) %copy-start) | copy-done | bytes 2097176
  32.3 8.2 %all-to-all-start.1 = ((f32[32,16,128]{2,1,0:T(8,128)}), f32[32,16,128]{2,1,0:T(8,128)S(1)}, u32[]{:S(2)}, u32[]{:S(2)}) async-start(f32[32,16,128]{2,1,0:T(8,128)} %bitcast.7), calls=%async_computation.1 | async-start | bytes 524288 | tf_op jit(solution)/shard_map/all_to_all | solution.py:325
  42.7 1.6 %copy-done.1 = bf16[4,512,512]{2,1,0:T(8,128)(2,1)S(1)} copy-done((bf16[4,512,512]{2,1,0:T(8,128)(2,1)S(1)}, bf16[4,512,512]{2,1,0:T(8,128)(2,1)}, u32[]{:S(2)}) %copy-start.1) | copy-done | bytes 2097176
  44.3 1.6 %left_gradient.1 = (f32[256,128]{1,0:T(8,128)S(1)}, f32[256,128]{1,0:T(8,128)S(1)}) custom-call(f32[4,64,128]{2,1,0:T(8,128)S(1)} %pad_maximum_fusion.1.refs_0_, f32[4,64,128]{2,1,0:T(8,128)S(1)} %collective-permute-done.3.refs_1_, f32[4,64,128]{2,1,0:T(8,128)S(1)} %collective-permute-done.4.refs_2_, f32[4,64,128]{2,1,0:T(8,128)S(1)} %collective-permute-done.5.refs_3_, ...), custom_call_target="tpu_custom_call" | custom-call | flops 805306368 | bytes 5505024 | tf_op jit(solution)/shard_map/left_gradient/pallas_call | solution.py:301
  46.5 1.2 %collective-permute-done.10 = f32[256,128]{1,0:T(8,128)} collective-permute-done((f32[256,128]{1,0:T(8,128)S(1)}, f32[256,128]{1,0:T(8,128)}, u32[]{:S(2)}, u32[]{:S(2)}) %collective-permute-start.10) | collective-permute-done | bytes 131104 | tf_op jit(solution)/shard_map/ppermute | solution.py:317
  47.7 3.0 %all-to-all-done.1 = f32[32,16,128]{2,1,0:T(8,128)S(1)} async-done(((f32[32,16,128]{2,1,0:T(8,128)}), f32[32,16,128]{2,1,0:T(8,128)S(1)}, u32[]{:S(2)}, u32[]{:S(2)}) %all-to-all-start.1) | async-done | bytes 262176 | tf_op jit(solution)/shard_map/all_to_all | solution.py:325
  50.6 1.0 copy-done.12
  51.7 4.9 %tile.1 = (f32[512,128]{1,0:T(8,128)S(1)}, f32[512,128]{1,0:T(8,128)S(1)}) custom-call(f32[512,128]{1,0:T(8,128)S(1)} %bitcast.34, f32[4,64,128]{2,1,0:T(8,128)S(1)} %pad_maximum_fusion.1.refs_0_, f32[4,64,128]{2,1,0:T(8,128)S(1)} %collective-permute-done.3.refs_1_, f32[4,64,128]{2,1,0:T(8,128)S(1)} %collective-permute-done.4.refs_2_, ...), custom_call_target="tpu_custom_call" | custom-call | flops 1610612736 | bytes 2359296 | tf_op jit(solution)/shard_map/tile/pallas_call | solution.py:301
  56.9 1.3 %collective-permute-done.11 = f32[512,128]{1,0:T(8,128)S(1)} collective-permute-done((f32[512,128]{1,0:T(8,128)S(1)}, f32[512,128]{1,0:T(8,128)S(1)}, u32[]{:S(2)}, u32[]{:S(2)}) %collective-permute-start.11) | collective-permute-done | bytes 262176 | tf_op jit(solution)/shard_map/ppermute | solution.py:317
  58.2 1.7 %pad_maximum_fusion = f32[16,64,128]{2,1,0:T(8,128)} fusion(f32[16,16,128]{2,1,0:T(8,128)} %bitcast.16, f32[16,16,128]{2,1,0:T(8,128)S(1)} %bitcast.39, f32[16,32,128]{2,1,0:T(8,128)S(1)} %bitcast.47), kind=kLoop, calls=%fused_computation | loop fusion | flops 262144 | bytes 1048576 | tf_op jit(solution)/shard_map/concatenate | solution.py:443
  59.9 5.3 %all-to-all-start.2 = ((f32[16,64,128]{2,1,0:T(8,128)}), f32[16,64,128]{2,1,0:T(8,128)}, u32[]{:S(2)}, u32[]{:S(2)}) async-start(f32[16,64,128]{2,1,0:T(8,128)} %pad_maximum_fusion), calls=%async_computation.2 | async-start | bytes 1048576 | tf_op jit(solution)/shard_map/all_to_all | solution.py:325
  65.2 1.6 %copy-done.2 = bf16[4,512,512]{2,1,0:T(8,128)(2,1)S(1)} copy-done((bf16[4,512,512]{2,1,0:T(8,128)(2,1)S(1)}, bf16[4,512,512]{2,1,0:T(8,128)(2,1)}, u32[]{:S(2)}) %copy-start.2) | copy-done | bytes 2097176
  66.8 1.9 %right_gradient.1 = (f32[4,64,128]{2,1,0:T(8,128)S(1)}, f32[4,64,128]{2,1,0:T(8,128)S(1)}, f32[4,64,128]{2,1,0:T(8,128)S(1)}, f32[4,64,128]{2,1,0:T(8,128)S(1)},...) custom-call(f32[512,128]{1,0:T(8,128)S(1)} %bitcast.35, ...), custom_call_target="tpu_custom_call" | custom-call | flops 805306368 | bytes 5505024 | tf_op jit(solution)/shard_map/right_gradient/pallas_call | solution.py:301
  70.2 2.8 %collective-permute-start.18 = (f32[4,64,128]{2,1,0:T(8,128)S(1)}, f32[4,64,128]{2,1,0:T(8,128)S(1)}, u32[]{:S(2)}, u32[]{:S(2)}) collective-permute-start(f32[4,64,128]{2,1,0:T(8,128)S(1)} %add.31), channel_id=1, source_target_pairs={{0,48},{16,32},{32,16},{48,0},{1,49},{17,33},{33,17},{49,1},{2,50}... | collective-permute-start | bytes 393224 | tf_op jit(solution)/shard_map/ppermute | solution.py:321
  73.4 1.8 %collective-permute-start.16 = (f32[4,64,128]{2,1,0:T(8,128)S(1)}, f32[4,64,128]{2,1,0:T(8,128)S(1)}, u32[]{:S(2)}, u32[]{:S(2)}) collective-permute-start(f32[4,64,128]{2,1,0:T(8,128)S(1)} %add.29), channel_id=1, source_target_pairs={{0,32},{16,48},{32,0},{48,16},{1,33},{17,49},{33,1},{49,17},{2,34}... | collective-permute-start | bytes 393224 | tf_op jit(solution)/shard_map/ppermute | solution.py:321
  75.2 3.7 %collective-permute-done.18 = f32[4,64,128]{2,1,0:T(8,128)S(1)} collective-permute-done((f32[4,64,128]{2,1,0:T(8,128)S(1)}, f32[4,64,128]{2,1,0:T(8,128)S(1)}, u32[]{:S(2)}, u32[]{:S(2)}) %collective-permute-start.18) | collective-permute-done | bytes 131104 | tf_op jit(solution)/shard_map/ppermute | solution.py:321
  78.9 1.6 %collective-permute-done.14 = f32[4,64,128]{2,1,0:T(8,128)S(1)} collective-permute-done((f32[4,64,128]{2,1,0:T(8,128)S(1)}, f32[4,64,128]{2,1,0:T(8,128)S(1)}, u32[]{:S(2)}, u32[]{:S(2)}) %collective-permute-start.14) | collective-permute-done | bytes 131104 | tf_op jit(solution)/shard_map/ppermute | solution.py:321
  80.6 2.9 %collective-permute-done.16 = f32[4,64,128]{2,1,0:T(8,128)S(1)} collective-permute-done((f32[4,64,128]{2,1,0:T(8,128)S(1)}, f32[4,64,128]{2,1,0:T(8,128)S(1)}, u32[]{:S(2)}, u32[]{:S(2)}) %collective-permute-start.16) | collective-permute-done | bytes 131104 | tf_op jit(solution)/shard_map/ppermute | solution.py:321
  83.5 1.1 fusion
  85.4 9.6 %all-to-all-start.3 = ((f32[8,72,128]{2,1,0:T(8,128)}), f32[8,72,128]{2,1,0:T(8,128)S(1)}, u32[]{:S(2)}, u32[]{:S(2)}) async-start(f32[8,72,128]{2,1,0:T(8,128)} %select_maximum_fusion), calls=%async_computation.3 | async-start | bytes 589824 | tf_op jit(solution)/shard_map/all_to_all | solution.py:325
  95.4 2.7 %collective-permute-start.20 = (f32[64,128]{1,0:T(8,128)S(1)}, f32[64,128]{1,0:T(8,128)S(1)}, u32[]{:S(2)}, u32[]{:S(2)}) collective-permute-start(f32[64,128]{1,0:T(8,128)S(1)} %get-tuple-element.76), channel_id=1, source_target_pairs={{0,128},{64,192},{128,0},{192,64},{1,129},{65,193},{129,1},{193,65... | collective-permute-start | bytes 98312 | tf_op jit(solution)/shard_map/ppermute | solution.py:321
  98.6 5.6 %pair.1 = f32[16,64,128]{2,1,0:T(8,128)} custom-call(f32[512,128]{1,0:T(8,128)S(1)} %bitcast.36, f32[4,64,128]{2,1,0:T(8,128)S(1)} %pad_maximum_fusion.1.refs_0_, f32[4,64,128]{2,1,0:T(8,128)S(1)} %collective-permute-done.3.refs_1_, f32[4,64,128]{2,1,0:T(8,128)S(1)} %collective-permute-done.4.refs_2_, f32[4,64,128]{2,1,0:T(8,128)S(1)} %collective-permute-done.5.refs_3_, ...), custom_call_target="tpu_custom_call" | custom-call | flops 1610612736 | bytes 2359808 | tf_op jit(solution)/shard_map/pair/pallas_call | solution.py:301
  104.8 5.2 %all-to-all-done.3.col_ref = f32[8,72,128]{2,1,0:T(8,128)S(1)} async-done(((f32[8,72,128]{2,1,0:T(8,128)}), f32[8,72,128]{2,1,0:T(8,128)S(1)}, u32[]{:S(2)}, u32[]{:S(2)}) %all-to-all-start.3) | async-done | bytes 294944 | tf_op jit(solution)/shard_map/all_to_all | solution.py:325
  110.0 1.3 %finish.1 = (f32[256,256]{1,0:T(8,128)}, f32[4,128]{1,0:T(4,128)}) custom-call(f32[256,256]{1,0:T(8,128)S(1)} %bitcast.33, f32[1,256]{1,0:T(1,128)S(1)} %bitcast.44, f32[32,256]{1,0:T(8,128)S(1)} %bitcast.41, f32[256,256]{1,0:T(8,128)S(1)} %right.1.part_ref, f32[8,72,128]{2,1,0:T(8,128)S(1)} %all-to-all-done.3.col_ref), custom_call_target="tpu_custom_call" | custom-call | flops 25165824 | bytes 1117184 | tf_op jit(solution)/shard_map/finish/pallas_call | solution.py:301
  (66 shorter events, 13.1 us)
Async XLA Ops:
  2.9 6.1 %collective-permute-start = (f32[64,128]{1,0:T(8,128)}, f32[64,128]{1,0:T(8,128)S(1)}, u32[]{:S(2)}, u32[]{:S(2)}) collective-permute-start(f32[64,128]{1,0:T(8,128)} %project_right.1), channel_id=1, source_target_pairs={{0,64},{64,0},{128,192},{192,128},{1,65},{65,1},{129,193},{193,129... | collective-permute-start | bytes 98312 | tf_op jit(solution)/shard_map/ppermute | solution.py:321
  4.7 5.0 %collective-permute-start.1 = (f32[64,128]{1,0:T(8,128)}, f32[64,128]{1,0:T(8,128)S(1)}, u32[]{:S(2)}, u32[]{:S(2)}) collective-permute-start(f32[64,128]{1,0:T(8,128)} %project_right.1), channel_id=1, source_target_pairs={{0,128},{64,192},{128,0},{192,64},{1,129},{65,193},{129,1},{193,65... | collective-permute-start | bytes 98312 | tf_op jit(solution)/shard_map/ppermute | solution.py:321
  6.2 4.1 %collective-permute-start.2 = (f32[64,128]{1,0:T(8,128)}, f32[64,128]{1,0:T(8,128)S(1)}, u32[]{:S(2)}, u32[]{:S(2)}) collective-permute-start(f32[64,128]{1,0:T(8,128)} %project_right.1), channel_id=1, source_target_pairs={{0,192},{64,128},{128,64},{192,0},{1,193},{65,129},{129,65},{193,1... | collective-permute-start | bytes 98312 | tf_op jit(solution)/shard_map/ppermute | solution.py:321
  10.4 22.0 %all-to-all-start = ((f32[8,64,128]{2,1,0:T(8,128)}), f32[8,64,128]{2,1,0:T(8,128)}, u32[]{:S(2)}, u32[]{:S(2)}) async-start(f32[8,64,128]{2,1,0:T(8,128)} %project_left.1), calls=%async_computation | async-start | bytes 524288 | tf_op jit(solution)/shard_map/all_to_all | solution.py:325
  20.6 11.8 %collective-permute-start.3 = (f32[4,64,128]{2,1,0:T(8,128)S(1)}, f32[4,64,128]{2,1,0:T(8,128)S(1)}, u32[]{:S(2)}, u32[]{:S(2)}) collective-permute-start(f32[4,64,128]{2,1,0:T(8,128)S(1)} %pad_maximum_fusion.1.refs_0_), channel_id=1, source_target_pairs={{0,16},{16,0},{32,48},{48,32},{1,17},{17,1},{33,49},{49,33},{2,18}... | collective-permute-start | bytes 393224 | tf_op jit(solution)/shard_map/ppermute | solution.py:321
  22.1 10.2 %collective-permute-start.4 = (f32[4,64,128]{2,1,0:T(8,128)S(1)}, f32[4,64,128]{2,1,0:T(8,128)S(1)}, u32[]{:S(2)}, u32[]{:S(2)}) collective-permute-start(f32[4,64,128]{2,1,0:T(8,128)S(1)} %pad_maximum_fusion.1.refs_0_), channel_id=1, source_target_pairs={{0,32},{16,48},{32,0},{48,16},{1,33},{17,49},{33,1},{49,17},{2,34}... | collective-permute-start | bytes 393224 | tf_op jit(solution)/shard_map/ppermute | solution.py:321
  24.9 7.5 %collective-permute-start.5 = (f32[4,64,128]{2,1,0:T(8,128)S(1)}, f32[4,64,128]{2,1,0:T(8,128)S(1)}, u32[]{:S(2)}, u32[]{:S(2)}) collective-permute-start(f32[4,64,128]{2,1,0:T(8,128)S(1)} %pad_maximum_fusion.1.refs_0_), channel_id=1, source_target_pairs={{0,48},{16,32},{32,16},{48,0},{1,49},{17,33},{33,17},{49,1},{2,50}... | collective-permute-start | bytes 393224 | tf_op jit(solution)/shard_map/ppermute | solution.py:321
  32.3 18.3 %all-to-all-start.1 = ((f32[32,16,128]{2,1,0:T(8,128)}), f32[32,16,128]{2,1,0:T(8,128)S(1)}, u32[]{:S(2)}, u32[]{:S(2)}) async-start(f32[32,16,128]{2,1,0:T(8,128)} %bitcast.7), calls=%async_computation.1 | async-start | bytes 524288 | tf_op jit(solution)/shard_map/all_to_all | solution.py:325
  40.6 1.4 %collective-permute-start.6 = (f32[4,64,128]{2,1,0:T(8,128)S(1)}, f32[4,64,128]{2,1,0:T(8,128)S(1)}, u32[]{:S(2)}, u32[]{:S(2)}) collective-permute-start(f32[4,64,128]{2,1,0:T(8,128)S(1)} %pad_maximum_fusion.1.refs_0_), channel_id=1, source_target_pairs={{0,8},{8,0},{1,9},{9,1},{2,10},{10,2},{3,11},{11,3},{4,12},{12,4},... | collective-permute-start | bytes 393224 | tf_op jit(solution)/shard_map/ppermute | solution.py:317
  40.8 1.4 %collective-permute-start.7 = (f32[4,64,128]{2,1,0:T(8,128)S(1)}, f32[4,64,128]{2,1,0:T(8,128)S(1)}, u32[]{:S(2)}, u32[]{:S(2)}) collective-permute-start(f32[4,64,128]{2,1,0:T(8,128)S(1)} %collective-permute-done.3.refs_1_), channel_id=1, source_target_pairs={{0,8},{8,0},{1,9},{9,1},{2,10},{10,2},{3,11},{11,3},{4,12},{12,4},... | collective-permute-start | bytes 393224 | tf_op jit(solution)/shard_map/ppermute | solution.py:317
  41.2 1.3 %collective-permute-start.8 = (f32[4,64,128]{2,1,0:T(8,128)S(1)}, f32[4,64,128]{2,1,0:T(8,128)S(1)}, u32[]{:S(2)}, u32[]{:S(2)}) collective-permute-start(f32[4,64,128]{2,1,0:T(8,128)S(1)} %collective-permute-done.4.refs_2_), channel_id=1, source_target_pairs={{0,8},{8,0},{1,9},{9,1},{2,10},{10,2},{3,11},{11,3},{4,12},{12,4},... | collective-permute-start | bytes 393224 | tf_op jit(solution)/shard_map/ppermute | solution.py:317
  41.3 1.4 %collective-permute-start.9 = (f32[4,64,128]{2,1,0:T(8,128)S(1)}, f32[4,64,128]{2,1,0:T(8,128)S(1)}, u32[]{:S(2)}, u32[]{:S(2)}) collective-permute-start(f32[4,64,128]{2,1,0:T(8,128)S(1)} %collective-permute-done.5.refs_3_), channel_id=1, source_target_pairs={{0,8},{8,0},{1,9},{9,1},{2,10},{10,2},{3,11},{11,3},{4,12},{12,4},... | collective-permute-start | bytes 393224 | tf_op jit(solution)/shard_map/ppermute | solution.py:317
  45.9 1.7 %collective-permute-start.10 = (f32[256,128]{1,0:T(8,128)S(1)}, f32[256,128]{1,0:T(8,128)}, u32[]{:S(2)}, u32[]{:S(2)}) collective-permute-start(f32[256,128]{1,0:T(8,128)S(1)} %get-tuple-element.54), channel_id=1, source_target_pairs={{0,8},{8,0},{1,9},{9,1},{2,10},{10,2},{3,11},{11,3},{4,12},{12,4},... | collective-permute-start | bytes 393224 | tf_op jit(solution)/shard_map/ppermute | solution.py:317
  56.5 1.6 %collective-permute-start.11 = (f32[512,128]{1,0:T(8,128)S(1)}, f32[512,128]{1,0:T(8,128)S(1)}, u32[]{:S(2)}, u32[]{:S(2)}) collective-permute-start(f32[512,128]{1,0:T(8,128)S(1)} %get-tuple-element.58), channel_id=1, source_target_pairs={{0,8},{8,0},{1,9},{9,1},{2,10},{10,2},{3,11},{11,3},{4,12},{12,4},... | collective-permute-start | bytes 786440 | tf_op jit(solution)/shard_map/ppermute | solution.py:317
  59.9 23.6 %all-to-all-start.2 = ((f32[16,64,128]{2,1,0:T(8,128)}), f32[16,64,128]{2,1,0:T(8,128)}, u32[]{:S(2)}, u32[]{:S(2)}) async-start(f32[16,64,128]{2,1,0:T(8,128)} %pad_maximum_fusion), calls=%async_computation.2 | async-start | bytes 1048576 | tf_op jit(solution)/shard_map/all_to_all | solution.py:325
  68.8 1.4 %collective-permute-start.17 = (f32[4,64,128]{2,1,0:T(8,128)S(1)}, f32[4,64,128]{2,1,0:T(8,128)S(1)}, u32[]{:S(2)}, u32[]{:S(2)}) collective-permute-start(f32[4,64,128]{2,1,0:T(8,128)S(1)} %get-tuple-element.68), channel_id=1, source_target_pairs={{0,8},{8,0},{1,9},{9,1},{2,10},{10,2},{3,11},{11,3},{4,12},{12,4},... | collective-permute-start | bytes 393224 | tf_op jit(solution)/shard_map/ppermute | solution.py:317
  68.9 4.1 %collective-permute-start.13 = (f32[4,64,128]{2,1,0:T(8,128)S(1)}, f32[4,64,128]{2,1,0:T(8,128)S(1)}, u32[]{:S(2)}, u32[]{:S(2)}) collective-permute-start(f32[4,64,128]{2,1,0:T(8,128)S(1)} %get-tuple-element.64), channel_id=1, source_target_pairs={{0,8},{8,0},{1,9},{9,1},{2,10},{10,2},{3,11},{11,3},{4,12},{12,4},... | collective-permute-start | bytes 393224 | tf_op jit(solution)/shard_map/ppermute | solution.py:317
  69.4 4.0 %collective-permute-start.15 = (f32[4,64,128]{2,1,0:T(8,128)S(1)}, f32[4,64,128]{2,1,0:T(8,128)S(1)}, u32[]{:S(2)}, u32[]{:S(2)}) collective-permute-start(f32[4,64,128]{2,1,0:T(8,128)S(1)} %get-tuple-element.66), channel_id=1, source_target_pairs={{0,8},{8,0},{1,9},{9,1},{2,10},{10,2},{3,11},{11,3},{4,12},{12,4},... | collective-permute-start | bytes 393224 | tf_op jit(solution)/shard_map/ppermute | solution.py:317
  69.5 5.8 %collective-permute-start.12 = (f32[4,64,128]{2,1,0:T(8,128)S(1)}, f32[4,64,128]{2,1,0:T(8,128)S(1)}, u32[]{:S(2)}, u32[]{:S(2)}) collective-permute-start(f32[4,64,128]{2,1,0:T(8,128)S(1)} %get-tuple-element.62), channel_id=1, source_target_pairs={{0,8},{8,0},{1,9},{9,1},{2,10},{10,2},{3,11},{11,3},{4,12},{12,4},... | collective-permute-start | bytes 393224 | tf_op jit(solution)/shard_map/ppermute | solution.py:317
  70.2 28.4 %copy-start.9 = (f32[1024,128]{1,0:T(8,128)S(1)}, f32[1024,128]{1,0:T(8,128)}, u32[]{:S(2)}) copy-start(f32[1024,128]{1,0:T(8,128)} %refs_9_.1) | copy-start | bytes 1572868
  70.2 28.4 %copy-start.10 = (f32[128]{0:T(128)S(1)}, f32[128]{0:T(128)}, u32[]{:S(2)}) copy-start(f32[128]{0:T(128)} %param.18) | copy-start | bytes 1540
  70.2 8.7 %collective-permute-start.18 = (f32[4,64,128]{2,1,0:T(8,128)S(1)}, f32[4,64,128]{2,1,0:T(8,128)S(1)}, u32[]{:S(2)}, u32[]{:S(2)}) collective-permute-start(f32[4,64,128]{2,1,0:T(8,128)S(1)} %add.31), channel_id=1, source_target_pairs={{0,48},{16,32},{32,16},{48,0},{1,49},{17,33},{33,17},{49,1},{2,50}... | collective-permute-start | bytes 393224 | tf_op jit(solution)/shard_map/ppermute | solution.py:321
  73.0 7.5 %collective-permute-start.14 = (f32[4,64,128]{2,1,0:T(8,128)S(1)}, f32[4,64,128]{2,1,0:T(8,128)S(1)}, u32[]{:S(2)}, u32[]{:S(2)}) collective-permute-start(f32[4,64,128]{2,1,0:T(8,128)S(1)} %add.28), channel_id=1, source_target_pairs={{0,16},{16,0},{32,48},{48,32},{1,17},{17,1},{33,49},{49,33},{2,18}... | collective-permute-start | bytes 393224 | tf_op jit(solution)/shard_map/ppermute | solution.py:321
  73.4 10.1 %collective-permute-start.16 = (f32[4,64,128]{2,1,0:T(8,128)S(1)}, f32[4,64,128]{2,1,0:T(8,128)S(1)}, u32[]{:S(2)}, u32[]{:S(2)}) collective-permute-start(f32[4,64,128]{2,1,0:T(8,128)S(1)} %add.29), channel_id=1, source_target_pairs={{0,32},{16,48},{32,0},{48,16},{1,33},{17,49},{33,1},{49,17},{2,34}... | collective-permute-start | bytes 393224 | tf_op jit(solution)/shard_map/ppermute | solution.py:321
  85.4 24.6 %all-to-all-start.3 = ((f32[8,72,128]{2,1,0:T(8,128)}), f32[8,72,128]{2,1,0:T(8,128)S(1)}, u32[]{:S(2)}, u32[]{:S(2)}) async-start(f32[8,72,128]{2,1,0:T(8,128)} %select_maximum_fusion), calls=%async_computation.3 | async-start | bytes 589824 | tf_op jit(solution)/shard_map/all_to_all | solution.py:325
  95.0 9.2 %collective-permute-start.19 = (f32[64,128]{1,0:T(8,128)S(1)}, f32[64,128]{1,0:T(8,128)S(1)}, u32[]{:S(2)}, u32[]{:S(2)}) collective-permute-start(f32[64,128]{1,0:T(8,128)S(1)} %get-tuple-element.77), channel_id=1, source_target_pairs={{0,64},{64,0},{128,192},{192,128},{1,65},{65,1},{129,193},{193,129... | collective-permute-start | bytes 98312 | tf_op jit(solution)/shard_map/ppermute | solution.py:321
  95.4 8.8 %collective-permute-start.20 = (f32[64,128]{1,0:T(8,128)S(1)}, f32[64,128]{1,0:T(8,128)S(1)}, u32[]{:S(2)}, u32[]{:S(2)}) collective-permute-start(f32[64,128]{1,0:T(8,128)S(1)} %get-tuple-element.76), channel_id=1, source_target_pairs={{0,128},{64,192},{128,0},{192,64},{1,129},{65,193},{129,1},{193,65... | collective-permute-start | bytes 98312 | tf_op jit(solution)/shard_map/ppermute | solution.py:321
  98.1 6.1 %collective-permute-start.21 = (f32[64,128]{1,0:T(8,128)S(1)}, f32[64,128]{1,0:T(8,128)S(1)}, u32[]{:S(2)}, u32[]{:S(2)}) collective-permute-start(f32[64,128]{1,0:T(8,128)S(1)} %get-tuple-element.75), channel_id=1, source_target_pairs={{0,192},{64,128},{128,64},{192,0},{1,193},{65,129},{129,65},{193,1... | collective-permute-start | bytes 98312 | tf_op jit(solution)/shard_map/ppermute | solution.py:321
  98.6 5.7 %copy-start.4 = (f32[256,32]{0,1:T(8,128)S(1)}, f32[256,32]{0,1:T(8,128)}, u32[]{:S(2)}) copy-start(f32[256,32]{0,1:T(8,128)} %param.15) | copy-start | bytes 98308
  98.6 11.4 %copy-start.3 = (f32[4,64,256]{2,1,0:T(8,128)S(1)}, f32[4,64,256]{2,1,0:T(8,128)}, u32[]{:S(2)}) copy-start(f32[4,64,256]{2,1,0:T(8,128)} %param.10) | copy-start | bytes 786436
  98.6 11.4 %copy-start.5 = (f32[256,32]{0,1:T(8,128)S(1)}, f32[256,32]{0,1:T(8,128)}, u32[]{:S(2)}) copy-start(f32[256,32]{0,1:T(8,128)} %param.13) | copy-start | bytes 98308
  98.6 11.4 %copy-start.6 = (f32[256]{0:T(256)S(1)}, f32[256]{0:T(256)}, u32[]{:S(2)}) copy-start(f32[256]{0:T(256)} %param.11) | copy-start | bytes 3076
  (7 other events, 8.4 us)

commit v6 on v5

--- a/solution.py
+++ b/solution.py
@@ -120,18 +120,17 @@
             w_hl[d, at : at + 32, 128:256] = lo
 
 
-def cotangent_kernel(w_ref, cot_ref, g_hi, g_lo, cot_t, wide_t, w_hl, w_cat, cot_cat):
+def cotangent_kernel(w_far, cot_far, g_hi, g_lo, wide_t, w_hl, w_cat, cot_cat, w_ref, cot_ref, sems):
+    copies = fetch([(w_far, w_ref), (cot_far, cot_ref)], sems)
+    copies[0].wait()
     weights_by_class(w_ref, w_hl)
+    copies[1].wait()
     for d in range(4):
         for quad in range(4):
             hi, lo = halves(cot_ref[quad * 4 + d])
             cot_cat[d, quad * 64 : quad * 64 + 64, 0:128] = hi
             cot_cat[d, quad * 64 : quad * 64 + 64, 128:256] = hi
             cot_cat[d, quad * 64 : quad * 64 + 64, 256:384] = lo
-    for d in range(4):
-        hi, lo = halves(jnp.concatenate([cot_ref[quad * 4 + d] for quad in range(4)], axis=0).T)
-        cot_t[d, 0:128, :] = hi
-        cot_t[d, 128:256, :] = lo
     for d in range(4):
         w_cat[:, 0:256] = w_hl[d]
         w_cat[:, 256:384] = w_hl[d, :, 0:128]
@@ -197,14 +196,15 @@
 
 def tile_kernel(left_ref, *refs):
     parts, (cot_far, own_out, other_out) = refs[:8], refs[8:11]
-    right_all, outer, lcat, rt, a_hi, a_lo, dw, cot_t, sems = refs[11:]
+    right_all, outer, lcat, rt, a_hi, a_lo, dw, cot_ref, sems = refs[11:]
     core = lax.axis_index("core")
-    (fetched,) = fetch([(cot_far, cot_t)], sems)
+    (fetched,) = fetch([(cot_far, cot_ref)], sems)
     outer_product(left_ref, parts, right_all, outer, lcat, rt, a_hi, a_lo)
     fetched.wait()
     for d in range(4):
-        both = matmul(cot_t[d], a_hi[d])
-        part = both[0:128] + both[128:256] + matmul(cot_t[d, 0:128, :], a_lo[d])
+        hi, lo = halves(jnp.concatenate([cot_ref[quad * 4 + d] for quad in range(4)], axis=0).T)
+        both = matmul(jnp.concatenate([hi, lo], axis=0), a_hi[d])
+        part = both[0:128] + both[128:256] + matmul(hi, a_lo[d])
         for block in range(8):
             v = part[:, block * 128 : block * 128 + 128]
             if d == 0:
@@ -222,13 +222,16 @@
 
 
 def left_gradient_kernel(*refs):
-    parts, (g_hi, g_lo, own_out, other_out, right_all, r_hl) = refs[:8], refs[8:]
+    parts, (hi_far, lo_far, own_out, other_out, right_all, r_hl, g_hi, g_lo, sems) = refs[:8], refs[8:]
+    copies = fetch([(hi_far, g_hi), (lo_far, g_lo)], sems)
     gather_right(parts, right_all)
     for e in range(16):
         g, m = e // 4, e % 4
         hi, lo = halves(right_rows(right_all, e))
         r_hl[m, 0:128, g * 128 : g * 128 + 128] = hi
         r_hl[m, 128:256, g * 128 : g * 128 + 128] = lo
+    for copy in copies:
+        copy.wait()
     total = [None] * 4
     for m in range(4):
         both = matmul(r_hl[m], g_hi[m])
@@ -246,9 +249,12 @@
                 out[pl.ds(s * 4 + quad, 16, stride=16), :] = t[at : at + 16]
 
 
-def right_gradient_kernel(left_ref, g_hi, g_lo, *refs):
-    outs, (lt, total) = refs[:8], refs[8:]
+def right_gradient_kernel(left_ref, hi_far, lo_far, *refs):
+    outs, (lt, total, g_hi, g_lo, sems) = refs[:8], refs[8:]
+    copies = fetch([(hi_far, g_hi), (lo_far, g_lo)], sems)
     left_turned(left_ref, lt)
+    for copy in copies:
+        copy.wait()
     for m in range(4):
         both = matmul(g_hi[m], lt[m])
         v = both[:, 0:128] + both[:, 128:256] + matmul(g_lo[m], lt[m, :, 0:128])
@@ -372,37 +378,39 @@
     )
     right = [right] + [from_peer(right, "zl", dz) for dz in (1, 2, 3)]
     left, right = lax.optimization_barrier((left, right))
-    g_hi, g_lo, cot_t = call(
+    g_hi, g_lo = call(
         cotangent_kernel,
         "cotangent",
-        [((4, 512, 512), bf16), ((4, 512, 512), bf16), ((4, 256, 256), bf16)],
+        [((4, 512, 512), bf16), ((4, 512, 512), bf16)],
         [
             ((4, 256, 1024), f32),
             ((4, 1024, 256), bf16),
             ((1024, 384), bf16),
             ((4, 256, 384), bf16),
+            ((1024, 128), f32),
+            ((16, 64, 128), f32),
         ],
-        24,
+        None,
         step,
-        result_matrix,
-        edge_incoming_sensitivity,
+        far=(result_matrix, edge_incoming_sensitivity),
+        copies=2,
     )
     left = exchange(left, COL).reshape(32, 16, 128)
     right = jnp.stack(right)
     parts = [right] + [from_peer(right, "x", dx) for dx in (1, 2, 3)]
-    left, parts, g_hi, g_lo, cot_t = lax.optimization_barrier((left, parts, g_hi, g_lo, cot_t))
+    left, parts, g_hi, g_lo = lax.optimization_barrier((left, parts, g_hi, g_lo))
     left = exchange(left, ROW).reshape(512, 128)
     parts = parts + [swap_cores(part) for part in parts]
     own_left, other_left = call(
         left_gradient_kernel,
         "left_gradient",
         [((256, 128), f32), ((256, 128), f32)],
-        [((2048, 128), f32), ((4, 256, 512), bf16)],
-        14,
+        [((2048, 128), f32), ((4, 256, 512), bf16)] + [((4, 512, 512), bf16)] * 2,
+        52,
         step,
         *parts,
-        g_hi,
-        g_lo,
+        far=(g_hi, g_lo),
+        copies=2,
     )
     got_left = swap_cores(other_left)
     left, own_left, got_left = lax.optimization_barrier((left, own_left, got_left))
@@ -418,12 +426,12 @@
         tile_kernel,
         "tile",
         [((16 * BWD, 128), f32)] * 2,
-        working + [((8, 128, 128), f32), ((4, 256, 256), bf16)],
-        22,
+        working + [((8, 128, 128), f32), ((16, 64, 128), f32)],
+        52,
         2 * step,
         left,
         *parts,
-        far=(cot_t,),
+        far=(edge_incoming_sensitivity,),
         copies=1,
     )
     got = swap_cores(other)
@@ -431,12 +439,12 @@
         right_gradient_kernel,
         "right_gradient",
         [((4, 64, 128), f32)] * 8,
-        [((4, 512, 256), bf16), ((2048, 128), f32)],
-        16,
+        [((4, 512, 256), bf16), ((2048, 128), f32)] + [((4, 512, 512), bf16)] * 2,
+        52,
         step,
         left,
-        g_hi,
-        g_lo,
+        far=(g_hi, g_lo),
+        copies=2,
     )
     weight = (own + got).reshape(16, BWD, 128)
     sent = [weight, own_left.reshape(16, 16, 128), got_left.reshape(16, 16, 128)]
@@ -448,7 +456,7 @@
         "pair",
         [((16, 64, 128), f32)],
         working + [((4, 1024, 256), bf16), ((1024, 128), f32)],
-        24,
+        52,
         2 * step,
         left,
         *parts,
@@ -460,7 +468,7 @@
     sent = jnp.concatenate(
         [back[:, 32:].reshape(8, 64, 128), jnp.pad(weight, ((0, 0), (0, 4), (0, 0)))], axis=1
     )
-    sent, right = lax.optimization_barrier((sent, right))
+    sent, right, pair = lax.optimization_barrier((sent, right, pair))
     cols = exchange(sent, COL)
     right = [right[0]] + [from_peer(right[dz], "zl", dz) for dz in (1, 2, 3)]
     (part,) = call(right_kernel, "right", [((256, 256), f32)], [], 8, small, w2, *right)

time: 112 us -> 106 us (0.946)
  local copies, waits for them, and re-layouts: 8.47 us -> 0.05 us
  Pallas kernels: 23 us -> 30.1 us
  starting transfers between devices: 52.9 us -> 49 us
  other arithmetic: 4.48 us -> 2.5 us
  waiting for transfers between devices: 21.6 us -> 22.9 us
    unnamed x26 -> x12, local copies, waits for them, and re-layouts: 8.46 us -> 0.04 us
    pallas_call x9, Pallas kernels: 23 us -> 30.1 us  [call(): pl.pallas_call(kernel, out_shape=shapes, in_specs=[VMEM] * len(args) + [H...]
    all_to_all x4, starting transfers between devices: 32.5 us -> 28.1 us  [exchange(): return lax.all_to_all(array, axes, 0, 0, tiled=True)]
    all_to_all x4, waiting for transfers between devices: 8.19 us -> 9.77 us  [exchange(): return lax.all_to_all(array, axes, 0, 0, tiled=True)]
  transfers between devices with their start and end apart: 26 -> 26, of which waited for: 14 -> 14; matrix products, arithmetic and copies ran while one was open for 1% -> 1% of each run, Pallas kernels for 13% -> 21%
where the time goes in v6:
time: 106 us; the launch traced here: 105 us
  starting transfers between devices  49 us (46%)
  Pallas kernels  30.1 us (28%)
  waiting for transfers between devices  22.9 us (22%)
  other arithmetic  2.5 us (2%)
    pallas_call x9, Pallas kernels, call(): pl.pallas_call(kernel, out_shape=shapes, in_specs=[VMEM] * len(args) + [H...  30.1 us
    all_to_all x4, starting transfers between devices, exchange(): return lax.all_to_all(array, axes, 0, 0, tiled=True)  28.1 us
    ppermute x12, starting transfers between devices, from_peer(): return lax.ppermute(array, axis, [(i, i ^ apart) for i in range(4)])  17.7 us
    all_to_all x4, waiting for transfers between devices, exchange(): return lax.all_to_all(array, axes, 0, 0, tiled=True)  9.77 us
    ppermute x12, waiting for transfers between devices, from_peer(): return lax.ppermute(array, axis, [(i, i ^ apart) for i in range(4)])  9.52 us
    ppermute x10, waiting for transfers between devices, swap_cores(): return lax.ppermute(array, 'core', [(0, 1), (1, 0)])  3.64 us
    ppermute x10, starting transfers between devices, swap_cores(): return lax.ppermute(array, 'core', [(0, 1), (1, 0)])  3.16 us
  transfers between devices with their start and end apart: 26, of which 14 were waited for; matrix products, arithmetic and copies ran while one was open for 1% of the time, Pallas kernels for 21%

profile of v6, /device:TPU:32, one launch (start us, length us, event | category | flops | bytes accessed | tf_op | source)
XLA Modules:
  0.0 105.4 jit_solution(132280716288655309)
XLA Ops:
  0.6 2.2 %project_right.1 = f32[64,128]{1,0:T(8,128)} custom-call(f32[256,256]{1,0:T(8,128)} %bitcast.31, f32[1,256]{1,0:T(1,128)} %bitcast.42, f32[1,256]{1,0:T(1,128)} %bitcast.55, f32[32,256]{1,0:T(8,128)} %bitcast.37, f32[1,32]{1,0:T(1,128)} %bitcast.57), custom_call_target="tpu_custom_call" | custom-call | flops 25165824 | bytes 329856 | tf_op jit(solution)/shard_map/project_right/pallas_call | solution.py:307
  2.9 1.9 %collective-permute-start.2 = (f32[64,128]{1,0:T(8,128)}, f32[64,128]{1,0:T(8,128)S(1)}, u32[]{:S(2)}, u32[]{:S(2)}) collective-permute-start(f32[64,128]{1,0:T(8,128)} %project_right.1), channel_id=1, source_target_pairs={{0,192},{64,128},{128,64},{192,0},{1,193},{65,129},{129,65},{193,1... | collective-permute-start | bytes 98312 | tf_op jit(solution)/shard_map/ppermute | solution.py:327
  4.8 2.3 %collective-permute-start.1 = (f32[64,128]{1,0:T(8,128)}, f32[64,128]{1,0:T(8,128)S(1)}, u32[]{:S(2)}, u32[]{:S(2)}) collective-permute-start(f32[64,128]{1,0:T(8,128)} %project_right.1), channel_id=1, source_target_pairs={{0,128},{64,192},{128,0},{192,64},{1,129},{65,193},{129,1},{193,65... | collective-permute-start | bytes 98312 | tf_op jit(solution)/shard_map/ppermute | solution.py:327
  7.6 2.3 %project_left.1 = f32[8,64,128]{2,1,0:T(8,128)} custom-call(f32[256,256]{1,0:T(8,128)} %bitcast.32, f32[1,256]{1,0:T(1,128)} %bitcast.43, f32[1,256]{1,0:T(1,128)} %bitcast.56, f32[32,256]{1,0:T(8,128)} %bitcast.40, f32[1,32]{1,0:T(1,128)} %bitcast.58), custom_call_target="tpu_custom_call" | custom-call | flops 25165824 | bytes 559232 | tf_op jit(solution)/shard_map/project_left/pallas_call | solution.py:307
  9.9 1.3 %collective-permute-done = f32[64,128]{1,0:T(8,128)S(1)} collective-permute-done((f32[64,128]{1,0:T(8,128)}, f32[64,128]{1,0:T(8,128)S(1)}, u32[]{:S(2)}, u32[]{:S(2)}) %collective-permute-start) | collective-permute-done | bytes 32800 | tf_op jit(solution)/shard_map/ppermute | solution.py:327
  11.2 9.4 %all-to-all-start = ((f32[8,64,128]{2,1,0:T(8,128)}), f32[8,64,128]{2,1,0:T(8,128)}, u32[]{:S(2)}, u32[]{:S(2)}) async-start(f32[8,64,128]{2,1,0:T(8,128)} %project_left.1), calls=%async_computation | async-start | bytes 524288 | tf_op jit(solution)/shard_map/all_to_all | solution.py:331
  20.5 0.8 pad_maximum_fusion.1.refs_0_
  21.3 2.8 %collective-permute-start.5 = (f32[4,64,128]{2,1,0:T(8,128)S(1)}, f32[4,64,128]{2,1,0:T(8,128)S(1)}, u32[]{:S(2)}, u32[]{:S(2)}) collective-permute-start(f32[4,64,128]{2,1,0:T(8,128)S(1)} %pad_maximum_fusion.1.refs_0_), channel_id=1, source_target_pairs={{0,48},{16,32},{32,16},{48,0},{1,49},{17,33},{33,17},{49,1},{2,50}... | collective-permute-start | bytes 393224 | tf_op jit(solution)/shard_map/ppermute | solution.py:327
  24.2 0.8 collective-permute-start.4
  25.5 5.8 %cotangent.1 = (bf16[4,512,512]{2,1,0:T(8,128)(2,1)}, bf16[4,512,512]{2,1,0:T(8,128)(2,1)}) custom-call(f32[1024,128]{1,0:T(8,128)} %refs_9_.1, f32[16,64,128]{2,1,0:T(8,128)} %refs_8_.1), custom_call_target="tpu_custom_call" | custom-call | flops 805306368 | bytes 5242880 | tf_op jit(solution)/shard_map/cotangent/pallas_call | solution.py:307
  31.3 2.0 %all-to-all-done = f32[8,64,128]{2,1,0:T(8,128)} async-done(((f32[8,64,128]{2,1,0:T(8,128)}), f32[8,64,128]{2,1,0:T(8,128)}, u32[]{:S(2)}, u32[]{:S(2)}) %all-to-all-start) | async-done | bytes 262176 | tf_op jit(solution)/shard_map/all_to_all | solution.py:331
  33.3 6.4 %all-to-all-start.1 = ((f32[32,16,128]{2,1,0:T(8,128)}), f32[32,16,128]{2,1,0:T(8,128)S(1)}, u32[]{:S(2)}, u32[]{:S(2)}) async-start(f32[32,16,128]{2,1,0:T(8,128)} %bitcast.7), calls=%async_computation.1 | async-start | bytes 524288 | tf_op jit(solution)/shard_map/all_to_all | solution.py:331
  41.8 3.3 %left_gradient.1 = (f32[256,128]{1,0:T(8,128)S(1)}, f32[256,128]{1,0:T(8,128)S(1)}) custom-call(f32[4,64,128]{2,1,0:T(8,128)S(1)} %pad_maximum_fusion.1.refs_0_, f32[4,64,128]{2,1,0:T(8,128)S(1)} %collective-permute-done.3.refs_1_, f32[4,64,128]{2,1,0:T(8,128)S(1)} %collective-permute-done.4.refs_2_, f32[4,64,128]{2,1,0:T(8,128)S(1)} %collective-permute-done.5.refs_3_, ...), custom_call_target="tpu_custom_call" | custom-call | flops 805306368 | bytes 5505024 | tf_op jit(solution)/shard_map/left_gradient/pallas_call | solution.py:307
  45.8 1.0 collective-permute-done.10
  46.8 2.9 %all-to-all-done.1 = f32[32,16,128]{2,1,0:T(8,128)S(1)} async-done(((f32[32,16,128]{2,1,0:T(8,128)}), f32[32,16,128]{2,1,0:T(8,128)S(1)}, u32[]{:S(2)}, u32[]{:S(2)}) %all-to-all-start.1) | async-done | bytes 262176 | tf_op jit(solution)/shard_map/all_to_all | solution.py:331
  49.7 4.9 %tile.1 = (f32[512,128]{1,0:T(8,128)S(1)}, f32[512,128]{1,0:T(8,128)S(1)}) custom-call(f32[512,128]{1,0:T(8,128)S(1)} %bitcast.34, f32[4,64,128]{2,1,0:T(8,128)S(1)} %pad_maximum_fusion.1.refs_0_, f32[4,64,128]{2,1,0:T(8,128)S(1)} %collective-permute-done.3.refs_1_, f32[4,64,128]{2,1,0:T(8,128)S(1)} %collective-permute-done.4.refs_2_, ...), custom_call_target="tpu_custom_call" | custom-call | flops 1610612736 | bytes 2359296 | tf_op jit(solution)/shard_map/tile/pallas_call | solution.py:307
  55.0 1.3 %collective-permute-done.11 = f32[512,128]{1,0:T(8,128)S(1)} collective-permute-done((f32[512,128]{1,0:T(8,128)S(1)}, f32[512,128]{1,0:T(8,128)S(1)}, u32[]{:S(2)}, u32[]{:S(2)}) %collective-permute-start.11) | collective-permute-done | bytes 262176 | tf_op jit(solution)/shard_map/ppermute | solution.py:323
  56.3 0.8 pad_maximum_fusion
  57.1 4.7 %all-to-all-start.2 = ((f32[16,64,128]{2,1,0:T(8,128)}), f32[16,64,128]{2,1,0:T(8,128)S(1)}, u32[]{:S(2)}, u32[]{:S(2)}) async-start(f32[16,64,128]{2,1,0:T(8,128)} %pad_maximum_fusion), calls=%async_computation.2 | async-start | bytes 1048576 | tf_op jit(solution)/shard_map/all_to_all | solution.py:331
  61.9 4.2 %right_gradient.1 = (f32[4,64,128]{2,1,0:T(8,128)S(1)}, f32[4,64,128]{2,1,0:T(8,128)S(1)}, f32[4,64,128]{2,1,0:T(8,128)S(1)}, f32[4,64,128]{2,1,0:T(8,128)S(1)},...) custom-call(f32[512,128]{1,0:T(8,128)S(1)} %bitcast.35, ...), custom_call_target="tpu_custom_call" | custom-call | flops 805306368 | bytes 5505024 | tf_op jit(solution)/shard_map/right_gradient/pallas_call | solution.py:307
  67.5 1.5 %collective-permute-start.14 = (f32[4,64,128]{2,1,0:T(8,128)S(1)}, f32[4,64,128]{2,1,0:T(8,128)S(1)}, u32[]{:S(2)}, u32[]{:S(2)}) collective-permute-start(f32[4,64,128]{2,1,0:T(8,128)S(1)} %add.28), channel_id=1, source_target_pairs={{0,16},{16,0},{32,48},{48,32},{1,17},{17,1},{33,49},{49,33},{2,18}... | collective-permute-start | bytes 393224 | tf_op jit(solution)/shard_map/ppermute | solution.py:327
  69.1 2.8 %collective-permute-start.16 = (f32[4,64,128]{2,1,0:T(8,128)S(1)}, f32[4,64,128]{2,1,0:T(8,128)S(1)}, u32[]{:S(2)}, u32[]{:S(2)}) collective-permute-start(f32[4,64,128]{2,1,0:T(8,128)S(1)} %add.29), channel_id=1, source_target_pairs={{0,32},{16,48},{32,0},{48,16},{1,33},{17,49},{33,1},{49,17},{2,34}... | collective-permute-start | bytes 393224 | tf_op jit(solution)/shard_map/ppermute | solution.py:327
  71.9 0.9 collective-permute-start.18
  72.8 5.6 %pair.1 = f32[16,64,128]{2,1,0:T(8,128)} custom-call(f32[512,128]{1,0:T(8,128)S(1)} %bitcast.36, f32[4,64,128]{2,1,0:T(8,128)S(1)} %pad_maximum_fusion.1.refs_0_, f32[4,64,128]{2,1,0:T(8,128)S(1)} %collective-permute-done.3.refs_1_, f32[4,64,128]{2,1,0:T(8,128)S(1)} %collective-permute-done.4.refs_2_, f32[4,64,128]{2,1,0:T(8,128)S(1)} %collective-permute-done.5.refs_3_, ...), custom_call_target="tpu_custom_call" | custom-call | flops 1610612736 | bytes 2359808 | tf_op jit(solution)/shard_map/pair/pallas_call | solution.py:307
  78.5 2.0 %collective-permute-done.16 = f32[4,64,128]{2,1,0:T(8,128)S(1)} collective-permute-done((f32[4,64,128]{2,1,0:T(8,128)S(1)}, f32[4,64,128]{2,1,0:T(8,128)S(1)}, u32[]{:S(2)}, u32[]{:S(2)}) %collective-permute-start.16) | collective-permute-done | bytes 131104 | tf_op jit(solution)/shard_map/ppermute | solution.py:327
  80.5 1.3 %collective-permute-done.18 = f32[4,64,128]{2,1,0:T(8,128)S(1)} collective-permute-done((f32[4,64,128]{2,1,0:T(8,128)S(1)}, f32[4,64,128]{2,1,0:T(8,128)S(1)}, u32[]{:S(2)}, u32[]{:S(2)}) %collective-permute-start.18) | collective-permute-done | bytes 131104 | tf_op jit(solution)/shard_map/ppermute | solution.py:327
  82.6 7.7 %all-to-all-start.3 = ((f32[8,72,128]{2,1,0:T(8,128)}), f32[8,72,128]{2,1,0:T(8,128)S(1)}, u32[]{:S(2)}, u32[]{:S(2)}) async-start(f32[8,72,128]{2,1,0:T(8,128)} %select_maximum_fusion), calls=%async_computation.3 | async-start | bytes 589824 | tf_op jit(solution)/shard_map/all_to_all | solution.py:331
  90.3 1.7 %collective-permute-start.21 = (f32[64,128]{1,0:T(8,128)S(1)}, f32[64,128]{1,0:T(8,128)S(1)}, u32[]{:S(2)}, u32[]{:S(2)}) collective-permute-start(f32[64,128]{1,0:T(8,128)S(1)} %get-tuple-element.73), channel_id=1, source_target_pairs={{0,192},{64,128},{128,64},{192,0},{1,193},{65,129},{129,65},{193,1... | collective-permute-start | bytes 98312 | tf_op jit(solution)/shard_map/ppermute | solution.py:327
  92.0 1.7 %collective-permute-start.20 = (f32[64,128]{1,0:T(8,128)S(1)}, f32[64,128]{1,0:T(8,128)S(1)}, u32[]{:S(2)}, u32[]{:S(2)}) collective-permute-start(f32[64,128]{1,0:T(8,128)S(1)} %get-tuple-element.74), channel_id=1, source_target_pairs={{0,128},{64,192},{128,0},{192,64},{1,129},{65,193},{129,1},{193,65... | collective-permute-start | bytes 98312 | tf_op jit(solution)/shard_map/ppermute | solution.py:327
  93.9 4.9 %collective-permute-done.21.d_ref = f32[64,128]{1,0:T(8,128)S(1)} collective-permute-done((f32[64,128]{1,0:T(8,128)S(1)}, f32[64,128]{1,0:T(8,128)S(1)}, u32[]{:S(2)}, u32[]{:S(2)}) %collective-permute-start.21) | collective-permute-done | bytes 32800 | tf_op jit(solution)/shard_map/ppermute | solution.py:327
  99.3 4.8 %all-to-all-done.3.col_ref = f32[8,72,128]{2,1,0:T(8,128)S(1)} async-done(((f32[8,72,128]{2,1,0:T(8,128)}), f32[8,72,128]{2,1,0:T(8,128)S(1)}, u32[]{:S(2)}, u32[]{:S(2)}) %all-to-all-start.3) | async-done | bytes 294944 | tf_op jit(solution)/shard_map/all_to_all | solution.py:331
  104.1 1.3 %finish.1 = (f32[256,256]{1,0:T(8,128)}, f32[4,128]{1,0:T(4,128)}) custom-call(f32[256,256]{1,0:T(8,128)S(1)} %bitcast.33, f32[1,256]{1,0:T(1,128)S(1)} %bitcast.44, f32[32,256]{1,0:T(8,128)S(1)} %bitcast.41, f32[256,256]{1,0:T(8,128)S(1)} %right.1.part_ref, f32[8,72,128]{2,1,0:T(8,128)S(1)} %all-to-all-done.3.col_ref), custom_call_target="tpu_custom_call" | custom-call | flops 25165824 | bytes 1117184 | tf_op jit(solution)/shard_map/finish/pallas_call | solution.py:307
  (52 shorter events, 7.3 us)
Async XLA Ops:
  2.9 7.0 %collective-permute-start.2 = (f32[64,128]{1,0:T(8,128)}, f32[64,128]{1,0:T(8,128)S(1)}, u32[]{:S(2)}, u32[]{:S(2)}) collective-permute-start(f32[64,128]{1,0:T(8,128)} %project_right.1), channel_id=1, source_target_pairs={{0,192},{64,128},{128,64},{192,0},{1,193},{65,129},{129,65},{193,1... | collective-permute-start | bytes 98312 | tf_op jit(solution)/shard_map/ppermute | solution.py:327
  4.8 5.1 %collective-permute-start.1 = (f32[64,128]{1,0:T(8,128)}, f32[64,128]{1,0:T(8,128)S(1)}, u32[]{:S(2)}, u32[]{:S(2)}) collective-permute-start(f32[64,128]{1,0:T(8,128)} %project_right.1), channel_id=1, source_target_pairs={{0,128},{64,192},{128,0},{192,64},{1,129},{65,193},{129,1},{193,65... | collective-permute-start | bytes 98312 | tf_op jit(solution)/shard_map/ppermute | solution.py:327
  7.1 4.1 %collective-permute-start = (f32[64,128]{1,0:T(8,128)}, f32[64,128]{1,0:T(8,128)S(1)}, u32[]{:S(2)}, u32[]{:S(2)}) collective-permute-start(f32[64,128]{1,0:T(8,128)} %project_right.1), channel_id=1, source_target_pairs={{0,64},{64,0},{128,192},{192,128},{1,65},{65,1},{129,193},{193,129... | collective-permute-start | bytes 98312 | tf_op jit(solution)/shard_map/ppermute | solution.py:327
  11.2 22.1 %all-to-all-start = ((f32[8,64,128]{2,1,0:T(8,128)}), f32[8,64,128]{2,1,0:T(8,128)}, u32[]{:S(2)}, u32[]{:S(2)}) async-start(f32[8,64,128]{2,1,0:T(8,128)} %project_left.1), calls=%async_computation | async-start | bytes 524288 | tf_op jit(solution)/shard_map/all_to_all | solution.py:331
  21.3 10.0 %collective-permute-start.5 = (f32[4,64,128]{2,1,0:T(8,128)S(1)}, f32[4,64,128]{2,1,0:T(8,128)S(1)}, u32[]{:S(2)}, u32[]{:S(2)}) collective-permute-start(f32[4,64,128]{2,1,0:T(8,128)S(1)} %pad_maximum_fusion.1.refs_0_), channel_id=1, source_target_pairs={{0,48},{16,32},{32,16},{48,0},{1,49},{17,33},{33,17},{49,1},{2,50}... | collective-permute-start | bytes 393224 | tf_op jit(solution)/shard_map/ppermute | solution.py:327
  24.2 7.1 %collective-permute-start.4 = (f32[4,64,128]{2,1,0:T(8,128)S(1)}, f32[4,64,128]{2,1,0:T(8,128)S(1)}, u32[]{:S(2)}, u32[]{:S(2)}) collective-permute-start(f32[4,64,128]{2,1,0:T(8,128)S(1)} %pad_maximum_fusion.1.refs_0_), channel_id=1, source_target_pairs={{0,32},{16,48},{32,0},{48,16},{1,33},{17,49},{33,1},{49,17},{2,34}... | collective-permute-start | bytes 393224 | tf_op jit(solution)/shard_map/ppermute | solution.py:327
  25.0 6.3 %collective-permute-start.3 = (f32[4,64,128]{2,1,0:T(8,128)S(1)}, f32[4,64,128]{2,1,0:T(8,128)S(1)}, u32[]{:S(2)}, u32[]{:S(2)}) collective-permute-start(f32[4,64,128]{2,1,0:T(8,128)S(1)} %pad_maximum_fusion.1.refs_0_), channel_id=1, source_target_pairs={{0,16},{16,0},{32,48},{48,32},{1,17},{17,1},{33,49},{49,33},{2,18}... | collective-permute-start | bytes 393224 | tf_op jit(solution)/shard_map/ppermute | solution.py:327
  33.3 16.4 %all-to-all-start.1 = ((f32[32,16,128]{2,1,0:T(8,128)}), f32[32,16,128]{2,1,0:T(8,128)S(1)}, u32[]{:S(2)}, u32[]{:S(2)}) async-start(f32[32,16,128]{2,1,0:T(8,128)} %bitcast.7), calls=%async_computation.1 | async-start | bytes 524288 | tf_op jit(solution)/shard_map/all_to_all | solution.py:331
  39.7 1.4 %collective-permute-start.6 = (f32[4,64,128]{2,1,0:T(8,128)S(1)}, f32[4,64,128]{2,1,0:T(8,128)S(1)}, u32[]{:S(2)}, u32[]{:S(2)}) collective-permute-start(f32[4,64,128]{2,1,0:T(8,128)S(1)} %pad_maximum_fusion.1.refs_0_), channel_id=1, source_target_pairs={{0,8},{8,0},{1,9},{9,1},{2,10},{10,2},{3,11},{11,3},{4,12},{12,4},... | collective-permute-start | bytes 393224 | tf_op jit(solution)/shard_map/ppermute | solution.py:323
  39.9 1.4 %collective-permute-start.7 = (f32[4,64,128]{2,1,0:T(8,128)S(1)}, f32[4,64,128]{2,1,0:T(8,128)S(1)}, u32[]{:S(2)}, u32[]{:S(2)}) collective-permute-start(f32[4,64,128]{2,1,0:T(8,128)S(1)} %collective-permute-done.3.refs_1_), channel_id=1, source_target_pairs={{0,8},{8,0},{1,9},{9,1},{2,10},{10,2},{3,11},{11,3},{4,12},{12,4},... | collective-permute-start | bytes 393224 | tf_op jit(solution)/shard_map/ppermute | solution.py:323
  40.3 1.3 %collective-permute-start.8 = (f32[4,64,128]{2,1,0:T(8,128)S(1)}, f32[4,64,128]{2,1,0:T(8,128)S(1)}, u32[]{:S(2)}, u32[]{:S(2)}) collective-permute-start(f32[4,64,128]{2,1,0:T(8,128)S(1)} %collective-permute-done.4.refs_2_), channel_id=1, source_target_pairs={{0,8},{8,0},{1,9},{9,1},{2,10},{10,2},{3,11},{11,3},{4,12},{12,4},... | collective-permute-start | bytes 393224 | tf_op jit(solution)/shard_map/ppermute | solution.py:323
  40.4 1.4 %collective-permute-start.9 = (f32[4,64,128]{2,1,0:T(8,128)S(1)}, f32[4,64,128]{2,1,0:T(8,128)S(1)}, u32[]{:S(2)}, u32[]{:S(2)}) collective-permute-start(f32[4,64,128]{2,1,0:T(8,128)S(1)} %collective-permute-done.5.refs_3_), channel_id=1, source_target_pairs={{0,8},{8,0},{1,9},{9,1},{2,10},{10,2},{3,11},{11,3},{4,12},{12,4},... | collective-permute-start | bytes 393224 | tf_op jit(solution)/shard_map/ppermute | solution.py:323
  45.2 1.6 %collective-permute-start.10 = (f32[256,128]{1,0:T(8,128)S(1)}, f32[256,128]{1,0:T(8,128)S(1)}, u32[]{:S(2)}, u32[]{:S(2)}) collective-permute-start(f32[256,128]{1,0:T(8,128)S(1)} %get-tuple-element.52), channel_id=1, source_target_pairs={{0,8},{8,0},{1,9},{9,1},{2,10},{10,2},{3,11},{11,3},{4,12},{12,4},... | collective-permute-start | bytes 393224 | tf_op jit(solution)/shard_map/ppermute | solution.py:323
  54.6 1.6 %collective-permute-start.11 = (f32[512,128]{1,0:T(8,128)S(1)}, f32[512,128]{1,0:T(8,128)S(1)}, u32[]{:S(2)}, u32[]{:S(2)}) collective-permute-start(f32[512,128]{1,0:T(8,128)S(1)} %get-tuple-element.55), channel_id=1, source_target_pairs={{0,8},{8,0},{1,9},{9,1},{2,10},{10,2},{3,11},{11,3},{4,12},{12,4},... | collective-permute-start | bytes 786440 | tf_op jit(solution)/shard_map/ppermute | solution.py:323
  57.1 24.7 %all-to-all-start.2 = ((f32[16,64,128]{2,1,0:T(8,128)}), f32[16,64,128]{2,1,0:T(8,128)S(1)}, u32[]{:S(2)}, u32[]{:S(2)}) async-start(f32[16,64,128]{2,1,0:T(8,128)} %pad_maximum_fusion), calls=%async_computation.2 | async-start | bytes 1048576 | tf_op jit(solution)/shard_map/all_to_all | solution.py:331
  61.9 10.9 %copy-start.4 = (f32[1024,128]{1,0:T(8,128)S(1)}, f32[1024,128]{1,0:T(8,128)}, u32[]{:S(2)}) copy-start(f32[1024,128]{1,0:T(8,128)} %refs_9_.1) | copy-start | bytes 1572868
  61.9 10.9 %copy-start.5 = (f32[128]{0:T(128)S(1)}, f32[128]{0:T(128)}, u32[]{:S(2)}) copy-start(f32[128]{0:T(128)} %param.18) | copy-start | bytes 1540
  66.1 1.4 %collective-permute-start.13 = (f32[4,64,128]{2,1,0:T(8,128)S(1)}, f32[4,64,128]{2,1,0:T(8,128)S(1)}, u32[]{:S(2)}, u32[]{:S(2)}) collective-permute-start(f32[4,64,128]{2,1,0:T(8,128)S(1)} %get-tuple-element.61), channel_id=1, source_target_pairs={{0,8},{8,0},{1,9},{9,1},{2,10},{10,2},{3,11},{11,3},{4,12},{12,4},... | collective-permute-start | bytes 393224 | tf_op jit(solution)/shard_map/ppermute | solution.py:323
  66.2 2.9 %collective-permute-start.15 = (f32[4,64,128]{2,1,0:T(8,128)S(1)}, f32[4,64,128]{2,1,0:T(8,128)S(1)}, u32[]{:S(2)}, u32[]{:S(2)}) collective-permute-start(f32[4,64,128]{2,1,0:T(8,128)S(1)} %get-tuple-element.63), channel_id=1, source_target_pairs={{0,8},{8,0},{1,9},{9,1},{2,10},{10,2},{3,11},{11,3},{4,12},{12,4},... | collective-permute-start | bytes 393224 | tf_op jit(solution)/shard_map/ppermute | solution.py:323
  66.7 5.2 %collective-permute-start.17 = (f32[4,64,128]{2,1,0:T(8,128)S(1)}, f32[4,64,128]{2,1,0:T(8,128)S(1)}, u32[]{:S(2)}, u32[]{:S(2)}) collective-permute-start(f32[4,64,128]{2,1,0:T(8,128)S(1)} %get-tuple-element.65), channel_id=1, source_target_pairs={{0,8},{8,0},{1,9},{9,1},{2,10},{10,2},{3,11},{11,3},{4,12},{12,4},... | collective-permute-start | bytes 393224 | tf_op jit(solution)/shard_map/ppermute | solution.py:323
  66.8 11.7 %collective-permute-start.12 = (f32[4,64,128]{2,1,0:T(8,128)S(1)}, f32[4,64,128]{2,1,0:T(8,128)S(1)}, u32[]{:S(2)}, u32[]{:S(2)}) collective-permute-start(f32[4,64,128]{2,1,0:T(8,128)S(1)} %get-tuple-element.59), channel_id=1, source_target_pairs={{0,8},{8,0},{1,9},{9,1},{2,10},{10,2},{3,11},{11,3},{4,12},{12,4},... | collective-permute-start | bytes 393224 | tf_op jit(solution)/shard_map/ppermute | solution.py:323
  67.5 10.9 %collective-permute-start.14 = (f32[4,64,128]{2,1,0:T(8,128)S(1)}, f32[4,64,128]{2,1,0:T(8,128)S(1)}, u32[]{:S(2)}, u32[]{:S(2)}) collective-permute-start(f32[4,64,128]{2,1,0:T(8,128)S(1)} %add.28), channel_id=1, source_target_pairs={{0,16},{16,0},{32,48},{48,32},{1,17},{17,1},{33,49},{49,33},{2,18}... | collective-permute-start | bytes 393224 | tf_op jit(solution)/shard_map/ppermute | solution.py:327
  69.1 11.4 %collective-permute-start.16 = (f32[4,64,128]{2,1,0:T(8,128)S(1)}, f32[4,64,128]{2,1,0:T(8,128)S(1)}, u32[]{:S(2)}, u32[]{:S(2)}) collective-permute-start(f32[4,64,128]{2,1,0:T(8,128)S(1)} %add.29), channel_id=1, source_target_pairs={{0,32},{16,48},{32,0},{48,16},{1,33},{17,49},{33,1},{49,17},{2,34}... | collective-permute-start | bytes 393224 | tf_op jit(solution)/shard_map/ppermute | solution.py:327
  71.9 9.9 %collective-permute-start.18 = (f32[4,64,128]{2,1,0:T(8,128)S(1)}, f32[4,64,128]{2,1,0:T(8,128)S(1)}, u32[]{:S(2)}, u32[]{:S(2)}) collective-permute-start(f32[4,64,128]{2,1,0:T(8,128)S(1)} %add.31), channel_id=1, source_target_pairs={{0,48},{16,32},{32,16},{48,0},{1,49},{17,33},{33,17},{49,1},{2,50}... | collective-permute-start | bytes 393224 | tf_op jit(solution)/shard_map/ppermute | solution.py:327
  78.4 20.4 %copy-start.1 = (f32[256,32]{0,1:T(8,128)S(1)}, f32[256,32]{0,1:T(8,128)}, u32[]{:S(2)}) copy-start(f32[256,32]{0,1:T(8,128)} %param.15) | copy-start | bytes 98308
  78.4 25.7 %copy-start = (f32[4,64,256]{2,1,0:T(8,128)S(1)}, f32[4,64,256]{2,1,0:T(8,128)}, u32[]{:S(2)}) copy-start(f32[4,64,256]{2,1,0:T(8,128)} %param.10) | copy-start | bytes 786436
  78.4 25.7 %copy-start.2 = (f32[256,32]{0,1:T(8,128)S(1)}, f32[256,32]{0,1:T(8,128)}, u32[]{:S(2)}) copy-start(f32[256,32]{0,1:T(8,128)} %param.13) | copy-start | bytes 98308
  78.4 25.7 %copy-start.3 = (f32[256]{0:T(256)S(1)}, f32[256]{0:T(256)}, u32[]{:S(2)}) copy-start(f32[256]{0:T(256)} %param.11) | copy-start | bytes 3076
  82.6 21.5 %all-to-all-start.3 = ((f32[8,72,128]{2,1,0:T(8,128)}), f32[8,72,128]{2,1,0:T(8,128)S(1)}, u32[]{:S(2)}, u32[]{:S(2)}) async-start(f32[8,72,128]{2,1,0:T(8,128)} %select_maximum_fusion), calls=%async_computation.3 | async-start | bytes 589824 | tf_op jit(solution)/shard_map/all_to_all | solution.py:331
  90.3 8.5 %collective-permute-start.21 = (f32[64,128]{1,0:T(8,128)S(1)}, f32[64,128]{1,0:T(8,128)S(1)}, u32[]{:S(2)}, u32[]{:S(2)}) collective-permute-start(f32[64,128]{1,0:T(8,128)S(1)} %get-tuple-element.73), channel_id=1, source_target_pairs={{0,192},{64,128},{128,64},{192,0},{1,193},{65,129},{129,65},{193,1... | collective-permute-start | bytes 98312 | tf_op jit(solution)/shard_map/ppermute | solution.py:327
  92.0 6.8 %collective-permute-start.20 = (f32[64,128]{1,0:T(8,128)S(1)}, f32[64,128]{1,0:T(8,128)S(1)}, u32[]{:S(2)}, u32[]{:S(2)}) collective-permute-start(f32[64,128]{1,0:T(8,128)S(1)} %get-tuple-element.74), channel_id=1, source_target_pairs={{0,128},{64,192},{128,0},{192,64},{1,129},{65,193},{129,1},{193,65... | collective-permute-start | bytes 98312 | tf_op jit(solution)/shard_map/ppermute | solution.py:327
  93.6 5.1 %collective-permute-start.19 = (f32[64,128]{1,0:T(8,128)S(1)}, f32[64,128]{1,0:T(8,128)S(1)}, u32[]{:S(2)}, u32[]{:S(2)}) collective-permute-start(f32[64,128]{1,0:T(8,128)S(1)} %get-tuple-element.75), channel_id=1, source_target_pairs={{0,64},{64,0},{128,192},{192,128},{1,65},{65,1},{129,193},{193,129... | collective-permute-start | bytes 98312 | tf_op jit(solution)/shard_map/ppermute | solution.py:327

commit v7 on v6

--- a/solution.py
+++ b/solution.py
@@ -67,6 +67,13 @@
     return copies
 
 
+def fetch_classes(hi_far, lo_far, g_hi, g_lo, sems):
+    pairs = []
+    for m in range(4):
+        pairs += [(hi_far.at[m], g_hi.at[m]), (lo_far.at[m], g_lo.at[m])]
+    return fetch(pairs, sems)
+
+
 def pick(parts):
     chunk = lax.broadcasted_iota(jnp.int32, (64, 128), 1) // 32
     low = jnp.where(chunk == 0, parts[0], parts[1])
@@ -120,7 +127,9 @@
             w_hl[d, at : at + 32, 128:256] = lo
 
 
-def cotangent_kernel(w_far, cot_far, g_hi, g_lo, wide_t, w_hl, w_cat, cot_cat, w_ref, cot_ref, sems):
+def cotangent_kernel(
+    w_far, cot_far, hi_far, lo_far, wide_t, w_hl, w_cat, cot_cat, w_ref, cot_ref, g_hi, g_lo, sems
+):
     copies = fetch([(w_far, w_ref), (cot_far, cot_ref)], sems)
     copies[0].wait()
     weights_by_class(w_ref, w_hl)
@@ -137,22 +146,29 @@
         wide_t[d] = lax.dot_general(
             cot_cat[d], w_cat[...], (((1,), (1,)), ((), ())), preferred_element_type=f32
         )
-    for block in range(8):
-        h, g = block // 4, block % 4
-        at = g * 128 + h * 64
-        for quad in range(4):
-            parts = [
-                wide_t[d, quad * 64 : quad * 64 + 64, block * 128 : block * 128 + 128]
-                for d in range(4)
-            ]
-            for m in range(4):
-                hi, lo = halves(pick([parts[(p - m) % 4] for p in range(4)]))
-                g_hi[m, at : at + 64, quad * 128 : quad * 128 + 128] = hi
-                g_lo[m, at : at + 64, quad * 128 : quad * 128 + 128] = lo
-
-
-def outer_product(left_ref, parts, right_all, outer, lcat, rt, a_hi, a_lo):
-    gather_right(parts, right_all)
+    sent = []
+    for g in range(4):
+        for h in range(2):
+            block = h * 4 + g
+            at = g * 128 + h * 64
+            for quad in range(4):
+                parts = [
+                    wide_t[d, quad * 64 : quad * 64 + 64, block * 128 : block * 128 + 128]
+                    for d in range(4)
+                ]
+                for m in range(4):
+                    hi, lo = halves(pick([parts[(p - m) % 4] for p in range(4)]))
+                    g_hi[m, at : at + 64, quad * 128 : quad * 128 + 128] = hi
+                    g_lo[m, at : at + 64, quad * 128 : quad * 128 + 128] = lo
+        slab = (slice(None), pl.ds(g * 128, 128))
+        pairs = [(g_hi.at[slab], hi_far.at[slab]), (g_lo.at[slab], lo_far.at[slab])]
+        sent += fetch(pairs, sems.at[pl.ds(2 + 2 * g, 2)])
+    for copy in sent:
+        copy.wait()
+
+
+def outer_product(left_ref, rt_far, outer, lcat, a_hi, a_lo, rt, sems):
+    copies = fetch([(rt_far.at[m], rt.at[m]) for m in range(4)], sems)
     for quad in range(4):
         v = left_rows(left_ref, quad)
         for m in range(4):
@@ -160,13 +176,8 @@
             lcat[m, 0:128, quad * 128 : quad * 128 + 128] = hi
             lcat[m, 128:256, quad * 128 : quad * 128 + 128] = lo
             lcat[m, 256:384, quad * 128 : quad * 128 + 128] = hi
-    for e in range(16):
-        g, m = e // 4, e % 4
-        hi, lo = halves(right_rows(right_all, e).T)
-        rt[m, g * 128 : g * 128 + 128, 0:128] = hi
-        rt[m, g * 128 : g * 128 + 128, 128:256] = hi
-        rt[m, g * 128 : g * 128 + 128, 256:384] = lo
     for m in range(4):
+        copies[m].wait()
         outer[m] = matmul(rt[m], lcat[m])
     for block in range(8):
         h, g = block // 4, block % 4
@@ -179,11 +190,11 @@
                 a_lo[d, quad * 64 : quad * 64 + 64, block * 128 : block * 128 + 128] = lo
 
 
-def pair_kernel(left_ref, *refs):
-    parts, (bias_ref, w_far, pair_ref, right_all, outer, lcat, rt, a_hi, a_lo) = refs[:8], refs[8:17]
-    w_hl, w_ref, sems = refs[17:]
+def pair_kernel(
+    left_ref, bias_ref, rt_far, w_far, pair_ref, outer, lcat, a_hi, a_lo, rt, w_hl, w_ref, sems
+):
     (fetched,) = fetch([(w_far, w_ref)], sems)
-    outer_product(left_ref, parts, right_all, outer, lcat, rt, a_hi, a_lo)
+    outer_product(left_ref, rt_far, outer, lcat, a_hi, a_lo, rt, sems.at[pl.ds(1, 4)])
     fetched.wait()
     weights_by_class(w_ref, w_hl)
     for d in range(4):
@@ -194,12 +205,12 @@
             pair_ref[quad * 4 + d] = pair[quad * 64 : quad * 64 + 64]
 
 
-def tile_kernel(left_ref, *refs):
-    parts, (cot_far, own_out, other_out) = refs[:8], refs[8:11]
-    right_all, outer, lcat, rt, a_hi, a_lo, dw, cot_ref, sems = refs[11:]
+def tile_kernel(
+    left_ref, rt_far, cot_far, own_out, other_out, outer, lcat, a_hi, a_lo, rt, dw, cot_ref, sems
+):
     core = lax.axis_index("core")
     (fetched,) = fetch([(cot_far, cot_ref)], sems)
-    outer_product(left_ref, parts, right_all, outer, lcat, rt, a_hi, a_lo)
+    outer_product(left_ref, rt_far, outer, lcat, a_hi, a_lo, rt, sems.at[pl.ds(1, 4)])
     fetched.wait()
     for d in range(4):
         hi, lo = halves(jnp.concatenate([cot_ref[quad * 4 + d] for quad in range(4)], axis=0).T)
@@ -222,18 +233,24 @@
 
 
 def left_gradient_kernel(*refs):
-    parts, (hi_far, lo_far, own_out, other_out, right_all, r_hl, g_hi, g_lo, sems) = refs[:8], refs[8:]
-    copies = fetch([(hi_far, g_hi), (lo_far, g_lo)], sems)
+    parts, (hi_far, lo_far, own_out, other_out, rt) = refs[:8], refs[8:13]
+    right_all, r_hl, g_hi, g_lo, sems = refs[13:]
+    copies = fetch_classes(hi_far, lo_far, g_hi, g_lo, sems)
     gather_right(parts, right_all)
     for e in range(16):
         g, m = e // 4, e % 4
-        hi, lo = halves(right_rows(right_all, e))
+        v = right_rows(right_all, e)
+        hi, lo = halves(v)
         r_hl[m, 0:128, g * 128 : g * 128 + 128] = hi
         r_hl[m, 128:256, g * 128 : g * 128 + 128] = lo
-    for copy in copies:
-        copy.wait()
+        hi, lo = halves(v.T)
+        rt[m, g * 128 : g * 128 + 128, 0:128] = hi
+        rt[m, g * 128 : g * 128 + 128, 128:256] = hi
+        rt[m, g * 128 : g * 128 + 128, 256:384] = lo
     total = [None] * 4
     for m in range(4):
+        copies[2 * m].wait()
+        copies[2 * m + 1].wait()
         both = matmul(r_hl[m], g_hi[m])
         v = both[0:128] + both[128:256] + matmul(r_hl[m, 0:128, :], g_lo[m])
         for quad in range(4):
@@ -251,11 +268,11 @@
 
 def right_gradient_kernel(left_ref, hi_far, lo_far, *refs):
     outs, (lt, total, g_hi, g_lo, sems) = refs[:8], refs[8:]
-    copies = fetch([(hi_far, g_hi), (lo_far, g_lo)], sems)
+    copies = fetch_classes(hi_far, lo_far, g_hi, g_lo, sems)
     left_turned(left_ref, lt)
-    for copy in copies:
-        copy.wait()
     for m in range(4):
+        copies[2 * m].wait()
+        copies[2 * m + 1].wait()
         both = matmul(g_hi[m], lt[m])
         v = both[:, 0:128] + both[:, 128:256] + matmul(g_lo[m], lt[m, :, 0:128])
         for g in range(4):
@@ -301,14 +318,14 @@
     out_ref[...] = inverse * (grad - mean - unit * along)
 
 
-def call(kernel, name, outs, scratch, mib, flops, *args, far=(), copies=0):
+def call(kernel, name, outs, scratch, mib, flops, *args, far=(), far_outs=0, copies=0):
     shapes = tuple(jax.ShapeDtypeStruct(*out) for out in outs)
     moved = sum(a.size * a.dtype.itemsize for a in args + tuple(far) + shapes)
     return pl.pallas_call(
         kernel,
         out_shape=shapes,
         in_specs=[VMEM] * len(args) + [HBM] * len(far),
-        out_specs=(VMEM,) * len(outs),
+        out_specs=(VMEM,) * (len(outs) - far_outs) + (HBM,) * far_outs,
         scratch_shapes=[pltpu.VMEM(*s) for s in scratch]
         + ([pltpu.SemaphoreType.DMA((copies,))] if copies else []),
         compiler_params=pltpu.CompilerParams(
@@ -389,11 +406,13 @@
             ((4, 256, 384), bf16),
             ((1024, 128), f32),
             ((16, 64, 128), f32),
-        ],
+        ]
+        + [((4, 512, 512), bf16)] * 2,
         None,
         step,
         far=(result_matrix, edge_incoming_sensitivity),
-        copies=2,
+        far_outs=2,
+        copies=10,
     )
     left = exchange(left, COL).reshape(32, 16, 128)
     right = jnp.stack(right)
@@ -401,38 +420,36 @@
     left, parts, g_hi, g_lo = lax.optimization_barrier((left, parts, g_hi, g_lo))
     left = exchange(left, ROW).reshape(512, 128)
     parts = parts + [swap_cores(part) for part in parts]
-    own_left, other_left = call(
+    own_left, other_left, turned = call(
         left_gradient_kernel,
         "left_gradient",
-        [((256, 128), f32), ((256, 128), f32)],
+        [((256, 128), f32), ((256, 128), f32), ((4, 512, 384), bf16)],
         [((2048, 128), f32), ((4, 256, 512), bf16)] + [((4, 512, 512), bf16)] * 2,
         52,
         step,
         *parts,
         far=(g_hi, g_lo),
-        copies=2,
+        copies=8,
     )
     got_left = swap_cores(other_left)
     left, own_left, got_left = lax.optimization_barrier((left, own_left, got_left))
     working = [
-        ((2048, 128), f32),
         ((4, 512, 512), f32),
         ((4, 384, 512), bf16),
-        ((4, 512, 384), bf16),
         ((4, 256, 1024), bf16),
         ((4, 256, 1024), bf16),
+        ((4, 512, 384), bf16),
     ]
     own, other = call(
         tile_kernel,
         "tile",
         [((16 * BWD, 128), f32)] * 2,
         working + [((8, 128, 128), f32), ((16, 64, 128), f32)],
-        52,
+        53,
         2 * step,
         left,
-        *parts,
-        far=(edge_incoming_sensitivity,),
-        copies=1,
+        far=(turned, edge_incoming_sensitivity),
+        copies=5,
     )
     got = swap_cores(other)
     sums = call(
@@ -444,7 +461,7 @@
         step,
         left,
         far=(g_hi, g_lo),
-        copies=2,
+        copies=8,
     )
     weight = (own + got).reshape(16, BWD, 128)
     sent = [weight, own_left.reshape(16, 16, 128), got_left.reshape(16, 16, 128)]
@@ -459,10 +476,9 @@
         52,
         2 * step,
         left,
-        *parts,
         result_intercept.reshape(1, 128),
-        far=(result_matrix,),
-        copies=1,
+        far=(turned, result_matrix),
+        copies=5,
     )
     weight = back[:, :32].sum(axis=0).reshape(4, 8, 128).transpose(1, 0, 2)
     sent = jnp.concatenate(

time: 106 us -> 107 us (level)
  Pallas kernels: 30.1 us -> 31.7 us
  waiting for transfers between devices: 22.9 us -> 21.8 us
    pallas_call x9, Pallas kernels: 30.1 us -> 31.7 us  [call(): pl.pallas_call(kernel, out_shape=shapes, in_specs=[VMEM] * len(args) + [H...]
where the time goes in v7:
time: 107 us; the launch traced here: 106 us
  starting transfers between devices  49.2 us (46%)
  Pallas kernels  31.7 us (30%)
  waiting for transfers between devices  21.8 us (20%)
  other arithmetic  2.53 us (2%)
    pallas_call x9, Pallas kernels, call(): pl.pallas_call(kernel, out_shape=shapes, in_specs=[VMEM] * len(args) + [H...  31.7 us
    all_to_all x4, starting transfers between devices, exchange(): return lax.all_to_all(array, axes, 0, 0, tiled=True)  28.4 us
    ppermute x12, starting transfers between devices, from_peer(): return lax.ppermute(array, axis, [(i, i ^ apart) for i in range(4)])  17.7 us
    all_to_all x4, waiting for transfers between devices, exchange(): return lax.all_to_all(array, axes, 0, 0, tiled=True)  9.1 us
    ppermute x12, waiting for transfers between devices, from_peer(): return lax.ppermute(array, axis, [(i, i ^ apart) for i in range(4)])  9.02 us
    ppermute x10, waiting for transfers between devices, swap_cores(): return lax.ppermute(array, 'core', [(0, 1), (1, 0)])  3.64 us
    ppermute x10, starting transfers between devices, swap_cores(): return lax.ppermute(array, 'core', [(0, 1), (1, 0)])  3.16 us
  transfers between devices with their start and end apart: 26, of which 14 were waited for; matrix products, arithmetic and copies ran while one was open for 1% of the time, Pallas kernels for 21%

profile of v7, /device:TPU:32, one launch (start us, length us, event | category | flops | bytes accessed | tf_op | source)
XLA Modules:
  0.0 106.1 jit_solution(17307370733432760813)
XLA Ops:
  0.6 2.2 %project_right.1 = f32[64,128]{1,0:T(8,128)} custom-call(f32[256,256]{1,0:T(8,128)} %bitcast.31, f32[1,256]{1,0:T(1,128)} %bitcast.42, f32[1,256]{1,0:T(1,128)} %bitcast.55, f32[32,256]{1,0:T(8,128)} %bitcast.37, f32[1,32]{1,0:T(1,128)} %bitcast.57), custom_call_target="tpu_custom_call" | custom-call | flops 25165824 | bytes 329856 | tf_op jit(solution)/shard_map/project_right/pallas_call | solution.py:324
  2.9 1.9 %collective-permute-start.2 = (f32[64,128]{1,0:T(8,128)}, f32[64,128]{1,0:T(8,128)S(1)}, u32[]{:S(2)}, u32[]{:S(2)}) collective-permute-start(f32[64,128]{1,0:T(8,128)} %project_right.1), channel_id=1, source_target_pairs={{0,192},{64,128},{128,64},{192,0},{1,193},{65,129},{129,65},{193,1... | collective-permute-start | bytes 98312 | tf_op jit(solution)/shard_map/ppermute | solution.py:344
  4.8 2.3 %collective-permute-start.1 = (f32[64,128]{1,0:T(8,128)}, f32[64,128]{1,0:T(8,128)S(1)}, u32[]{:S(2)}, u32[]{:S(2)}) collective-permute-start(f32[64,128]{1,0:T(8,128)} %project_right.1), channel_id=1, source_target_pairs={{0,128},{64,192},{128,0},{192,64},{1,129},{65,193},{129,1},{193,65... | collective-permute-start | bytes 98312 | tf_op jit(solution)/shard_map/ppermute | solution.py:344
  7.6 2.3 %project_left.1 = f32[8,64,128]{2,1,0:T(8,128)} custom-call(f32[256,256]{1,0:T(8,128)} %bitcast.32, f32[1,256]{1,0:T(1,128)} %bitcast.43, f32[1,256]{1,0:T(1,128)} %bitcast.56, f32[32,256]{1,0:T(8,128)} %bitcast.40, f32[1,32]{1,0:T(1,128)} %bitcast.58), custom_call_target="tpu_custom_call" | custom-call | flops 25165824 | bytes 559232 | tf_op jit(solution)/shard_map/project_left/pallas_call | solution.py:324
  9.9 1.3 %collective-permute-done = f32[64,128]{1,0:T(8,128)S(1)} collective-permute-done((f32[64,128]{1,0:T(8,128)}, f32[64,128]{1,0:T(8,128)S(1)}, u32[]{:S(2)}, u32[]{:S(2)}) %collective-permute-start) | collective-permute-done | bytes 32800 | tf_op jit(solution)/shard_map/ppermute | solution.py:344
  11.2 9.4 %all-to-all-start = ((f32[8,64,128]{2,1,0:T(8,128)}), f32[8,64,128]{2,1,0:T(8,128)}, u32[]{:S(2)}, u32[]{:S(2)}) async-start(f32[8,64,128]{2,1,0:T(8,128)} %project_left.1), calls=%async_computation | async-start | bytes 524288 | tf_op jit(solution)/shard_map/all_to_all | solution.py:348
  20.5 0.8 pad_maximum_fusion.1.refs_0_
  21.3 2.8 %collective-permute-start.5 = (f32[4,64,128]{2,1,0:T(8,128)S(1)}, f32[4,64,128]{2,1,0:T(8,128)S(1)}, u32[]{:S(2)}, u32[]{:S(2)}) collective-permute-start(f32[4,64,128]{2,1,0:T(8,128)S(1)} %pad_maximum_fusion.1.refs_0_), channel_id=1, source_target_pairs={{0,48},{16,32},{32,16},{48,0},{1,49},{17,33},{33,17},{49,1},{2,50}... | collective-permute-start | bytes 393224 | tf_op jit(solution)/shard_map/ppermute | solution.py:344
  24.2 0.8 collective-permute-start.4
  25.5 5.6 %cotangent.1 = (bf16[4,512,512]{2,1,0:T(8,128)(2,1)}, bf16[4,512,512]{2,1,0:T(8,128)(2,1)}) custom-call(f32[1024,128]{1,0:T(8,128)} %w_far.3, f32[16,64,128]{2,1,0:T(8,128)} %cot_far.3), custom_call_target="tpu_custom_call" | custom-call | flops 805306368 | bytes 5242880 | tf_op jit(solution)/shard_map/cotangent/pallas_call | solution.py:324
  31.1 2.2 %all-to-all-done = f32[8,64,128]{2,1,0:T(8,128)} async-done(((f32[8,64,128]{2,1,0:T(8,128)}), f32[8,64,128]{2,1,0:T(8,128)}, u32[]{:S(2)}, u32[]{:S(2)}) %all-to-all-start) | async-done | bytes 262176 | tf_op jit(solution)/shard_map/all_to_all | solution.py:348
  33.3 6.4 %all-to-all-start.1 = ((f32[32,16,128]{2,1,0:T(8,128)}), f32[32,16,128]{2,1,0:T(8,128)S(1)}, u32[]{:S(2)}, u32[]{:S(2)}) async-start(f32[32,16,128]{2,1,0:T(8,128)} %bitcast.7), calls=%async_computation.1 | async-start | bytes 524288 | tf_op jit(solution)/shard_map/all_to_all | solution.py:348
  41.8 3.8 %left_gradient.1 = (f32[256,128]{1,0:T(8,128)S(1)}, f32[256,128]{1,0:T(8,128)S(1)}, bf16[4,512,384]{2,1,0:T(8,128)(2,1)}) custom-call(f32[4,64,128]{2,1,0:T(8,128)S(1)} %pad_maximum_fusion.1.refs_0_, f32[4,64,128]{2,1,0:T(8,128)S(1)} %collective-permute-done.3.refs_1_, f32[4,64,128]{2,1,0:T(8,128)S(1)} %collective-permute-done.4.refs_2_, ...), custom_call_target="tpu_custom_call" | custom-call | flops 805306368 | bytes 7077888 | tf_op jit(solution)/shard_map/left_gradient/pallas_call | solution.py:324
  46.3 1.0 collective-permute-done.10
  47.3 2.4 %all-to-all-done.1 = f32[32,16,128]{2,1,0:T(8,128)S(1)} async-done(((f32[32,16,128]{2,1,0:T(8,128)}), f32[32,16,128]{2,1,0:T(8,128)S(1)}, u32[]{:S(2)}, u32[]{:S(2)}) %all-to-all-start.1) | async-done | bytes 262176 | tf_op jit(solution)/shard_map/all_to_all | solution.py:348
  49.7 5.7 %tile.1 = (f32[512,128]{1,0:T(8,128)S(1)}, f32[512,128]{1,0:T(8,128)S(1)}) custom-call(f32[512,128]{1,0:T(8,128)S(1)} %bitcast.34, bf16[4,512,384]{2,1,0:T(8,128)(2,1)} %get-tuple-element.55.rt_far, f32[16,64,128]{2,1,0:T(8,128)} %cot_far.3), custom_call_target="tpu_custom_call" | custom-call | flops 1610612736 | bytes 2883584 | tf_op jit(solution)/shard_map/tile/pallas_call | solution.py:324
  55.8 1.3 %collective-permute-done.11 = f32[512,128]{1,0:T(8,128)S(1)} collective-permute-done((f32[512,128]{1,0:T(8,128)S(1)}, f32[512,128]{1,0:T(8,128)S(1)}, u32[]{:S(2)}, u32[]{:S(2)}) %collective-permute-start.11) | collective-permute-done | bytes 262176 | tf_op jit(solution)/shard_map/ppermute | solution.py:340
  57.1 0.9 pad_maximum_fusion
  58.0 5.1 %all-to-all-start.2 = ((f32[16,64,128]{2,1,0:T(8,128)}), f32[16,64,128]{2,1,0:T(8,128)S(1)}, u32[]{:S(2)}, u32[]{:S(2)}) async-start(f32[16,64,128]{2,1,0:T(8,128)} %pad_maximum_fusion), calls=%async_computation.2 | async-start | bytes 1048576 | tf_op jit(solution)/shard_map/all_to_all | solution.py:348
  63.2 3.9 %right_gradient.1 = (f32[4,64,128]{2,1,0:T(8,128)S(1)}, f32[4,64,128]{2,1,0:T(8,128)S(1)}, f32[4,64,128]{2,1,0:T(8,128)S(1)}, f32[4,64,128]{2,1,0:T(8,128)S(1)},...) custom-call(f32[512,128]{1,0:T(8,128)S(1)} %bitcast.35, ...), custom_call_target="tpu_custom_call" | custom-call | flops 805306368 | bytes 5505024 | tf_op jit(solution)/shard_map/right_gradient/pallas_call | solution.py:324
  68.5 1.5 %collective-permute-start.14 = (f32[4,64,128]{2,1,0:T(8,128)S(1)}, f32[4,64,128]{2,1,0:T(8,128)S(1)}, u32[]{:S(2)}, u32[]{:S(2)}) collective-permute-start(f32[4,64,128]{2,1,0:T(8,128)S(1)} %add.28), channel_id=1, source_target_pairs={{0,16},{16,0},{32,48},{48,32},{1,17},{17,1},{33,49},{49,33},{2,18}... | collective-permute-start | bytes 393224 | tf_op jit(solution)/shard_map/ppermute | solution.py:344
  70.1 2.8 %collective-permute-start.16 = (f32[4,64,128]{2,1,0:T(8,128)S(1)}, f32[4,64,128]{2,1,0:T(8,128)S(1)}, u32[]{:S(2)}, u32[]{:S(2)}) collective-permute-start(f32[4,64,128]{2,1,0:T(8,128)S(1)} %add.29), channel_id=1, source_target_pairs={{0,32},{16,48},{32,0},{48,16},{1,33},{17,49},{33,1},{49,17},{2,34}... | collective-permute-start | bytes 393224 | tf_op jit(solution)/shard_map/ppermute | solution.py:344
  72.9 0.9 collective-permute-start.18
  73.8 6.3 %pair.1 = f32[16,64,128]{2,1,0:T(8,128)} custom-call(f32[512,128]{1,0:T(8,128)S(1)} %bitcast.36, f32[1,128]{1,0:T(1,128)S(1)} %bitcast.45, bf16[4,512,384]{2,1,0:T(8,128)(2,1)} %get-tuple-element.55.rt_far, f32[1024,128]{1,0:T(8,128)S(1)} %copy-done.4), custom_call_target="tpu_custom_call" | custom-call | flops 1610612736 | bytes 2884096 | tf_op jit(solution)/shard_map/pair/pallas_call | solution.py:324
  80.2 1.4 %collective-permute-done.16 = f32[4,64,128]{2,1,0:T(8,128)S(1)} collective-permute-done((f32[4,64,128]{2,1,0:T(8,128)S(1)}, f32[4,64,128]{2,1,0:T(8,128)S(1)}, u32[]{:S(2)}, u32[]{:S(2)}) %collective-permute-start.16) | collective-permute-done | bytes 131104 | tf_op jit(solution)/shard_map/ppermute | solution.py:344
  81.6 1.1 %collective-permute-done.18 = f32[4,64,128]{2,1,0:T(8,128)S(1)} collective-permute-done((f32[4,64,128]{2,1,0:T(8,128)S(1)}, f32[4,64,128]{2,1,0:T(8,128)S(1)}, u32[]{:S(2)}, u32[]{:S(2)}) %collective-permute-start.18) | collective-permute-done | bytes 131104 | tf_op jit(solution)/shard_map/ppermute | solution.py:344
  83.5 7.5 %all-to-all-start.3 = ((f32[8,72,128]{2,1,0:T(8,128)}), f32[8,72,128]{2,1,0:T(8,128)S(1)}, u32[]{:S(2)}, u32[]{:S(2)}) async-start(f32[8,72,128]{2,1,0:T(8,128)} %select_maximum_fusion), calls=%async_computation.3 | async-start | bytes 589824 | tf_op jit(solution)/shard_map/all_to_all | solution.py:348
  91.0 1.8 %collective-permute-start.21 = (f32[64,128]{1,0:T(8,128)S(1)}, f32[64,128]{1,0:T(8,128)S(1)}, u32[]{:S(2)}, u32[]{:S(2)}) collective-permute-start(f32[64,128]{1,0:T(8,128)S(1)} %get-tuple-element.75), channel_id=1, source_target_pairs={{0,192},{64,128},{128,64},{192,0},{1,193},{65,129},{129,65},{193,1... | collective-permute-start | bytes 98312 | tf_op jit(solution)/shard_map/ppermute | solution.py:344
  92.8 1.6 %collective-permute-start.20 = (f32[64,128]{1,0:T(8,128)S(1)}, f32[64,128]{1,0:T(8,128)S(1)}, u32[]{:S(2)}, u32[]{:S(2)}) collective-permute-start(f32[64,128]{1,0:T(8,128)S(1)} %get-tuple-element.76), channel_id=1, source_target_pairs={{0,128},{64,192},{128,0},{192,64},{1,129},{65,193},{129,1},{193,65... | collective-permute-start | bytes 98312 | tf_op jit(solution)/shard_map/ppermute | solution.py:344
  94.6 5.2 %collective-permute-done.21.d_ref = f32[64,128]{1,0:T(8,128)S(1)} collective-permute-done((f32[64,128]{1,0:T(8,128)S(1)}, f32[64,128]{1,0:T(8,128)S(1)}, u32[]{:S(2)}, u32[]{:S(2)}) %collective-permute-start.21) | collective-permute-done | bytes 32800 | tf_op jit(solution)/shard_map/ppermute | solution.py:344
  100.3 4.5 %all-to-all-done.3.col_ref = f32[8,72,128]{2,1,0:T(8,128)S(1)} async-done(((f32[8,72,128]{2,1,0:T(8,128)}), f32[8,72,128]{2,1,0:T(8,128)S(1)}, u32[]{:S(2)}, u32[]{:S(2)}) %all-to-all-start.3) | async-done | bytes 294944 | tf_op jit(solution)/shard_map/all_to_all | solution.py:348
  104.8 1.3 %finish.1 = (f32[256,256]{1,0:T(8,128)}, f32[4,128]{1,0:T(4,128)}) custom-call(f32[256,256]{1,0:T(8,128)S(1)} %bitcast.33, f32[1,256]{1,0:T(1,128)S(1)} %bitcast.44, f32[32,256]{1,0:T(8,128)S(1)} %bitcast.41, f32[256,256]{1,0:T(8,128)S(1)} %right.1.part_ref, f32[8,72,128]{2,1,0:T(8,128)S(1)} %all-to-all-done.3.col_ref), custom_call_target="tpu_custom_call" | custom-call | flops 25165824 | bytes 1117184 | tf_op jit(solution)/shard_map/finish/pallas_call | solution.py:324
  (52 shorter events, 7.2 us)
Async XLA Ops:
  2.9 7.0 %collective-permute-start.2 = (f32[64,128]{1,0:T(8,128)}, f32[64,128]{1,0:T(8,128)S(1)}, u32[]{:S(2)}, u32[]{:S(2)}) collective-permute-start(f32[64,128]{1,0:T(8,128)} %project_right.1), channel_id=1, source_target_pairs={{0,192},{64,128},{128,64},{192,0},{1,193},{65,129},{129,65},{193,1... | collective-permute-start | bytes 98312 | tf_op jit(solution)/shard_map/ppermute | solution.py:344
  4.8 5.1 %collective-permute-start.1 = (f32[64,128]{1,0:T(8,128)}, f32[64,128]{1,0:T(8,128)S(1)}, u32[]{:S(2)}, u32[]{:S(2)}) collective-permute-start(f32[64,128]{1,0:T(8,128)} %project_right.1), channel_id=1, source_target_pairs={{0,128},{64,192},{128,0},{192,64},{1,129},{65,193},{129,1},{193,65... | collective-permute-start | bytes 98312 | tf_op jit(solution)/shard_map/ppermute | solution.py:344
  7.1 4.1 %collective-permute-start = (f32[64,128]{1,0:T(8,128)}, f32[64,128]{1,0:T(8,128)S(1)}, u32[]{:S(2)}, u32[]{:S(2)}) collective-permute-start(f32[64,128]{1,0:T(8,128)} %project_right.1), channel_id=1, source_target_pairs={{0,64},{64,0},{128,192},{192,128},{1,65},{65,1},{129,193},{193,129... | collective-permute-start | bytes 98312 | tf_op jit(solution)/shard_map/ppermute | solution.py:344
  11.2 22.1 %all-to-all-start = ((f32[8,64,128]{2,1,0:T(8,128)}), f32[8,64,128]{2,1,0:T(8,128)}, u32[]{:S(2)}, u32[]{:S(2)}) async-start(f32[8,64,128]{2,1,0:T(8,128)} %project_left.1), calls=%async_computation | async-start | bytes 524288 | tf_op jit(solution)/shard_map/all_to_all | solution.py:348
  21.3 9.8 %collective-permute-start.5 = (f32[4,64,128]{2,1,0:T(8,128)S(1)}, f32[4,64,128]{2,1,0:T(8,128)S(1)}, u32[]{:S(2)}, u32[]{:S(2)}) collective-permute-start(f32[4,64,128]{2,1,0:T(8,128)S(1)} %pad_maximum_fusion.1.refs_0_), channel_id=1, source_target_pairs={{0,48},{16,32},{32,16},{48,0},{1,49},{17,33},{33,17},{49,1},{2,50}... | collective-permute-start | bytes 393224 | tf_op jit(solution)/shard_map/ppermute | solution.py:344
  24.2 7.0 %collective-permute-start.4 = (f32[4,64,128]{2,1,0:T(8,128)S(1)}, f32[4,64,128]{2,1,0:T(8,128)S(1)}, u32[]{:S(2)}, u32[]{:S(2)}) collective-permute-start(f32[4,64,128]{2,1,0:T(8,128)S(1)} %pad_maximum_fusion.1.refs_0_), channel_id=1, source_target_pairs={{0,32},{16,48},{32,0},{48,16},{1,33},{17,49},{33,1},{49,17},{2,34}... | collective-permute-start | bytes 393224 | tf_op jit(solution)/shard_map/ppermute | solution.py:344
  25.0 6.2 %collective-permute-start.3 = (f32[4,64,128]{2,1,0:T(8,128)S(1)}, f32[4,64,128]{2,1,0:T(8,128)S(1)}, u32[]{:S(2)}, u32[]{:S(2)}) collective-permute-start(f32[4,64,128]{2,1,0:T(8,128)S(1)} %pad_maximum_fusion.1.refs_0_), channel_id=1, source_target_pairs={{0,16},{16,0},{32,48},{48,32},{1,17},{17,1},{33,49},{49,33},{2,18}... | collective-permute-start | bytes 393224 | tf_op jit(solution)/shard_map/ppermute | solution.py:344
  33.3 16.4 %all-to-all-start.1 = ((f32[32,16,128]{2,1,0:T(8,128)}), f32[32,16,128]{2,1,0:T(8,128)S(1)}, u32[]{:S(2)}, u32[]{:S(2)}) async-start(f32[32,16,128]{2,1,0:T(8,128)} %bitcast.7), calls=%async_computation.1 | async-start | bytes 524288 | tf_op jit(solution)/shard_map/all_to_all | solution.py:348
  39.7 1.4 %collective-permute-start.6 = (f32[4,64,128]{2,1,0:T(8,128)S(1)}, f32[4,64,128]{2,1,0:T(8,128)S(1)}, u32[]{:S(2)}, u32[]{:S(2)}) collective-permute-start(f32[4,64,128]{2,1,0:T(8,128)S(1)} %pad_maximum_fusion.1.refs_0_), channel_id=1, source_target_pairs={{0,8},{8,0},{1,9},{9,1},{2,10},{10,2},{3,11},{11,3},{4,12},{12,4},... | collective-permute-start | bytes 393224 | tf_op jit(solution)/shard_map/ppermute | solution.py:340
  39.9 1.4 %collective-permute-start.7 = (f32[4,64,128]{2,1,0:T(8,128)S(1)}, f32[4,64,128]{2,1,0:T(8,128)S(1)}, u32[]{:S(2)}, u32[]{:S(2)}) collective-permute-start(f32[4,64,128]{2,1,0:T(8,128)S(1)} %collective-permute-done.3.refs_1_), channel_id=1, source_target_pairs={{0,8},{8,0},{1,9},{9,1},{2,10},{10,2},{3,11},{11,3},{4,12},{12,4},... | collective-permute-start | bytes 393224 | tf_op jit(solution)/shard_map/ppermute | solution.py:340
  40.3 1.3 %collective-permute-start.8 = (f32[4,64,128]{2,1,0:T(8,128)S(1)}, f32[4,64,128]{2,1,0:T(8,128)S(1)}, u32[]{:S(2)}, u32[]{:S(2)}) collective-permute-start(f32[4,64,128]{2,1,0:T(8,128)S(1)} %collective-permute-done.4.refs_2_), channel_id=1, source_target_pairs={{0,8},{8,0},{1,9},{9,1},{2,10},{10,2},{3,11},{11,3},{4,12},{12,4},... | collective-permute-start | bytes 393224 | tf_op jit(solution)/shard_map/ppermute | solution.py:340
  40.4 1.4 %collective-permute-start.9 = (f32[4,64,128]{2,1,0:T(8,128)S(1)}, f32[4,64,128]{2,1,0:T(8,128)S(1)}, u32[]{:S(2)}, u32[]{:S(2)}) collective-permute-start(f32[4,64,128]{2,1,0:T(8,128)S(1)} %collective-permute-done.5.refs_3_), channel_id=1, source_target_pairs={{0,8},{8,0},{1,9},{9,1},{2,10},{10,2},{3,11},{11,3},{4,12},{12,4},... | collective-permute-start | bytes 393224 | tf_op jit(solution)/shard_map/ppermute | solution.py:340
  45.7 1.6 %collective-permute-start.10 = (f32[256,128]{1,0:T(8,128)S(1)}, f32[256,128]{1,0:T(8,128)S(1)}, u32[]{:S(2)}, u32[]{:S(2)}) collective-permute-start(f32[256,128]{1,0:T(8,128)S(1)} %get-tuple-element.53), channel_id=1, source_target_pairs={{0,8},{8,0},{1,9},{9,1},{2,10},{10,2},{3,11},{11,3},{4,12},{12,4},... | collective-permute-start | bytes 393224 | tf_op jit(solution)/shard_map/ppermute | solution.py:340
  55.5 1.6 %collective-permute-start.11 = (f32[512,128]{1,0:T(8,128)S(1)}, f32[512,128]{1,0:T(8,128)S(1)}, u32[]{:S(2)}, u32[]{:S(2)}) collective-permute-start(f32[512,128]{1,0:T(8,128)S(1)} %get-tuple-element.57), channel_id=1, source_target_pairs={{0,8},{8,0},{1,9},{9,1},{2,10},{10,2},{3,11},{11,3},{4,12},{12,4},... | collective-permute-start | bytes 786440 | tf_op jit(solution)/shard_map/ppermute | solution.py:340
  58.0 24.7 %all-to-all-start.2 = ((f32[16,64,128]{2,1,0:T(8,128)}), f32[16,64,128]{2,1,0:T(8,128)S(1)}, u32[]{:S(2)}, u32[]{:S(2)}) async-start(f32[16,64,128]{2,1,0:T(8,128)} %pad_maximum_fusion), calls=%async_computation.2 | async-start | bytes 1048576 | tf_op jit(solution)/shard_map/all_to_all | solution.py:348
  63.1 10.6 %copy-start.4 = (f32[1024,128]{1,0:T(8,128)S(1)}, f32[1024,128]{1,0:T(8,128)}, u32[]{:S(2)}) copy-start(f32[1024,128]{1,0:T(8,128)} %w_far.3) | copy-start | bytes 1572868
  63.2 10.6 %copy-start.5 = (f32[128]{0:T(128)S(1)}, f32[128]{0:T(128)}, u32[]{:S(2)}) copy-start(f32[128]{0:T(128)} %param.18) | copy-start | bytes 1540
  67.1 1.4 %collective-permute-start.13 = (f32[4,64,128]{2,1,0:T(8,128)S(1)}, f32[4,64,128]{2,1,0:T(8,128)S(1)}, u32[]{:S(2)}, u32[]{:S(2)}) collective-permute-start(f32[4,64,128]{2,1,0:T(8,128)S(1)} %get-tuple-element.63), channel_id=1, source_target_pairs={{0,8},{8,0},{1,9},{9,1},{2,10},{10,2},{3,11},{11,3},{4,12},{12,4},... | collective-permute-start | bytes 393224 | tf_op jit(solution)/shard_map/ppermute | solution.py:340
  67.2 2.9 %collective-permute-start.15 = (f32[4,64,128]{2,1,0:T(8,128)S(1)}, f32[4,64,128]{2,1,0:T(8,128)S(1)}, u32[]{:S(2)}, u32[]{:S(2)}) collective-permute-start(f32[4,64,128]{2,1,0:T(8,128)S(1)} %get-tuple-element.65), channel_id=1, source_target_pairs={{0,8},{8,0},{1,9},{9,1},{2,10},{10,2},{3,11},{11,3},{4,12},{12,4},... | collective-permute-start | bytes 393224 | tf_op jit(solution)/shard_map/ppermute | solution.py:340
  67.7 5.2 %collective-permute-start.17 = (f32[4,64,128]{2,1,0:T(8,128)S(1)}, f32[4,64,128]{2,1,0:T(8,128)S(1)}, u32[]{:S(2)}, u32[]{:S(2)}) collective-permute-start(f32[4,64,128]{2,1,0:T(8,128)S(1)} %get-tuple-element.67), channel_id=1, source_target_pairs={{0,8},{8,0},{1,9},{9,1},{2,10},{10,2},{3,11},{11,3},{4,12},{12,4},... | collective-permute-start | bytes 393224 | tf_op jit(solution)/shard_map/ppermute | solution.py:340
  67.8 12.4 %collective-permute-start.12 = (f32[4,64,128]{2,1,0:T(8,128)S(1)}, f32[4,64,128]{2,1,0:T(8,128)S(1)}, u32[]{:S(2)}, u32[]{:S(2)}) collective-permute-start(f32[4,64,128]{2,1,0:T(8,128)S(1)} %get-tuple-element.61), channel_id=1, source_target_pairs={{0,8},{8,0},{1,9},{9,1},{2,10},{10,2},{3,11},{11,3},{4,12},{12,4},... | collective-permute-start | bytes 393224 | tf_op jit(solution)/shard_map/ppermute | solution.py:340
  68.5 11.6 %collective-permute-start.14 = (f32[4,64,128]{2,1,0:T(8,128)S(1)}, f32[4,64,128]{2,1,0:T(8,128)S(1)}, u32[]{:S(2)}, u32[]{:S(2)}) collective-permute-start(f32[4,64,128]{2,1,0:T(8,128)S(1)} %add.28), channel_id=1, source_target_pairs={{0,16},{16,0},{32,48},{48,32},{1,17},{17,1},{33,49},{49,33},{2,18}... | collective-permute-start | bytes 393224 | tf_op jit(solution)/shard_map/ppermute | solution.py:344
  70.1 11.5 %collective-permute-start.16 = (f32[4,64,128]{2,1,0:T(8,128)S(1)}, f32[4,64,128]{2,1,0:T(8,128)S(1)}, u32[]{:S(2)}, u32[]{:S(2)}) collective-permute-start(f32[4,64,128]{2,1,0:T(8,128)S(1)} %add.29), channel_id=1, source_target_pairs={{0,32},{16,48},{32,0},{48,16},{1,33},{17,49},{33,1},{49,17},{2,34}... | collective-permute-start | bytes 393224 | tf_op jit(solution)/shard_map/ppermute | solution.py:344
  72.9 9.8 %collective-permute-start.18 = (f32[4,64,128]{2,1,0:T(8,128)S(1)}, f32[4,64,128]{2,1,0:T(8,128)S(1)}, u32[]{:S(2)}, u32[]{:S(2)}) collective-permute-start(f32[4,64,128]{2,1,0:T(8,128)S(1)} %add.31), channel_id=1, source_target_pairs={{0,48},{16,32},{32,16},{48,0},{1,49},{17,33},{33,17},{49,1},{2,50}... | collective-permute-start | bytes 393224 | tf_op jit(solution)/shard_map/ppermute | solution.py:344
  80.1 19.7 %copy-start.1 = (f32[256,32]{0,1:T(8,128)S(1)}, f32[256,32]{0,1:T(8,128)}, u32[]{:S(2)}) copy-start(f32[256,32]{0,1:T(8,128)} %param.15) | copy-start | bytes 98308
  80.1 24.7 %copy-start = (f32[4,64,256]{2,1,0:T(8,128)S(1)}, f32[4,64,256]{2,1,0:T(8,128)}, u32[]{:S(2)}) copy-start(f32[4,64,256]{2,1,0:T(8,128)} %param.10) | copy-start | bytes 786436
  80.1 24.7 %copy-start.2 = (f32[256,32]{0,1:T(8,128)S(1)}, f32[256,32]{0,1:T(8,128)}, u32[]{:S(2)}) copy-start(f32[256,32]{0,1:T(8,128)} %param.13) | copy-start | bytes 98308
  80.1 24.7 %copy-start.3 = (f32[256]{0:T(256)S(1)}, f32[256]{0:T(256)}, u32[]{:S(2)}) copy-start(f32[256]{0:T(256)} %param.11) | copy-start | bytes 3076
  83.5 21.3 %all-to-all-start.3 = ((f32[8,72,128]{2,1,0:T(8,128)}), f32[8,72,128]{2,1,0:T(8,128)S(1)}, u32[]{:S(2)}, u32[]{:S(2)}) async-start(f32[8,72,128]{2,1,0:T(8,128)} %select_maximum_fusion), calls=%async_computation.3 | async-start | bytes 589824 | tf_op jit(solution)/shard_map/all_to_all | solution.py:348
  91.0 8.8 %collective-permute-start.21 = (f32[64,128]{1,0:T(8,128)S(1)}, f32[64,128]{1,0:T(8,128)S(1)}, u32[]{:S(2)}, u32[]{:S(2)}) collective-permute-start(f32[64,128]{1,0:T(8,128)S(1)} %get-tuple-element.75), channel_id=1, source_target_pairs={{0,192},{64,128},{128,64},{192,0},{1,193},{65,129},{129,65},{193,1... | collective-permute-start | bytes 98312 | tf_op jit(solution)/shard_map/ppermute | solution.py:344
  92.8 7.0 %collective-permute-start.20 = (f32[64,128]{1,0:T(8,128)S(1)}, f32[64,128]{1,0:T(8,128)S(1)}, u32[]{:S(2)}, u32[]{:S(2)}) collective-permute-start(f32[64,128]{1,0:T(8,128)S(1)} %get-tuple-element.76), channel_id=1, source_target_pairs={{0,128},{64,192},{128,0},{192,64},{1,129},{65,193},{129,1},{193,65... | collective-permute-start | bytes 98312 | tf_op jit(solution)/shard_map/ppermute | solution.py:344
  94.4 5.4 %collective-permute-start.19 = (f32[64,128]{1,0:T(8,128)S(1)}, f32[64,128]{1,0:T(8,128)S(1)}, u32[]{:S(2)}, u32[]{:S(2)}) collective-permute-start(f32[64,128]{1,0:T(8,128)S(1)} %get-tuple-element.77), channel_id=1, source_target_pairs={{0,64},{64,0},{128,192},{192,128},{1,65},{65,1},{129,193},{193,129... | collective-permute-start | bytes 98312 | tf_op jit(solution)/shard_map/ppermute | solution.py:344

commit v8 on v3

--- a/solution.py
+++ b/solution.py
@@ -15,6 +15,7 @@
 ROW = ("zl", "x", "core")
 COL = ("zh", "y")
 VMEM = pl.BlockSpec(memory_space=pltpu.VMEM)
+HBM = pl.BlockSpec(memory_space=pltpu.HBM)
 
 BWD = 48
 
@@ -55,6 +56,13 @@
         right_ref[s * 16 : s * 16 + 16, :] = jnp.concatenate([cols[0:16], cols[16:32]], axis=1)
 
 
+def fetch(pairs, sems):
+    copies = [pltpu.make_async_copy(a, b, sems.at[i]) for i, (a, b) in enumerate(pairs)]
+    for copy in copies:
+        copy.start()
+    return copies
+
+
 def pick(parts):
     chunk = lax.broadcasted_iota(jnp.int32, (64, 128), 1) // 32
     low = jnp.where(chunk == 0, parts[0], parts[1])
@@ -108,18 +116,17 @@
             w_hl[d, at : at + 32, 128:256] = lo
 
 
-def cotangent_kernel(w_ref, cot_ref, g_hi, g_lo, cot_t, wide_t, w_hl, w_cat, cot_cat):
+def cotangent_kernel(w_far, cot_far, g_hi, g_lo, wide_t, w_hl, w_cat, cot_cat, w_ref, cot_ref, sems):
+    copies = fetch([(w_far, w_ref), (cot_far, cot_ref)], sems)
+    copies[0].wait()
     weights_by_class(w_ref, w_hl)
+    copies[1].wait()
     for d in range(4):
         for quad in range(4):
             hi, lo = halves(cot_ref[quad * 4 + d])
             cot_cat[d, quad * 64 : quad * 64 + 64, 0:128] = hi
             cot_cat[d, quad * 64 : quad * 64 + 64, 128:256] = hi
             cot_cat[d, quad * 64 : quad * 64 + 64, 256:384] = lo
-    for d in range(4):
-        hi, lo = halves(jnp.concatenate([cot_ref[quad * 4 + d] for quad in range(4)], axis=0).T)
-        cot_t[d, 0:128, :] = hi
-        cot_t[d, 128:256, :] = lo
     for d in range(4):
         w_cat[:, 0:256] = w_hl[d]
         w_cat[:, 256:384] = w_hl[d, :, 0:128]
@@ -140,7 +147,7 @@
                 g_lo[m, at : at + 64, quad * 128 : quad * 128 + 128] = lo
 
 
-def outer_product(left_ref, parts, right_all, outer, lcat, rt, a_hi, a_lo, r_hl=None):
+def outer_product(left_ref, parts, right_all, outer, lcat, rt, a_hi, a_lo, r_hl=None, lt=None):
     gather_right(parts, right_all)
     for quad in range(4):
         v = left_rows(left_ref, quad)
@@ -149,6 +156,8 @@
             lcat[m, 0:128, quad * 128 : quad * 128 + 128] = hi
             lcat[m, 128:256, quad * 128 : quad * 128 + 128] = lo
             lcat[m, 256:384, quad * 128 : quad * 128 + 128] = hi
+    if lt is not None:
+        left_turned(left_ref, lt)
     for e in range(16):
         g, m = e // 4, e % 4
         v = right_rows(right_all, e)
@@ -174,9 +183,12 @@
 
 
 def pair_kernel(left_ref, *refs):
-    parts, (w_ref, bias_ref, pair_ref, right_all, outer, lcat, rt, a_hi, a_lo, w_hl) = refs[:8], refs[8:]
+    parts, (bias_ref, w_far, pair_ref, right_all, outer, lcat, rt, a_hi, a_lo) = refs[:8], refs[8:17]
+    w_hl, w_ref, sems = refs[17:]
+    (fetched,) = fetch([(w_far, w_ref)], sems)
+    outer_product(left_ref, parts, right_all, outer, lcat, rt, a_hi, a_lo)
+    fetched.wait()
     weights_by_class(w_ref, w_hl)
-    outer_product(left_ref, parts, right_all, outer, lcat, rt, a_hi, a_lo)
     for d in range(4):
         both = matmul(a_hi[d], w_hl[d])
         pair = both[:, 0:128] + both[:, 128:256] + matmul(a_lo[d], w_hl[d, :, 0:128])
@@ -186,13 +198,21 @@
 
 
 def tile_kernel(left_ref, *refs):
-    parts, (g_hi, g_lo, cot_t, own_out, other_out) = refs[:8], refs[8:13]
-    right_all, outer, lcat, rt, a_hi, a_lo, r_hl, dw = refs[13:]
+    parts, (hi_far, lo_far, cot_far, own_out, other_out) = refs[:8], refs[8:13]
+    sums, (right_all, outer, lcat, rt, a_hi, a_lo) = refs[13:21], refs[21:27]
+    r_hl, lt, g_hi, g_lo, dw, cot_ref, sems = refs[27:]
     core = lax.axis_index("core")
-    outer_product(left_ref, parts, right_all, outer, lcat, rt, a_hi, a_lo, r_hl)
+    (fetched,) = fetch([(cot_far, cot_ref)], sems)
+    pairs = []
+    for m in range(4):
+        pairs += [(hi_far.at[m], g_hi.at[m]), (lo_far.at[m], g_lo.at[m])]
+    copies = fetch(pairs, sems.at[pl.ds(1, 8)])
+    outer_product(left_ref, parts, right_all, outer, lcat, rt, a_hi, a_lo, r_hl, lt)
+    fetched.wait()
     for d in range(4):
-        both = matmul(cot_t[d], a_hi[d])
-        part = both[0:128] + both[128:256] + matmul(cot_t[d, 0:128, :], a_lo[d])
+        hi, lo = halves(jnp.concatenate([cot_ref[quad * 4 + d] for quad in range(4)], axis=0).T)
+        both = matmul(jnp.concatenate([hi, lo], axis=0), a_hi[d])
+        part = both[0:128] + both[128:256] + matmul(hi, a_lo[d])
         for block in range(8):
             v = part[:, block * 128 : block * 128 + 128]
             if d == 0:
@@ -207,6 +227,22 @@
                 out[pl.ds(p * 8 + block, 16, stride=BWD), :] = dw[
                     block, pl.ds(p * 32 + side, 16, stride=2), :
                 ]
+    for m in range(4):
+        copies[2 * m].wait()
+        copies[2 * m + 1].wait()
+        both = matmul(g_hi[m], lt[m])
+        v = both[:, 0:128] + both[:, 128:256] + matmul(g_lo[m], lt[m, :, 0:128])
+        for g in range(4):
+            t = v[g * 128 : g * 128 + 128].T * (1.0 / 128)
+            for half in range(2):
+                for s in range(4):
+                    at = (half * 4 + s) * 16
+                    row = half * 1024 + s * 16 + g * 4 + m
+                    right_all[pl.ds(row, 16, stride=64), :] = t[at : at + 16]
+    for at, ref in enumerate(sums):
+        for dz in range(4):
+            start = (at // 4) * 1024 + chip_of(dz, at % 4) * 64
+            ref[dz] = right_all[pl.ds(pl.multiple_of(start, 64), 64), :]
     total = [None] * 4
     for m in range(4):
         both = matmul(r_hl[m], g_hi[m])
@@ -222,25 +258,6 @@
             for s in range(4):
                 at = (half * 4 + s) * 16
                 out[pl.ds(32 + s * 4 + quad, 16, stride=BWD), :] = t[at : at + 16]
-
-
-def right_gradient_kernel(left_ref, g_hi, g_lo, *refs):
-    outs, (lt, total) = refs[:8], refs[8:]
-    left_turned(left_ref, lt)
-    for m in range(4):
-        both = matmul(g_hi[m], lt[m])
-        v = both[:, 0:128] + both[:, 128:256] + matmul(g_lo[m], lt[m, :, 0:128])
-        for g in range(4):
-            t = v[g * 128 : g * 128 + 128].T * (1.0 / 128)
-            for half in range(2):
-                for s in range(4):
-                    at = (half * 4 + s) * 16
-                    row = half * 1024 + s * 16 + g * 4 + m
-                    total[pl.ds(row, 16, stride=64), :] = t[at : at + 16]
-    for at, ref in enumerate(outs):
-        for dz in range(4):
-            start = (at // 4) * 1024 + chip_of(dz, at % 4) * 64
-            ref[dz] = total[pl.ds(pl.multiple_of(start, 64), 64), :]
 
 
 def right_kernel(w2_ref, a_ref, b_ref, c_ref, d_ref, out_ref):
@@ -273,21 +290,22 @@
     out_ref[...] = inverse * (grad - mean - unit * along)
 
 
-def call(kernel, name, outs, scratch, mib, flops, *args):
+def call(kernel, name, outs, scratch, mib, flops, *args, far=(), copies=0):
     shapes = tuple(jax.ShapeDtypeStruct(*out) for out in outs)
-    moved = sum(a.size * a.dtype.itemsize for a in args + shapes)
+    moved = sum(a.size * a.dtype.itemsize for a in args + tuple(far) + shapes)
     return pl.pallas_call(
         kernel,
         out_shape=shapes,
-        in_specs=[VMEM] * len(args),
+        in_specs=[VMEM] * len(args) + [HBM] * len(far),
         out_specs=(VMEM,) * len(outs),
-        scratch_shapes=[pltpu.VMEM(*s) for s in scratch],
+        scratch_shapes=[pltpu.VMEM(*s) for s in scratch]
+        + ([pltpu.SemaphoreType.DMA((copies,))] if copies else []),
         compiler_params=pltpu.CompilerParams(
             vmem_limit_bytes=mib * 1024 * 1024 if mib else None
         ),
         cost_estimate=pl.CostEstimate(flops=flops, bytes_accessed=moved, transcendentals=0),
         name=name,
-    )(*args)
+    )(*args, *far)
 
 
 def swap_cores(array):
@@ -320,6 +338,7 @@
     w2 = second_operand_matrix.T
     small = 2 * 256 * 256 * 32 * 6
     step = 2 * 1024 * 1024 * 128 * 3
+    offset = standardize_offset.reshape(1, 256)
     left, right = call(
         project_kernel,
         "project",
@@ -329,30 +348,33 @@
         2 * small,
         x,
         scale,
-        standardize_offset.reshape(1, 256),
+        offset,
         w1,
         first_operand_intercept.reshape(1, 32),
         w2,
         second_operand_intercept.reshape(1, 32),
     )
-    g_hi, g_lo, cot_t = call(
+    g_hi, g_lo = call(
         cotangent_kernel,
         "cotangent",
-        [((4, 512, 512), bf16), ((4, 512, 512), bf16), ((4, 256, 256), bf16)],
+        [((4, 512, 512), bf16), ((4, 512, 512), bf16)],
         [
             ((4, 256, 1024), f32),
             ((4, 1024, 256), bf16),
             ((1024, 384), bf16),
             ((4, 256, 384), bf16),
+            ((1024, 128), f32),
+            ((16, 64, 128), f32),
         ],
-        24,
+        None,
         step,
-        result_matrix,
-        edge_incoming_sensitivity,
+        far=(result_matrix, edge_incoming_sensitivity),
+        copies=2,
     )
     left = exchange(left, COL).reshape(32, 16, 128)
-    right = jnp.stack([right] + [from_peer(right, "zl", dz) for dz in (1, 2, 3)])
-    left, right, g_hi, g_lo, cot_t = lax.optimization_barrier((left, right, g_hi, g_lo, cot_t))
+    right = [right] + [from_peer(right, "zl", dz) for dz in (1, 2, 3)]
+    right, g_hi, g_lo = lax.optimization_barrier((right, g_hi, g_lo))
+    left, right = lax.optimization_barrier((left, jnp.stack(right)))
     left = exchange(left, ROW).reshape(512, 128)
     parts = [right] + [from_peer(right, "x", dx) for dx in (1, 2, 3)]
     parts = parts + [swap_cores(part) for part in parts]
@@ -364,47 +386,39 @@
         ((4, 256, 1024), bf16),
         ((4, 256, 1024), bf16),
     ]
-    own, other = call(
+    own, other, *sums = call(
         tile_kernel,
         "tile",
-        [((16 * BWD, 128), f32), ((16 * BWD, 128), f32)],
-        working + [((4, 256, 512), bf16), ((8, 128, 128), f32)],
-        28,
-        3 * step,
+        [((16 * BWD, 128), f32)] * 2 + [((4, 64, 128), f32)] * 8,
+        working
+        + [((4, 256, 512), bf16), ((4, 512, 256), bf16)]
+        + [((4, 512, 512), bf16)] * 2
+        + [((8, 128, 128), f32), ((16, 64, 128), f32)],
+        51,
+        4 * step,
         left,
         *parts,
-        g_hi,
-        g_lo,
-        cot_t,
+        far=(g_hi, g_lo, edge_incoming_sensitivity),
+        copies=9,
     )
     own = own.reshape(16, BWD, 128)
     got = swap_cores(other.reshape(16, BWD, 128))
     sent = jnp.concatenate([own[:, :32] + got[:, :32], own[:, 32:], got[:, 32:]], axis=1)
     back = exchange(sent, CHIP)
-    sums = call(
-        right_gradient_kernel,
-        "right_gradient",
-        [((4, 64, 128), f32)] * 8,
-        [((4, 512, 256), bf16), ((2048, 128), f32)],
-        16,
-        step,
-        left,
-        g_hi,
-        g_lo,
-    )
     sums = [a + swap_cores(b) for a, b in zip(sums[:4], sums[4:])]
     right = sums[0] + sum(from_peer(sums[dx], "x", dx) for dx in (1, 2, 3))
     (pair,) = call(
         pair_kernel,
         "pair",
         [((16, 64, 128), f32)],
-        working + [((4, 1024, 256), bf16)],
-        28,
+        working + [((4, 1024, 256), bf16), ((1024, 128), f32)],
+        52,
         2 * step,
         left,
         *parts,
-        result_matrix,
         result_intercept.reshape(1, 128),
+        far=(result_matrix,),
+        copies=1,
     )
     weight = back[:, :32].sum(axis=0).reshape(4, 8, 128).transpose(1, 0, 2)
     sent = jnp.concatenate(

time: 109 us -> 106 us (0.972)
  local copies, waits for them, and re-layouts: 8.49 us -> 0.08 us
  Pallas kernels: 19.8 us -> 24.7 us
  waiting for transfers between devices: 29.4 us -> 31.1 us
    unnamed x28 -> x14, local copies, waits for them, and re-layouts: 8.46 us -> 0.04 us
    pallas_call x7 -> x6, Pallas kernels: 19.8 us -> 24.7 us  [call(): pl.pallas_call(kernel, out_shape=shapes, in_specs=[VMEM] * len(args) + [H...]
    all_to_all x4, waiting for transfers between devices: 9.58 us -> 11 us  [exchange(): return lax.all_to_all(array, axes, 0, 0, tiled=True)]
  transfers between devices with their start and end apart: 25 -> 25, of which waited for: 10 -> 13; matrix products, arithmetic and copies ran while one was open for 0% -> 0% of each run, Pallas kernels for 10% -> 11%
where the time goes in v8:
time: 106 us
  starting transfers between devices  47.1 us (44%)
  waiting for transfers between devices  31.1 us (29%)
  Pallas kernels  24.7 us (23%)
  other arithmetic  1.74 us (2%)
    all_to_all x4, starting transfers between devices, exchange(): return lax.all_to_all(array, axes, 0, 0, tiled=True)  28.5 us
    pallas_call x6, Pallas kernels, call(): pl.pallas_call(kernel, out_shape=shapes, in_specs=[VMEM] * len(args) + [H...  24.7 us
    ppermute x12, waiting for transfers between devices, from_peer(): return lax.ppermute(array, axis, [(i, i ^ apart) for i in range(4)])  17.1 us
    ppermute x12, starting transfers between devices, from_peer(): return lax.ppermute(array, axis, [(i, i ^ apart) for i in range(4)])  16.4 us
    all_to_all x4, waiting for transfers between devices, exchange(): return lax.all_to_all(array, axes, 0, 0, tiled=True)  11 us
    ppermute x9, waiting for transfers between devices, swap_cores(): return lax.ppermute(array, 'core', [(0, 1), (1, 0)])  3.03 us
    ppermute x9, starting transfers between devices, swap_cores(): return lax.ppermute(array, 'core', [(0, 1), (1, 0)])  2.17 us
  transfers between devices with their start and end apart: 25, of which 13 were waited for; matrix products, arithmetic and copies ran while one was open for 0% of the time, Pallas kernels for 11%

profile of v8, /device:TPU:32, one launch (start us, length us, event | category | flops | bytes accessed | tf_op | source)
XLA Modules:
  0.0 105.5 jit_solution(13208293023506578138)
XLA Ops:
  0.6 2.5 %project.1 = (f32[8,64,128]{2,1,0:T(8,128)}, f32[64,128]{1,0:T(8,128)}) custom-call(f32[256,256]{1,0:T(8,128)} %bitcast.30, f32[1,256]{1,0:T(1,128)} %bitcast.40, f32[1,256]{1,0:T(1,128)} %bitcast.50, f32[32,256]{1,0:T(8,128)} %bitcast.38, f32[1,32]{1,0:T(1,128)} %bitcast.51, f32[32,256]{1,0:T(8,128)} %bitcast.36, f32[1,32]{1,0:T(1,128)} %bitcast.52), custom_call_target="tpu_custom_call" | custom-call | flops 50331648 | bytes 624896 | tf_op jit(solution)/shard_map/project/pallas_call | solution.py:296
  3.2 10.3 %all-to-all-start = ((f32[8,64,128]{2,1,0:T(8,128)}), f32[8,64,128]{2,1,0:T(8,128)}, u32[]{:S(2)}, u32[]{:S(2)}) async-start(f32[8,64,128]{2,1,0:T(8,128)} %get-tuple-element.30), calls=%async_computation | async-start | bytes 524288 | tf_op jit(solution)/shard_map/all_to_all | solution.py:320
  13.5 1.0 collective-permute-start.2
  14.5 2.4 %collective-permute-start.1 = (f32[64,128]{1,0:T(8,128)}, f32[64,128]{1,0:T(8,128)S(1)}, u32[]{:S(2)}, u32[]{:S(2)}) collective-permute-start(f32[64,128]{1,0:T(8,128)} %get-tuple-element.34), channel_id=1, source_target_pairs={{0,128},{64,192},{128,0},{192,64},{1,129},{65,193},{129,1},{193,65... | collective-permute-start | bytes 98312 | tf_op jit(solution)/shard_map/ppermute | solution.py:316
  17.0 5.8 %cotangent.1 = (bf16[4,512,512]{2,1,0:T(8,128)(2,1)}, bf16[4,512,512]{2,1,0:T(8,128)(2,1)}) custom-call(f32[1024,128]{1,0:T(8,128)} %refs_9_.1, f32[16,64,128]{2,1,0:T(8,128)} %refs_10_.1), custom_call_target="tpu_custom_call" | custom-call | flops 805306368 | bytes 5242880 | tf_op jit(solution)/shard_map/cotangent/pallas_call | solution.py:296
  22.8 5.0 %all-to-all-done = f32[8,64,128]{2,1,0:T(8,128)} async-done(((f32[8,64,128]{2,1,0:T(8,128)}), f32[8,64,128]{2,1,0:T(8,128)}, u32[]{:S(2)}, u32[]{:S(2)}) %all-to-all-start) | async-done | bytes 262176 | tf_op jit(solution)/shard_map/all_to_all | solution.py:320
  27.9 6.4 %all-to-all-start.1 = ((f32[32,16,128]{2,1,0:T(8,128)}), f32[32,16,128]{2,1,0:T(8,128)S(1)}, u32[]{:S(2)}, u32[]{:S(2)}) async-start(f32[32,16,128]{2,1,0:T(8,128)} %bitcast.7), calls=%async_computation.1 | async-start | bytes 524288 | tf_op jit(solution)/shard_map/all_to_all | solution.py:320
  34.2 2.8 %collective-permute-start.5 = (f32[4,64,128]{2,1,0:T(8,128)S(1)}, f32[4,64,128]{2,1,0:T(8,128)S(1)}, u32[]{:S(2)}, u32[]{:S(2)}) collective-permute-start(f32[4,64,128]{2,1,0:T(8,128)S(1)} %pad_maximum_fusion.1.refs_0_), channel_id=1, source_target_pairs={{0,48},{16,32},{32,16},{48,0},{1,49},{17,33},{33,17},{49,1},{2,50}... | collective-permute-start | bytes 393224 | tf_op jit(solution)/shard_map/ppermute | solution.py:316
  37.0 0.9 collective-permute-start.4
  37.9 0.6 collective-permute-start.3
  38.4 8.1 %collective-permute-done.5.refs_3_ = f32[4,64,128]{2,1,0:T(8,128)S(1)} collective-permute-done((f32[4,64,128]{2,1,0:T(8,128)S(1)}, f32[4,64,128]{2,1,0:T(8,128)S(1)}, u32[]{:S(2)}, u32[]{:S(2)}) %collective-permute-start.5) | collective-permute-done | bytes 131104 | tf_op jit(solution)/shard_map/ppermute | solution.py:316
  47.3 0.6 collective-permute-done.9.refs_7_
  48.4 9.0 %tile.1 = (f32[768,128]{1,0:T(8,128)S(1)}, f32[768,128]{1,0:T(8,128)}, f32[4,64,128]{2,1,0:T(8,128)S(1)}, f32[4,64,128]{2,1,0:T(8,128)S(1)}, f32[4,64,128]{2,1,0...) custom-call(f32[512,128]{1,0:T(8,128)S(1)} %bitcast.34, ...), custom_call_target="tpu_custom_call" | custom-call | flops 3221225472 | bytes 7864320 | tf_op jit(solution)/shard_map/tile/pallas_call | solution.py:296
  57.8 1.6 %collective-permute-done.10 = f32[16,48,128]{2,1,0:T(8,128)S(1)} collective-permute-done((f32[16,48,128]{2,1,0:T(8,128)}, f32[16,48,128]{2,1,0:T(8,128)S(1)}, u32[]{:S(2)}, u32[]{:S(2)}) %collective-permute-start.10) | collective-permute-done | bytes 393248 | tf_op jit(solution)/shard_map/ppermute | solution.py:312
  59.5 0.8 pad_maximum_fusion
  60.3 5.9 %all-to-all-start.2 = ((f32[16,64,128]{2,1,0:T(8,128)}), f32[16,64,128]{2,1,0:T(8,128)S(1)}, u32[]{:S(2)}, u32[]{:S(2)}) async-start(f32[16,64,128]{2,1,0:T(8,128)} %pad_maximum_fusion), calls=%async_computation.2 | async-start | bytes 1048576 | tf_op jit(solution)/shard_map/all_to_all | solution.py:320
  67.6 1.5 %collective-permute-start.13 = (f32[4,64,128]{2,1,0:T(8,128)S(1)}, f32[4,64,128]{2,1,0:T(8,128)S(1)}, u32[]{:S(2)}, u32[]{:S(2)}) collective-permute-start(f32[4,64,128]{2,1,0:T(8,128)S(1)} %add.28), channel_id=1, source_target_pairs={{0,16},{16,0},{32,48},{48,32},{1,17},{17,1},{33,49},{49,33},{2,18}... | collective-permute-start | bytes 393224 | tf_op jit(solution)/shard_map/ppermute | solution.py:316
  69.2 2.8 %collective-permute-start.15 = (f32[4,64,128]{2,1,0:T(8,128)S(1)}, f32[4,64,128]{2,1,0:T(8,128)S(1)}, u32[]{:S(2)}, u32[]{:S(2)}) collective-permute-start(f32[4,64,128]{2,1,0:T(8,128)S(1)} %add.29), channel_id=1, source_target_pairs={{0,32},{16,48},{32,0},{48,16},{1,33},{17,49},{33,1},{49,17},{2,34}... | collective-permute-start | bytes 393224 | tf_op jit(solution)/shard_map/ppermute | solution.py:316
  71.9 0.9 collective-permute-start.17
  72.8 5.6 %pair.1 = f32[16,64,128]{2,1,0:T(8,128)} custom-call(f32[512,128]{1,0:T(8,128)S(1)} %bitcast.35, f32[4,64,128]{2,1,0:T(8,128)S(1)} %pad_maximum_fusion.1.refs_0_, f32[4,64,128]{2,1,0:T(8,128)S(1)} %collective-permute-done.3.refs_1_, f32[4,64,128]{2,1,0:T(8,128)S(1)} %collective-permute-done.4.refs_2_, f32[4,64,128]{2,1,0:T(8,128)S(1)} %collective-permute-done.5.refs_3_, ...), custom_call_target="tpu_custom_call" | custom-call | flops 1610612736 | bytes 2359808 | tf_op jit(solution)/shard_map/pair/pallas_call | solution.py:296
  78.5 3.3 %collective-permute-done.15 = f32[4,64,128]{2,1,0:T(8,128)S(1)} collective-permute-done((f32[4,64,128]{2,1,0:T(8,128)S(1)}, f32[4,64,128]{2,1,0:T(8,128)S(1)}, u32[]{:S(2)}, u32[]{:S(2)}) %collective-permute-start.15) | collective-permute-done | bytes 131104 | tf_op jit(solution)/shard_map/ppermute | solution.py:316
  81.8 1.8 %collective-permute-done.17 = f32[4,64,128]{2,1,0:T(8,128)S(1)} collective-permute-done((f32[4,64,128]{2,1,0:T(8,128)S(1)}, f32[4,64,128]{2,1,0:T(8,128)S(1)}, u32[]{:S(2)}, u32[]{:S(2)}) %collective-permute-start.17) | collective-permute-done | bytes 131104 | tf_op jit(solution)/shard_map/ppermute | solution.py:316
  83.6 0.7 select_maximum_fusion
  84.4 5.9 %all-to-all-start.3 = ((f32[8,72,128]{2,1,0:T(8,128)}), f32[8,72,128]{2,1,0:T(8,128)S(1)}, u32[]{:S(2)}, u32[]{:S(2)}) async-start(f32[8,72,128]{2,1,0:T(8,128)} %select_maximum_fusion), calls=%async_computation.3 | async-start | bytes 589824 | tf_op jit(solution)/shard_map/all_to_all | solution.py:320
  90.3 1.3 %collective-permute-start.20 = (f32[64,128]{1,0:T(8,128)S(1)}, f32[64,128]{1,0:T(8,128)S(1)}, u32[]{:S(2)}, u32[]{:S(2)}) collective-permute-start(f32[64,128]{1,0:T(8,128)S(1)} %get-tuple-element.59), channel_id=1, source_target_pairs={{0,192},{64,128},{128,64},{192,0},{1,193},{65,129},{129,65},{193,1... | collective-permute-start | bytes 98312 | tf_op jit(solution)/shard_map/ppermute | solution.py:316
  91.6 1.3 %collective-permute-start.19 = (f32[64,128]{1,0:T(8,128)S(1)}, f32[64,128]{1,0:T(8,128)S(1)}, u32[]{:S(2)}, u32[]{:S(2)}) collective-permute-start(f32[64,128]{1,0:T(8,128)S(1)} %get-tuple-element.60), channel_id=1, source_target_pairs={{0,128},{64,192},{128,0},{192,64},{1,129},{65,193},{129,1},{193,65... | collective-permute-start | bytes 98312 | tf_op jit(solution)/shard_map/ppermute | solution.py:316
  92.9 1.0 collective-permute-start.18
  93.9 2.0 %collective-permute-done.20.d_ref = f32[64,128]{1,0:T(8,128)S(1)} collective-permute-done((f32[64,128]{1,0:T(8,128)S(1)}, f32[64,128]{1,0:T(8,128)S(1)}, u32[]{:S(2)}, u32[]{:S(2)}) %collective-permute-start.20) | collective-permute-done | bytes 32800 | tf_op jit(solution)/shard_map/ppermute | solution.py:316
  95.9 0.6 collective-permute-done.19.c_ref
  96.5 1.3 %collective-permute-done.18.b_ref = f32[64,128]{1,0:T(8,128)S(1)} collective-permute-done((f32[64,128]{1,0:T(8,128)S(1)}, f32[64,128]{1,0:T(8,128)S(1)}, u32[]{:S(2)}, u32[]{:S(2)}) %collective-permute-start.18) | collective-permute-done | bytes 32800 | tf_op jit(solution)/shard_map/ppermute | solution.py:316
  98.3 5.9 %all-to-all-done.3.col_ref = f32[8,72,128]{2,1,0:T(8,128)S(1)} async-done(((f32[8,72,128]{2,1,0:T(8,128)}), f32[8,72,128]{2,1,0:T(8,128)S(1)}, u32[]{:S(2)}, u32[]{:S(2)}) %all-to-all-start.3) | async-done | bytes 294944 | tf_op jit(solution)/shard_map/all_to_all | solution.py:320
  104.2 1.3 %finish.1 = (f32[256,256]{1,0:T(8,128)}, f32[4,128]{1,0:T(4,128)}) custom-call(f32[256,256]{1,0:T(8,128)S(1)} %bitcast.31, f32[1,256]{1,0:T(1,128)S(1)} %bitcast.41, f32[32,256]{1,0:T(8,128)S(1)} %bitcast.39, f32[256,256]{1,0:T(8,128)S(1)} %right.1.part_ref, f32[8,72,128]{2,1,0:T(8,128)S(1)} %all-to-all-done.3.col_ref), custom_call_target="tpu_custom_call" | custom-call | flops 25165824 | bytes 1117184 | tf_op jit(solution)/shard_map/finish/pallas_call | solution.py:296
  (51 shorter events, 3.9 us)
Async XLA Ops:
  3.2 19.6 %copy-start.6 = (f32[64,128]{1,0:T(8,128)S(1)}, f32[64,128]{1,0:T(8,128)}, u32[]{:S(2)}) copy-start(f32[64,128]{1,0:T(8,128)} %get-tuple-element.34) | copy-start | bytes 98308
  3.2 24.7 %all-to-all-start = ((f32[8,64,128]{2,1,0:T(8,128)}), f32[8,64,128]{2,1,0:T(8,128)}, u32[]{:S(2)}, u32[]{:S(2)}) async-start(f32[8,64,128]{2,1,0:T(8,128)} %get-tuple-element.30), calls=%async_computation | async-start | bytes 524288 | tf_op jit(solution)/shard_map/all_to_all | solution.py:320
  13.5 9.3 %collective-permute-start.2 = (f32[64,128]{1,0:T(8,128)}, f32[64,128]{1,0:T(8,128)S(1)}, u32[]{:S(2)}, u32[]{:S(2)}) collective-permute-start(f32[64,128]{1,0:T(8,128)} %get-tuple-element.34), channel_id=1, source_target_pairs={{0,192},{64,128},{128,64},{192,0},{1,193},{65,129},{129,65},{193,1... | collective-permute-start | bytes 98312 | tf_op jit(solution)/shard_map/ppermute | solution.py:316
  14.5 8.3 %collective-permute-start.1 = (f32[64,128]{1,0:T(8,128)}, f32[64,128]{1,0:T(8,128)S(1)}, u32[]{:S(2)}, u32[]{:S(2)}) collective-permute-start(f32[64,128]{1,0:T(8,128)} %get-tuple-element.34), channel_id=1, source_target_pairs={{0,128},{64,192},{128,0},{192,64},{1,129},{65,193},{129,1},{193,65... | collective-permute-start | bytes 98312 | tf_op jit(solution)/shard_map/ppermute | solution.py:316
  16.9 5.9 %collective-permute-start = (f32[64,128]{1,0:T(8,128)}, f32[64,128]{1,0:T(8,128)S(1)}, u32[]{:S(2)}, u32[]{:S(2)}) collective-permute-start(f32[64,128]{1,0:T(8,128)} %get-tuple-element.34), channel_id=1, source_target_pairs={{0,64},{64,0},{128,192},{192,128},{1,65},{65,1},{129,193},{193,129... | collective-permute-start | bytes 98312 | tf_op jit(solution)/shard_map/ppermute | solution.py:316
  27.9 20.5 %all-to-all-start.1 = ((f32[32,16,128]{2,1,0:T(8,128)}), f32[32,16,128]{2,1,0:T(8,128)S(1)}, u32[]{:S(2)}, u32[]{:S(2)}) async-start(f32[32,16,128]{2,1,0:T(8,128)} %bitcast.7), calls=%async_computation.1 | async-start | bytes 524288 | tf_op jit(solution)/shard_map/all_to_all | solution.py:320
  34.2 12.3 %collective-permute-start.5 = (f32[4,64,128]{2,1,0:T(8,128)S(1)}, f32[4,64,128]{2,1,0:T(8,128)S(1)}, u32[]{:S(2)}, u32[]{:S(2)}) collective-permute-start(f32[4,64,128]{2,1,0:T(8,128)S(1)} %pad_maximum_fusion.1.refs_0_), channel_id=1, source_target_pairs={{0,48},{16,32},{32,16},{48,0},{1,49},{17,33},{33,17},{49,1},{2,50}... | collective-permute-start | bytes 393224 | tf_op jit(solution)/shard_map/ppermute | solution.py:316
  37.0 9.5 %collective-permute-start.4 = (f32[4,64,128]{2,1,0:T(8,128)S(1)}, f32[4,64,128]{2,1,0:T(8,128)S(1)}, u32[]{:S(2)}, u32[]{:S(2)}) collective-permute-start(f32[4,64,128]{2,1,0:T(8,128)S(1)} %pad_maximum_fusion.1.refs_0_), channel_id=1, source_target_pairs={{0,32},{16,48},{32,0},{48,16},{1,33},{17,49},{33,1},{49,17},{2,34}... | collective-permute-start | bytes 393224 | tf_op jit(solution)/shard_map/ppermute | solution.py:316
  37.9 9.2 %collective-permute-start.3 = (f32[4,64,128]{2,1,0:T(8,128)S(1)}, f32[4,64,128]{2,1,0:T(8,128)S(1)}, u32[]{:S(2)}, u32[]{:S(2)}) collective-permute-start(f32[4,64,128]{2,1,0:T(8,128)S(1)} %pad_maximum_fusion.1.refs_0_), channel_id=1, source_target_pairs={{0,16},{16,0},{32,48},{48,32},{1,17},{17,1},{33,49},{49,33},{2,18}... | collective-permute-start | bytes 393224 | tf_op jit(solution)/shard_map/ppermute | solution.py:316
  38.4 8.9 %collective-permute-start.6 = (f32[4,64,128]{2,1,0:T(8,128)S(1)}, f32[4,64,128]{2,1,0:T(8,128)S(1)}, u32[]{:S(2)}, u32[]{:S(2)}) collective-permute-start(f32[4,64,128]{2,1,0:T(8,128)S(1)} %pad_maximum_fusion.1.refs_0_), channel_id=1, source_target_pairs={{0,8},{8,0},{1,9},{9,1},{2,10},{10,2},{3,11},{11,3},{4,12},{12,4},... | collective-permute-start | bytes 393224 | tf_op jit(solution)/shard_map/ppermute | solution.py:312
  46.5 1.3 %collective-permute-start.9 = (f32[4,64,128]{2,1,0:T(8,128)S(1)}, f32[4,64,128]{2,1,0:T(8,128)S(1)}, u32[]{:S(2)}, u32[]{:S(2)}) collective-permute-start(f32[4,64,128]{2,1,0:T(8,128)S(1)} %collective-permute-done.5.refs_3_), channel_id=1, source_target_pairs={{0,8},{8,0},{1,9},{9,1},{2,10},{10,2},{3,11},{11,3},{4,12},{12,4},... | collective-permute-start | bytes 393224 | tf_op jit(solution)/shard_map/ppermute | solution.py:312
  46.5 1.5 %collective-permute-start.8 = (f32[4,64,128]{2,1,0:T(8,128)S(1)}, f32[4,64,128]{2,1,0:T(8,128)S(1)}, u32[]{:S(2)}, u32[]{:S(2)}) collective-permute-start(f32[4,64,128]{2,1,0:T(8,128)S(1)} %collective-permute-done.4.refs_2_), channel_id=1, source_target_pairs={{0,8},{8,0},{1,9},{9,1},{2,10},{10,2},{3,11},{11,3},{4,12},{12,4},... | collective-permute-start | bytes 393224 | tf_op jit(solution)/shard_map/ppermute | solution.py:312
  47.1 1.3 %collective-permute-start.7 = (f32[4,64,128]{2,1,0:T(8,128)S(1)}, f32[4,64,128]{2,1,0:T(8,128)S(1)}, u32[]{:S(2)}, u32[]{:S(2)}) collective-permute-start(f32[4,64,128]{2,1,0:T(8,128)S(1)} %collective-permute-done.3.refs_1_), channel_id=1, source_target_pairs={{0,8},{8,0},{1,9},{9,1},{2,10},{10,2},{3,11},{11,3},{4,12},{12,4},... | collective-permute-start | bytes 393224 | tf_op jit(solution)/shard_map/ppermute | solution.py:312
  57.4 2.0 %collective-permute-start.10 = (f32[16,48,128]{2,1,0:T(8,128)}, f32[16,48,128]{2,1,0:T(8,128)S(1)}, u32[]{:S(2)}, u32[]{:S(2)}) collective-permute-start(f32[16,48,128]{2,1,0:T(8,128)} %bitcast.53), channel_id=1, source_target_pairs={{0,8},{8,0},{1,9},{9,1},{2,10},{10,2},{3,11},{11,3},{4,12},{12,4},... | collective-permute-start | bytes 1179656 | tf_op jit(solution)/shard_map/ppermute | solution.py:312
  57.8 15.0 %copy-start.4 = (f32[1024,128]{1,0:T(8,128)S(1)}, f32[1024,128]{1,0:T(8,128)}, u32[]{:S(2)}) copy-start(f32[1024,128]{1,0:T(8,128)} %refs_9_.1) | copy-start | bytes 1572868
  57.8 15.0 %copy-start.5 = (f32[128]{0:T(128)S(1)}, f32[128]{0:T(128)}, u32[]{:S(2)}) copy-start(f32[128]{0:T(128)} %param.18) | copy-start | bytes 1540
  60.3 23.2 %all-to-all-start.2 = ((f32[16,64,128]{2,1,0:T(8,128)}), f32[16,64,128]{2,1,0:T(8,128)S(1)}, u32[]{:S(2)}, u32[]{:S(2)}) async-start(f32[16,64,128]{2,1,0:T(8,128)} %pad_maximum_fusion), calls=%async_computation.2 | async-start | bytes 1048576 | tf_op jit(solution)/shard_map/all_to_all | solution.py:320
  66.2 1.3 %collective-permute-start.12 = (f32[4,64,128]{2,1,0:T(8,128)S(1)}, f32[4,64,128]{2,1,0:T(8,128)S(1)}, u32[]{:S(2)}, u32[]{:S(2)}) collective-permute-start(f32[4,64,128]{2,1,0:T(8,128)S(1)} %get-tuple-element.47), channel_id=1, source_target_pairs={{0,8},{8,0},{1,9},{9,1},{2,10},{10,2},{3,11},{11,3},{4,12},{12,4},... | collective-permute-start | bytes 393224 | tf_op jit(solution)/shard_map/ppermute | solution.py:312
  66.2 2.9 %collective-permute-start.14 = (f32[4,64,128]{2,1,0:T(8,128)S(1)}, f32[4,64,128]{2,1,0:T(8,128)S(1)}, u32[]{:S(2)}, u32[]{:S(2)}) collective-permute-start(f32[4,64,128]{2,1,0:T(8,128)S(1)} %get-tuple-element.49), channel_id=1, source_target_pairs={{0,8},{8,0},{1,9},{9,1},{2,10},{10,2},{3,11},{11,3},{4,12},{12,4},... | collective-permute-start | bytes 393224 | tf_op jit(solution)/shard_map/ppermute | solution.py:312
  66.7 5.2 %collective-permute-start.16 = (f32[4,64,128]{2,1,0:T(8,128)S(1)}, f32[4,64,128]{2,1,0:T(8,128)S(1)}, u32[]{:S(2)}, u32[]{:S(2)}) collective-permute-start(f32[4,64,128]{2,1,0:T(8,128)S(1)} %get-tuple-element.51), channel_id=1, source_target_pairs={{0,8},{8,0},{1,9},{9,1},{2,10},{10,2},{3,11},{11,3},{4,12},{12,4},... | collective-permute-start | bytes 393224 | tf_op jit(solution)/shard_map/ppermute | solution.py:312
  66.8 11.7 %collective-permute-start.11 = (f32[4,64,128]{2,1,0:T(8,128)S(1)}, f32[4,64,128]{2,1,0:T(8,128)S(1)}, u32[]{:S(2)}, u32[]{:S(2)}) collective-permute-start(f32[4,64,128]{2,1,0:T(8,128)S(1)} %get-tuple-element.45), channel_id=1, source_target_pairs={{0,8},{8,0},{1,9},{9,1},{2,10},{10,2},{3,11},{11,3},{4,12},{12,4},... | collective-permute-start | bytes 393224 | tf_op jit(solution)/shard_map/ppermute | solution.py:312
  67.6 10.9 %collective-permute-start.13 = (f32[4,64,128]{2,1,0:T(8,128)S(1)}, f32[4,64,128]{2,1,0:T(8,128)S(1)}, u32[]{:S(2)}, u32[]{:S(2)}) collective-permute-start(f32[4,64,128]{2,1,0:T(8,128)S(1)} %add.28), channel_id=1, source_target_pairs={{0,16},{16,0},{32,48},{48,32},{1,17},{17,1},{33,49},{49,33},{2,18}... | collective-permute-start | bytes 393224 | tf_op jit(solution)/shard_map/ppermute | solution.py:316
  69.2 12.6 %collective-permute-start.15 = (f32[4,64,128]{2,1,0:T(8,128)S(1)}, f32[4,64,128]{2,1,0:T(8,128)S(1)}, u32[]{:S(2)}, u32[]{:S(2)}) collective-permute-start(f32[4,64,128]{2,1,0:T(8,128)S(1)} %add.29), channel_id=1, source_target_pairs={{0,32},{16,48},{32,0},{48,16},{1,33},{17,49},{33,1},{49,17},{2,34}... | collective-permute-start | bytes 393224 | tf_op jit(solution)/shard_map/ppermute | solution.py:316
  71.9 11.6 %collective-permute-start.17 = (f32[4,64,128]{2,1,0:T(8,128)S(1)}, f32[4,64,128]{2,1,0:T(8,128)S(1)}, u32[]{:S(2)}, u32[]{:S(2)}) collective-permute-start(f32[4,64,128]{2,1,0:T(8,128)S(1)} %add.31), channel_id=1, source_target_pairs={{0,48},{16,32},{32,16},{48,0},{1,49},{17,33},{33,17},{49,1},{2,50}... | collective-permute-start | bytes 393224 | tf_op jit(solution)/shard_map/ppermute | solution.py:316
  78.4 19.4 %copy-start.1 = (f32[256,32]{0,1:T(8,128)S(1)}, f32[256,32]{0,1:T(8,128)}, u32[]{:S(2)}) copy-start(f32[256,32]{0,1:T(8,128)} %param.15) | copy-start | bytes 98308
  78.4 25.8 %copy-start = (f32[4,64,256]{2,1,0:T(8,128)S(1)}, f32[4,64,256]{2,1,0:T(8,128)}, u32[]{:S(2)}) copy-start(f32[4,64,256]{2,1,0:T(8,128)} %param.10) | copy-start | bytes 786436
  78.5 25.8 %copy-start.2 = (f32[256,32]{0,1:T(8,128)S(1)}, f32[256,32]{0,1:T(8,128)}, u32[]{:S(2)}) copy-start(f32[256,32]{0,1:T(8,128)} %param.13) | copy-start | bytes 98308
  78.5 25.8 %copy-start.3 = (f32[256]{0:T(256)S(1)}, f32[256]{0:T(256)}, u32[]{:S(2)}) copy-start(f32[256]{0:T(256)} %param.11) | copy-start | bytes 3076
  84.4 19.9 %all-to-all-start.3 = ((f32[8,72,128]{2,1,0:T(8,128)}), f32[8,72,128]{2,1,0:T(8,128)S(1)}, u32[]{:S(2)}, u32[]{:S(2)}) async-start(f32[8,72,128]{2,1,0:T(8,128)} %select_maximum_fusion), calls=%async_computation.3 | async-start | bytes 589824 | tf_op jit(solution)/shard_map/all_to_all | solution.py:320
  90.3 5.6 %collective-permute-start.20 = (f32[64,128]{1,0:T(8,128)S(1)}, f32[64,128]{1,0:T(8,128)S(1)}, u32[]{:S(2)}, u32[]{:S(2)}) collective-permute-start(f32[64,128]{1,0:T(8,128)S(1)} %get-tuple-element.59), channel_id=1, source_target_pairs={{0,192},{64,128},{128,64},{192,0},{1,193},{65,129},{129,65},{193,1... | collective-permute-start | bytes 98312 | tf_op jit(solution)/shard_map/ppermute | solution.py:316
  91.6 4.9 %collective-permute-start.19 = (f32[64,128]{1,0:T(8,128)S(1)}, f32[64,128]{1,0:T(8,128)S(1)}, u32[]{:S(2)}, u32[]{:S(2)}) collective-permute-start(f32[64,128]{1,0:T(8,128)S(1)} %get-tuple-element.60), channel_id=1, source_target_pairs={{0,128},{64,192},{128,0},{192,64},{1,129},{65,193},{129,1},{193,65... | collective-permute-start | bytes 98312 | tf_op jit(solution)/shard_map/ppermute | solution.py:316
  92.9 5.0 %collective-permute-start.18 = (f32[64,128]{1,0:T(8,128)S(1)}, f32[64,128]{1,0:T(8,128)S(1)}, u32[]{:S(2)}, u32[]{:S(2)}) collective-permute-start(f32[64,128]{1,0:T(8,128)S(1)} %get-tuple-element.61), channel_id=1, source_target_pairs={{0,64},{64,0},{128,192},{192,128},{1,65},{65,1},{129,193},{193,129... | collective-permute-start | bytes 98312 | tf_op jit(solution)/shard_map/ppermute | solution.py:316

commit v9 on v6

--- a/solution.py
+++ b/solution.py
@@ -65,6 +65,13 @@
     for copy in copies:
         copy.start()
     return copies
+
+
+def fetch_classes(hi_far, lo_far, g_hi, g_lo, sems):
+    pairs = []
+    for m in range(4):
+        pairs += [(hi_far.at[m], g_hi.at[m]), (lo_far.at[m], g_lo.at[m])]
+    return fetch(pairs, sems)
 
 
 def pick(parts):
@@ -151,7 +158,7 @@
                 g_lo[m, at : at + 64, quad * 128 : quad * 128 + 128] = lo
 
 
-def outer_product(left_ref, parts, right_all, outer, lcat, rt, a_hi, a_lo):
+def outer_product(left_ref, parts, right_all, outer, lcat, rt, a_hi, a_lo, lt=None):
     gather_right(parts, right_all)
     for quad in range(4):
         v = left_rows(left_ref, quad)
@@ -160,6 +167,8 @@
             lcat[m, 0:128, quad * 128 : quad * 128 + 128] = hi
             lcat[m, 128:256, quad * 128 : quad * 128 + 128] = lo
             lcat[m, 256:384, quad * 128 : quad * 128 + 128] = hi
+    if lt is not None:
+        left_turned(left_ref, lt)
     for e in range(16):
         g, m = e // 4, e % 4
         hi, lo = halves(right_rows(right_all, e).T)
@@ -195,11 +204,13 @@
 
 
 def tile_kernel(left_ref, *refs):
-    parts, (cot_far, own_out, other_out) = refs[:8], refs[8:11]
-    right_all, outer, lcat, rt, a_hi, a_lo, dw, cot_ref, sems = refs[11:]
+    parts, (hi_far, lo_far, cot_far, own_out, other_out) = refs[:8], refs[8:13]
+    sums, (right_all, outer, lcat, rt, a_hi, a_lo) = refs[13:21], refs[21:27]
+    lt, g_hi, g_lo, dw, cot_ref, sems = refs[27:]
     core = lax.axis_index("core")
     (fetched,) = fetch([(cot_far, cot_ref)], sems)
-    outer_product(left_ref, parts, right_all, outer, lcat, rt, a_hi, a_lo)
+    copies = fetch_classes(hi_far, lo_far, g_hi, g_lo, sems.at[pl.ds(1, 8)])
+    outer_product(left_ref, parts, right_all, outer, lcat, rt, a_hi, a_lo, lt)
     fetched.wait()
     for d in range(4):
         hi, lo = halves(jnp.concatenate([cot_ref[quad * 4 + d] for quad in range(4)], axis=0).T)
@@ -219,21 +230,37 @@
                 out[pl.ds(p * 8 + block, 16, stride=BWD), :] = dw[
                     block, pl.ds(p * 32 + side, 16, stride=2), :
                 ]
+    for m in range(4):
+        copies[2 * m].wait()
+        copies[2 * m + 1].wait()
+        both = matmul(g_hi[m], lt[m])
+        v = both[:, 0:128] + both[:, 128:256] + matmul(g_lo[m], lt[m, :, 0:128])
+        for g in range(4):
+            t = v[g * 128 : g * 128 + 128].T * (1.0 / 128)
+            for half in range(2):
+                for s in range(4):
+                    at = (half * 4 + s) * 16
+                    row = half * 1024 + s * 16 + g * 4 + m
+                    right_all[pl.ds(row, 16, stride=64), :] = t[at : at + 16]
+    for at, ref in enumerate(sums):
+        for dz in range(4):
+            start = (at // 4) * 1024 + chip_of(dz, at % 4) * 64
+            ref[dz] = right_all[pl.ds(pl.multiple_of(start, 64), 64), :]
 
 
 def left_gradient_kernel(*refs):
     parts, (hi_far, lo_far, own_out, other_out, right_all, r_hl, g_hi, g_lo, sems) = refs[:8], refs[8:]
-    copies = fetch([(hi_far, g_hi), (lo_far, g_lo)], sems)
+    copies = fetch_classes(hi_far, lo_far, g_hi, g_lo, sems)
     gather_right(parts, right_all)
     for e in range(16):
         g, m = e // 4, e % 4
         hi, lo = halves(right_rows(right_all, e))
         r_hl[m, 0:128, g * 128 : g * 128 + 128] = hi
         r_hl[m, 128:256, g * 128 : g * 128 + 128] = lo
-    for copy in copies:
-        copy.wait()
     total = [None] * 4
     for m in range(4):
+        copies[2 * m].wait()
+        copies[2 * m + 1].wait()
         both = matmul(r_hl[m], g_hi[m])
         v = both[0:128] + both[128:256] + matmul(r_hl[m, 0:128, :], g_lo[m])
         for quad in range(4):
@@ -247,28 +274,6 @@
             for s in range(4):
                 at = (half * 4 + s) * 16
                 out[pl.ds(s * 4 + quad, 16, stride=16), :] = t[at : at + 16]
-
-
-def right_gradient_kernel(left_ref, hi_far, lo_far, *refs):
-    outs, (lt, total, g_hi, g_lo, sems) = refs[:8], refs[8:]
-    copies = fetch([(hi_far, g_hi), (lo_far, g_lo)], sems)
-    left_turned(left_ref, lt)
-    for copy in copies:
-        copy.wait()
-    for m in range(4):
-        both = matmul(g_hi[m], lt[m])
-        v = both[:, 0:128] + both[:, 128:256] + matmul(g_lo[m], lt[m, :, 0:128])
-        for g in range(4):
-            t = v[g * 128 : g * 128 + 128].T * (1.0 / 128)
-            for half in range(2):
-                for s in range(4):
-                    at = (half * 4 + s) * 16
-                    row = half * 1024 + s * 16 + g * 4 + m
-                    total[pl.ds(row, 16, stride=64), :] = t[at : at + 16]
-    for at, ref in enumerate(outs):
-        for dz in range(4):
-            start = (at // 4) * 1024 + chip_of(dz, at % 4) * 64
-            ref[dz] = total[pl.ds(pl.multiple_of(start, 64), 64), :]
 
 
 def right_kernel(w2_ref, a_ref, b_ref, c_ref, d_ref, out_ref):
@@ -410,7 +415,7 @@
         step,
         *parts,
         far=(g_hi, g_lo),
-        copies=2,
+        copies=8,
     )
     got_left = swap_cores(other_left)
     left, own_left, got_left = lax.optimization_barrier((left, own_left, got_left))
@@ -422,30 +427,22 @@
         ((4, 256, 1024), bf16),
         ((4, 256, 1024), bf16),
     ]
-    own, other = call(
+    own, other, *sums = call(
         tile_kernel,
         "tile",
-        [((16 * BWD, 128), f32)] * 2,
-        working + [((8, 128, 128), f32), ((16, 64, 128), f32)],
-        52,
-        2 * step,
+        [((16 * BWD, 128), f32)] * 2 + [((4, 64, 128), f32)] * 8,
+        working
+        + [((4, 512, 256), bf16)]
+        + [((4, 512, 512), bf16)] * 2
+        + [((8, 128, 128), f32), ((16, 64, 128), f32)],
+        51,
+        3 * step,
         left,
         *parts,
-        far=(edge_incoming_sensitivity,),
-        copies=1,
+        far=(g_hi, g_lo, edge_incoming_sensitivity),
+        copies=9,
     )
     got = swap_cores(other)
-    sums = call(
-        right_gradient_kernel,
-        "right_gradient",
-        [((4, 64, 128), f32)] * 8,
-        [((4, 512, 256), bf16), ((2048, 128), f32)] + [((4, 512, 512), bf16)] * 2,
-        52,
-        step,
-        left,
-        far=(g_hi, g_lo),
-        copies=2,
-    )
     weight = (own + got).reshape(16, BWD, 128)
     sent = [weight, own_left.reshape(16, 16, 128), got_left.reshape(16, 16, 128)]
     back = exchange(jnp.concatenate(sent, axis=1), CHIP)

time: 106 us -> 107 us (level)
  starting transfers between devices: 49 us -> 51.6 us
  Pallas kernels: 30.1 us -> 28.5 us
    all_to_all x4, waiting for transfers between devices: 9.77 us -> 5.55 us  [exchange(): return lax.all_to_all(array, axes, 0, 0, tiled=True)]
    ppermute x12, waiting for transfers between devices: 9.52 us -> 13 us  [from_peer(): return lax.ppermute(array, axis, [(i, i ^ apart) for i in range(4)])]
    all_to_all x4, starting transfers between devices: 28.1 us -> 31.2 us  [exchange(): return lax.all_to_all(array, axes, 0, 0, tiled=True)]
    pallas_call x9 -> x8, Pallas kernels: 30.1 us -> 28.5 us  [call(): pl.pallas_call(kernel, out_shape=shapes, in_specs=[VMEM] * len(args) + [H...]
  transfers between devices with their start and end apart: 26 -> 26, of which waited for: 14 -> 16; matrix products, arithmetic and copies ran while one was open for 1% -> 1% of each run, Pallas kernels for 21% -> 16%
where the time goes in v9:
time: 107 us; the launch traced here: 106 us
  starting transfers between devices  51.6 us (48%)
  Pallas kernels  28.5 us (27%)
  waiting for transfers between devices  22.2 us (21%)
  other arithmetic  2.5 us (2%)
    all_to_all x4, starting transfers between devices, exchange(): return lax.all_to_all(array, axes, 0, 0, tiled=True)  31.2 us
    pallas_call x8, Pallas kernels, call(): pl.pallas_call(kernel, out_shape=shapes, in_specs=[VMEM] * len(args) + [H...  28.5 us
    ppermute x12, starting transfers between devices, from_peer(): return lax.ppermute(array, axis, [(i, i ^ apart) for i in range(4)])  17.4 us
    ppermute x12, waiting for transfers between devices, from_peer(): return lax.ppermute(array, axis, [(i, i ^ apart) for i in range(4)])  13 us
    all_to_all x4, waiting for transfers between devices, exchange(): return lax.all_to_all(array, axes, 0, 0, tiled=True)  5.55 us
    ppermute x10, waiting for transfers between devices, swap_cores(): return lax.ppermute(array, 'core', [(0, 1), (1, 0)])  3.64 us
    ppermute x10, starting transfers between devices, swap_cores(): return lax.ppermute(array, 'core', [(0, 1), (1, 0)])  3.07 us
  transfers between devices with their start and end apart: 26, of which 16 were waited for; matrix products, arithmetic and copies ran while one was open for 1% of the time, Pallas kernels for 16%

profile of v9, /device:TPU:32, one launch (start us, length us, event | category | flops | bytes accessed | tf_op | source)
XLA Modules:
  0.0 105.7 jit_solution(8242891528188812800)
XLA Ops:
  0.6 2.2 %project_right.1 = f32[64,128]{1,0:T(8,128)} custom-call(f32[256,256]{1,0:T(8,128)} %bitcast.31, f32[1,256]{1,0:T(1,128)} %bitcast.41, f32[1,256]{1,0:T(1,128)} %bitcast.54, f32[32,256]{1,0:T(8,128)} %bitcast.36, f32[1,32]{1,0:T(1,128)} %bitcast.56), custom_call_target="tpu_custom_call" | custom-call | flops 25165824 | bytes 329856 | tf_op jit(solution)/shard_map/project_right/pallas_call | solution.py:312
  2.9 1.8 %collective-permute-start = (f32[64,128]{1,0:T(8,128)}, f32[64,128]{1,0:T(8,128)S(1)}, u32[]{:S(2)}, u32[]{:S(2)}) collective-permute-start(f32[64,128]{1,0:T(8,128)} %project_right.1), channel_id=1, source_target_pairs={{0,64},{64,0},{128,192},{192,128},{1,65},{65,1},{129,193},{193,129... | collective-permute-start | bytes 98312 | tf_op jit(solution)/shard_map/ppermute | solution.py:332
  4.7 1.5 %collective-permute-start.1 = (f32[64,128]{1,0:T(8,128)}, f32[64,128]{1,0:T(8,128)S(1)}, u32[]{:S(2)}, u32[]{:S(2)}) collective-permute-start(f32[64,128]{1,0:T(8,128)} %project_right.1), channel_id=1, source_target_pairs={{0,128},{64,192},{128,0},{192,64},{1,129},{65,193},{129,1},{193,65... | collective-permute-start | bytes 98312 | tf_op jit(solution)/shard_map/ppermute | solution.py:332
  6.7 2.3 %project_left.1 = f32[8,64,128]{2,1,0:T(8,128)} custom-call(f32[256,256]{1,0:T(8,128)} %bitcast.32, f32[1,256]{1,0:T(1,128)} %bitcast.42, f32[1,256]{1,0:T(1,128)} %bitcast.55, f32[32,256]{1,0:T(8,128)} %bitcast.39, f32[1,32]{1,0:T(1,128)} %bitcast.57), custom_call_target="tpu_custom_call" | custom-call | flops 25165824 | bytes 559232 | tf_op jit(solution)/shard_map/project_left/pallas_call | solution.py:312
  9.0 0.7 collective-permute-done.1
  10.4 9.4 %all-to-all-start = ((f32[8,64,128]{2,1,0:T(8,128)}), f32[8,64,128]{2,1,0:T(8,128)}, u32[]{:S(2)}, u32[]{:S(2)}) async-start(f32[8,64,128]{2,1,0:T(8,128)} %project_left.1), calls=%async_computation | async-start | bytes 524288 | tf_op jit(solution)/shard_map/all_to_all | solution.py:336
  19.8 0.8 pad_maximum_fusion.1.refs_0_
  20.6 1.6 %collective-permute-start.3 = (f32[4,64,128]{2,1,0:T(8,128)S(1)}, f32[4,64,128]{2,1,0:T(8,128)S(1)}, u32[]{:S(2)}, u32[]{:S(2)}) collective-permute-start(f32[4,64,128]{2,1,0:T(8,128)S(1)} %pad_maximum_fusion.1.refs_0_), channel_id=1, source_target_pairs={{0,16},{16,0},{32,48},{48,32},{1,17},{17,1},{33,49},{49,33},{2,18}... | collective-permute-start | bytes 393224 | tf_op jit(solution)/shard_map/ppermute | solution.py:332
  22.1 2.7 %collective-permute-start.4 = (f32[4,64,128]{2,1,0:T(8,128)S(1)}, f32[4,64,128]{2,1,0:T(8,128)S(1)}, u32[]{:S(2)}, u32[]{:S(2)}) collective-permute-start(f32[4,64,128]{2,1,0:T(8,128)S(1)} %pad_maximum_fusion.1.refs_0_), channel_id=1, source_target_pairs={{0,32},{16,48},{32,0},{48,16},{1,33},{17,49},{33,1},{49,17},{2,34}... | collective-permute-start | bytes 393224 | tf_op jit(solution)/shard_map/ppermute | solution.py:332
  25.3 5.8 %cotangent.1 = (bf16[4,512,512]{2,1,0:T(8,128)(2,1)}, bf16[4,512,512]{2,1,0:T(8,128)(2,1)}) custom-call(f32[1024,128]{1,0:T(8,128)} %refs_9_.1, f32[16,64,128]{2,1,0:T(8,128)} %refs_10_.1), custom_call_target="tpu_custom_call" | custom-call | flops 805306368 | bytes 5242880 | tf_op jit(solution)/shard_map/cotangent/pallas_call | solution.py:312
  31.2 0.9 all-to-all-done
  32.0 7.5 %all-to-all-start.1 = ((f32[32,16,128]{2,1,0:T(8,128)}), f32[32,16,128]{2,1,0:T(8,128)S(1)}, u32[]{:S(2)}, u32[]{:S(2)}) async-start(f32[32,16,128]{2,1,0:T(8,128)} %bitcast.7), calls=%async_computation.1 | async-start | bytes 524288 | tf_op jit(solution)/shard_map/all_to_all | solution.py:336
  41.6 3.1 %left_gradient.1 = (f32[256,128]{1,0:T(8,128)S(1)}, f32[256,128]{1,0:T(8,128)S(1)}) custom-call(f32[4,64,128]{2,1,0:T(8,128)S(1)} %pad_maximum_fusion.1.refs_0_, f32[4,64,128]{2,1,0:T(8,128)S(1)} %collective-permute-done.3.refs_1_, f32[4,64,128]{2,1,0:T(8,128)S(1)} %collective-permute-done.4.refs_2_, f32[4,64,128]{2,1,0:T(8,128)S(1)} %collective-permute-done.5.refs_3_, ...), custom_call_target="tpu_custom_call" | custom-call | flops 805306368 | bytes 5505024 | tf_op jit(solution)/shard_map/left_gradient/pallas_call | solution.py:312
  45.3 1.0 collective-permute-done.10
  46.4 3.2 %all-to-all-done.1 = f32[32,16,128]{2,1,0:T(8,128)S(1)} async-done(((f32[32,16,128]{2,1,0:T(8,128)}), f32[32,16,128]{2,1,0:T(8,128)S(1)}, u32[]{:S(2)}, u32[]{:S(2)}) %all-to-all-start.1) | async-done | bytes 262176 | tf_op jit(solution)/shard_map/all_to_all | solution.py:336
  49.6 7.7 %tile.1 = (f32[512,128]{1,0:T(8,128)S(1)}, f32[512,128]{1,0:T(8,128)S(1)}, f32[4,64,128]{2,1,0:T(8,128)S(1)}, f32[4,64,128]{2,1,0:T(8,128)S(1)}, f32[4,64,128]{2...) custom-call(f32[512,128]{1,0:T(8,128)S(1)} %bitcast.34, ...), custom_call_target="tpu_custom_call" | custom-call | flops 2415919104 | bytes 7602176 | tf_op jit(solution)/shard_map/tile/pallas_call | solution.py:312
  57.7 1.3 %collective-permute-done.11 = f32[512,128]{1,0:T(8,128)S(1)} collective-permute-done((f32[512,128]{1,0:T(8,128)S(1)}, f32[512,128]{1,0:T(8,128)S(1)}, u32[]{:S(2)}, u32[]{:S(2)}) %collective-permute-start.11) | collective-permute-done | bytes 262176 | tf_op jit(solution)/shard_map/ppermute | solution.py:328
  59.0 0.8 pad_maximum_fusion
  59.8 4.8 %all-to-all-start.2 = ((f32[16,64,128]{2,1,0:T(8,128)}), f32[16,64,128]{2,1,0:T(8,128)S(1)}, u32[]{:S(2)}, u32[]{:S(2)}) async-start(f32[16,64,128]{2,1,0:T(8,128)} %pad_maximum_fusion), calls=%async_computation.2 | async-start | bytes 1048576 | tf_op jit(solution)/shard_map/all_to_all | solution.py:336
  65.9 2.8 %collective-permute-start.18 = (f32[4,64,128]{2,1,0:T(8,128)S(1)}, f32[4,64,128]{2,1,0:T(8,128)S(1)}, u32[]{:S(2)}, u32[]{:S(2)}) collective-permute-start(f32[4,64,128]{2,1,0:T(8,128)S(1)} %add.31), channel_id=1, source_target_pairs={{0,48},{16,32},{32,16},{48,0},{1,49},{17,33},{33,17},{49,1},{2,50}... | collective-permute-start | bytes 393224 | tf_op jit(solution)/shard_map/ppermute | solution.py:332
  69.1 2.1 %collective-permute-start.16 = (f32[4,64,128]{2,1,0:T(8,128)S(1)}, f32[4,64,128]{2,1,0:T(8,128)S(1)}, u32[]{:S(2)}, u32[]{:S(2)}) collective-permute-start(f32[4,64,128]{2,1,0:T(8,128)S(1)} %add.29), channel_id=1, source_target_pairs={{0,32},{16,48},{32,0},{48,16},{1,33},{17,49},{33,1},{49,17},{2,34}... | collective-permute-start | bytes 393224 | tf_op jit(solution)/shard_map/ppermute | solution.py:332
  71.2 5.6 %pair.1 = f32[16,64,128]{2,1,0:T(8,128)} custom-call(f32[512,128]{1,0:T(8,128)S(1)} %bitcast.35, f32[4,64,128]{2,1,0:T(8,128)S(1)} %pad_maximum_fusion.1.refs_0_, f32[4,64,128]{2,1,0:T(8,128)S(1)} %collective-permute-done.3.refs_1_, f32[4,64,128]{2,1,0:T(8,128)S(1)} %collective-permute-done.4.refs_2_, f32[4,64,128]{2,1,0:T(8,128)S(1)} %collective-permute-done.5.refs_3_, ...), custom_call_target="tpu_custom_call" | custom-call | flops 1610612736 | bytes 2359808 | tf_op jit(solution)/shard_map/pair/pallas_call | solution.py:312
  76.9 3.7 %collective-permute-done.16 = f32[4,64,128]{2,1,0:T(8,128)S(1)} collective-permute-done((f32[4,64,128]{2,1,0:T(8,128)S(1)}, f32[4,64,128]{2,1,0:T(8,128)S(1)}, u32[]{:S(2)}, u32[]{:S(2)}) %collective-permute-start.16) | collective-permute-done | bytes 131104 | tf_op jit(solution)/shard_map/ppermute | solution.py:332
  80.7 0.7 select_maximum_fusion
  81.4 9.5 %all-to-all-start.3 = ((f32[8,72,128]{2,1,0:T(8,128)}), f32[8,72,128]{2,1,0:T(8,128)S(1)}, u32[]{:S(2)}, u32[]{:S(2)}) async-start(f32[8,72,128]{2,1,0:T(8,128)} %select_maximum_fusion), calls=%async_computation.3 | async-start | bytes 589824 | tf_op jit(solution)/shard_map/all_to_all | solution.py:336
  91.1 2.6 %collective-permute-start.20 = (f32[64,128]{1,0:T(8,128)S(1)}, f32[64,128]{1,0:T(8,128)S(1)}, u32[]{:S(2)}, u32[]{:S(2)}) collective-permute-start(f32[64,128]{1,0:T(8,128)S(1)} %get-tuple-element.74), channel_id=1, source_target_pairs={{0,128},{64,192},{128,0},{192,64},{1,129},{65,193},{129,1},{193,65... | collective-permute-start | bytes 98312 | tf_op jit(solution)/shard_map/ppermute | solution.py:332
  93.6 0.9 collective-permute-start.21
  94.5 2.5 %collective-permute-done.19.b_ref = f32[64,128]{1,0:T(8,128)S(1)} collective-permute-done((f32[64,128]{1,0:T(8,128)S(1)}, f32[64,128]{1,0:T(8,128)S(1)}, u32[]{:S(2)}, u32[]{:S(2)}) %collective-permute-start.19) | collective-permute-done | bytes 32800 | tf_op jit(solution)/shard_map/ppermute | solution.py:332
  97.0 2.9 %collective-permute-done.20.c_ref = f32[64,128]{1,0:T(8,128)S(1)} collective-permute-done((f32[64,128]{1,0:T(8,128)S(1)}, f32[64,128]{1,0:T(8,128)S(1)}, u32[]{:S(2)}, u32[]{:S(2)}) %collective-permute-start.20) | collective-permute-done | bytes 32800 | tf_op jit(solution)/shard_map/ppermute | solution.py:332
  100.0 2.5 %collective-permute-done.21.d_ref = f32[64,128]{1,0:T(8,128)S(1)} collective-permute-done((f32[64,128]{1,0:T(8,128)S(1)}, f32[64,128]{1,0:T(8,128)S(1)}, u32[]{:S(2)}, u32[]{:S(2)}) %collective-permute-start.21) | collective-permute-done | bytes 32800 | tf_op jit(solution)/shard_map/ppermute | solution.py:332
  102.9 1.5 %all-to-all-done.3.col_ref = f32[8,72,128]{2,1,0:T(8,128)S(1)} async-done(((f32[8,72,128]{2,1,0:T(8,128)}), f32[8,72,128]{2,1,0:T(8,128)S(1)}, u32[]{:S(2)}, u32[]{:S(2)}) %all-to-all-start.3) | async-done | bytes 294944 | tf_op jit(solution)/shard_map/all_to_all | solution.py:336
  104.4 1.3 %finish.1 = (f32[256,256]{1,0:T(8,128)}, f32[4,128]{1,0:T(4,128)}) custom-call(f32[256,256]{1,0:T(8,128)S(1)} %bitcast.33, f32[1,256]{1,0:T(1,128)S(1)} %bitcast.43, f32[32,256]{1,0:T(8,128)S(1)} %bitcast.40, f32[256,256]{1,0:T(8,128)S(1)} %right.1.part_ref, f32[8,72,128]{2,1,0:T(8,128)S(1)} %all-to-all-done.3.col_ref), custom_call_target="tpu_custom_call" | custom-call | flops 25165824 | bytes 1117184 | tf_op jit(solution)/shard_map/finish/pallas_call | solution.py:312
  (51 shorter events, 7.2 us)
Async XLA Ops:
  2.9 6.1 %collective-permute-start = (f32[64,128]{1,0:T(8,128)}, f32[64,128]{1,0:T(8,128)S(1)}, u32[]{:S(2)}, u32[]{:S(2)}) collective-permute-start(f32[64,128]{1,0:T(8,128)} %project_right.1), channel_id=1, source_target_pairs={{0,64},{64,0},{128,192},{192,128},{1,65},{65,1},{129,193},{193,129... | collective-permute-start | bytes 98312 | tf_op jit(solution)/shard_map/ppermute | solution.py:332
  4.7 5.0 %collective-permute-start.1 = (f32[64,128]{1,0:T(8,128)}, f32[64,128]{1,0:T(8,128)S(1)}, u32[]{:S(2)}, u32[]{:S(2)}) collective-permute-start(f32[64,128]{1,0:T(8,128)} %project_right.1), channel_id=1, source_target_pairs={{0,128},{64,192},{128,0},{192,64},{1,129},{65,193},{129,1},{193,65... | collective-permute-start | bytes 98312 | tf_op jit(solution)/shard_map/ppermute | solution.py:332
  6.2 4.1 %collective-permute-start.2 = (f32[64,128]{1,0:T(8,128)}, f32[64,128]{1,0:T(8,128)S(1)}, u32[]{:S(2)}, u32[]{:S(2)}) collective-permute-start(f32[64,128]{1,0:T(8,128)} %project_right.1), channel_id=1, source_target_pairs={{0,192},{64,128},{128,64},{192,0},{1,193},{65,129},{129,65},{193,1... | collective-permute-start | bytes 98312 | tf_op jit(solution)/shard_map/ppermute | solution.py:332
  10.4 21.7 %all-to-all-start = ((f32[8,64,128]{2,1,0:T(8,128)}), f32[8,64,128]{2,1,0:T(8,128)}, u32[]{:S(2)}, u32[]{:S(2)}) async-start(f32[8,64,128]{2,1,0:T(8,128)} %project_left.1), calls=%async_computation | async-start | bytes 524288 | tf_op jit(solution)/shard_map/all_to_all | solution.py:336
  20.6 10.6 %collective-permute-start.3 = (f32[4,64,128]{2,1,0:T(8,128)S(1)}, f32[4,64,128]{2,1,0:T(8,128)S(1)}, u32[]{:S(2)}, u32[]{:S(2)}) collective-permute-start(f32[4,64,128]{2,1,0:T(8,128)S(1)} %pad_maximum_fusion.1.refs_0_), channel_id=1, source_target_pairs={{0,16},{16,0},{32,48},{48,32},{1,17},{17,1},{33,49},{49,33},{2,18}... | collective-permute-start | bytes 393224 | tf_op jit(solution)/shard_map/ppermute | solution.py:332
  22.1 9.0 %collective-permute-start.4 = (f32[4,64,128]{2,1,0:T(8,128)S(1)}, f32[4,64,128]{2,1,0:T(8,128)S(1)}, u32[]{:S(2)}, u32[]{:S(2)}) collective-permute-start(f32[4,64,128]{2,1,0:T(8,128)S(1)} %pad_maximum_fusion.1.refs_0_), channel_id=1, source_target_pairs={{0,32},{16,48},{32,0},{48,16},{1,33},{17,49},{33,1},{49,17},{2,34}... | collective-permute-start | bytes 393224 | tf_op jit(solution)/shard_map/ppermute | solution.py:332
  24.9 6.3 %collective-permute-start.5 = (f32[4,64,128]{2,1,0:T(8,128)S(1)}, f32[4,64,128]{2,1,0:T(8,128)S(1)}, u32[]{:S(2)}, u32[]{:S(2)}) collective-permute-start(f32[4,64,128]{2,1,0:T(8,128)S(1)} %pad_maximum_fusion.1.refs_0_), channel_id=1, source_target_pairs={{0,48},{16,32},{32,16},{48,0},{1,49},{17,33},{33,17},{49,1},{2,50}... | collective-permute-start | bytes 393224 | tf_op jit(solution)/shard_map/ppermute | solution.py:332
  32.0 17.5 %all-to-all-start.1 = ((f32[32,16,128]{2,1,0:T(8,128)}), f32[32,16,128]{2,1,0:T(8,128)S(1)}, u32[]{:S(2)}, u32[]{:S(2)}) async-start(f32[32,16,128]{2,1,0:T(8,128)} %bitcast.7), calls=%async_computation.1 | async-start | bytes 524288 | tf_op jit(solution)/shard_map/all_to_all | solution.py:336
  39.5 1.4 %collective-permute-start.6 = (f32[4,64,128]{2,1,0:T(8,128)S(1)}, f32[4,64,128]{2,1,0:T(8,128)S(1)}, u32[]{:S(2)}, u32[]{:S(2)}) collective-permute-start(f32[4,64,128]{2,1,0:T(8,128)S(1)} %pad_maximum_fusion.1.refs_0_), channel_id=1, source_target_pairs={{0,8},{8,0},{1,9},{9,1},{2,10},{10,2},{3,11},{11,3},{4,12},{12,4},... | collective-permute-start | bytes 393224 | tf_op jit(solution)/shard_map/ppermute | solution.py:328
  39.7 1.4 %collective-permute-start.7 = (f32[4,64,128]{2,1,0:T(8,128)S(1)}, f32[4,64,128]{2,1,0:T(8,128)S(1)}, u32[]{:S(2)}, u32[]{:S(2)}) collective-permute-start(f32[4,64,128]{2,1,0:T(8,128)S(1)} %collective-permute-done.3.refs_1_), channel_id=1, source_target_pairs={{0,8},{8,0},{1,9},{9,1},{2,10},{10,2},{3,11},{11,3},{4,12},{12,4},... | collective-permute-start | bytes 393224 | tf_op jit(solution)/shard_map/ppermute | solution.py:328
  40.1 1.3 %collective-permute-start.8 = (f32[4,64,128]{2,1,0:T(8,128)S(1)}, f32[4,64,128]{2,1,0:T(8,128)S(1)}, u32[]{:S(2)}, u32[]{:S(2)}) collective-permute-start(f32[4,64,128]{2,1,0:T(8,128)S(1)} %collective-permute-done.4.refs_2_), channel_id=1, source_target_pairs={{0,8},{8,0},{1,9},{9,1},{2,10},{10,2},{3,11},{11,3},{4,12},{12,4},... | collective-permute-start | bytes 393224 | tf_op jit(solution)/shard_map/ppermute | solution.py:328
  40.3 1.4 %collective-permute-start.9 = (f32[4,64,128]{2,1,0:T(8,128)S(1)}, f32[4,64,128]{2,1,0:T(8,128)S(1)}, u32[]{:S(2)}, u32[]{:S(2)}) collective-permute-start(f32[4,64,128]{2,1,0:T(8,128)S(1)} %collective-permute-done.5.refs_3_), channel_id=1, source_target_pairs={{0,8},{8,0},{1,9},{9,1},{2,10},{10,2},{3,11},{11,3},{4,12},{12,4},... | collective-permute-start | bytes 393224 | tf_op jit(solution)/shard_map/ppermute | solution.py:328
  44.7 1.6 %collective-permute-start.10 = (f32[256,128]{1,0:T(8,128)S(1)}, f32[256,128]{1,0:T(8,128)S(1)}, u32[]{:S(2)}, u32[]{:S(2)}) collective-permute-start(f32[256,128]{1,0:T(8,128)S(1)} %get-tuple-element.52), channel_id=1, source_target_pairs={{0,8},{8,0},{1,9},{9,1},{2,10},{10,2},{3,11},{11,3},{4,12},{12,4},... | collective-permute-start | bytes 393224 | tf_op jit(solution)/shard_map/ppermute | solution.py:328
  57.3 13.9 %copy-start.4 = (f32[1024,128]{1,0:T(8,128)S(1)}, f32[1024,128]{1,0:T(8,128)}, u32[]{:S(2)}) copy-start(f32[1024,128]{1,0:T(8,128)} %refs_9_.1) | copy-start | bytes 1572868
  57.3 13.9 %copy-start.5 = (f32[128]{0:T(128)S(1)}, f32[128]{0:T(128)}, u32[]{:S(2)}) copy-start(f32[128]{0:T(128)} %param.18) | copy-start | bytes 1540
  57.3 1.6 %collective-permute-start.11 = (f32[512,128]{1,0:T(8,128)S(1)}, f32[512,128]{1,0:T(8,128)S(1)}, u32[]{:S(2)}, u32[]{:S(2)}) collective-permute-start(f32[512,128]{1,0:T(8,128)S(1)} %get-tuple-element.55), channel_id=1, source_target_pairs={{0,8},{8,0},{1,9},{9,1},{2,10},{10,2},{3,11},{11,3},{4,12},{12,4},... | collective-permute-start | bytes 786440 | tf_op jit(solution)/shard_map/ppermute | solution.py:328
  59.8 20.8 %all-to-all-start.2 = ((f32[16,64,128]{2,1,0:T(8,128)}), f32[16,64,128]{2,1,0:T(8,128)S(1)}, u32[]{:S(2)}, u32[]{:S(2)}) async-start(f32[16,64,128]{2,1,0:T(8,128)} %pad_maximum_fusion), calls=%async_computation.2 | async-start | bytes 1048576 | tf_op jit(solution)/shard_map/all_to_all | solution.py:336
  64.6 1.3 %collective-permute-start.17 = (f32[4,64,128]{2,1,0:T(8,128)S(1)}, f32[4,64,128]{2,1,0:T(8,128)S(1)}, u32[]{:S(2)}, u32[]{:S(2)}) collective-permute-start(f32[4,64,128]{2,1,0:T(8,128)S(1)} %get-tuple-element.65), channel_id=1, source_target_pairs={{0,8},{8,0},{1,9},{9,1},{2,10},{10,2},{3,11},{11,3},{4,12},{12,4},... | collective-permute-start | bytes 393224 | tf_op jit(solution)/shard_map/ppermute | solution.py:328
  64.6 4.1 %collective-permute-start.13 = (f32[4,64,128]{2,1,0:T(8,128)S(1)}, f32[4,64,128]{2,1,0:T(8,128)S(1)}, u32[]{:S(2)}, u32[]{:S(2)}) collective-permute-start(f32[4,64,128]{2,1,0:T(8,128)S(1)} %get-tuple-element.61), channel_id=1, source_target_pairs={{0,8},{8,0},{1,9},{9,1},{2,10},{10,2},{3,11},{11,3},{4,12},{12,4},... | collective-permute-start | bytes 393224 | tf_op jit(solution)/shard_map/ppermute | solution.py:328
  65.1 4.0 %collective-permute-start.15 = (f32[4,64,128]{2,1,0:T(8,128)S(1)}, f32[4,64,128]{2,1,0:T(8,128)S(1)}, u32[]{:S(2)}, u32[]{:S(2)}) collective-permute-start(f32[4,64,128]{2,1,0:T(8,128)S(1)} %get-tuple-element.63), channel_id=1, source_target_pairs={{0,8},{8,0},{1,9},{9,1},{2,10},{10,2},{3,11},{11,3},{4,12},{12,4},... | collective-permute-start | bytes 393224 | tf_op jit(solution)/shard_map/ppermute | solution.py:328
  65.2 11.7 %collective-permute-start.12 = (f32[4,64,128]{2,1,0:T(8,128)S(1)}, f32[4,64,128]{2,1,0:T(8,128)S(1)}, u32[]{:S(2)}, u32[]{:S(2)}) collective-permute-start(f32[4,64,128]{2,1,0:T(8,128)S(1)} %get-tuple-element.59), channel_id=1, source_target_pairs={{0,8},{8,0},{1,9},{9,1},{2,10},{10,2},{3,11},{11,3},{4,12},{12,4},... | collective-permute-start | bytes 393224 | tf_op jit(solution)/shard_map/ppermute | solution.py:328
  65.9 10.9 %collective-permute-start.18 = (f32[4,64,128]{2,1,0:T(8,128)S(1)}, f32[4,64,128]{2,1,0:T(8,128)S(1)}, u32[]{:S(2)}, u32[]{:S(2)}) collective-permute-start(f32[4,64,128]{2,1,0:T(8,128)S(1)} %add.31), channel_id=1, source_target_pairs={{0,48},{16,32},{32,16},{48,0},{1,49},{17,33},{33,17},{49,1},{2,50}... | collective-permute-start | bytes 393224 | tf_op jit(solution)/shard_map/ppermute | solution.py:332
  68.7 8.1 %collective-permute-start.14 = (f32[4,64,128]{2,1,0:T(8,128)S(1)}, f32[4,64,128]{2,1,0:T(8,128)S(1)}, u32[]{:S(2)}, u32[]{:S(2)}) collective-permute-start(f32[4,64,128]{2,1,0:T(8,128)S(1)} %add.28), channel_id=1, source_target_pairs={{0,16},{16,0},{32,48},{48,32},{1,17},{17,1},{33,49},{49,33},{2,18}... | collective-permute-start | bytes 393224 | tf_op jit(solution)/shard_map/ppermute | solution.py:332
  69.1 11.5 %collective-permute-start.16 = (f32[4,64,128]{2,1,0:T(8,128)S(1)}, f32[4,64,128]{2,1,0:T(8,128)S(1)}, u32[]{:S(2)}, u32[]{:S(2)}) collective-permute-start(f32[4,64,128]{2,1,0:T(8,128)S(1)} %add.29), channel_id=1, source_target_pairs={{0,32},{16,48},{32,0},{48,16},{1,33},{17,49},{33,1},{49,17},{2,34}... | collective-permute-start | bytes 393224 | tf_op jit(solution)/shard_map/ppermute | solution.py:332
  76.8 25.7 %copy-start.1 = (f32[256,32]{0,1:T(8,128)S(1)}, f32[256,32]{0,1:T(8,128)}, u32[]{:S(2)}) copy-start(f32[256,32]{0,1:T(8,128)} %param.15) | copy-start | bytes 98308
  76.8 27.6 %copy-start = (f32[4,64,256]{2,1,0:T(8,128)S(1)}, f32[4,64,256]{2,1,0:T(8,128)}, u32[]{:S(2)}) copy-start(f32[4,64,256]{2,1,0:T(8,128)} %param.10) | copy-start | bytes 786436
  76.8 27.6 %copy-start.2 = (f32[256,32]{0,1:T(8,128)S(1)}, f32[256,32]{0,1:T(8,128)}, u32[]{:S(2)}) copy-start(f32[256,32]{0,1:T(8,128)} %param.13) | copy-start | bytes 98308
  76.8 27.6 %copy-start.3 = (f32[256]{0:T(256)S(1)}, f32[256]{0:T(256)}, u32[]{:S(2)}) copy-start(f32[256]{0:T(256)} %param.11) | copy-start | bytes 3076
  81.4 23.0 %all-to-all-start.3 = ((f32[8,72,128]{2,1,0:T(8,128)}), f32[8,72,128]{2,1,0:T(8,128)S(1)}, u32[]{:S(2)}, u32[]{:S(2)}) async-start(f32[8,72,128]{2,1,0:T(8,128)} %select_maximum_fusion), calls=%async_computation.3 | async-start | bytes 589824 | tf_op jit(solution)/shard_map/all_to_all | solution.py:336
  91.0 6.0 %collective-permute-start.19 = (f32[64,128]{1,0:T(8,128)S(1)}, f32[64,128]{1,0:T(8,128)S(1)}, u32[]{:S(2)}, u32[]{:S(2)}) collective-permute-start(f32[64,128]{1,0:T(8,128)S(1)} %get-tuple-element.75), channel_id=1, source_target_pairs={{0,64},{64,0},{128,192},{192,128},{1,65},{65,1},{129,193},{193,129... | collective-permute-start | bytes 98312 | tf_op jit(solution)/shard_map/ppermute | solution.py:332
  91.1 8.9 %collective-permute-start.20 = (f32[64,128]{1,0:T(8,128)S(1)}, f32[64,128]{1,0:T(8,128)S(1)}, u32[]{:S(2)}, u32[]{:S(2)}) collective-permute-start(f32[64,128]{1,0:T(8,128)S(1)} %get-tuple-element.74), channel_id=1, source_target_pairs={{0,128},{64,192},{128,0},{192,64},{1,129},{65,193},{129,1},{193,65... | collective-permute-start | bytes 98312 | tf_op jit(solution)/shard_map/ppermute | solution.py:332
  93.6 8.8 %collective-permute-start.21 = (f32[64,128]{1,0:T(8,128)S(1)}, f32[64,128]{1,0:T(8,128)S(1)}, u32[]{:S(2)}, u32[]{:S(2)}) collective-permute-start(f32[64,128]{1,0:T(8,128)S(1)} %get-tuple-element.73), channel_id=1, source_target_pairs={{0,192},{64,128},{128,64},{192,0},{1,193},{65,129},{129,65},{193,1... | collective-permute-start | bytes 98312 | tf_op jit(solution)/shard_map/ppermute | solution.py:332

commit v10 on v9

--- a/solution.py
+++ b/solution.py
@@ -446,8 +446,9 @@
     weight = (own + got).reshape(16, BWD, 128)
     sent = [weight, own_left.reshape(16, 16, 128), got_left.reshape(16, 16, 128)]
     back = exchange(jnp.concatenate(sent, axis=1), CHIP)
-    sums = [a + swap_cores(b) for a, b in zip(sums[:4], sums[4:])]
-    right = sums[0] + sum(from_peer(sums[dx], "x", dx) for dx in (1, 2, 3))
+    order = (0, 2, 3, 1)
+    sums = [sums[dx] + swap_cores(sums[4 + dx]) for dx in order]
+    right = sums[0] + sum(from_peer(sums[k], "x", order[k]) for k in (1, 2, 3))
     (pair,) = call(
         pair_kernel,
         "pair",
@@ -467,7 +468,7 @@
     )
     sent, right, pair = lax.optimization_barrier((sent, right, pair))
     cols = exchange(sent, COL)
-    right = [right[0]] + [from_peer(right[dz], "zl", dz) for dz in (1, 2, 3)]
+    right = [right[0]] + [from_peer(right[dz], "zl", dz) for dz in (3, 2, 1)]
     (part,) = call(right_kernel, "right", [((256, 256), f32)], [], 8, small, w2, *right)
     grad, weight = call(
         finish_kernel,

time: 107 us -> 109 us (1.019)
  waiting for transfers between devices: 22.2 us -> 24.5 us
    all_to_all x4, waiting for transfers between devices: 5.55 us -> 9.78 us  [exchange(): return lax.all_to_all(array, axes, 0, 0, tiled=True)]
    ppermute x12, waiting for transfers between devices: 13 us -> 11.1 us  [from_peer(): return lax.ppermute(array, axis, [(i, i ^ apart) for i in range(4)])]
where the time goes in v10:
time: 109 us; the launch traced here: 108 us
  starting transfers between devices  51.6 us (47%)
  Pallas kernels  28.5 us (26%)
  waiting for transfers between devices  24.5 us (22%)
  other arithmetic  2.5 us (2%)
    all_to_all x4, starting transfers between devices, exchange(): return lax.all_to_all(array, axes, 0, 0, tiled=True)  31.1 us
    pallas_call x8, Pallas kernels, call(): pl.pallas_call(kernel, out_shape=shapes, in_specs=[VMEM] * len(args) + [H...  28.5 us
    ppermute x12, starting transfers between devices, from_peer(): return lax.ppermute(array, axis, [(i, i ^ apart) for i in range(4)])  17.4 us
    ppermute x12, waiting for transfers between devices, from_peer(): return lax.ppermute(array, axis, [(i, i ^ apart) for i in range(4)])  11.1 us
    all_to_all x4, waiting for transfers between devices, exchange(): return lax.all_to_all(array, axes, 0, 0, tiled=True)  9.78 us
    ppermute x10, waiting for transfers between devices, swap_cores(): return lax.ppermute(array, 'core', [(0, 1), (1, 0)])  3.64 us
    ppermute x10, starting transfers between devices, swap_cores(): return lax.ppermute(array, 'core', [(0, 1), (1, 0)])  3.07 us
  transfers between devices with their start and end apart: 26, of which 16 were waited for; matrix products, arithmetic and copies ran while one was open for 1% of the time, Pallas kernels for 16%

profile of v10, /device:TPU:32, one launch (start us, length us, event | category | flops | bytes accessed | tf_op | source)
XLA Modules:
  0.0 108.0 jit_solution(8194019642806804282)
XLA Ops:
  0.6 2.2 %project_right.1 = f32[64,128]{1,0:T(8,128)} custom-call(f32[256,256]{1,0:T(8,128)} %bitcast.31, f32[1,256]{1,0:T(1,128)} %bitcast.41, f32[1,256]{1,0:T(1,128)} %bitcast.54, f32[32,256]{1,0:T(8,128)} %bitcast.36, f32[1,32]{1,0:T(1,128)} %bitcast.56), custom_call_target="tpu_custom_call" | custom-call | flops 25165824 | bytes 329856 | tf_op jit(solution)/shard_map/project_right/pallas_call | solution.py:312
  2.9 1.8 %collective-permute-start = (f32[64,128]{1,0:T(8,128)}, f32[64,128]{1,0:T(8,128)S(1)}, u32[]{:S(2)}, u32[]{:S(2)}) collective-permute-start(f32[64,128]{1,0:T(8,128)} %project_right.1), channel_id=1, source_target_pairs={{0,64},{64,0},{128,192},{192,128},{1,65},{65,1},{129,193},{193,129... | collective-permute-start | bytes 98312 | tf_op jit(solution)/shard_map/ppermute | solution.py:332
  4.7 1.5 %collective-permute-start.1 = (f32[64,128]{1,0:T(8,128)}, f32[64,128]{1,0:T(8,128)S(1)}, u32[]{:S(2)}, u32[]{:S(2)}) collective-permute-start(f32[64,128]{1,0:T(8,128)} %project_right.1), channel_id=1, source_target_pairs={{0,128},{64,192},{128,0},{192,64},{1,129},{65,193},{129,1},{193,65... | collective-permute-start | bytes 98312 | tf_op jit(solution)/shard_map/ppermute | solution.py:332
  6.7 2.3 %project_left.1 = f32[8,64,128]{2,1,0:T(8,128)} custom-call(f32[256,256]{1,0:T(8,128)} %bitcast.32, f32[1,256]{1,0:T(1,128)} %bitcast.42, f32[1,256]{1,0:T(1,128)} %bitcast.55, f32[32,256]{1,0:T(8,128)} %bitcast.39, f32[1,32]{1,0:T(1,128)} %bitcast.57), custom_call_target="tpu_custom_call" | custom-call | flops 25165824 | bytes 559232 | tf_op jit(solution)/shard_map/project_left/pallas_call | solution.py:312
  10.4 9.4 %all-to-all-start = ((f32[8,64,128]{2,1,0:T(8,128)}), f32[8,64,128]{2,1,0:T(8,128)}, u32[]{:S(2)}, u32[]{:S(2)}) async-start(f32[8,64,128]{2,1,0:T(8,128)} %project_left.1), calls=%async_computation | async-start | bytes 524288 | tf_op jit(solution)/shard_map/all_to_all | solution.py:336
  19.8 0.8 pad_maximum_fusion.1.refs_0_
  20.6 1.6 %collective-permute-start.3 = (f32[4,64,128]{2,1,0:T(8,128)S(1)}, f32[4,64,128]{2,1,0:T(8,128)S(1)}, u32[]{:S(2)}, u32[]{:S(2)}) collective-permute-start(f32[4,64,128]{2,1,0:T(8,128)S(1)} %pad_maximum_fusion.1.refs_0_), channel_id=1, source_target_pairs={{0,16},{16,0},{32,48},{48,32},{1,17},{17,1},{33,49},{49,33},{2,18}... | collective-permute-start | bytes 393224 | tf_op jit(solution)/shard_map/ppermute | solution.py:332
  22.1 2.7 %collective-permute-start.4 = (f32[4,64,128]{2,1,0:T(8,128)S(1)}, f32[4,64,128]{2,1,0:T(8,128)S(1)}, u32[]{:S(2)}, u32[]{:S(2)}) collective-permute-start(f32[4,64,128]{2,1,0:T(8,128)S(1)} %pad_maximum_fusion.1.refs_0_), channel_id=1, source_target_pairs={{0,32},{16,48},{32,0},{48,16},{1,33},{17,49},{33,1},{49,17},{2,34}... | collective-permute-start | bytes 393224 | tf_op jit(solution)/shard_map/ppermute | solution.py:332
  25.3 5.8 %cotangent.1 = (bf16[4,512,512]{2,1,0:T(8,128)(2,1)}, bf16[4,512,512]{2,1,0:T(8,128)(2,1)}) custom-call(f32[1024,128]{1,0:T(8,128)} %refs_9_.1, f32[16,64,128]{2,1,0:T(8,128)} %refs_10_.1), custom_call_target="tpu_custom_call" | custom-call | flops 805306368 | bytes 5242880 | tf_op jit(solution)/shard_map/cotangent/pallas_call | solution.py:312
  31.2 0.9 all-to-all-done
  32.0 7.5 %all-to-all-start.1 = ((f32[32,16,128]{2,1,0:T(8,128)}), f32[32,16,128]{2,1,0:T(8,128)S(1)}, u32[]{:S(2)}, u32[]{:S(2)}) async-start(f32[32,16,128]{2,1,0:T(8,128)} %bitcast.7), calls=%async_computation.1 | async-start | bytes 524288 | tf_op jit(solution)/shard_map/all_to_all | solution.py:336
  41.6 3.1 %left_gradient.1 = (f32[256,128]{1,0:T(8,128)S(1)}, f32[256,128]{1,0:T(8,128)S(1)}) custom-call(f32[4,64,128]{2,1,0:T(8,128)S(1)} %pad_maximum_fusion.1.refs_0_, f32[4,64,128]{2,1,0:T(8,128)S(1)} %collective-permute-done.3.refs_1_, f32[4,64,128]{2,1,0:T(8,128)S(1)} %collective-permute-done.4.refs_2_, f32[4,64,128]{2,1,0:T(8,128)S(1)} %collective-permute-done.5.refs_3_, ...), custom_call_target="tpu_custom_call" | custom-call | flops 805306368 | bytes 5505024 | tf_op jit(solution)/shard_map/left_gradient/pallas_call | solution.py:312
  45.3 1.0 collective-permute-done.10
  46.4 3.2 %all-to-all-done.1 = f32[32,16,128]{2,1,0:T(8,128)S(1)} async-done(((f32[32,16,128]{2,1,0:T(8,128)}), f32[32,16,128]{2,1,0:T(8,128)S(1)}, u32[]{:S(2)}, u32[]{:S(2)}) %all-to-all-start.1) | async-done | bytes 262176 | tf_op jit(solution)/shard_map/all_to_all | solution.py:336
  49.6 7.7 %tile.1 = (f32[512,128]{1,0:T(8,128)S(1)}, f32[512,128]{1,0:T(8,128)S(1)}, f32[4,64,128]{2,1,0:T(8,128)S(1)}, f32[4,64,128]{2,1,0:T(8,128)S(1)}, f32[4,64,128]{2...) custom-call(f32[512,128]{1,0:T(8,128)S(1)} %bitcast.34, ...), custom_call_target="tpu_custom_call" | custom-call | flops 2415919104 | bytes 7602176 | tf_op jit(solution)/shard_map/tile/pallas_call | solution.py:312
  57.7 1.3 %collective-permute-done.11 = f32[512,128]{1,0:T(8,128)S(1)} collective-permute-done((f32[512,128]{1,0:T(8,128)S(1)}, f32[512,128]{1,0:T(8,128)S(1)}, u32[]{:S(2)}, u32[]{:S(2)}) %collective-permute-start.11) | collective-permute-done | bytes 262176 | tf_op jit(solution)/shard_map/ppermute | solution.py:328
  59.0 0.8 pad_maximum_fusion
  59.8 4.8 %all-to-all-start.2 = ((f32[16,64,128]{2,1,0:T(8,128)}), f32[16,64,128]{2,1,0:T(8,128)S(1)}, u32[]{:S(2)}, u32[]{:S(2)}) async-start(f32[16,64,128]{2,1,0:T(8,128)} %pad_maximum_fusion), calls=%async_computation.2 | async-start | bytes 1048576 | tf_op jit(solution)/shard_map/all_to_all | solution.py:336
  65.9 1.5 %collective-permute-start.18 = (f32[4,64,128]{2,1,0:T(8,128)S(1)}, f32[4,64,128]{2,1,0:T(8,128)S(1)}, u32[]{:S(2)}, u32[]{:S(2)}) collective-permute-start(f32[4,64,128]{2,1,0:T(8,128)S(1)} %add.31), channel_id=1, source_target_pairs={{0,16},{16,0},{32,48},{48,32},{1,17},{17,1},{33,49},{49,33},{2,18}... | collective-permute-start | bytes 393224 | tf_op jit(solution)/shard_map/ppermute | solution.py:332
  67.5 2.8 %collective-permute-start.14 = (f32[4,64,128]{2,1,0:T(8,128)S(1)}, f32[4,64,128]{2,1,0:T(8,128)S(1)}, u32[]{:S(2)}, u32[]{:S(2)}) collective-permute-start(f32[4,64,128]{2,1,0:T(8,128)S(1)} %add.28), channel_id=1, source_target_pairs={{0,32},{16,48},{32,0},{48,16},{1,33},{17,49},{33,1},{49,17},{2,34}... | collective-permute-start | bytes 393224 | tf_op jit(solution)/shard_map/ppermute | solution.py:332
  70.3 0.9 collective-permute-start.16
  71.2 5.6 %pair.1 = f32[16,64,128]{2,1,0:T(8,128)} custom-call(f32[512,128]{1,0:T(8,128)S(1)} %bitcast.35, f32[4,64,128]{2,1,0:T(8,128)S(1)} %pad_maximum_fusion.1.refs_0_, f32[4,64,128]{2,1,0:T(8,128)S(1)} %collective-permute-done.3.refs_1_, f32[4,64,128]{2,1,0:T(8,128)S(1)} %collective-permute-done.4.refs_2_, f32[4,64,128]{2,1,0:T(8,128)S(1)} %collective-permute-done.5.refs_3_, ...), custom_call_target="tpu_custom_call" | custom-call | flops 1610612736 | bytes 2359808 | tf_op jit(solution)/shard_map/pair/pallas_call | solution.py:312
  76.9 3.7 %collective-permute-done.14 = f32[4,64,128]{2,1,0:T(8,128)S(1)} collective-permute-done((f32[4,64,128]{2,1,0:T(8,128)S(1)}, f32[4,64,128]{2,1,0:T(8,128)S(1)}, u32[]{:S(2)}, u32[]{:S(2)}) %collective-permute-start.14) | collective-permute-done | bytes 131104 | tf_op jit(solution)/shard_map/ppermute | solution.py:332
  80.5 1.5 %collective-permute-done.16 = f32[4,64,128]{2,1,0:T(8,128)S(1)} collective-permute-done((f32[4,64,128]{2,1,0:T(8,128)S(1)}, f32[4,64,128]{2,1,0:T(8,128)S(1)}, u32[]{:S(2)}, u32[]{:S(2)}) %collective-permute-start.16) | collective-permute-done | bytes 131104 | tf_op jit(solution)/shard_map/ppermute | solution.py:332
  82.9 9.5 %all-to-all-start.3 = ((f32[8,72,128]{2,1,0:T(8,128)}), f32[8,72,128]{2,1,0:T(8,128)S(1)}, u32[]{:S(2)}, u32[]{:S(2)}) async-start(f32[8,72,128]{2,1,0:T(8,128)} %select_maximum_fusion), calls=%async_computation.3 | async-start | bytes 589824 | tf_op jit(solution)/shard_map/all_to_all | solution.py:336
  92.4 1.3 %collective-permute-start.19 = (f32[64,128]{1,0:T(8,128)S(1)}, f32[64,128]{1,0:T(8,128)S(1)}, u32[]{:S(2)}, u32[]{:S(2)}) collective-permute-start(f32[64,128]{1,0:T(8,128)S(1)} %get-tuple-element.75), channel_id=1, source_target_pairs={{0,192},{64,128},{128,64},{192,0},{1,193},{65,129},{129,65},{193,1... | collective-permute-start | bytes 98312 | tf_op jit(solution)/shard_map/ppermute | solution.py:332
  93.7 1.3 %collective-permute-start.20 = (f32[64,128]{1,0:T(8,128)S(1)}, f32[64,128]{1,0:T(8,128)S(1)}, u32[]{:S(2)}, u32[]{:S(2)}) collective-permute-start(f32[64,128]{1,0:T(8,128)S(1)} %get-tuple-element.74), channel_id=1, source_target_pairs={{0,128},{64,192},{128,0},{192,64},{1,129},{65,193},{129,1},{193,65... | collective-permute-start | bytes 98312 | tf_op jit(solution)/shard_map/ppermute | solution.py:332
  95.0 1.0 collective-permute-start.21
  96.0 2.8 %collective-permute-done.19.b_ref = f32[64,128]{1,0:T(8,128)S(1)} collective-permute-done((f32[64,128]{1,0:T(8,128)S(1)}, f32[64,128]{1,0:T(8,128)S(1)}, u32[]{:S(2)}, u32[]{:S(2)}) %collective-permute-start.19) | collective-permute-done | bytes 32800 | tf_op jit(solution)/shard_map/ppermute | solution.py:332
  98.8 1.7 %collective-permute-done.21.d_ref = f32[64,128]{1,0:T(8,128)S(1)} collective-permute-done((f32[64,128]{1,0:T(8,128)S(1)}, f32[64,128]{1,0:T(8,128)S(1)}, u32[]{:S(2)}, u32[]{:S(2)}) %collective-permute-start.21) | collective-permute-done | bytes 32800 | tf_op jit(solution)/shard_map/ppermute | solution.py:332
  101.0 5.7 %all-to-all-done.3.col_ref = f32[8,72,128]{2,1,0:T(8,128)S(1)} async-done(((f32[8,72,128]{2,1,0:T(8,128)}), f32[8,72,128]{2,1,0:T(8,128)S(1)}, u32[]{:S(2)}, u32[]{:S(2)}) %all-to-all-start.3) | async-done | bytes 294944 | tf_op jit(solution)/shard_map/all_to_all | solution.py:336
  106.7 1.3 %finish.1 = (f32[256,256]{1,0:T(8,128)}, f32[4,128]{1,0:T(4,128)}) custom-call(f32[256,256]{1,0:T(8,128)S(1)} %bitcast.33, f32[1,256]{1,0:T(1,128)S(1)} %bitcast.43, f32[32,256]{1,0:T(8,128)S(1)} %bitcast.40, f32[256,256]{1,0:T(8,128)S(1)} %right.1.part_ref, f32[8,72,128]{2,1,0:T(8,128)S(1)} %all-to-all-done.3.col_ref), custom_call_target="tpu_custom_call" | custom-call | flops 25165824 | bytes 1117184 | tf_op jit(solution)/shard_map/finish/pallas_call | solution.py:312
  (51 shorter events, 8.2 us)
Async XLA Ops:
  2.9 6.1 %collective-permute-start = (f32[64,128]{1,0:T(8,128)}, f32[64,128]{1,0:T(8,128)S(1)}, u32[]{:S(2)}, u32[]{:S(2)}) collective-permute-start(f32[64,128]{1,0:T(8,128)} %project_right.1), channel_id=1, source_target_pairs={{0,64},{64,0},{128,192},{192,128},{1,65},{65,1},{129,193},{193,129... | collective-permute-start | bytes 98312 | tf_op jit(solution)/shard_map/ppermute | solution.py:332
  4.7 5.0 %collective-permute-start.1 = (f32[64,128]{1,0:T(8,128)}, f32[64,128]{1,0:T(8,128)S(1)}, u32[]{:S(2)}, u32[]{:S(2)}) collective-permute-start(f32[64,128]{1,0:T(8,128)} %project_right.1), channel_id=1, source_target_pairs={{0,128},{64,192},{128,0},{192,64},{1,129},{65,193},{129,1},{193,65... | collective-permute-start | bytes 98312 | tf_op jit(solution)/shard_map/ppermute | solution.py:332
  6.2 4.1 %collective-permute-start.2 = (f32[64,128]{1,0:T(8,128)}, f32[64,128]{1,0:T(8,128)S(1)}, u32[]{:S(2)}, u32[]{:S(2)}) collective-permute-start(f32[64,128]{1,0:T(8,128)} %project_right.1), channel_id=1, source_target_pairs={{0,192},{64,128},{128,64},{192,0},{1,193},{65,129},{129,65},{193,1... | collective-permute-start | bytes 98312 | tf_op jit(solution)/shard_map/ppermute | solution.py:332
  10.4 21.7 %all-to-all-start = ((f32[8,64,128]{2,1,0:T(8,128)}), f32[8,64,128]{2,1,0:T(8,128)}, u32[]{:S(2)}, u32[]{:S(2)}) async-start(f32[8,64,128]{2,1,0:T(8,128)} %project_left.1), calls=%async_computation | async-start | bytes 524288 | tf_op jit(solution)/shard_map/all_to_all | solution.py:336
  20.6 10.6 %collective-permute-start.3 = (f32[4,64,128]{2,1,0:T(8,128)S(1)}, f32[4,64,128]{2,1,0:T(8,128)S(1)}, u32[]{:S(2)}, u32[]{:S(2)}) collective-permute-start(f32[4,64,128]{2,1,0:T(8,128)S(1)} %pad_maximum_fusion.1.refs_0_), channel_id=1, source_target_pairs={{0,16},{16,0},{32,48},{48,32},{1,17},{17,1},{33,49},{49,33},{2,18}... | collective-permute-start | bytes 393224 | tf_op jit(solution)/shard_map/ppermute | solution.py:332
  22.1 9.0 %collective-permute-start.4 = (f32[4,64,128]{2,1,0:T(8,128)S(1)}, f32[4,64,128]{2,1,0:T(8,128)S(1)}, u32[]{:S(2)}, u32[]{:S(2)}) collective-permute-start(f32[4,64,128]{2,1,0:T(8,128)S(1)} %pad_maximum_fusion.1.refs_0_), channel_id=1, source_target_pairs={{0,32},{16,48},{32,0},{48,16},{1,33},{17,49},{33,1},{49,17},{2,34}... | collective-permute-start | bytes 393224 | tf_op jit(solution)/shard_map/ppermute | solution.py:332
  24.9 6.3 %collective-permute-start.5 = (f32[4,64,128]{2,1,0:T(8,128)S(1)}, f32[4,64,128]{2,1,0:T(8,128)S(1)}, u32[]{:S(2)}, u32[]{:S(2)}) collective-permute-start(f32[4,64,128]{2,1,0:T(8,128)S(1)} %pad_maximum_fusion.1.refs_0_), channel_id=1, source_target_pairs={{0,48},{16,32},{32,16},{48,0},{1,49},{17,33},{33,17},{49,1},{2,50}... | collective-permute-start | bytes 393224 | tf_op jit(solution)/shard_map/ppermute | solution.py:332
  32.0 17.5 %all-to-all-start.1 = ((f32[32,16,128]{2,1,0:T(8,128)}), f32[32,16,128]{2,1,0:T(8,128)S(1)}, u32[]{:S(2)}, u32[]{:S(2)}) async-start(f32[32,16,128]{2,1,0:T(8,128)} %bitcast.7), calls=%async_computation.1 | async-start | bytes 524288 | tf_op jit(solution)/shard_map/all_to_all | solution.py:336
  39.5 1.4 %collective-permute-start.6 = (f32[4,64,128]{2,1,0:T(8,128)S(1)}, f32[4,64,128]{2,1,0:T(8,128)S(1)}, u32[]{:S(2)}, u32[]{:S(2)}) collective-permute-start(f32[4,64,128]{2,1,0:T(8,128)S(1)} %pad_maximum_fusion.1.refs_0_), channel_id=1, source_target_pairs={{0,8},{8,0},{1,9},{9,1},{2,10},{10,2},{3,11},{11,3},{4,12},{12,4},... | collective-permute-start | bytes 393224 | tf_op jit(solution)/shard_map/ppermute | solution.py:328
  39.7 1.4 %collective-permute-start.7 = (f32[4,64,128]{2,1,0:T(8,128)S(1)}, f32[4,64,128]{2,1,0:T(8,128)S(1)}, u32[]{:S(2)}, u32[]{:S(2)}) collective-permute-start(f32[4,64,128]{2,1,0:T(8,128)S(1)} %collective-permute-done.3.refs_1_), channel_id=1, source_target_pairs={{0,8},{8,0},{1,9},{9,1},{2,10},{10,2},{3,11},{11,3},{4,12},{12,4},... | collective-permute-start | bytes 393224 | tf_op jit(solution)/shard_map/ppermute | solution.py:328
  40.1 1.3 %collective-permute-start.8 = (f32[4,64,128]{2,1,0:T(8,128)S(1)}, f32[4,64,128]{2,1,0:T(8,128)S(1)}, u32[]{:S(2)}, u32[]{:S(2)}) collective-permute-start(f32[4,64,128]{2,1,0:T(8,128)S(1)} %collective-permute-done.4.refs_2_), channel_id=1, source_target_pairs={{0,8},{8,0},{1,9},{9,1},{2,10},{10,2},{3,11},{11,3},{4,12},{12,4},... | collective-permute-start | bytes 393224 | tf_op jit(solution)/shard_map/ppermute | solution.py:328
  40.3 1.4 %collective-permute-start.9 = (f32[4,64,128]{2,1,0:T(8,128)S(1)}, f32[4,64,128]{2,1,0:T(8,128)S(1)}, u32[]{:S(2)}, u32[]{:S(2)}) collective-permute-start(f32[4,64,128]{2,1,0:T(8,128)S(1)} %collective-permute-done.5.refs_3_), channel_id=1, source_target_pairs={{0,8},{8,0},{1,9},{9,1},{2,10},{10,2},{3,11},{11,3},{4,12},{12,4},... | collective-permute-start | bytes 393224 | tf_op jit(solution)/shard_map/ppermute | solution.py:328
  44.7 1.6 %collective-permute-start.10 = (f32[256,128]{1,0:T(8,128)S(1)}, f32[256,128]{1,0:T(8,128)S(1)}, u32[]{:S(2)}, u32[]{:S(2)}) collective-permute-start(f32[256,128]{1,0:T(8,128)S(1)} %get-tuple-element.52), channel_id=1, source_target_pairs={{0,8},{8,0},{1,9},{9,1},{2,10},{10,2},{3,11},{11,3},{4,12},{12,4},... | collective-permute-start | bytes 393224 | tf_op jit(solution)/shard_map/ppermute | solution.py:328
  57.3 13.9 %copy-start.4 = (f32[1024,128]{1,0:T(8,128)S(1)}, f32[1024,128]{1,0:T(8,128)}, u32[]{:S(2)}) copy-start(f32[1024,128]{1,0:T(8,128)} %refs_9_.1) | copy-start | bytes 1572868
  57.3 13.9 %copy-start.5 = (f32[128]{0:T(128)S(1)}, f32[128]{0:T(128)}, u32[]{:S(2)}) copy-start(f32[128]{0:T(128)} %param.18) | copy-start | bytes 1540
  57.3 1.6 %collective-permute-start.11 = (f32[512,128]{1,0:T(8,128)S(1)}, f32[512,128]{1,0:T(8,128)S(1)}, u32[]{:S(2)}, u32[]{:S(2)}) collective-permute-start(f32[512,128]{1,0:T(8,128)S(1)} %get-tuple-element.55), channel_id=1, source_target_pairs={{0,8},{8,0},{1,9},{9,1},{2,10},{10,2},{3,11},{11,3},{4,12},{12,4},... | collective-permute-start | bytes 786440 | tf_op jit(solution)/shard_map/ppermute | solution.py:328
  59.8 22.3 %all-to-all-start.2 = ((f32[16,64,128]{2,1,0:T(8,128)}), f32[16,64,128]{2,1,0:T(8,128)S(1)}, u32[]{:S(2)}, u32[]{:S(2)}) async-start(f32[16,64,128]{2,1,0:T(8,128)} %pad_maximum_fusion), calls=%async_computation.2 | async-start | bytes 1048576 | tf_op jit(solution)/shard_map/all_to_all | solution.py:336
  64.6 1.3 %collective-permute-start.17 = (f32[4,64,128]{2,1,0:T(8,128)S(1)}, f32[4,64,128]{2,1,0:T(8,128)S(1)}, u32[]{:S(2)}, u32[]{:S(2)}) collective-permute-start(f32[4,64,128]{2,1,0:T(8,128)S(1)} %get-tuple-element.65), channel_id=1, source_target_pairs={{0,8},{8,0},{1,9},{9,1},{2,10},{10,2},{3,11},{11,3},{4,12},{12,4},... | collective-permute-start | bytes 393224 | tf_op jit(solution)/shard_map/ppermute | solution.py:328
  64.6 2.9 %collective-permute-start.13 = (f32[4,64,128]{2,1,0:T(8,128)S(1)}, f32[4,64,128]{2,1,0:T(8,128)S(1)}, u32[]{:S(2)}, u32[]{:S(2)}) collective-permute-start(f32[4,64,128]{2,1,0:T(8,128)S(1)} %get-tuple-element.61), channel_id=1, source_target_pairs={{0,8},{8,0},{1,9},{9,1},{2,10},{10,2},{3,11},{11,3},{4,12},{12,4},... | collective-permute-start | bytes 393224 | tf_op jit(solution)/shard_map/ppermute | solution.py:328
  65.1 5.2 %collective-permute-start.15 = (f32[4,64,128]{2,1,0:T(8,128)S(1)}, f32[4,64,128]{2,1,0:T(8,128)S(1)}, u32[]{:S(2)}, u32[]{:S(2)}) collective-permute-start(f32[4,64,128]{2,1,0:T(8,128)S(1)} %get-tuple-element.63), channel_id=1, source_target_pairs={{0,8},{8,0},{1,9},{9,1},{2,10},{10,2},{3,11},{11,3},{4,12},{12,4},... | collective-permute-start | bytes 393224 | tf_op jit(solution)/shard_map/ppermute | solution.py:328
  65.2 11.7 %collective-permute-start.12 = (f32[4,64,128]{2,1,0:T(8,128)S(1)}, f32[4,64,128]{2,1,0:T(8,128)S(1)}, u32[]{:S(2)}, u32[]{:S(2)}) collective-permute-start(f32[4,64,128]{2,1,0:T(8,128)S(1)} %get-tuple-element.59), channel_id=1, source_target_pairs={{0,8},{8,0},{1,9},{9,1},{2,10},{10,2},{3,11},{11,3},{4,12},{12,4},... | collective-permute-start | bytes 393224 | tf_op jit(solution)/shard_map/ppermute | solution.py:328
  65.9 10.9 %collective-permute-start.18 = (f32[4,64,128]{2,1,0:T(8,128)S(1)}, f32[4,64,128]{2,1,0:T(8,128)S(1)}, u32[]{:S(2)}, u32[]{:S(2)}) collective-permute-start(f32[4,64,128]{2,1,0:T(8,128)S(1)} %add.31), channel_id=1, source_target_pairs={{0,16},{16,0},{32,48},{48,32},{1,17},{17,1},{33,49},{49,33},{2,18}... | collective-permute-start | bytes 393224 | tf_op jit(solution)/shard_map/ppermute | solution.py:332
  67.5 13.0 %collective-permute-start.14 = (f32[4,64,128]{2,1,0:T(8,128)S(1)}, f32[4,64,128]{2,1,0:T(8,128)S(1)}, u32[]{:S(2)}, u32[]{:S(2)}) collective-permute-start(f32[4,64,128]{2,1,0:T(8,128)S(1)} %add.28), channel_id=1, source_target_pairs={{0,32},{16,48},{32,0},{48,16},{1,33},{17,49},{33,1},{49,17},{2,34}... | collective-permute-start | bytes 393224 | tf_op jit(solution)/shard_map/ppermute | solution.py:332
  70.3 11.8 %collective-permute-start.16 = (f32[4,64,128]{2,1,0:T(8,128)S(1)}, f32[4,64,128]{2,1,0:T(8,128)S(1)}, u32[]{:S(2)}, u32[]{:S(2)}) collective-permute-start(f32[4,64,128]{2,1,0:T(8,128)S(1)} %add.29), channel_id=1, source_target_pairs={{0,48},{16,32},{32,16},{48,0},{1,49},{17,33},{33,17},{49,1},{2,50}... | collective-permute-start | bytes 393224 | tf_op jit(solution)/shard_map/ppermute | solution.py:332
  76.8 23.7 %copy-start.1 = (f32[256,32]{0,1:T(8,128)S(1)}, f32[256,32]{0,1:T(8,128)}, u32[]{:S(2)}) copy-start(f32[256,32]{0,1:T(8,128)} %param.15) | copy-start | bytes 98308
  76.8 29.9 %copy-start = (f32[4,64,256]{2,1,0:T(8,128)S(1)}, f32[4,64,256]{2,1,0:T(8,128)}, u32[]{:S(2)}) copy-start(f32[4,64,256]{2,1,0:T(8,128)} %param.10) | copy-start | bytes 786436
  76.8 29.9 %copy-start.2 = (f32[256,32]{0,1:T(8,128)S(1)}, f32[256,32]{0,1:T(8,128)}, u32[]{:S(2)}) copy-start(f32[256,32]{0,1:T(8,128)} %param.13) | copy-start | bytes 98308
  76.8 29.9 %copy-start.3 = (f32[256]{0:T(256)S(1)}, f32[256]{0:T(256)}, u32[]{:S(2)}) copy-start(f32[256]{0:T(256)} %param.11) | copy-start | bytes 3076
  82.9 23.8 %all-to-all-start.3 = ((f32[8,72,128]{2,1,0:T(8,128)}), f32[8,72,128]{2,1,0:T(8,128)S(1)}, u32[]{:S(2)}, u32[]{:S(2)}) async-start(f32[8,72,128]{2,1,0:T(8,128)} %select_maximum_fusion), calls=%async_computation.3 | async-start | bytes 589824 | tf_op jit(solution)/shard_map/all_to_all | solution.py:336
  92.4 6.4 %collective-permute-start.19 = (f32[64,128]{1,0:T(8,128)S(1)}, f32[64,128]{1,0:T(8,128)S(1)}, u32[]{:S(2)}, u32[]{:S(2)}) collective-permute-start(f32[64,128]{1,0:T(8,128)S(1)} %get-tuple-element.75), channel_id=1, source_target_pairs={{0,192},{64,128},{128,64},{192,0},{1,193},{65,129},{129,65},{193,1... | collective-permute-start | bytes 98312 | tf_op jit(solution)/shard_map/ppermute | solution.py:332
  93.7 5.1 %collective-permute-start.20 = (f32[64,128]{1,0:T(8,128)S(1)}, f32[64,128]{1,0:T(8,128)S(1)}, u32[]{:S(2)}, u32[]{:S(2)}) collective-permute-start(f32[64,128]{1,0:T(8,128)S(1)} %get-tuple-element.74), channel_id=1, source_target_pairs={{0,128},{64,192},{128,0},{192,64},{1,129},{65,193},{129,1},{193,65... | collective-permute-start | bytes 98312 | tf_op jit(solution)/shard_map/ppermute | solution.py:332
  95.0 5.5 %collective-permute-start.21 = (f32[64,128]{1,0:T(8,128)S(1)}, f32[64,128]{1,0:T(8,128)S(1)}, u32[]{:S(2)}, u32[]{:S(2)}) collective-permute-start(f32[64,128]{1,0:T(8,128)S(1)} %get-tuple-element.73), channel_id=1, source_target_pairs={{0,64},{64,0},{128,192},{192,128},{1,65},{65,1},{129,193},{193,129... | collective-permute-start | bytes 98312 | tf_op jit(solution)/shard_map/ppermute | solution.py:332

commit v11 on v7

--- a/solution.py
+++ b/solution.py
@@ -167,8 +167,8 @@
         copy.wait()
 
 
-def outer_product(left_ref, rt_far, outer, lcat, a_hi, a_lo, rt, sems):
-    copies = fetch([(rt_far.at[m], rt.at[m]) for m in range(4)], sems)
+def outer_product(left_ref, parts, right_all, outer, lcat, rt, a_hi, a_lo):
+    gather_right(parts, right_all)
     for quad in range(4):
         v = left_rows(left_ref, quad)
         for m in range(4):
@@ -176,8 +176,13 @@
             lcat[m, 0:128, quad * 128 : quad * 128 + 128] = hi
             lcat[m, 128:256, quad * 128 : quad * 128 + 128] = lo
             lcat[m, 256:384, quad * 128 : quad * 128 + 128] = hi
+    for e in range(16):
+        g, m = e // 4, e % 4
+        hi, lo = halves(right_rows(right_all, e).T)
+        rt[m, g * 128 : g * 128 + 128, 0:128] = hi
+        rt[m, g * 128 : g * 128 + 128, 128:256] = hi
+        rt[m, g * 128 : g * 128 + 128, 256:384] = lo
     for m in range(4):
-        copies[m].wait()
         outer[m] = matmul(rt[m], lcat[m])
     for block in range(8):
         h, g = block // 4, block % 4
@@ -190,11 +195,11 @@
                 a_lo[d, quad * 64 : quad * 64 + 64, block * 128 : block * 128 + 128] = lo
 
 
-def pair_kernel(
-    left_ref, bias_ref, rt_far, w_far, pair_ref, outer, lcat, a_hi, a_lo, rt, w_hl, w_ref, sems
-):
+def pair_kernel(left_ref, *refs):
+    parts, (bias_ref, w_far, pair_ref, right_all, outer, lcat, rt, a_hi, a_lo) = refs[:8], refs[8:17]
+    w_hl, w_ref, sems = refs[17:]
     (fetched,) = fetch([(w_far, w_ref)], sems)
-    outer_product(left_ref, rt_far, outer, lcat, a_hi, a_lo, rt, sems.at[pl.ds(1, 4)])
+    outer_product(left_ref, parts, right_all, outer, lcat, rt, a_hi, a_lo)
     fetched.wait()
     weights_by_class(w_ref, w_hl)
     for d in range(4):
@@ -205,12 +210,12 @@
             pair_ref[quad * 4 + d] = pair[quad * 64 : quad * 64 + 64]
 
 
-def tile_kernel(
-    left_ref, rt_far, cot_far, own_out, other_out, outer, lcat, a_hi, a_lo, rt, dw, cot_ref, sems
-):
+def tile_kernel(left_ref, *refs):
+    parts, (cot_far, own_out, other_out) = refs[:8], refs[8:11]
+    right_all, outer, lcat, rt, a_hi, a_lo, dw, cot_ref, sems = refs[11:]
     core = lax.axis_index("core")
     (fetched,) = fetch([(cot_far, cot_ref)], sems)
-    outer_product(left_ref, rt_far, outer, lcat, a_hi, a_lo, rt, sems.at[pl.ds(1, 4)])
+    outer_product(left_ref, parts, right_all, outer, lcat, rt, a_hi, a_lo)
     fetched.wait()
     for d in range(4):
         hi, lo = halves(jnp.concatenate([cot_ref[quad * 4 + d] for quad in range(4)], axis=0).T)
@@ -233,20 +238,14 @@
 
 
 def left_gradient_kernel(*refs):
-    parts, (hi_far, lo_far, own_out, other_out, rt) = refs[:8], refs[8:13]
-    right_all, r_hl, g_hi, g_lo, sems = refs[13:]
+    parts, (hi_far, lo_far, own_out, other_out, right_all, r_hl, g_hi, g_lo, sems) = refs[:8], refs[8:]
     copies = fetch_classes(hi_far, lo_far, g_hi, g_lo, sems)
     gather_right(parts, right_all)
     for e in range(16):
         g, m = e // 4, e % 4
-        v = right_rows(right_all, e)
-        hi, lo = halves(v)
+        hi, lo = halves(right_rows(right_all, e))
         r_hl[m, 0:128, g * 128 : g * 128 + 128] = hi
         r_hl[m, 128:256, g * 128 : g * 128 + 128] = lo
-        hi, lo = halves(v.T)
-        rt[m, g * 128 : g * 128 + 128, 0:128] = hi
-        rt[m, g * 128 : g * 128 + 128, 128:256] = hi
-        rt[m, g * 128 : g * 128 + 128, 256:384] = lo
     total = [None] * 4
     for m in range(4):
         copies[2 * m].wait()
@@ -420,10 +419,10 @@
     left, parts, g_hi, g_lo = lax.optimization_barrier((left, parts, g_hi, g_lo))
     left = exchange(left, ROW).reshape(512, 128)
     parts = parts + [swap_cores(part) for part in parts]
-    own_left, other_left, turned = call(
+    own_left, other_left = call(
         left_gradient_kernel,
         "left_gradient",
-        [((256, 128), f32), ((256, 128), f32), ((4, 512, 384), bf16)],
+        [((256, 128), f32), ((256, 128), f32)],
         [((2048, 128), f32), ((4, 256, 512), bf16)] + [((4, 512, 512), bf16)] * 2,
         52,
         step,
@@ -434,22 +433,24 @@
     got_left = swap_cores(other_left)
     left, own_left, got_left = lax.optimization_barrier((left, own_left, got_left))
     working = [
+        ((2048, 128), f32),
         ((4, 512, 512), f32),
         ((4, 384, 512), bf16),
+        ((4, 512, 384), bf16),
         ((4, 256, 1024), bf16),
         ((4, 256, 1024), bf16),
-        ((4, 512, 384), bf16),
     ]
     own, other = call(
         tile_kernel,
         "tile",
         [((16 * BWD, 128), f32)] * 2,
         working + [((8, 128, 128), f32), ((16, 64, 128), f32)],
-        53,
+        52,
         2 * step,
         left,
-        far=(turned, edge_incoming_sensitivity),
-        copies=5,
+        *parts,
+        far=(edge_incoming_sensitivity,),
+        copies=1,
     )
     got = swap_cores(other)
     sums = call(
@@ -476,9 +477,10 @@
         52,
         2 * step,
         left,
+        *parts,
         result_intercept.reshape(1, 128),
-        far=(turned, result_matrix),
-        copies=5,
+        far=(result_matrix,),
+        copies=1,
     )
     weight = back[:, :32].sum(axis=0).reshape(4, 8, 128).transpose(1, 0, 2)
     sent = jnp.concatenate(

time: 107 us -> 106 us (level)
  Pallas kernels: 31.7 us -> 29.4 us
  waiting for transfers between devices: 21.8 us -> 23.7 us
    pallas_call x9, Pallas kernels: 31.7 us -> 29.4 us  [call(): pl.pallas_call(kernel, out_shape=shapes, in_specs=[VMEM] * len(args) + [H...]
    all_to_all x4, waiting for transfers between devices: 9.1 us -> 10.4 us  [exchange(): return lax.all_to_all(array, axes, 0, 0, tiled=True)]
  transfers between devices with their start and end apart: 26 -> 26, of which waited for: 14 -> 14; matrix products, arithmetic and copies ran while one was open for 1% -> 1% of each run, Pallas kernels for 21% -> 20%
where the time goes in v11:
time: 106 us; the launch traced here: 105 us
  starting transfers between devices  48.8 us (46%)
  Pallas kernels  29.4 us (28%)
  waiting for transfers between devices  23.7 us (22%)
  other arithmetic  2.5 us (2%)
    pallas_call x9, Pallas kernels, call(): pl.pallas_call(kernel, out_shape=shapes, in_specs=[VMEM] * len(args) + [H...  29.4 us
    all_to_all x4, starting transfers between devices, exchange(): return lax.all_to_all(array, axes, 0, 0, tiled=True)  28 us
    ppermute x12, starting transfers between devices, from_peer(): return lax.ppermute(array, axis, [(i, i ^ apart) for i in range(4)])  17.7 us
    all_to_all x4, waiting for transfers between devices, exchange(): return lax.all_to_all(array, axes, 0, 0, tiled=True)  10.4 us
    ppermute x12, waiting for transfers between devices, from_peer(): return lax.ppermute(array, axis, [(i, i ^ apart) for i in range(4)])  9.7 us
    ppermute x10, waiting for transfers between devices, swap_cores(): return lax.ppermute(array, 'core', [(0, 1), (1, 0)])  3.64 us
    ppermute x10, starting transfers between devices, swap_cores(): return lax.ppermute(array, 'core', [(0, 1), (1, 0)])  3.16 us
  transfers between devices with their start and end apart: 26, of which 14 were waited for; matrix products, arithmetic and copies ran while one was open for 1% of the time, Pallas kernels for 20%

profile of v11, /device:TPU:32, one launch (start us, length us, event | category | flops | bytes accessed | tf_op | source)
XLA Modules:
  0.0 105.3 jit_solution(10348886975431966598)
XLA Ops:
  0.6 2.2 %project_right.1 = f32[64,128]{1,0:T(8,128)} custom-call(f32[256,256]{1,0:T(8,128)} %bitcast.31, f32[1,256]{1,0:T(1,128)} %bitcast.42, f32[1,256]{1,0:T(1,128)} %bitcast.55, f32[32,256]{1,0:T(8,128)} %bitcast.37, f32[1,32]{1,0:T(1,128)} %bitcast.57), custom_call_target="tpu_custom_call" | custom-call | flops 25165824 | bytes 329856 | tf_op jit(solution)/shard_map/project_right/pallas_call | solution.py:323
  2.9 1.9 %collective-permute-start.2 = (f32[64,128]{1,0:T(8,128)}, f32[64,128]{1,0:T(8,128)S(1)}, u32[]{:S(2)}, u32[]{:S(2)}) collective-permute-start(f32[64,128]{1,0:T(8,128)} %project_right.1), channel_id=1, source_target_pairs={{0,192},{64,128},{128,64},{192,0},{1,193},{65,129},{129,65},{193,1... | collective-permute-start | bytes 98312 | tf_op jit(solution)/shard_map/ppermute | solution.py:343
  4.8 2.3 %collective-permute-start.1 = (f32[64,128]{1,0:T(8,128)}, f32[64,128]{1,0:T(8,128)S(1)}, u32[]{:S(2)}, u32[]{:S(2)}) collective-permute-start(f32[64,128]{1,0:T(8,128)} %project_right.1), channel_id=1, source_target_pairs={{0,128},{64,192},{128,0},{192,64},{1,129},{65,193},{129,1},{193,65... | collective-permute-start | bytes 98312 | tf_op jit(solution)/shard_map/ppermute | solution.py:343
  7.6 2.3 %project_left.1 = f32[8,64,128]{2,1,0:T(8,128)} custom-call(f32[256,256]{1,0:T(8,128)} %bitcast.32, f32[1,256]{1,0:T(1,128)} %bitcast.43, f32[1,256]{1,0:T(1,128)} %bitcast.56, f32[32,256]{1,0:T(8,128)} %bitcast.40, f32[1,32]{1,0:T(1,128)} %bitcast.58), custom_call_target="tpu_custom_call" | custom-call | flops 25165824 | bytes 559232 | tf_op jit(solution)/shard_map/project_left/pallas_call | solution.py:323
  9.9 1.3 %collective-permute-done = f32[64,128]{1,0:T(8,128)S(1)} collective-permute-done((f32[64,128]{1,0:T(8,128)}, f32[64,128]{1,0:T(8,128)S(1)}, u32[]{:S(2)}, u32[]{:S(2)}) %collective-permute-start) | collective-permute-done | bytes 32800 | tf_op jit(solution)/shard_map/ppermute | solution.py:343
  11.2 9.4 %all-to-all-start = ((f32[8,64,128]{2,1,0:T(8,128)}), f32[8,64,128]{2,1,0:T(8,128)}, u32[]{:S(2)}, u32[]{:S(2)}) async-start(f32[8,64,128]{2,1,0:T(8,128)} %project_left.1), calls=%async_computation | async-start | bytes 524288 | tf_op jit(solution)/shard_map/all_to_all | solution.py:347
  20.5 0.8 pad_maximum_fusion.1.refs_0_
  21.3 2.8 %collective-permute-start.5 = (f32[4,64,128]{2,1,0:T(8,128)S(1)}, f32[4,64,128]{2,1,0:T(8,128)S(1)}, u32[]{:S(2)}, u32[]{:S(2)}) collective-permute-start(f32[4,64,128]{2,1,0:T(8,128)S(1)} %pad_maximum_fusion.1.refs_0_), channel_id=1, source_target_pairs={{0,48},{16,32},{32,16},{48,0},{1,49},{17,33},{33,17},{49,1},{2,50}... | collective-permute-start | bytes 393224 | tf_op jit(solution)/shard_map/ppermute | solution.py:343
  24.2 0.8 collective-permute-start.4
  25.5 5.6 %cotangent.1 = (bf16[4,512,512]{2,1,0:T(8,128)(2,1)}, bf16[4,512,512]{2,1,0:T(8,128)(2,1)}) custom-call(f32[1024,128]{1,0:T(8,128)} %refs_9_.1, f32[16,64,128]{2,1,0:T(8,128)} %refs_8_.1), custom_call_target="tpu_custom_call" | custom-call | flops 805306368 | bytes 5242880 | tf_op jit(solution)/shard_map/cotangent/pallas_call | solution.py:323
  31.1 2.2 %all-to-all-done = f32[8,64,128]{2,1,0:T(8,128)} async-done(((f32[8,64,128]{2,1,0:T(8,128)}), f32[8,64,128]{2,1,0:T(8,128)}, u32[]{:S(2)}, u32[]{:S(2)}) %all-to-all-start) | async-done | bytes 262176 | tf_op jit(solution)/shard_map/all_to_all | solution.py:347
  33.3 6.4 %all-to-all-start.1 = ((f32[32,16,128]{2,1,0:T(8,128)}), f32[32,16,128]{2,1,0:T(8,128)S(1)}, u32[]{:S(2)}, u32[]{:S(2)}) async-start(f32[32,16,128]{2,1,0:T(8,128)} %bitcast.7), calls=%async_computation.1 | async-start | bytes 524288 | tf_op jit(solution)/shard_map/all_to_all | solution.py:347
  41.8 3.1 %left_gradient.1 = (f32[256,128]{1,0:T(8,128)S(1)}, f32[256,128]{1,0:T(8,128)S(1)}) custom-call(f32[4,64,128]{2,1,0:T(8,128)S(1)} %pad_maximum_fusion.1.refs_0_, f32[4,64,128]{2,1,0:T(8,128)S(1)} %collective-permute-done.3.refs_1_, f32[4,64,128]{2,1,0:T(8,128)S(1)} %collective-permute-done.4.refs_2_, f32[4,64,128]{2,1,0:T(8,128)S(1)} %collective-permute-done.5.refs_3_, ...), custom_call_target="tpu_custom_call" | custom-call | flops 805306368 | bytes 5505024 | tf_op jit(solution)/shard_map/left_gradient/pallas_call | solution.py:323
  45.5 1.0 collective-permute-done.10
  46.5 3.2 %all-to-all-done.1 = f32[32,16,128]{2,1,0:T(8,128)S(1)} async-done(((f32[32,16,128]{2,1,0:T(8,128)}), f32[32,16,128]{2,1,0:T(8,128)S(1)}, u32[]{:S(2)}, u32[]{:S(2)}) %all-to-all-start.1) | async-done | bytes 262176 | tf_op jit(solution)/shard_map/all_to_all | solution.py:347
  49.7 4.9 %tile.1 = (f32[512,128]{1,0:T(8,128)S(1)}, f32[512,128]{1,0:T(8,128)S(1)}) custom-call(f32[512,128]{1,0:T(8,128)S(1)} %bitcast.34, f32[4,64,128]{2,1,0:T(8,128)S(1)} %pad_maximum_fusion.1.refs_0_, f32[4,64,128]{2,1,0:T(8,128)S(1)} %collective-permute-done.3.refs_1_, f32[4,64,128]{2,1,0:T(8,128)S(1)} %collective-permute-done.4.refs_2_, ...), custom_call_target="tpu_custom_call" | custom-call | flops 1610612736 | bytes 2359296 | tf_op jit(solution)/shard_map/tile/pallas_call | solution.py:323
  55.0 1.3 %collective-permute-done.11 = f32[512,128]{1,0:T(8,128)S(1)} collective-permute-done((f32[512,128]{1,0:T(8,128)S(1)}, f32[512,128]{1,0:T(8,128)S(1)}, u32[]{:S(2)}, u32[]{:S(2)}) %collective-permute-start.11) | collective-permute-done | bytes 262176 | tf_op jit(solution)/shard_map/ppermute | solution.py:339
  56.3 0.8 pad_maximum_fusion
  57.1 4.7 %all-to-all-start.2 = ((f32[16,64,128]{2,1,0:T(8,128)}), f32[16,64,128]{2,1,0:T(8,128)S(1)}, u32[]{:S(2)}, u32[]{:S(2)}) async-start(f32[16,64,128]{2,1,0:T(8,128)} %pad_maximum_fusion), calls=%async_computation.2 | async-start | bytes 1048576 | tf_op jit(solution)/shard_map/all_to_all | solution.py:347
  61.9 3.9 %right_gradient.1 = (f32[4,64,128]{2,1,0:T(8,128)S(1)}, f32[4,64,128]{2,1,0:T(8,128)S(1)}, f32[4,64,128]{2,1,0:T(8,128)S(1)}, f32[4,64,128]{2,1,0:T(8,128)S(1)},...) custom-call(f32[512,128]{1,0:T(8,128)S(1)} %bitcast.35, ...), custom_call_target="tpu_custom_call" | custom-call | flops 805306368 | bytes 5505024 | tf_op jit(solution)/shard_map/right_gradient/pallas_call | solution.py:323
  67.3 1.6 %collective-permute-start.14 = (f32[4,64,128]{2,1,0:T(8,128)S(1)}, f32[4,64,128]{2,1,0:T(8,128)S(1)}, u32[]{:S(2)}, u32[]{:S(2)}) collective-permute-start(f32[4,64,128]{2,1,0:T(8,128)S(1)} %add.28), channel_id=1, source_target_pairs={{0,16},{16,0},{32,48},{48,32},{1,17},{17,1},{33,49},{49,33},{2,18}... | collective-permute-start | bytes 393224 | tf_op jit(solution)/shard_map/ppermute | solution.py:343
  68.8 2.8 %collective-permute-start.16 = (f32[4,64,128]{2,1,0:T(8,128)S(1)}, f32[4,64,128]{2,1,0:T(8,128)S(1)}, u32[]{:S(2)}, u32[]{:S(2)}) collective-permute-start(f32[4,64,128]{2,1,0:T(8,128)S(1)} %add.29), channel_id=1, source_target_pairs={{0,32},{16,48},{32,0},{48,16},{1,33},{17,49},{33,1},{49,17},{2,34}... | collective-permute-start | bytes 393224 | tf_op jit(solution)/shard_map/ppermute | solution.py:343
  71.6 0.9 collective-permute-start.18
  72.5 5.6 %pair.1 = f32[16,64,128]{2,1,0:T(8,128)} custom-call(f32[512,128]{1,0:T(8,128)S(1)} %bitcast.36, f32[4,64,128]{2,1,0:T(8,128)S(1)} %pad_maximum_fusion.1.refs_0_, f32[4,64,128]{2,1,0:T(8,128)S(1)} %collective-permute-done.3.refs_1_, f32[4,64,128]{2,1,0:T(8,128)S(1)} %collective-permute-done.4.refs_2_, f32[4,64,128]{2,1,0:T(8,128)S(1)} %collective-permute-done.5.refs_3_, ...), custom_call_target="tpu_custom_call" | custom-call | flops 1610612736 | bytes 2359808 | tf_op jit(solution)/shard_map/pair/pallas_call | solution.py:323
  78.2 2.0 %collective-permute-done.16 = f32[4,64,128]{2,1,0:T(8,128)S(1)} collective-permute-done((f32[4,64,128]{2,1,0:T(8,128)S(1)}, f32[4,64,128]{2,1,0:T(8,128)S(1)}, u32[]{:S(2)}, u32[]{:S(2)}) %collective-permute-start.16) | collective-permute-done | bytes 131104 | tf_op jit(solution)/shard_map/ppermute | solution.py:343
  80.2 1.4 %collective-permute-done.18 = f32[4,64,128]{2,1,0:T(8,128)S(1)} collective-permute-done((f32[4,64,128]{2,1,0:T(8,128)S(1)}, f32[4,64,128]{2,1,0:T(8,128)S(1)}, u32[]{:S(2)}, u32[]{:S(2)}) %collective-permute-start.18) | collective-permute-done | bytes 131104 | tf_op jit(solution)/shard_map/ppermute | solution.py:343
  82.4 7.5 %all-to-all-start.3 = ((f32[8,72,128]{2,1,0:T(8,128)}), f32[8,72,128]{2,1,0:T(8,128)S(1)}, u32[]{:S(2)}, u32[]{:S(2)}) async-start(f32[8,72,128]{2,1,0:T(8,128)} %select_maximum_fusion), calls=%async_computation.3 | async-start | bytes 589824 | tf_op jit(solution)/shard_map/all_to_all | solution.py:347
  89.9 1.6 %collective-permute-start.21 = (f32[64,128]{1,0:T(8,128)S(1)}, f32[64,128]{1,0:T(8,128)S(1)}, u32[]{:S(2)}, u32[]{:S(2)}) collective-permute-start(f32[64,128]{1,0:T(8,128)S(1)} %get-tuple-element.73), channel_id=1, source_target_pairs={{0,192},{64,128},{128,64},{192,0},{1,193},{65,129},{129,65},{193,1... | collective-permute-start | bytes 98312 | tf_op jit(solution)/shard_map/ppermute | solution.py:343
  91.5 1.8 %collective-permute-start.20 = (f32[64,128]{1,0:T(8,128)S(1)}, f32[64,128]{1,0:T(8,128)S(1)}, u32[]{:S(2)}, u32[]{:S(2)}) collective-permute-start(f32[64,128]{1,0:T(8,128)S(1)} %get-tuple-element.74), channel_id=1, source_target_pairs={{0,128},{64,192},{128,0},{192,64},{1,129},{65,193},{129,1},{193,65... | collective-permute-start | bytes 98312 | tf_op jit(solution)/shard_map/ppermute | solution.py:343
  93.5 5.0 %collective-permute-done.21.d_ref = f32[64,128]{1,0:T(8,128)S(1)} collective-permute-done((f32[64,128]{1,0:T(8,128)S(1)}, f32[64,128]{1,0:T(8,128)S(1)}, u32[]{:S(2)}, u32[]{:S(2)}) %collective-permute-start.21) | collective-permute-done | bytes 32800 | tf_op jit(solution)/shard_map/ppermute | solution.py:343
  99.0 5.0 %all-to-all-done.3.col_ref = f32[8,72,128]{2,1,0:T(8,128)S(1)} async-done(((f32[8,72,128]{2,1,0:T(8,128)}), f32[8,72,128]{2,1,0:T(8,128)S(1)}, u32[]{:S(2)}, u32[]{:S(2)}) %all-to-all-start.3) | async-done | bytes 294944 | tf_op jit(solution)/shard_map/all_to_all | solution.py:347
  104.0 1.3 %finish.1 = (f32[256,256]{1,0:T(8,128)}, f32[4,128]{1,0:T(4,128)}) custom-call(f32[256,256]{1,0:T(8,128)S(1)} %bitcast.33, f32[1,256]{1,0:T(1,128)S(1)} %bitcast.44, f32[32,256]{1,0:T(8,128)S(1)} %bitcast.41, f32[256,256]{1,0:T(8,128)S(1)} %right.1.part_ref, f32[8,72,128]{2,1,0:T(8,128)S(1)} %all-to-all-done.3.col_ref), custom_call_target="tpu_custom_call" | custom-call | flops 25165824 | bytes 1117184 | tf_op jit(solution)/shard_map/finish/pallas_call | solution.py:323
  (52 shorter events, 7.2 us)
Async XLA Ops:
  2.9 7.0 %collective-permute-start.2 = (f32[64,128]{1,0:T(8,128)}, f32[64,128]{1,0:T(8,128)S(1)}, u32[]{:S(2)}, u32[]{:S(2)}) collective-permute-start(f32[64,128]{1,0:T(8,128)} %project_right.1), channel_id=1, source_target_pairs={{0,192},{64,128},{128,64},{192,0},{1,193},{65,129},{129,65},{193,1... | collective-permute-start | bytes 98312 | tf_op jit(solution)/shard_map/ppermute | solution.py:343
  4.8 5.1 %collective-permute-start.1 = (f32[64,128]{1,0:T(8,128)}, f32[64,128]{1,0:T(8,128)S(1)}, u32[]{:S(2)}, u32[]{:S(2)}) collective-permute-start(f32[64,128]{1,0:T(8,128)} %project_right.1), channel_id=1, source_target_pairs={{0,128},{64,192},{128,0},{192,64},{1,129},{65,193},{129,1},{193,65... | collective-permute-start | bytes 98312 | tf_op jit(solution)/shard_map/ppermute | solution.py:343
  7.1 4.1 %collective-permute-start = (f32[64,128]{1,0:T(8,128)}, f32[64,128]{1,0:T(8,128)S(1)}, u32[]{:S(2)}, u32[]{:S(2)}) collective-permute-start(f32[64,128]{1,0:T(8,128)} %project_right.1), channel_id=1, source_target_pairs={{0,64},{64,0},{128,192},{192,128},{1,65},{65,1},{129,193},{193,129... | collective-permute-start | bytes 98312 | tf_op jit(solution)/shard_map/ppermute | solution.py:343
  11.2 22.1 %all-to-all-start = ((f32[8,64,128]{2,1,0:T(8,128)}), f32[8,64,128]{2,1,0:T(8,128)}, u32[]{:S(2)}, u32[]{:S(2)}) async-start(f32[8,64,128]{2,1,0:T(8,128)} %project_left.1), calls=%async_computation | async-start | bytes 524288 | tf_op jit(solution)/shard_map/all_to_all | solution.py:347
  21.3 9.8 %collective-permute-start.5 = (f32[4,64,128]{2,1,0:T(8,128)S(1)}, f32[4,64,128]{2,1,0:T(8,128)S(1)}, u32[]{:S(2)}, u32[]{:S(2)}) collective-permute-start(f32[4,64,128]{2,1,0:T(8,128)S(1)} %pad_maximum_fusion.1.refs_0_), channel_id=1, source_target_pairs={{0,48},{16,32},{32,16},{48,0},{1,49},{17,33},{33,17},{49,1},{2,50}... | collective-permute-start | bytes 393224 | tf_op jit(solution)/shard_map/ppermute | solution.py:343
  24.2 7.0 %collective-permute-start.4 = (f32[4,64,128]{2,1,0:T(8,128)S(1)}, f32[4,64,128]{2,1,0:T(8,128)S(1)}, u32[]{:S(2)}, u32[]{:S(2)}) collective-permute-start(f32[4,64,128]{2,1,0:T(8,128)S(1)} %pad_maximum_fusion.1.refs_0_), channel_id=1, source_target_pairs={{0,32},{16,48},{32,0},{48,16},{1,33},{17,49},{33,1},{49,17},{2,34}... | collective-permute-start | bytes 393224 | tf_op jit(solution)/shard_map/ppermute | solution.py:343
  25.0 6.2 %collective-permute-start.3 = (f32[4,64,128]{2,1,0:T(8,128)S(1)}, f32[4,64,128]{2,1,0:T(8,128)S(1)}, u32[]{:S(2)}, u32[]{:S(2)}) collective-permute-start(f32[4,64,128]{2,1,0:T(8,128)S(1)} %pad_maximum_fusion.1.refs_0_), channel_id=1, source_target_pairs={{0,16},{16,0},{32,48},{48,32},{1,17},{17,1},{33,49},{49,33},{2,18}... | collective-permute-start | bytes 393224 | tf_op jit(solution)/shard_map/ppermute | solution.py:343
  33.3 16.4 %all-to-all-start.1 = ((f32[32,16,128]{2,1,0:T(8,128)}), f32[32,16,128]{2,1,0:T(8,128)S(1)}, u32[]{:S(2)}, u32[]{:S(2)}) async-start(f32[32,16,128]{2,1,0:T(8,128)} %bitcast.7), calls=%async_computation.1 | async-start | bytes 524288 | tf_op jit(solution)/shard_map/all_to_all | solution.py:347
  39.7 1.4 %collective-permute-start.6 = (f32[4,64,128]{2,1,0:T(8,128)S(1)}, f32[4,64,128]{2,1,0:T(8,128)S(1)}, u32[]{:S(2)}, u32[]{:S(2)}) collective-permute-start(f32[4,64,128]{2,1,0:T(8,128)S(1)} %pad_maximum_fusion.1.refs_0_), channel_id=1, source_target_pairs={{0,8},{8,0},{1,9},{9,1},{2,10},{10,2},{3,11},{11,3},{4,12},{12,4},... | collective-permute-start | bytes 393224 | tf_op jit(solution)/shard_map/ppermute | solution.py:339
  39.9 1.4 %collective-permute-start.7 = (f32[4,64,128]{2,1,0:T(8,128)S(1)}, f32[4,64,128]{2,1,0:T(8,128)S(1)}, u32[]{:S(2)}, u32[]{:S(2)}) collective-permute-start(f32[4,64,128]{2,1,0:T(8,128)S(1)} %collective-permute-done.3.refs_1_), channel_id=1, source_target_pairs={{0,8},{8,0},{1,9},{9,1},{2,10},{10,2},{3,11},{11,3},{4,12},{12,4},... | collective-permute-start | bytes 393224 | tf_op jit(solution)/shard_map/ppermute | solution.py:339
  40.3 1.3 %collective-permute-start.8 = (f32[4,64,128]{2,1,0:T(8,128)S(1)}, f32[4,64,128]{2,1,0:T(8,128)S(1)}, u32[]{:S(2)}, u32[]{:S(2)}) collective-permute-start(f32[4,64,128]{2,1,0:T(8,128)S(1)} %collective-permute-done.4.refs_2_), channel_id=1, source_target_pairs={{0,8},{8,0},{1,9},{9,1},{2,10},{10,2},{3,11},{11,3},{4,12},{12,4},... | collective-permute-start | bytes 393224 | tf_op jit(solution)/shard_map/ppermute | solution.py:339
  40.4 1.4 %collective-permute-start.9 = (f32[4,64,128]{2,1,0:T(8,128)S(1)}, f32[4,64,128]{2,1,0:T(8,128)S(1)}, u32[]{:S(2)}, u32[]{:S(2)}) collective-permute-start(f32[4,64,128]{2,1,0:T(8,128)S(1)} %collective-permute-done.5.refs_3_), channel_id=1, source_target_pairs={{0,8},{8,0},{1,9},{9,1},{2,10},{10,2},{3,11},{11,3},{4,12},{12,4},... | collective-permute-start | bytes 393224 | tf_op jit(solution)/shard_map/ppermute | solution.py:339
  44.9 1.6 %collective-permute-start.10 = (f32[256,128]{1,0:T(8,128)S(1)}, f32[256,128]{1,0:T(8,128)S(1)}, u32[]{:S(2)}, u32[]{:S(2)}) collective-permute-start(f32[256,128]{1,0:T(8,128)S(1)} %get-tuple-element.52), channel_id=1, source_target_pairs={{0,8},{8,0},{1,9},{9,1},{2,10},{10,2},{3,11},{11,3},{4,12},{12,4},... | collective-permute-start | bytes 393224 | tf_op jit(solution)/shard_map/ppermute | solution.py:339
  54.6 1.6 %collective-permute-start.11 = (f32[512,128]{1,0:T(8,128)S(1)}, f32[512,128]{1,0:T(8,128)S(1)}, u32[]{:S(2)}, u32[]{:S(2)}) collective-permute-start(f32[512,128]{1,0:T(8,128)S(1)} %get-tuple-element.55), channel_id=1, source_target_pairs={{0,8},{8,0},{1,9},{9,1},{2,10},{10,2},{3,11},{11,3},{4,12},{12,4},... | collective-permute-start | bytes 786440 | tf_op jit(solution)/shard_map/ppermute | solution.py:339
  57.1 24.5 %all-to-all-start.2 = ((f32[16,64,128]{2,1,0:T(8,128)}), f32[16,64,128]{2,1,0:T(8,128)S(1)}, u32[]{:S(2)}, u32[]{:S(2)}) async-start(f32[16,64,128]{2,1,0:T(8,128)} %pad_maximum_fusion), calls=%async_computation.2 | async-start | bytes 1048576 | tf_op jit(solution)/shard_map/all_to_all | solution.py:347
  61.9 10.6 %copy-start.4 = (f32[1024,128]{1,0:T(8,128)S(1)}, f32[1024,128]{1,0:T(8,128)}, u32[]{:S(2)}) copy-start(f32[1024,128]{1,0:T(8,128)} %refs_9_.1) | copy-start | bytes 1572868
  61.9 10.6 %copy-start.5 = (f32[128]{0:T(128)S(1)}, f32[128]{0:T(128)}, u32[]{:S(2)}) copy-start(f32[128]{0:T(128)} %param.18) | copy-start | bytes 1540
  65.8 1.4 %collective-permute-start.13 = (f32[4,64,128]{2,1,0:T(8,128)S(1)}, f32[4,64,128]{2,1,0:T(8,128)S(1)}, u32[]{:S(2)}, u32[]{:S(2)}) collective-permute-start(f32[4,64,128]{2,1,0:T(8,128)S(1)} %get-tuple-element.61), channel_id=1, source_target_pairs={{0,8},{8,0},{1,9},{9,1},{2,10},{10,2},{3,11},{11,3},{4,12},{12,4},... | collective-permute-start | bytes 393224 | tf_op jit(solution)/shard_map/ppermute | solution.py:339
  65.9 2.9 %collective-permute-start.15 = (f32[4,64,128]{2,1,0:T(8,128)S(1)}, f32[4,64,128]{2,1,0:T(8,128)S(1)}, u32[]{:S(2)}, u32[]{:S(2)}) collective-permute-start(f32[4,64,128]{2,1,0:T(8,128)S(1)} %get-tuple-element.63), channel_id=1, source_target_pairs={{0,8},{8,0},{1,9},{9,1},{2,10},{10,2},{3,11},{11,3},{4,12},{12,4},... | collective-permute-start | bytes 393224 | tf_op jit(solution)/shard_map/ppermute | solution.py:339
  66.4 5.2 %collective-permute-start.17 = (f32[4,64,128]{2,1,0:T(8,128)S(1)}, f32[4,64,128]{2,1,0:T(8,128)S(1)}, u32[]{:S(2)}, u32[]{:S(2)}) collective-permute-start(f32[4,64,128]{2,1,0:T(8,128)S(1)} %get-tuple-element.65), channel_id=1, source_target_pairs={{0,8},{8,0},{1,9},{9,1},{2,10},{10,2},{3,11},{11,3},{4,12},{12,4},... | collective-permute-start | bytes 393224 | tf_op jit(solution)/shard_map/ppermute | solution.py:339
  66.5 11.7 %collective-permute-start.12 = (f32[4,64,128]{2,1,0:T(8,128)S(1)}, f32[4,64,128]{2,1,0:T(8,128)S(1)}, u32[]{:S(2)}, u32[]{:S(2)}) collective-permute-start(f32[4,64,128]{2,1,0:T(8,128)S(1)} %get-tuple-element.59), channel_id=1, source_target_pairs={{0,8},{8,0},{1,9},{9,1},{2,10},{10,2},{3,11},{11,3},{4,12},{12,4},... | collective-permute-start | bytes 393224 | tf_op jit(solution)/shard_map/ppermute | solution.py:339
  67.3 10.9 %collective-permute-start.14 = (f32[4,64,128]{2,1,0:T(8,128)S(1)}, f32[4,64,128]{2,1,0:T(8,128)S(1)}, u32[]{:S(2)}, u32[]{:S(2)}) collective-permute-start(f32[4,64,128]{2,1,0:T(8,128)S(1)} %add.28), channel_id=1, source_target_pairs={{0,16},{16,0},{32,48},{48,32},{1,17},{17,1},{33,49},{49,33},{2,18}... | collective-permute-start | bytes 393224 | tf_op jit(solution)/shard_map/ppermute | solution.py:343
  68.8 11.4 %collective-permute-start.16 = (f32[4,64,128]{2,1,0:T(8,128)S(1)}, f32[4,64,128]{2,1,0:T(8,128)S(1)}, u32[]{:S(2)}, u32[]{:S(2)}) collective-permute-start(f32[4,64,128]{2,1,0:T(8,128)S(1)} %add.29), channel_id=1, source_target_pairs={{0,32},{16,48},{32,0},{48,16},{1,33},{17,49},{33,1},{49,17},{2,34}... | collective-permute-start | bytes 393224 | tf_op jit(solution)/shard_map/ppermute | solution.py:343
  71.6 10.0 %collective-permute-start.18 = (f32[4,64,128]{2,1,0:T(8,128)S(1)}, f32[4,64,128]{2,1,0:T(8,128)S(1)}, u32[]{:S(2)}, u32[]{:S(2)}) collective-permute-start(f32[4,64,128]{2,1,0:T(8,128)S(1)} %add.31), channel_id=1, source_target_pairs={{0,48},{16,32},{32,16},{48,0},{1,49},{17,33},{33,17},{49,1},{2,50}... | collective-permute-start | bytes 393224 | tf_op jit(solution)/shard_map/ppermute | solution.py:343
  78.1 20.4 %copy-start.1 = (f32[256,32]{0,1:T(8,128)S(1)}, f32[256,32]{0,1:T(8,128)}, u32[]{:S(2)}) copy-start(f32[256,32]{0,1:T(8,128)} %param.15) | copy-start | bytes 98308
  78.1 25.9 %copy-start = (f32[4,64,256]{2,1,0:T(8,128)S(1)}, f32[4,64,256]{2,1,0:T(8,128)}, u32[]{:S(2)}) copy-start(f32[4,64,256]{2,1,0:T(8,128)} %param.10) | copy-start | bytes 786436
  78.1 25.9 %copy-start.2 = (f32[256,32]{0,1:T(8,128)S(1)}, f32[256,32]{0,1:T(8,128)}, u32[]{:S(2)}) copy-start(f32[256,32]{0,1:T(8,128)} %param.13) | copy-start | bytes 98308
  78.1 25.8 %copy-start.3 = (f32[256]{0:T(256)S(1)}, f32[256]{0:T(256)}, u32[]{:S(2)}) copy-start(f32[256]{0:T(256)} %param.11) | copy-start | bytes 3076
  82.4 21.5 %all-to-all-start.3 = ((f32[8,72,128]{2,1,0:T(8,128)}), f32[8,72,128]{2,1,0:T(8,128)S(1)}, u32[]{:S(2)}, u32[]{:S(2)}) async-start(f32[8,72,128]{2,1,0:T(8,128)} %select_maximum_fusion), calls=%async_computation.3 | async-start | bytes 589824 | tf_op jit(solution)/shard_map/all_to_all | solution.py:347
  89.9 8.6 %collective-permute-start.21 = (f32[64,128]{1,0:T(8,128)S(1)}, f32[64,128]{1,0:T(8,128)S(1)}, u32[]{:S(2)}, u32[]{:S(2)}) collective-permute-start(f32[64,128]{1,0:T(8,128)S(1)} %get-tuple-element.73), channel_id=1, source_target_pairs={{0,192},{64,128},{128,64},{192,0},{1,193},{65,129},{129,65},{193,1... | collective-permute-start | bytes 98312 | tf_op jit(solution)/shard_map/ppermute | solution.py:343
  91.5 7.0 %collective-permute-start.20 = (f32[64,128]{1,0:T(8,128)S(1)}, f32[64,128]{1,0:T(8,128)S(1)}, u32[]{:S(2)}, u32[]{:S(2)}) collective-permute-start(f32[64,128]{1,0:T(8,128)S(1)} %get-tuple-element.74), channel_id=1, source_target_pairs={{0,128},{64,192},{128,0},{192,64},{1,129},{65,193},{129,1},{193,65... | collective-permute-start | bytes 98312 | tf_op jit(solution)/shard_map/ppermute | solution.py:343
  93.3 5.2 %collective-permute-start.19 = (f32[64,128]{1,0:T(8,128)S(1)}, f32[64,128]{1,0:T(8,128)S(1)}, u32[]{:S(2)}, u32[]{:S(2)}) collective-permute-start(f32[64,128]{1,0:T(8,128)S(1)} %get-tuple-element.75), channel_id=1, source_target_pairs={{0,64},{64,0},{128,192},{192,128},{1,65},{65,1},{129,193},{193,129... | collective-permute-start | bytes 98312 | tf_op jit(solution)/shard_map/ppermute | solution.py:343
